TPU v7x, 256 devices: a whole 4x4x8 slice. The times are simulated.
256 devices in a mesh: down: 64 (over x_lo, y, z), cross: 4 (over x_hi, core).
Axes of the slice: x: 4 (x_hi: 2, x_lo: 2; x = x_hi * 2 + x_lo), y: 4, z: 8, core: 2. Of those that a mesh axis runs over, the one named last changes fastest.
Arguments:
- positions: float32 [3, 128, 32, 128], P(None, 'down', 'cross'), may hold values from 0 to 1
- velocities: float32 [3, 128, 32, 128], P(None, 'down', 'cross'), may hold values from -3 to 3
- plastic_viscosity: float32 [128, 32, 128], P('down', 'cross'), may hold values from 0.3 to 3
- yield_stress: float32 [128, 32, 128], P('down', 'cross'), may hold values from 0.3 to 3
- counts: int32 [128, 32], P('down', 'cross'), may hold values from 1 to 128, as said below
- moving: int32 [128, 32], P('down', 'cross'), may hold values from 0 to 32, as said below
Outputs:
- new_positions: float32 [3, 128, 32, 128], P(None, 'down', 'cross')
- new_velocities: float32 [3, 128, 32, 128], P(None, 'down', 'cross')
Inputs may be any that keep to these rules, and one draw needn't show every extreme that they name: At least one; the first counts slots of a block are its live particles; 128 is reached in every draw. Never more than counts of the same block; counts minus moving of a block plus moving of the block just upslope is at most 128; both 32 and that bound of 128 are reached in every draw.
All inputs are finite; a program needn't handle non-finite values.
Results may differ from a plain program's by a relative error of at most 0.0001.
Values sent between devices are 32-bit elements; how exact they have to be, the bound alone decides.
A program may use at most 64 MiB of HBM per device.

v0:
```python
import math

import jax
import jax.numpy as jnp
from jax import lax
from jax.sharding import PartitionSpec as P

MOVE_MAX = 32
JACOBI = 2


KERNEL_NORM = 21.0 / (2.0 * math.pi)
PARTICLE_MASS = 0.02
REST_DENSITY = 1.0
STIFFNESS = 2.0
TIME_STEP = 0.05
GRAVITY_DOWN = 0.5
GRAVITY_UP = -1.0
NEIGHBOUR_STEPS = [(-1, -1), (-1, 0), (-1, 1), (0, -1), (0, 0), (0, 1), (1, -1), (1, 0), (1, 1)]


def with_halo(array, sides, width):
    for axis, dim in sides:
        count, length = (lax.axis_size(axis), array.shape[dim])
        up = [(i, (i + 1) % count) for i in range(count - 1)]
        down = [(j, i) for i, j in up]
        last = lax.slice_in_dim(array, length - width, length, axis=dim)
        initial = lax.slice_in_dim(array, 0, width, axis=dim)
        before = lax.ppermute(last, axis, up)
        after = lax.ppermute(initial, axis, down)
        array = jnp.concatenate([before, array, after], axis=dim)
    return array


def from_behind(block, axis, distance):
    devices = range(lax.axis_size(axis))
    route = [(i - distance, i) for i in devices if i - distance in devices]
    return lax.ppermute(block, axis, route)


def take_row(padded, lead_blocks, row_index, step_down, step_cross, col_count):
    whole_row = lax.dynamic_index_in_dim(
        padded, row_index + lead_blocks + step_down, axis=1, keepdims=False
    )
    return whole_row[:, lead_blocks + step_cross : lead_blocks + step_cross + col_count, :]


def separation(target, source, step_down, step_cross):
    offsets = (float(step_down), float(step_cross), 0.0)
    separations = [
        source[component][:, None, :] - target[component][:, :, None] + offsets[component]
        for component in range(3)
    ]
    distance = jnp.sqrt(
        separations[0] * separations[0]
        + separations[1] * separations[1]
        + separations[2] * separations[2]
    )
    falloff = jnp.maximum(1.0 - distance, 0.0)
    falloff_cubed = falloff * falloff * falloff
    weight = KERNEL_NORM * falloff_cubed * falloff * (4.0 * distance + 1.0)
    strength = 20.0 * KERNEL_NORM * falloff_cubed
    return (separations, weight, strength)


def density_pass(state_pad, lead_blocks, row_count, col_count):
    slot_count = state_pad.shape[3]

    def density_one_row(row_index):
        target = take_row(state_pad, lead_blocks, row_index, 0, 0, col_count)
        kernel_sum = jnp.zeros((col_count, slot_count), jnp.float32)
        strain = jnp.zeros((col_count, slot_count), jnp.float32)
        for step_down, step_cross in NEIGHBOUR_STEPS:
            source = take_row(state_pad, lead_blocks, row_index, step_down, step_cross, col_count)
            separations, weight, strength = separation(target, source, step_down, step_cross)
            present = source[6][:, None, :]
            spread = jnp.zeros_like(weight)
            for component in range(3):
                change = source[3 + component][:, None, :] - target[3 + component][:, :, None]
                spread = spread + change * change
            kernel_sum = kernel_sum + jnp.sum(present * weight, axis=2)
            strain = strain + jnp.sum(present * strength * spread, axis=2)
        density = PARTICLE_MASS * (kernel_sum + KERNEL_NORM * (1.0 - target[6]))
        return jnp.stack([density, PARTICLE_MASS * strain])

    result = lax.map(density_one_row, jnp.arange(row_count, dtype=jnp.int32))
    return jnp.moveaxis(result, 0, 1)


def force_pass(state_pad, state_lead, dens_pad, dens_lead, row_count, col_count):
    slot_count = state_pad.shape[3]

    def force_one_row(row_index):
        target = take_row(state_pad, state_lead, row_index, 0, 0, col_count)
        target_dens = take_row(dens_pad, dens_lead, row_index, 0, 0, col_count)
        totals = [jnp.zeros((col_count, slot_count), jnp.float32) for component in range(4)]
        for step_down, step_cross in NEIGHBOUR_STEPS:
            source = take_row(state_pad, state_lead, row_index, step_down, step_cross, col_count)
            source_dens = take_row(dens_pad, dens_lead, row_index, step_down, step_cross, col_count)
            separations, weight, strength = separation(target, source, step_down, step_cross)
            present = source[6][:, None, :]
            pressure_push = (
                present * (target_dens[1][:, :, None] + source_dens[1][:, None, :]) * strength
            )
            for component in range(3):
                totals[component] = totals[component] - jnp.sum(
                    pressure_push * separations[component], axis=2
                )
            coupling = (
                present
                * (target_dens[2][:, :, None] + source_dens[2][:, None, :])
                * strength
                * target_dens[0][:, :, None]
                * source_dens[0][:, None, :]
            )
            totals[3] = totals[3] + jnp.sum(coupling, axis=2)
        return PARTICLE_MASS * jnp.stack(totals)

    result = lax.map(force_one_row, jnp.arange(row_count, dtype=jnp.int32))
    return jnp.moveaxis(result, 0, 1)


def jacobi_pass(state_pad, state_lead, dens_pad, dens_lead, speed_pad, row_count, col_count):
    slot_count = state_pad.shape[3]

    def jacobi_one_row(row_index):
        target = take_row(state_pad, state_lead, row_index, 0, 0, col_count)
        target_dens = take_row(dens_pad, dens_lead, row_index, 0, 0, col_count)
        totals = [jnp.zeros((col_count, slot_count), jnp.float32) for component in range(3)]
        for step_down, step_cross in NEIGHBOUR_STEPS:
            source = take_row(state_pad, state_lead, row_index, step_down, step_cross, col_count)
            source_dens = take_row(dens_pad, dens_lead, row_index, step_down, step_cross, col_count)
            source_speed = take_row(speed_pad, 1, row_index, step_down, step_cross, col_count)
            separations, weight, strength = separation(target, source, step_down, step_cross)
            present = source[6][:, None, :]
            coupling = (
                present
                * (target_dens[2][:, :, None] + source_dens[2][:, None, :])
                * strength
                * target_dens[0][:, :, None]
                * source_dens[0][:, None, :]
            )
            for component in range(3):
                totals[component] = totals[component] + jnp.sum(
                    coupling * source_speed[component][:, None, :], axis=2
                )
        return PARTICLE_MASS * jnp.stack(totals)

    result = lax.map(jacobi_one_row, jnp.arange(row_count, dtype=jnp.int32))
    return jnp.moveaxis(result, 0, 1)


def pack_departing(field_six, keep_count, moving_count):
    offsets = lax.broadcasted_iota(jnp.int32, keep_count.shape + (MOVE_MAX,), 2)
    index = jnp.minimum(keep_count[..., None] + offsets, field_six.shape[3] - 1)
    taken = jnp.take_along_axis(
        field_six, jnp.broadcast_to(index[None], (6,) + index.shape), axis=3
    )
    shifted = jnp.concatenate([taken[:1] - 1.0, taken[1:]], axis=0)
    valid = (offsets < moving_count[..., None]).astype(jnp.float32)
    return shifted * valid[None]


def place_arrivals(field_six, keep_count, arrivals, arriving):
    slot_ids = lax.broadcasted_iota(jnp.int32, field_six.shape[1:], 2)
    relative = slot_ids - keep_count[..., None]
    index = jnp.clip(relative, 0, arrivals.shape[3] - 1)
    incoming = jnp.take_along_axis(
        arrivals, jnp.broadcast_to(index[None], (6,) + index.shape), axis=3
    )
    own_mask = (slot_ids < keep_count[..., None]).astype(jnp.float32)
    new_mask = ((relative >= 0) & (relative < arriving[..., None])).astype(jnp.float32)
    return field_six * own_mask[None] + incoming * new_mask[None]


def per_device(positions, velocities, plastic_viscosity, yield_stress, counts, moving):
    row_count, col_count, slot_count = positions.shape[1:]
    slot_ids = lax.broadcasted_iota(jnp.int32, (row_count, col_count, slot_count), 2)
    live = (slot_ids < counts[:, :, None]).astype(jnp.float32)
    state = jnp.concatenate([positions, velocities, live[None]], axis=0)
    state_pad = with_halo(state, (("down", 1), ("cross", 2)), 1)
    state_lead = 1
    density_strain = density_pass(state_pad, 1, row_count, col_count)
    inverse = 1.0 / density_strain[0]
    pressure = STIFFNESS * (density_strain[0] - REST_DENSITY) * inverse * inverse
    viscosity = plastic_viscosity + yield_stress / jnp.sqrt(1.0 + density_strain[1])
    dens_pad = with_halo(jnp.stack([inverse, pressure, viscosity]), (("down", 1), ("cross", 2)), 1)
    forces = force_pass(state_pad, state_lead, dens_pad, 1, row_count, col_count)
    gravity = jnp.array([GRAVITY_DOWN, 0.0, GRAVITY_UP], jnp.float32)[:, None, None, None]
    predicted = velocities + TIME_STEP * (forces[:3] + gravity)
    diagonal = 1.0 + TIME_STEP * forces[3]
    current = predicted
    for sweep_index in range(JACOBI):
        speed_pad = with_halo(current, (("down", 1), ("cross", 2)), 1)
        pulled = jacobi_pass(state_pad, state_lead, dens_pad, 1, speed_pad, row_count, col_count)
        current = (predicted + TIME_STEP * pulled) / diagonal
    moved_positions = positions + TIME_STEP * current
    field_six = jnp.concatenate([moved_positions, current], axis=0)
    keep_count = counts - moving
    packed = pack_departing(field_six, keep_count, moving)
    move_plane = jnp.broadcast_to(moving[-1].astype(jnp.float32)[:, None], (col_count, MOVE_MAX))
    edge_pack = jnp.concatenate([packed[:, -1], move_plane[None]], axis=0)
    received = from_behind(edge_pack, "down", 1)
    arrivals = jnp.concatenate([received[:6][:, None], packed[:, :-1]], axis=1)
    arriving = jnp.concatenate([received[6, :, 0].astype(jnp.int32)[None], moving[:-1]], axis=0)
    result = place_arrivals(field_six, keep_count, arrivals, arriving)
    return (result[:3], result[3:])


def solution(mesh):
    return jax.shard_map(
        per_device,
        mesh=mesh,
        in_specs=(
            P(None, "down", "cross", None),
            P(None, "down", "cross", None),
            P("down", "cross", None),
            P("down", "cross", None),
            P("down", "cross"),
            P("down", "cross"),
        ),
        out_specs=(P(None, "down", "cross", None), P(None, "down", "cross", None)),
        check_vma=False,
    )
```

profile of v0, /device:TPU:3, one launch (start us, length us, event | category | flops | bytes accessed | tf_op | source)
XLA Modules:
  0.0 359.2 jit_solution(17511111223297506983)
XLA Ops:
  2.2 3.5 collective-permute-start
  5.8 8.3 %collective-permute-start.1 = (f32[7,1,8,128]{3,2,0,1:T(8,128)S(1)}, f32[7,1,8,128]{3,2,0,1:T(8,128)S(1)}, u32[]{:S(2)}, u32[]{:S(2)}) collective-permute-start(f32[7,1,8,128]{3,2,0,1:T(8,128)S(1)} %get-tuple-element.983), channel_id=1, source_target_pairs={{4,0},{8,4},{12,8},{16,12},{20,16},{24,20},{28,24},{32,28},{36,32}... | collective-permute-start | bytes 86024 | tf_op jit(solution)/shard_map/ppermute | solution.py:30
  15.1 5.5 %collective-permute-start.2 = (f32[7,4,1,128]{3,2,0,1:T(1,128)S(1)}, f32[7,4,1,128]{3,2,0,1:T(1,128)S(1)}, u32[]{:S(2)}, u32[]{:S(2)}) collective-permute-start(f32[7,4,1,128]{3,2,0,1:T(1,128)S(1)} %get-tuple-element.980), channel_id=1, source_target_pairs={{0,1},{1,2},{2,3},{4,5},{5,6},{6,7},{8,9},{9,10},{10,11},{12,13},{... | collective-permute-start | bytes 43016 | tf_op jit(solution)/shard_map/ppermute | solution.py:29
  20.5 1.9 collective-permute-start.3
  22.5 4.6 %collective-permute-done.3 = f32[7,4,1,128]{3,2,0,1:T(1,128)S(1)} collective-permute-done((f32[7,4,1,128]{3,2,0,1:T(1,128)S(1)}, f32[7,4,1,128]{3,2,0,1:T(1,128)S(1)}, u32[]{:S(2)}, u32[]{:S(2)}) %collective-permute-start.3) | collective-permute-done | bytes 14368 | tf_op jit(solution)/shard_map/ppermute | solution.py:30
  27.2 34.0 %while.56 = (s32[]{:T(128)}, f32[2,2,8,128]{3,2,0,1:T(8,128)S(1)}, s32[2]{0:T(128)S(1)}, f32[7,4,10,128]{3,2,0,1:T(8,128)S(1)}, s32[]{:T(128)}, /*index=5*/s32[]...) while((s32[]{:T(128)}, f32[2,2,8,128]{3,2,0,1:T(8,128)S(1)}, s32[2]{0:T(128)S(1)}, ...), condition=%wide.region_19.20_spmd, body=%wide.region_0.19_spmd.sunk | while | flops 36976652 | bytes 1448191 | solution.py:86
  61.2 1.9 collective-permute-start.4
  63.1 8.8 %collective-permute-start.5 = (f32[3,1,8,128]{3,2,1,0:T(8,128)S(1)}, f32[3,1,8,128]{3,2,1,0:T(8,128)S(1)}, u32[]{:S(2)}, u32[]{:S(2)}) collective-permute-start(f32[3,1,8,128]{3,2,1,0:T(8,128)S(1)} %get-tuple-element.999), channel_id=1, source_target_pairs={{4,0},{8,4},{12,8},{16,12},{20,16},{24,20},{28,24},{32,28},{36,32}... | collective-permute-start | bytes 36872 | tf_op jit(solution)/shard_map/ppermute | solution.py:30
  72.7 2.2 collective-permute-start.6
  74.9 2.3 collective-permute-start.7
  77.3 4.0 %collective-permute-done.7 = f32[3,4,1,128]{3,2,1,0:T(1,128)S(1)} collective-permute-done((f32[3,4,1,128]{3,2,1,0:T(1,128)S(1)}, f32[3,4,1,128]{3,2,1,0:T(1,128)S(1)}, u32[]{:S(2)}, u32[]{:S(2)}) %collective-permute-start.7) | collective-permute-done | bytes 6176 | tf_op jit(solution)/shard_map/ppermute | solution.py:30
  81.4 39.3 %while.57 = (s32[]{:T(128)}, f32[2,4,8,128]{3,2,0,1:T(8,128)S(1)}, s32[2]{0:T(128)S(1)}, f32[7,4,10,128]{3,2,0,1:T(8,128)S(1)}, f32[3,4,10,128]{3,2,0,1:T(8,128)...) while((s32[]{:T(128)}, f32[2,4,8,128]{3,2,0,1:T(8,128)S(1)}, ...), condition=%wide.region_57.58_spmd, body=%wide.region_20.57_spmd.sunk | while | flops 34618380 | bytes 1597715 | solution.py:119
  98.5 2.5 multiply_reduce_fusion.131
  118.2 2.5 multiply_reduce_fusion.131
  122.8 8.7 %collective-permute-start.9 = (f32[3,1,8,128]{3,2,1,0:T(8,128)S(1)}, f32[3,1,8,128]{3,2,1,0:T(8,128)S(1)}, u32[]{:S(2)}, u32[]{:S(2)}) collective-permute-start(f32[3,1,8,128]{3,2,1,0:T(8,128)S(1)} %get-tuple-element.997), channel_id=1, source_target_pairs={{4,0},{8,4},{12,8},{16,12},{20,16},{24,20},{28,24},{32,28},{36,32}... | collective-permute-start | bytes 36872 | tf_op jit(solution)/shard_map/ppermute | solution.py:30
  132.4 2.2 collective-permute-start.10
  134.6 2.3 collective-permute-start.11
  137.0 4.1 %collective-permute-done.11 = f32[3,4,1,128]{3,2,1,0:T(1,128)S(1)} collective-permute-done((f32[3,4,1,128]{3,2,1,0:T(1,128)S(1)}, f32[3,4,1,128]{3,2,1,0:T(1,128)S(1)}, u32[]{:S(2)}, u32[]{:S(2)}) %collective-permute-start.11) | collective-permute-done | bytes 6176 | tf_op jit(solution)/shard_map/ppermute | solution.py:30
  141.1 34.6 %while.58 = (s32[]{:T(128)}, f32[2,3,8,128]{3,2,0,1:T(8,128)S(1)}, s32[2]{0:T(128)S(1)}, f32[7,4,10,128]{3,2,0,1:T(8,128)S(1)}, f32[3,4,10,128]{3,2,0,1:T(8,128)...) while((s32[]{:T(128)}, f32[2,3,8,128]{3,2,0,1:T(8,128)S(1)}, ...), condition=%wide.region_86.87_spmd, body=%wide.region_58.86_spmd.sunk | while | flops 29890572 | bytes 1796379 | solution.py:149
  150.6 2.0 multiply_reduce_fusion.141
  167.9 2.0 multiply_reduce_fusion.141
  175.8 1.9 collective-permute-start.12
  177.7 8.7 %collective-permute-start.13 = (f32[3,1,8,128]{3,2,1,0:T(8,128)S(1)}, f32[3,1,8,128]{3,2,1,0:T(8,128)S(1)}, u32[]{:S(2)}, u32[]{:S(2)}) collective-permute-start(f32[3,1,8,128]{3,2,1,0:T(8,128)S(1)} %get-tuple-element.995), channel_id=1, source_target_pairs={{4,0},{8,4},{12,8},{16,12},{20,16},{24,20},{28,24},{32,28},{36,32}... | collective-permute-start | bytes 36872 | tf_op jit(solution)/shard_map/ppermute | solution.py:30
  187.3 2.2 collective-permute-start.14
  189.5 2.4 collective-permute-start.15
  192.0 4.0 %collective-permute-done.15 = f32[3,4,1,128]{3,2,1,0:T(1,128)S(1)} collective-permute-done((f32[3,4,1,128]{3,2,1,0:T(1,128)S(1)}, f32[3,4,1,128]{3,2,1,0:T(1,128)S(1)}, u32[]{:S(2)}, u32[]{:S(2)}) %collective-permute-start.15) | collective-permute-done | bytes 6176 | tf_op jit(solution)/shard_map/ppermute | solution.py:30
  196.0 34.6 %while.59 = (s32[]{:T(128)}, f32[2,3,8,128]{3,2,0,1:T(8,128)S(1)}, s32[2]{0:T(128)S(1)}, f32[7,4,10,128]{3,2,0,1:T(8,128)S(1)}, f32[3,4,10,128]{3,2,0,1:T(8,128)...) while((s32[]{:T(128)}, f32[2,3,8,128]{3,2,0,1:T(8,128)S(1)}, ...), condition=%wide.region_115.116_spmd, body=%wide.region_87.115_spmd.sunk | while | flops 29890572 | bytes 1796379 | solution.py:149
  205.5 2.0 multiply_reduce_fusion.149
  222.8 2.0 multiply_reduce_fusion.149
  230.7 23.3 %gather_fusion = f32[3072]{0:T(1024)S(1)} fusion(f32[6,2,8,128]{3,2,1,0:T(8,128)S(1)} %pad_maximum_fusion.5, s32[3072]{0:T(1024)S(1)} %reshape.2553), kind=kCustom, calls=%fused_computation | custom fusion | bytes 73728 | tf_op jit(solution)/shard_map/jit(take_along_axis)/gather | solution.py:156
  256.2 8.0 %collective-permute-done.16 = f32[7,8,32]{2,1,0:T(8,128)S(1)} collective-permute-done((f32[7,8,32]{2,1,0:T(8,128)S(1)}, f32[7,8,32]{2,1,0:T(8,128)S(1)}, u32[]{:S(2)}, u32[]{:S(2)}) %collective-permute-start.16) | collective-permute-done | bytes 7200 | tf_op jit(solution)/shard_map/ppermute | solution.py:38
  264.4 94.1 %gather_fusion.1 = f32[12288]{0:T(1024)S(1)} fusion(f32[6,2,8,32]{3,2,1,0:T(8,128)S(1)} %pad_maximum_fusion.6, s32[12288]{0:T(1024)S(1)} %bitcast.848), kind=kCustom, calls=%fused_computation.1 | custom fusion | bytes 294912 | tf_op jit(solution)/shard_map/jit(take_along_axis)/gather | solution.py:168
  (257 shorter events, 102.3 us)
Async XLA Ops:
  0.6 21.8 %copy-start.5 = (s32[2,8]{1,0:T(2,128)S(1)}, s32[2,8]{1,0:T(2,128)}, u32[]{:S(2)}) copy-start(s32[2,8]{1,0:T(2,128)} %param.19) | copy-start | bytes 196
  0.6 14.4 %copy-start = (f32[3,2,8,128]{3,2,1,0:T(8,128)S(1)}, f32[3,2,8,128]{3,2,1,0:T(8,128)}, u32[]{:S(2)}) copy-start(f32[3,2,8,128]{3,2,1,0:T(8,128)} %param.15) | copy-start | bytes 73732
  0.7 14.4 %copy-start.1 = (f32[3,2,8,128]{3,2,1,0:T(8,128)S(1)}, f32[3,2,8,128]{3,2,1,0:T(8,128)}, u32[]{:S(2)}) copy-start(f32[3,2,8,128]{3,2,1,0:T(8,128)} %param.16) | copy-start | bytes 73732
  0.7 21.8 %copy-start.2 = (s32[2,8]{1,0:T(2,128)S(1)}, s32[2,8]{1,0:T(2,128)}, u32[]{:S(2)}) copy-start(s32[2,8]{1,0:T(2,128)} %param.20) | copy-start | bytes 196
  2.2 11.8 %collective-permute-start = (f32[7,1,8,128]{3,2,0,1:T(8,128)S(1)}, f32[7,1,8,128]{3,2,0,1:T(8,128)S(1)}, u32[]{:S(2)}, u32[]{:S(2)}) collective-permute-start(f32[7,1,8,128]{3,2,0,1:T(8,128)S(1)} %get-tuple-element.982), channel_id=1, source_target_pairs={{0,4},{4,8},{8,12},{12,16},{16,20},{20,24},{24,28},{28,32},{32,36}... | collective-permute-start | bytes 86024 | tf_op jit(solution)/shard_map/ppermute | solution.py:29
  5.8 9.3 %collective-permute-start.1 = (f32[7,1,8,128]{3,2,0,1:T(8,128)S(1)}, f32[7,1,8,128]{3,2,0,1:T(8,128)S(1)}, u32[]{:S(2)}, u32[]{:S(2)}) collective-permute-start(f32[7,1,8,128]{3,2,0,1:T(8,128)S(1)} %get-tuple-element.983), channel_id=1, source_target_pairs={{4,0},{8,4},{12,8},{16,12},{20,16},{24,20},{28,24},{32,28},{36,32}... | collective-permute-start | bytes 86024 | tf_op jit(solution)/shard_map/ppermute | solution.py:30
  15.1 7.4 %collective-permute-start.2 = (f32[7,4,1,128]{3,2,0,1:T(1,128)S(1)}, f32[7,4,1,128]{3,2,0,1:T(1,128)S(1)}, u32[]{:S(2)}, u32[]{:S(2)}) collective-permute-start(f32[7,4,1,128]{3,2,0,1:T(1,128)S(1)} %get-tuple-element.980), channel_id=1, source_target_pairs={{0,1},{1,2},{2,3},{4,5},{5,6},{6,7},{8,9},{9,10},{10,11},{12,13},{... | collective-permute-start | bytes 43016 | tf_op jit(solution)/shard_map/ppermute | solution.py:29
  20.5 6.5 %collective-permute-start.3 = (f32[7,4,1,128]{3,2,0,1:T(1,128)S(1)}, f32[7,4,1,128]{3,2,0,1:T(1,128)S(1)}, u32[]{:S(2)}, u32[]{:S(2)}) collective-permute-start(f32[7,4,1,128]{3,2,0,1:T(1,128)S(1)} %get-tuple-element.981), channel_id=1, source_target_pairs={{1,0},{2,1},{3,2},{5,4},{6,5},{7,6},{9,8},{10,9},{11,10},{13,12},{... | collective-permute-start | bytes 43016 | tf_op jit(solution)/shard_map/ppermute | solution.py:30
  27.1 34.0 %copy-start.3 = (f32[2,8,128]{2,1,0:T(8,128)S(1)}, f32[2,8,128]{2,1,0:T(8,128)}, u32[]{:S(2)}) copy-start(f32[2,8,128]{2,1,0:T(8,128)} %param.17) | copy-start | bytes 24580
  27.1 34.0 %copy-start.4 = (f32[2,8,128]{2,1,0:T(8,128)S(1)}, f32[2,8,128]{2,1,0:T(8,128)}, u32[]{:S(2)}) copy-start(f32[2,8,128]{2,1,0:T(8,128)} %param.18) | copy-start | bytes 24580
  61.2 10.8 %collective-permute-start.4 = (f32[3,1,8,128]{3,2,1,0:T(8,128)S(1)}, f32[3,1,8,128]{3,2,1,0:T(8,128)S(1)}, u32[]{:S(2)}, u32[]{:S(2)}) collective-permute-start(f32[3,1,8,128]{3,2,1,0:T(8,128)S(1)} %get-tuple-element.998), channel_id=1, source_target_pairs={{0,4},{4,8},{8,12},{12,16},{16,20},{20,24},{24,28},{28,32},{32,36}... | collective-permute-start | bytes 36872 | tf_op jit(solution)/shard_map/ppermute | solution.py:29
  63.1 9.6 %collective-permute-start.5 = (f32[3,1,8,128]{3,2,1,0:T(8,128)S(1)}, f32[3,1,8,128]{3,2,1,0:T(8,128)S(1)}, u32[]{:S(2)}, u32[]{:S(2)}) collective-permute-start(f32[3,1,8,128]{3,2,1,0:T(8,128)S(1)} %get-tuple-element.999), channel_id=1, source_target_pairs={{4,0},{8,4},{12,8},{16,12},{20,16},{24,20},{28,24},{32,28},{36,32}... | collective-permute-start | bytes 36872 | tf_op jit(solution)/shard_map/ppermute | solution.py:30
  72.7 4.6 %collective-permute-start.6 = (f32[3,4,1,128]{3,2,1,0:T(1,128)S(1)}, f32[3,4,1,128]{3,2,1,0:T(1,128)S(1)}, u32[]{:S(2)}, u32[]{:S(2)}) collective-permute-start(f32[3,4,1,128]{3,2,1,0:T(1,128)S(1)} %get-tuple-element.992), channel_id=1, source_target_pairs={{0,1},{1,2},{2,3},{4,5},{5,6},{6,7},{8,9},{9,10},{10,11},{12,13},{... | collective-permute-start | bytes 18440 | tf_op jit(solution)/shard_map/ppermute | solution.py:29
  74.9 6.5 %collective-permute-start.7 = (f32[3,4,1,128]{3,2,1,0:T(1,128)S(1)}, f32[3,4,1,128]{3,2,1,0:T(1,128)S(1)}, u32[]{:S(2)}, u32[]{:S(2)}) collective-permute-start(f32[3,4,1,128]{3,2,1,0:T(1,128)S(1)} %get-tuple-element.993), channel_id=1, source_target_pairs={{1,0},{2,1},{3,2},{5,4},{6,5},{7,6},{9,8},{10,9},{11,10},{13,12},{... | collective-permute-start | bytes 18440 | tf_op jit(solution)/shard_map/ppermute | solution.py:30
  81.4 39.4 %copy-start.6 = (f32[3]{0:T(128)S(1)}, f32[3]{0:T(128)}, u32[]{:S(2)}) copy-start(f32[3]{0:T(128)} %constant.593.clone) | copy-start | bytes 40
  120.9 10.7 %collective-permute-start.8 = (f32[3,1,8,128]{3,2,1,0:T(8,128)S(1)}, f32[3,1,8,128]{3,2,1,0:T(8,128)S(1)}, u32[]{:S(2)}, u32[]{:S(2)}) collective-permute-start(f32[3,1,8,128]{3,2,1,0:T(8,128)S(1)} %get-tuple-element.996), channel_id=1, source_target_pairs={{0,4},{4,8},{8,12},{12,16},{16,20},{20,24},{24,28},{28,32},{32,36}... | collective-permute-start | bytes 36872 | tf_op jit(solution)/shard_map/ppermute | solution.py:29
  122.8 9.6 %collective-permute-start.9 = (f32[3,1,8,128]{3,2,1,0:T(8,128)S(1)}, f32[3,1,8,128]{3,2,1,0:T(8,128)S(1)}, u32[]{:S(2)}, u32[]{:S(2)}) collective-permute-start(f32[3,1,8,128]{3,2,1,0:T(8,128)S(1)} %get-tuple-element.997), channel_id=1, source_target_pairs={{4,0},{8,4},{12,8},{16,12},{20,16},{24,20},{28,24},{32,28},{36,32}... | collective-permute-start | bytes 36872 | tf_op jit(solution)/shard_map/ppermute | solution.py:30
  132.4 4.6 %collective-permute-start.10 = (f32[3,4,1,128]{3,2,1,0:T(1,128)S(1)}, f32[3,4,1,128]{3,2,1,0:T(1,128)S(1)}, u32[]{:S(2)}, u32[]{:S(2)}) collective-permute-start(f32[3,4,1,128]{3,2,1,0:T(1,128)S(1)} %get-tuple-element.990), channel_id=1, source_target_pairs={{0,1},{1,2},{2,3},{4,5},{5,6},{6,7},{8,9},{9,10},{10,11},{12,13},{... | collective-permute-start | bytes 18440 | tf_op jit(solution)/shard_map/ppermute | solution.py:29
  134.6 6.5 %collective-permute-start.11 = (f32[3,4,1,128]{3,2,1,0:T(1,128)S(1)}, f32[3,4,1,128]{3,2,1,0:T(1,128)S(1)}, u32[]{:S(2)}, u32[]{:S(2)}) collective-permute-start(f32[3,4,1,128]{3,2,1,0:T(1,128)S(1)} %get-tuple-element.991), channel_id=1, source_target_pairs={{1,0},{2,1},{3,2},{5,4},{6,5},{7,6},{9,8},{10,9},{11,10},{13,12},{... | collective-permute-start | bytes 18440 | tf_op jit(solution)/shard_map/ppermute | solution.py:30
  175.8 10.8 %collective-permute-start.12 = (f32[3,1,8,128]{3,2,1,0:T(8,128)S(1)}, f32[3,1,8,128]{3,2,1,0:T(8,128)S(1)}, u32[]{:S(2)}, u32[]{:S(2)}) collective-permute-start(f32[3,1,8,128]{3,2,1,0:T(8,128)S(1)} %get-tuple-element.994), channel_id=1, source_target_pairs={{0,4},{4,8},{8,12},{12,16},{16,20},{20,24},{24,28},{28,32},{32,36}... | collective-permute-start | bytes 36872 | tf_op jit(solution)/shard_map/ppermute | solution.py:29
  177.7 9.6 %collective-permute-start.13 = (f32[3,1,8,128]{3,2,1,0:T(8,128)S(1)}, f32[3,1,8,128]{3,2,1,0:T(8,128)S(1)}, u32[]{:S(2)}, u32[]{:S(2)}) collective-permute-start(f32[3,1,8,128]{3,2,1,0:T(8,128)S(1)} %get-tuple-element.995), channel_id=1, source_target_pairs={{4,0},{8,4},{12,8},{16,12},{20,16},{24,20},{28,24},{32,28},{36,32}... | collective-permute-start | bytes 36872 | tf_op jit(solution)/shard_map/ppermute | solution.py:30
  187.3 4.7 %collective-permute-start.14 = (f32[3,4,1,128]{3,2,1,0:T(1,128)S(1)}, f32[3,4,1,128]{3,2,1,0:T(1,128)S(1)}, u32[]{:S(2)}, u32[]{:S(2)}) collective-permute-start(f32[3,4,1,128]{3,2,1,0:T(1,128)S(1)} %get-tuple-element.988), channel_id=1, source_target_pairs={{0,1},{1,2},{2,3},{4,5},{5,6},{6,7},{8,9},{9,10},{10,11},{12,13},{... | collective-permute-start | bytes 18440 | tf_op jit(solution)/shard_map/ppermute | solution.py:29
  189.5 6.5 %collective-permute-start.15 = (f32[3,4,1,128]{3,2,1,0:T(1,128)S(1)}, f32[3,4,1,128]{3,2,1,0:T(1,128)S(1)}, u32[]{:S(2)}, u32[]{:S(2)}) collective-permute-start(f32[3,4,1,128]{3,2,1,0:T(1,128)S(1)} %get-tuple-element.989), channel_id=1, source_target_pairs={{1,0},{2,1},{3,2},{5,4},{6,5},{7,6},{9,8},{10,9},{11,10},{13,12},{... | collective-permute-start | bytes 18440 | tf_op jit(solution)/shard_map/ppermute | solution.py:30
  254.2 10.0 %collective-permute-start.16 = (f32[7,8,32]{2,1,0:T(8,128)S(1)}, f32[7,8,32]{2,1,0:T(8,128)S(1)}, u32[]{:S(2)}, u32[]{:S(2)}) collective-permute-start(f32[7,8,32]{2,1,0:T(8,128)S(1)} %pad_maximum_fusion.7), channel_id=1, source_target_pairs={{0,4},{4,8},{8,12},{12,16},{16,20},{20,24},{24,28},{28,32},{32,36}... | collective-permute-start | bytes 21512 | tf_op jit(solution)/shard_map/ppermute | solution.py:38
where the time goes:
time: 360 us; the launch traced here: 359 us
  local copies, waits for them, and re-layouts  124 us (34%)
  other arithmetic  102 us (28%)
  starting transfers between devices  66.7 us (19%)
  loops' own time  37.6 us (10%)
  waiting for transfers between devices  27.8 us (8%)
    gather x1, local copies, waits for them, and re-layouts, place_arrivals(): jnp.take_along_axis(arrivals, jnp.broadcast_to(index[None], (6,) + index....  94.1 us
    reduce_sum x32, other arithmetic, jacobi_one_row(): jnp.sum(coupling * source_speed[component][:, None, :], axis=2)  47.4 us
    ppermute x8, starting transfers between devices, with_halo(): after = lax.ppermute(initial, axis, down)  43.5 us
    reduce_sum x16, other arithmetic, force_one_row(): jnp.sum(pressure_push * separations[component], axis=2)  28.5 us
    gather x3, local copies, waits for them, and re-layouts, pack_departing(): jnp.take_along_axis(field_six, jnp.broadcast_to(index[None], (6,) + index...  23.4 us
    reduce_sum x16, other arithmetic, density_one_row(): kernel_sum = kernel_sum + jnp.sum(present * weight, axis=2)  23.2 us
    ppermute x8, starting transfers between devices, with_halo(): before = lax.ppermute(last, axis, up)  21.3 us
    ppermute x8, waiting for transfers between devices, with_halo(): after = lax.ppermute(initial, axis, down)  19.8 us
  transfers between devices with their start and end apart: 17, of which 9 were waited for; matrix products, arithmetic and copies ran while one was open for 0% of the time, Pallas kernels for 0%

commit v1 on v0

--- a/solution.py
+++ b/solution.py
@@ -150,27 +150,35 @@
     return jnp.moveaxis(result, 0, 1)
 
 
-def pack_departing(field_six, keep_count, moving_count):
-    offsets = lax.broadcasted_iota(jnp.int32, keep_count.shape + (MOVE_MAX,), 2)
-    index = jnp.minimum(keep_count[..., None] + offsets, field_six.shape[3] - 1)
-    taken = jnp.take_along_axis(
-        field_six, jnp.broadcast_to(index[None], (6,) + index.shape), axis=3
-    )
-    shifted = jnp.concatenate([taken[:1] - 1.0, taken[1:]], axis=0)
-    valid = (offsets < moving_count[..., None]).astype(jnp.float32)
-    return shifted * valid[None]
-
-
-def place_arrivals(field_six, keep_count, arrivals, arriving):
+def shift_lanes(field, distance):
+    slot_count = field.shape[-1]
+    step = 1
+    while step < slot_count:
+        rolled = jnp.roll(field, -step, axis=-1)
+        chosen = ((distance & step) != 0)[None, :, :, None]
+        field = jnp.where(chosen, rolled, field)
+        step *= 2
+    return field
+
+
+def place_arrivals(field_six, keep_count, moving):
+    slot_count = field_six.shape[3]
+    keep_plane = jnp.broadcast_to(keep_count[-1].astype(jnp.float32)[:, None], field_six.shape[2:])
+    move_plane = jnp.broadcast_to(moving[-1].astype(jnp.float32)[:, None], field_six.shape[2:])
+    edge_pack = jnp.concatenate([field_six[:, -1], keep_plane[None], move_plane[None]], axis=0)
+    received = from_behind(edge_pack, "down", 1)
+    source_field = jnp.concatenate([received[:6][:, None], field_six[:, :-1]], axis=1)
+    source_keep = jnp.concatenate([received[6, :, 0].astype(jnp.int32)[None], keep_count[:-1]], axis=0)
+    arriving = jnp.concatenate([received[7, :, 0].astype(jnp.int32)[None], moving[:-1]], axis=0)
+    distance = jnp.mod(source_keep - keep_count, slot_count)
+    incoming = shift_lanes(source_field, distance)
+    incoming = jnp.concatenate([incoming[:1] - 1.0, incoming[1:]], axis=0)
     slot_ids = lax.broadcasted_iota(jnp.int32, field_six.shape[1:], 2)
-    relative = slot_ids - keep_count[..., None]
-    index = jnp.clip(relative, 0, arrivals.shape[3] - 1)
-    incoming = jnp.take_along_axis(
-        arrivals, jnp.broadcast_to(index[None], (6,) + index.shape), axis=3
-    )
-    own_mask = (slot_ids < keep_count[..., None]).astype(jnp.float32)
-    new_mask = ((relative >= 0) & (relative < arriving[..., None])).astype(jnp.float32)
-    return field_six * own_mask[None] + incoming * new_mask[None]
+    own_mask = slot_ids < keep_count[..., None]
+    new_mask = (slot_ids >= keep_count[..., None]) & (
+        slot_ids < (keep_count + arriving)[..., None]
+    )
+    return jnp.where(own_mask[None], field_six, jnp.where(new_mask[None], incoming, 0.0))
 
 
 def per_device(positions, velocities, plastic_viscosity, yield_stress, counts, moving):
@@ -197,13 +205,7 @@
     moved_positions = positions + TIME_STEP * current
     field_six = jnp.concatenate([moved_positions, current], axis=0)
     keep_count = counts - moving
-    packed = pack_departing(field_six, keep_count, moving)
-    move_plane = jnp.broadcast_to(moving[-1].astype(jnp.float32)[:, None], (col_count, MOVE_MAX))
-    edge_pack = jnp.concatenate([packed[:, -1], move_plane[None]], axis=0)
-    received = from_behind(edge_pack, "down", 1)
-    arrivals = jnp.concatenate([received[:6][:, None], packed[:, :-1]], axis=1)
-    arriving = jnp.concatenate([received[6, :, 0].astype(jnp.int32)[None], moving[:-1]], axis=0)
-    result = place_arrivals(field_six, keep_count, arrivals, arriving)
+    result = place_arrivals(field_six, keep_count, moving)
     return (result[:3], result[3:])
 
 

time: 360 us -> 246 us (0.68)
  local copies, waits for them, and re-layouts: 124 us -> 8.15 us
    gather x4 -> x0, local copies, waits for them, and re-layouts: 118 us -> none  [the longest x1 94.1 us: place_arrivals(): jnp.take_along_axis(arrivals, jnp.broadcast_to(index[None], (6,) + index....]
where the time goes in v1:
time: 246 us; the launch traced here: 244 us
  other arithmetic  102 us (41%)
  starting transfers between devices  66.7 us (27%)
  loops' own time  37.6 us (15%)
  waiting for transfers between devices  28.2 us (11%)
  local copies, waits for them, and re-layouts  8.15 us (3%)
    reduce_sum x32, other arithmetic, jacobi_one_row(): jnp.sum(coupling * source_speed[component][:, None, :], axis=2)  47.4 us
    ppermute x8, starting transfers between devices, with_halo(): after = lax.ppermute(initial, axis, down)  43.5 us
    reduce_sum x16, other arithmetic, force_one_row(): jnp.sum(pressure_push * separations[component], axis=2)  28.5 us
    reduce_sum x16, other arithmetic, density_one_row(): kernel_sum = kernel_sum + jnp.sum(present * weight, axis=2)  23.2 us
    ppermute x8, starting transfers between devices, with_halo(): before = lax.ppermute(last, axis, up)  21.3 us
    ppermute x8, waiting for transfers between devices, with_halo(): after = lax.ppermute(initial, axis, down)  20.1 us
    another operation x2, loops' own time, jacobi_pass(): result = lax.map(jacobi_one_row, jnp.arange(row_count, dtype=jnp.int32))  18.9 us
    another operation x1, loops' own time, force_pass(): result = lax.map(force_one_row, jnp.arange(row_count, dtype=jnp.int32))  9.39 us
  transfers between devices with their start and end apart: 17, of which 9 were waited for; matrix products, arithmetic and copies ran while one was open for 0% of the time, Pallas kernels for 0%

profile of v1, /device:TPU:3, one launch (start us, length us, event | category | flops | bytes accessed | tf_op | source)
XLA Modules:
  0.0 244.3 jit_solution(16618745385783197346)
XLA Ops:
  2.2 3.5 %collective-permute-start = (f32[7,1,8,128]{3,2,0,1:T(8,128)S(1)}, f32[7,1,8,128]{3,2,0,1:T(8,128)S(1)}, u32[]{:S(2)}, u32[]{:S(2)}) collective-permute-start(f32[7,1,8,128]{3,2,0,1:T(8,128)S(1)} %get-tuple-element.978), channel_id=1, source_target_pairs={{0,4},{4,8},{8,12},{12,16},{16,20},{20,24},{24,28},{28,32},{32,36}... | collective-permute-start | bytes 86024 | tf_op jit(solution)/shard_map/ppermute | solution.py:29
  5.7 8.3 %collective-permute-start.1 = (f32[7,1,8,128]{3,2,0,1:T(8,128)S(1)}, f32[7,1,8,128]{3,2,0,1:T(8,128)S(1)}, u32[]{:S(2)}, u32[]{:S(2)}) collective-permute-start(f32[7,1,8,128]{3,2,0,1:T(8,128)S(1)} %get-tuple-element.979), channel_id=1, source_target_pairs={{4,0},{8,4},{12,8},{16,12},{20,16},{24,20},{28,24},{32,28},{36,32}... | collective-permute-start | bytes 86024 | tf_op jit(solution)/shard_map/ppermute | solution.py:30
  15.0 5.5 %collective-permute-start.2 = (f32[7,4,1,128]{3,2,0,1:T(1,128)S(1)}, f32[7,4,1,128]{3,2,0,1:T(1,128)S(1)}, u32[]{:S(2)}, u32[]{:S(2)}) collective-permute-start(f32[7,4,1,128]{3,2,0,1:T(1,128)S(1)} %get-tuple-element.976), channel_id=1, source_target_pairs={{0,1},{1,2},{2,3},{4,5},{5,6},{6,7},{8,9},{9,10},{10,11},{12,13},{... | collective-permute-start | bytes 43016 | tf_op jit(solution)/shard_map/ppermute | solution.py:29
  20.5 1.9 collective-permute-start.3
  22.4 4.6 %collective-permute-done.3 = f32[7,4,1,128]{3,2,0,1:T(1,128)S(1)} collective-permute-done((f32[7,4,1,128]{3,2,0,1:T(1,128)S(1)}, f32[7,4,1,128]{3,2,0,1:T(1,128)S(1)}, u32[]{:S(2)}, u32[]{:S(2)}) %collective-permute-start.3) | collective-permute-done | bytes 14368 | tf_op jit(solution)/shard_map/ppermute | solution.py:30
  27.1 34.0 %while.56 = (s32[]{:T(128)}, f32[2,2,8,128]{3,2,0,1:T(8,128)S(1)}, s32[2]{0:T(128)S(1)}, f32[7,4,10,128]{3,2,0,1:T(8,128)S(1)}, s32[]{:T(128)}, /*index=5*/s32[]...) while((s32[]{:T(128)}, f32[2,2,8,128]{3,2,0,1:T(8,128)S(1)}, s32[2]{0:T(128)S(1)}, ...), condition=%wide.region_19.20_spmd, body=%wide.region_0.19_spmd.sunk | while | flops 36976652 | bytes 1448191 | solution.py:86
  61.8 1.9 collective-permute-start.4
  63.7 8.8 %collective-permute-start.5 = (f32[3,1,8,128]{3,2,1,0:T(8,128)S(1)}, f32[3,1,8,128]{3,2,1,0:T(8,128)S(1)}, u32[]{:S(2)}, u32[]{:S(2)}) collective-permute-start(f32[3,1,8,128]{3,2,1,0:T(8,128)S(1)} %get-tuple-element.997), channel_id=1, source_target_pairs={{4,0},{8,4},{12,8},{16,12},{20,16},{24,20},{28,24},{32,28},{36,32}... | collective-permute-start | bytes 36872 | tf_op jit(solution)/shard_map/ppermute | solution.py:30
  73.3 2.2 collective-permute-start.6
  75.5 2.3 collective-permute-start.7
  77.9 4.1 %collective-permute-done.7 = f32[3,4,1,128]{3,2,1,0:T(1,128)S(1)} collective-permute-done((f32[3,4,1,128]{3,2,1,0:T(1,128)S(1)}, f32[3,4,1,128]{3,2,1,0:T(1,128)S(1)}, u32[]{:S(2)}, u32[]{:S(2)}) %collective-permute-start.7) | collective-permute-done | bytes 6176 | tf_op jit(solution)/shard_map/ppermute | solution.py:30
  82.0 39.3 %while.57 = (s32[]{:T(128)}, f32[2,4,8,128]{3,2,0,1:T(8,128)S(1)}, s32[2]{0:T(128)S(1)}, f32[7,4,10,128]{3,2,0,1:T(8,128)S(1)}, f32[3,4,10,128]{3,2,0,1:T(8,128)...) while((s32[]{:T(128)}, f32[2,4,8,128]{3,2,0,1:T(8,128)S(1)}, ...), condition=%wide.region_57.58_spmd, body=%wide.region_20.57_spmd.sunk | while | flops 34618380 | bytes 1597715 | solution.py:119
  99.1 2.5 %multiply_reduce_fusion.131 = (f32[8,128]{1,0:T(8,128)S(1)}, f32[8,128]{1,0:T(8,128)S(1)}, f32[8,128]{1,0:T(8,128)S(1)}, f32[8,128]{1,0:T(8,128)S(1)}, f32[8,128...) fusion(f32[8,128]{1,0:T(8,128)S(1)} %get-tuple-element.1656, ...), kind=kLoop, calls=%fused_computation.244.clone.1 | loop fusion | flops 7593984 | bytes 90112 | tf_op jit(solution)/shard_map/while/body/eval_jaxpr/reduce_sum | solution.py:106
  118.8 2.5 %multiply_reduce_fusion.131 = (f32[8,128]{1,0:T(8,128)S(1)}, f32[8,128]{1,0:T(8,128)S(1)}, f32[8,128]{1,0:T(8,128)S(1)}, f32[8,128]{1,0:T(8,128)S(1)}, f32[8,128...) fusion(f32[8,128]{1,0:T(8,128)S(1)} %get-tuple-element.1656, ...), kind=kLoop, calls=%fused_computation.244.clone.1 | loop fusion | flops 7593984 | bytes 90112 | tf_op jit(solution)/shard_map/while/body/eval_jaxpr/reduce_sum | solution.py:106
  122.1 1.9 collective-permute-start.8
  124.0 8.7 %collective-permute-start.9 = (f32[3,1,8,128]{3,2,1,0:T(8,128)S(1)}, f32[3,1,8,128]{3,2,1,0:T(8,128)S(1)}, u32[]{:S(2)}, u32[]{:S(2)}) collective-permute-start(f32[3,1,8,128]{3,2,1,0:T(8,128)S(1)} %get-tuple-element.995), channel_id=1, source_target_pairs={{4,0},{8,4},{12,8},{16,12},{20,16},{24,20},{28,24},{32,28},{36,32}... | collective-permute-start | bytes 36872 | tf_op jit(solution)/shard_map/ppermute | solution.py:30
  133.6 2.2 collective-permute-start.10
  135.8 2.3 collective-permute-start.11
  138.2 4.1 %collective-permute-done.11 = f32[3,4,1,128]{3,2,1,0:T(1,128)S(1)} collective-permute-done((f32[3,4,1,128]{3,2,1,0:T(1,128)S(1)}, f32[3,4,1,128]{3,2,1,0:T(1,128)S(1)}, u32[]{:S(2)}, u32[]{:S(2)}) %collective-permute-start.11) | collective-permute-done | bytes 6176 | tf_op jit(solution)/shard_map/ppermute | solution.py:30
  142.3 34.7 %while.58 = (s32[]{:T(128)}, f32[2,3,8,128]{3,2,0,1:T(8,128)S(1)}, s32[2]{0:T(128)S(1)}, f32[7,4,10,128]{3,2,0,1:T(8,128)S(1)}, f32[3,4,10,128]{3,2,0,1:T(8,128)...) while((s32[]{:T(128)}, f32[2,3,8,128]{3,2,0,1:T(8,128)S(1)}, ...), condition=%wide.region_86.87_spmd, body=%wide.region_58.86_spmd.sunk | while | flops 29890572 | bytes 1796379 | solution.py:149
  151.8 2.0 multiply_reduce_fusion.141
  169.2 2.0 multiply_reduce_fusion.141
  177.0 1.9 collective-permute-start.12
  179.0 8.7 %collective-permute-start.13 = (f32[3,1,8,128]{3,2,1,0:T(8,128)S(1)}, f32[3,1,8,128]{3,2,1,0:T(8,128)S(1)}, u32[]{:S(2)}, u32[]{:S(2)}) collective-permute-start(f32[3,1,8,128]{3,2,1,0:T(8,128)S(1)} %get-tuple-element.993), channel_id=1, source_target_pairs={{4,0},{8,4},{12,8},{16,12},{20,16},{24,20},{28,24},{32,28},{36,32}... | collective-permute-start | bytes 36872 | tf_op jit(solution)/shard_map/ppermute | solution.py:30
  188.5 2.2 collective-permute-start.14
  190.7 2.4 collective-permute-start.15
  193.2 4.0 %collective-permute-done.15 = f32[3,4,1,128]{3,2,1,0:T(1,128)S(1)} collective-permute-done((f32[3,4,1,128]{3,2,1,0:T(1,128)S(1)}, f32[3,4,1,128]{3,2,1,0:T(1,128)S(1)}, u32[]{:S(2)}, u32[]{:S(2)}) %collective-permute-start.15) | collective-permute-done | bytes 6176 | tf_op jit(solution)/shard_map/ppermute | solution.py:30
  197.3 34.6 %while.59 = (s32[]{:T(128)}, f32[2,3,8,128]{3,2,0,1:T(8,128)S(1)}, s32[2]{0:T(128)S(1)}, f32[7,4,10,128]{3,2,0,1:T(8,128)S(1)}, f32[3,4,10,128]{3,2,0,1:T(8,128)...) while((s32[]{:T(128)}, f32[2,3,8,128]{3,2,0,1:T(8,128)S(1)}, ...), condition=%wide.region_115.116_spmd, body=%wide.region_87.115_spmd.sunk | while | flops 29890572 | bytes 1796379 | solution.py:149
  206.8 2.0 multiply_reduce_fusion.149
  224.1 2.0 multiply_reduce_fusion.149
  232.1 1.9 collective-permute-start.16
  234.0 8.1 %collective-permute-done.16 = f32[8,8,128]{2,1,0:T(8,128)S(1)} collective-permute-done((f32[8,8,128]{2,1,0:T(8,128)S(1)}, f32[8,8,128]{2,1,0:T(8,128)S(1)}, u32[]{:S(2)}, u32[]{:S(2)}) %collective-permute-start.16) | collective-permute-done | bytes 32800 | tf_op jit(solution)/shard_map/ppermute | solution.py:38
  (262 shorter events, 100.7 us)
Async XLA Ops:
  2.1 12.8 %copy-start = (f32[3,2,8,128]{3,2,1,0:T(8,128)S(1)}, f32[3,2,8,128]{3,2,1,0:T(8,128)}, u32[]{:S(2)}) copy-start(f32[3,2,8,128]{3,2,1,0:T(8,128)} %param.15) | copy-start | bytes 73732
  2.1 12.8 %copy-start.1 = (f32[3,2,8,128]{3,2,1,0:T(8,128)S(1)}, f32[3,2,8,128]{3,2,1,0:T(8,128)}, u32[]{:S(2)}) copy-start(f32[3,2,8,128]{3,2,1,0:T(8,128)} %param.16) | copy-start | bytes 73732
  2.2 11.8 %collective-permute-start = (f32[7,1,8,128]{3,2,0,1:T(8,128)S(1)}, f32[7,1,8,128]{3,2,0,1:T(8,128)S(1)}, u32[]{:S(2)}, u32[]{:S(2)}) collective-permute-start(f32[7,1,8,128]{3,2,0,1:T(8,128)S(1)} %get-tuple-element.978), channel_id=1, source_target_pairs={{0,4},{4,8},{8,12},{12,16},{16,20},{20,24},{24,28},{28,32},{32,36}... | collective-permute-start | bytes 86024 | tf_op jit(solution)/shard_map/ppermute | solution.py:29
  5.7 9.3 %collective-permute-start.1 = (f32[7,1,8,128]{3,2,0,1:T(8,128)S(1)}, f32[7,1,8,128]{3,2,0,1:T(8,128)S(1)}, u32[]{:S(2)}, u32[]{:S(2)}) collective-permute-start(f32[7,1,8,128]{3,2,0,1:T(8,128)S(1)} %get-tuple-element.979), channel_id=1, source_target_pairs={{4,0},{8,4},{12,8},{16,12},{20,16},{24,20},{28,24},{32,28},{36,32}... | collective-permute-start | bytes 86024 | tf_op jit(solution)/shard_map/ppermute | solution.py:30
  15.0 7.4 %collective-permute-start.2 = (f32[7,4,1,128]{3,2,0,1:T(1,128)S(1)}, f32[7,4,1,128]{3,2,0,1:T(1,128)S(1)}, u32[]{:S(2)}, u32[]{:S(2)}) collective-permute-start(f32[7,4,1,128]{3,2,0,1:T(1,128)S(1)} %get-tuple-element.976), channel_id=1, source_target_pairs={{0,1},{1,2},{2,3},{4,5},{5,6},{6,7},{8,9},{9,10},{10,11},{12,13},{... | collective-permute-start | bytes 43016 | tf_op jit(solution)/shard_map/ppermute | solution.py:29
  20.5 6.5 %collective-permute-start.3 = (f32[7,4,1,128]{3,2,0,1:T(1,128)S(1)}, f32[7,4,1,128]{3,2,0,1:T(1,128)S(1)}, u32[]{:S(2)}, u32[]{:S(2)}) collective-permute-start(f32[7,4,1,128]{3,2,0,1:T(1,128)S(1)} %get-tuple-element.977), channel_id=1, source_target_pairs={{1,0},{2,1},{3,2},{5,4},{6,5},{7,6},{9,8},{10,9},{11,10},{13,12},{... | collective-permute-start | bytes 43016 | tf_op jit(solution)/shard_map/ppermute | solution.py:30
  61.1 0.7 copy-start.2
  61.1 0.7 copy-start.3
  61.8 10.7 %collective-permute-start.4 = (f32[3,1,8,128]{3,2,1,0:T(8,128)S(1)}, f32[3,1,8,128]{3,2,1,0:T(8,128)S(1)}, u32[]{:S(2)}, u32[]{:S(2)}) collective-permute-start(f32[3,1,8,128]{3,2,1,0:T(8,128)S(1)} %get-tuple-element.996), channel_id=1, source_target_pairs={{0,4},{4,8},{8,12},{12,16},{16,20},{20,24},{24,28},{28,32},{32,36}... | collective-permute-start | bytes 36872 | tf_op jit(solution)/shard_map/ppermute | solution.py:29
  63.7 9.6 %collective-permute-start.5 = (f32[3,1,8,128]{3,2,1,0:T(8,128)S(1)}, f32[3,1,8,128]{3,2,1,0:T(8,128)S(1)}, u32[]{:S(2)}, u32[]{:S(2)}) collective-permute-start(f32[3,1,8,128]{3,2,1,0:T(8,128)S(1)} %get-tuple-element.997), channel_id=1, source_target_pairs={{4,0},{8,4},{12,8},{16,12},{20,16},{24,20},{28,24},{32,28},{36,32}... | collective-permute-start | bytes 36872 | tf_op jit(solution)/shard_map/ppermute | solution.py:30
  73.3 4.5 %collective-permute-start.6 = (f32[3,4,1,128]{3,2,1,0:T(1,128)S(1)}, f32[3,4,1,128]{3,2,1,0:T(1,128)S(1)}, u32[]{:S(2)}, u32[]{:S(2)}) collective-permute-start(f32[3,4,1,128]{3,2,1,0:T(1,128)S(1)} %get-tuple-element.990), channel_id=1, source_target_pairs={{0,1},{1,2},{2,3},{4,5},{5,6},{6,7},{8,9},{9,10},{10,11},{12,13},{... | collective-permute-start | bytes 18440 | tf_op jit(solution)/shard_map/ppermute | solution.py:29
  75.5 6.5 %collective-permute-start.7 = (f32[3,4,1,128]{3,2,1,0:T(1,128)S(1)}, f32[3,4,1,128]{3,2,1,0:T(1,128)S(1)}, u32[]{:S(2)}, u32[]{:S(2)}) collective-permute-start(f32[3,4,1,128]{3,2,1,0:T(1,128)S(1)} %get-tuple-element.991), channel_id=1, source_target_pairs={{1,0},{2,1},{3,2},{5,4},{6,5},{7,6},{9,8},{10,9},{11,10},{13,12},{... | collective-permute-start | bytes 18440 | tf_op jit(solution)/shard_map/ppermute | solution.py:30
  121.4 0.7 copy-start.6
  122.1 10.7 %collective-permute-start.8 = (f32[3,1,8,128]{3,2,1,0:T(8,128)S(1)}, f32[3,1,8,128]{3,2,1,0:T(8,128)S(1)}, u32[]{:S(2)}, u32[]{:S(2)}) collective-permute-start(f32[3,1,8,128]{3,2,1,0:T(8,128)S(1)} %get-tuple-element.994), channel_id=1, source_target_pairs={{0,4},{4,8},{8,12},{12,16},{16,20},{20,24},{24,28},{28,32},{32,36}... | collective-permute-start | bytes 36872 | tf_op jit(solution)/shard_map/ppermute | solution.py:29
  124.0 9.6 %collective-permute-start.9 = (f32[3,1,8,128]{3,2,1,0:T(8,128)S(1)}, f32[3,1,8,128]{3,2,1,0:T(8,128)S(1)}, u32[]{:S(2)}, u32[]{:S(2)}) collective-permute-start(f32[3,1,8,128]{3,2,1,0:T(8,128)S(1)} %get-tuple-element.995), channel_id=1, source_target_pairs={{4,0},{8,4},{12,8},{16,12},{20,16},{24,20},{28,24},{32,28},{36,32}... | collective-permute-start | bytes 36872 | tf_op jit(solution)/shard_map/ppermute | solution.py:30
  133.6 4.6 %collective-permute-start.10 = (f32[3,4,1,128]{3,2,1,0:T(1,128)S(1)}, f32[3,4,1,128]{3,2,1,0:T(1,128)S(1)}, u32[]{:S(2)}, u32[]{:S(2)}) collective-permute-start(f32[3,4,1,128]{3,2,1,0:T(1,128)S(1)} %get-tuple-element.988), channel_id=1, source_target_pairs={{0,1},{1,2},{2,3},{4,5},{5,6},{6,7},{8,9},{9,10},{10,11},{12,13},{... | collective-permute-start | bytes 18440 | tf_op jit(solution)/shard_map/ppermute | solution.py:29
  135.8 6.5 %collective-permute-start.11 = (f32[3,4,1,128]{3,2,1,0:T(1,128)S(1)}, f32[3,4,1,128]{3,2,1,0:T(1,128)S(1)}, u32[]{:S(2)}, u32[]{:S(2)}) collective-permute-start(f32[3,4,1,128]{3,2,1,0:T(1,128)S(1)} %get-tuple-element.989), channel_id=1, source_target_pairs={{1,0},{2,1},{3,2},{5,4},{6,5},{7,6},{9,8},{10,9},{11,10},{13,12},{... | collective-permute-start | bytes 18440 | tf_op jit(solution)/shard_map/ppermute | solution.py:30
  177.0 10.7 %copy-start.5 = (s32[2,8]{1,0:T(2,128)S(1)}, s32[2,8]{1,0:T(2,128)}, u32[]{:S(2)}) copy-start(s32[2,8]{1,0:T(2,128)} %param.20) | copy-start | bytes 196
  177.0 10.7 %collective-permute-start.12 = (f32[3,1,8,128]{3,2,1,0:T(8,128)S(1)}, f32[3,1,8,128]{3,2,1,0:T(8,128)S(1)}, u32[]{:S(2)}, u32[]{:S(2)}) collective-permute-start(f32[3,1,8,128]{3,2,1,0:T(8,128)S(1)} %get-tuple-element.992), channel_id=1, source_target_pairs={{0,4},{4,8},{8,12},{12,16},{16,20},{20,24},{24,28},{28,32},{32,36}... | collective-permute-start | bytes 36872 | tf_op jit(solution)/shard_map/ppermute | solution.py:29
  179.0 8.8 %copy-start.4 = (s32[2,8]{1,0:T(2,128)S(1)}, s32[2,8]{1,0:T(2,128)}, u32[]{:S(2)}) copy-start(s32[2,8]{1,0:T(2,128)} %param.19) | copy-start | bytes 196
  179.0 9.6 %collective-permute-start.13 = (f32[3,1,8,128]{3,2,1,0:T(8,128)S(1)}, f32[3,1,8,128]{3,2,1,0:T(8,128)S(1)}, u32[]{:S(2)}, u32[]{:S(2)}) collective-permute-start(f32[3,1,8,128]{3,2,1,0:T(8,128)S(1)} %get-tuple-element.993), channel_id=1, source_target_pairs={{4,0},{8,4},{12,8},{16,12},{20,16},{24,20},{28,24},{32,28},{36,32}... | collective-permute-start | bytes 36872 | tf_op jit(solution)/shard_map/ppermute | solution.py:30
  188.5 4.6 %collective-permute-start.14 = (f32[3,4,1,128]{3,2,1,0:T(1,128)S(1)}, f32[3,4,1,128]{3,2,1,0:T(1,128)S(1)}, u32[]{:S(2)}, u32[]{:S(2)}) collective-permute-start(f32[3,4,1,128]{3,2,1,0:T(1,128)S(1)} %get-tuple-element.986), channel_id=1, source_target_pairs={{0,1},{1,2},{2,3},{4,5},{5,6},{6,7},{8,9},{9,10},{10,11},{12,13},{... | collective-permute-start | bytes 18440 | tf_op jit(solution)/shard_map/ppermute | solution.py:29
  190.7 6.5 %collective-permute-start.15 = (f32[3,4,1,128]{3,2,1,0:T(1,128)S(1)}, f32[3,4,1,128]{3,2,1,0:T(1,128)S(1)}, u32[]{:S(2)}, u32[]{:S(2)}) collective-permute-start(f32[3,4,1,128]{3,2,1,0:T(1,128)S(1)} %get-tuple-element.987), channel_id=1, source_target_pairs={{1,0},{2,1},{3,2},{5,4},{6,5},{7,6},{9,8},{10,9},{11,10},{13,12},{... | collective-permute-start | bytes 18440 | tf_op jit(solution)/shard_map/ppermute | solution.py:30
  232.1 10.0 %collective-permute-start.16 = (f32[8,8,128]{2,1,0:T(8,128)S(1)}, f32[8,8,128]{2,1,0:T(8,128)S(1)}, u32[]{:S(2)}, u32[]{:S(2)}) collective-permute-start(f32[8,8,128]{2,1,0:T(8,128)S(1)} %pad_maximum_fusion.7), channel_id=1, source_target_pairs={{0,4},{4,8},{8,12},{12,16},{16,20},{20,24},{24,28},{28,32},{32,36}... | collective-permute-start | bytes 98312 | tf_op jit(solution)/shard_map/ppermute | solution.py:38

commit v2 on v1

v2 whole, which is shorter than its diff:
```python
import math

import jax
import jax.numpy as jnp
from jax import lax
from jax.experimental import pallas as pl
from jax.sharding import PartitionSpec as P

MOVE_MAX = 32
JACOBI = 2


KERNEL_NORM = 21.0 / (2.0 * math.pi)
PARTICLE_MASS = 0.02
REST_DENSITY = 1.0
STIFFNESS = 2.0
TIME_STEP = 0.05
GRAVITY_DOWN = 0.5
GRAVITY_UP = -1.0
NEIGHBOUR_STEPS = [(-1, -1), (-1, 0), (-1, 1), (0, -1), (0, 0), (0, 1), (1, -1), (1, 0), (1, 1)]


def with_halo(array, sides, width):
    for axis, dim in sides:
        count, length = (lax.axis_size(axis), array.shape[dim])
        up = [(i, (i + 1) % count) for i in range(count - 1)]
        down = [(j, i) for i, j in up]
        last = lax.slice_in_dim(array, length - width, length, axis=dim)
        initial = lax.slice_in_dim(array, 0, width, axis=dim)
        before = lax.ppermute(last, axis, up)
        after = lax.ppermute(initial, axis, down)
        array = jnp.concatenate([before, array, after], axis=dim)
    return array


def from_behind(block, axis, distance):
    devices = range(lax.axis_size(axis))
    route = [(i - distance, i) for i in devices if i - distance in devices]
    return lax.ppermute(block, axis, route)


def take_row(padded, lead_blocks, row_index, step_down, step_cross, col_count):
    whole_row = lax.dynamic_index_in_dim(
        padded, row_index + lead_blocks + step_down, axis=1, keepdims=False
    )
    return whole_row[:, lead_blocks + step_cross : lead_blocks + step_cross + col_count, :]


def separation(target, source, step_down, step_cross):
    offsets = (float(step_down), float(step_cross), 0.0)
    separations = [
        source[component][:, None, :] - target[component][:, :, None] + offsets[component]
        for component in range(3)
    ]
    distance = jnp.sqrt(
        separations[0] * separations[0]
        + separations[1] * separations[1]
        + separations[2] * separations[2]
    )
    falloff = jnp.maximum(1.0 - distance, 0.0)
    falloff_cubed = falloff * falloff * falloff
    weight = KERNEL_NORM * falloff_cubed * falloff * (4.0 * distance + 1.0)
    strength = 20.0 * KERNEL_NORM * falloff_cubed
    return (separations, weight, strength)


FAR_AWAY = 1.0e4
CHUNK = 16


def pair_pass(kind, target, source, row_count, col_count):
    slot_count = target.shape[-1]
    block_count = row_count * col_count
    chunk_count = slot_count // CHUNK
    padded_cols = col_count + 2
    target_count = target.shape[0]
    source_count = source.shape[0]
    output_count = {"density": 2, "force": 4, "jacobi": 3}[kind]
    target_cols = jnp.moveaxis(target.reshape(target_count, block_count, slot_count), 0, 2)
    source_rows = source.reshape(source_count, (row_count + 2) * padded_cols, slot_count)

    def kernel(target_ref, source_ref, out_ref):
        def body(step, carry):
            block = step // chunk_count
            first = pl.multiple_of((step % chunk_count) * CHUNK, CHUNK)
            row = block // col_count
            col = block % col_count
            own = target_ref[block, pl.ds(first, CHUNK), :]
            mine = [
                jnp.broadcast_to(own[:, k : k + 1], (CHUNK, slot_count)) for k in range(target_count)
            ]
            totals = [jnp.zeros((CHUNK, slot_count), jnp.float32) for k in range(output_count)]
            for step_down, step_cross in NEIGHBOUR_STEPS:
                near = (row + 1 + step_down) * padded_cols + (col + 1 + step_cross)
                other = [source_ref[k, pl.ds(near, 1), :] for k in range(source_count)]
                gaps = [
                    other[0] + float(step_down) - mine[0],
                    other[1] + float(step_cross) - mine[1],
                    other[2] - mine[2],
                ]
                distance = jnp.sqrt(gaps[0] * gaps[0] + gaps[1] * gaps[1] + gaps[2] * gaps[2])
                falloff = jnp.maximum(1.0 - distance, 0.0)
                cubed = falloff * falloff * falloff
                if kind == "density":
                    totals[0] = totals[0] + cubed * falloff * (4.0 * distance + 1.0)
                    spread = None
                    for k in range(3):
                        change = other[3 + k] - mine[3 + k]
                        term = change * change
                        spread = term if spread is None else spread + term
                    totals[1] = totals[1] + cubed * spread
                elif kind == "force":
                    push = (mine[3] + other[3]) * cubed
                    for k in range(3):
                        totals[k] = totals[k] + push * gaps[k]
                    totals[3] = totals[3] + (mine[4] + other[5]) * other[4] * cubed
                else:
                    pull = (mine[3] + other[3]) * cubed
                    for k in range(3):
                        totals[k] = totals[k] + pull * other[4 + k]
            for k in range(output_count):
                out_ref[block, pl.ds(first, CHUNK), pl.ds(k, 1)] = jnp.sum(
                    totals[k], axis=1, keepdims=True
                )
            return carry

        lax.fori_loop(0, block_count * chunk_count, body, 0)

    result = pl.pallas_call(
        kernel,
        out_shape=jax.ShapeDtypeStruct((block_count, slot_count, output_count), jnp.float32),
    )(target_cols, source_rows)
    return jnp.moveaxis(result, 2, 0).reshape(output_count, row_count, col_count, slot_count)


def shift_lanes(field, distance):
    slot_count = field.shape[-1]
    step = 1
    while step < slot_count:
        rolled = jnp.roll(field, -step, axis=-1)
        chosen = ((distance & step) != 0)[None, :, :, None]
        field = jnp.where(chosen, rolled, field)
        step *= 2
    return field


def place_arrivals(field_six, keep_count, moving):
    slot_count = field_six.shape[3]
    keep_plane = jnp.broadcast_to(keep_count[-1].astype(jnp.float32)[:, None], field_six.shape[2:])
    move_plane = jnp.broadcast_to(moving[-1].astype(jnp.float32)[:, None], field_six.shape[2:])
    edge_pack = jnp.concatenate([field_six[:, -1], keep_plane[None], move_plane[None]], axis=0)
    received = from_behind(edge_pack, "down", 1)
    source_field = jnp.concatenate([received[:6][:, None], field_six[:, :-1]], axis=1)
    source_keep = jnp.concatenate([received[6, :, 0].astype(jnp.int32)[None], keep_count[:-1]], axis=0)
    arriving = jnp.concatenate([received[7, :, 0].astype(jnp.int32)[None], moving[:-1]], axis=0)
    distance = jnp.mod(source_keep - keep_count, slot_count)
    incoming = shift_lanes(source_field, distance)
    incoming = jnp.concatenate([incoming[:1] - 1.0, incoming[1:]], axis=0)
    slot_ids = lax.broadcasted_iota(jnp.int32, field_six.shape[1:], 2)
    own_mask = slot_ids < keep_count[..., None]
    new_mask = (slot_ids >= keep_count[..., None]) & (
        slot_ids < (keep_count + arriving)[..., None]
    )
    return jnp.where(own_mask[None], field_six, jnp.where(new_mask[None], incoming, 0.0))


def per_device(positions, velocities, plastic_viscosity, yield_stress, counts, moving):
    row_count, col_count, slot_count = positions.shape[1:]
    slot_ids = lax.broadcasted_iota(jnp.int32, (row_count, col_count, slot_count), 2)
    live = (slot_ids < counts[:, :, None]).astype(jnp.float32)
    state = jnp.concatenate([positions, velocities, live[None]], axis=0)
    state_pad = with_halo(state, (("down", 1), ("cross", 2)), 1)
    far = jnp.where(state_pad[6:7] > 0.0, state_pad[:3], FAR_AWAY)
    sums = pair_pass(
        "density",
        jnp.concatenate([positions, velocities], axis=0),
        jnp.concatenate([far, state_pad[3:6]], axis=0),
        row_count,
        col_count,
    )
    density = PARTICLE_MASS * (KERNEL_NORM * sums[0] + KERNEL_NORM * (1.0 - live))
    strain = (PARTICLE_MASS * 20.0 * KERNEL_NORM) * sums[1]
    inverse = 1.0 / density
    pressure = STIFFNESS * (density - REST_DENSITY) * inverse * inverse
    viscosity = plastic_viscosity + yield_stress / jnp.sqrt(1.0 + strain)
    dens_pad = with_halo(jnp.stack([inverse, pressure, viscosity]), (("down", 1), ("cross", 2)), 1)
    forces = pair_pass(
        "force",
        jnp.concatenate([positions, pressure[None], viscosity[None]], axis=0),
        jnp.concatenate([far, dens_pad[1:2], dens_pad[0:1], dens_pad[2:3]], axis=0),
        row_count,
        col_count,
    )
    scale = PARTICLE_MASS * 20.0 * KERNEL_NORM
    gravity = jnp.array([GRAVITY_DOWN, 0.0, GRAVITY_UP], jnp.float32)[:, None, None, None]
    predicted = velocities + TIME_STEP * (-scale * forces[:3] + gravity)
    diagonal = 1.0 + TIME_STEP * (scale * inverse * forces[3])
    target = jnp.concatenate([positions, viscosity[None]], axis=0)
    current = predicted
    for sweep_index in range(JACOBI):
        speed_pad = with_halo(current, (("down", 1), ("cross", 2)), 1)
        pulled = pair_pass(
            "jacobi",
            target,
            jnp.concatenate([far, dens_pad[2:3], speed_pad * dens_pad[0:1]], axis=0),
            row_count,
            col_count,
        )
        current = (predicted + TIME_STEP * (scale * inverse * pulled)) / diagonal
    moved_positions = positions + TIME_STEP * current
    field_six = jnp.concatenate([moved_positions, current], axis=0)
    keep_count = counts - moving
    result = place_arrivals(field_six, keep_count, moving)
    return (result[:3], result[3:])


def solution(mesh):
    return jax.shard_map(
        per_device,
        mesh=mesh,
        in_specs=(
            P(None, "down", "cross", None),
            P(None, "down", "cross", None),
            P("down", "cross", None),
            P("down", "cross", None),
            P("down", "cross"),
            P("down", "cross"),
        ),
        out_specs=(P(None, "down", "cross", None), P(None, "down", "cross", None)),
        check_vma=False,
    )
```

time: 246 us -> 238 us (0.967)
  Pallas kernels: 0 us -> 121 us
  other arithmetic: 102 us -> 7 us
  loops' own time: 37.6 us -> 0 us
  local copies, waits for them, and re-layouts: 8.15 us -> 13.8 us
  starting transfers between devices: 66.7 us -> 61.5 us
    pallas_call x0 -> x4, Pallas kernels: none -> 121 us  [pair_pass(): pl.pallas_call(kernel, out_shape=jax.ShapeDtypeStruct((block_count, slot_...]
    reduce_sum x64 -> x0, other arithmetic: 99.1 us -> none  [the longest x32 47.4 us: jacobi_one_row(): jnp.sum(coupling * source_speed[component][:, None, :], axis=2)]
    another operation x4 -> x0, loops' own time: 37.6 us -> none  [the longest x2 18.9 us: jacobi_pass(): result = lax.map(jacobi_one_row, jnp.arange(row_count, dtype=jnp.int32))]
    ppermute x8, waiting for transfers between devices: 0.02 us -> 23.5 us  [with_halo(): before = lax.ppermute(last, axis, up)]
    ppermute x8, waiting for transfers between devices: 20.1 us -> 0.02 us  [with_halo(): after = lax.ppermute(initial, axis, down)]
    ppermute x8, starting transfers between devices: 43.5 us -> 25.5 us  [with_halo(): after = lax.ppermute(initial, axis, down)]
    ppermute x8, starting transfers between devices: 21.3 us -> 34.1 us  [with_halo(): before = lax.ppermute(last, axis, up)]
    reshape x0 -> x6, local copies, waits for them, and re-layouts: none -> 5.78 us  [the longest x2 3.1 us: pair_pass(): jnp.moveaxis(result, 2, 0)]
  transfers between devices with their start and end apart: 17 -> 17, of which waited for: 9 -> 7; matrix products, arithmetic and copies ran while one was open for 0% -> 2% of each run, Pallas kernels for 0% -> 0%
where the time goes in v2:
time: 238 us; the launch traced here: 235 us
  Pallas kernels  121 us (51%)
  starting transfers between devices  61.5 us (26%)
  waiting for transfers between devices  30.5 us (13%)
  local copies, waits for them, and re-layouts  13.8 us (6%)
  other arithmetic  7 us (3%)
    pallas_call x4, Pallas kernels, pair_pass(): pl.pallas_call(kernel, out_shape=jax.ShapeDtypeStruct((block_count, slot_...  121 us
    ppermute x8, starting transfers between devices, with_halo(): before = lax.ppermute(last, axis, up)  34.1 us
    ppermute x8, starting transfers between devices, with_halo(): after = lax.ppermute(initial, axis, down)  25.5 us
    ppermute x8, waiting for transfers between devices, with_halo(): before = lax.ppermute(last, axis, up)  23.5 us
    ppermute x1, waiting for transfers between devices, from_behind(): return lax.ppermute(block, axis, route)  6.95 us
  transfers between devices with their start and end apart: 17, of which 7 were waited for; matrix products, arithmetic and copies ran while one was open for 2% of the time, Pallas kernels for 0%

profile of v2, /device:TPU:3, one launch (start us, length us, event | category | flops | bytes accessed | tf_op | source)
XLA Modules:
  0.0 234.8 jit_solution(13465337964643138876)
XLA Ops:
  2.2 9.9 %collective-permute-start.1 = (f32[7,1,8,128]{3,2,1,0:T(8,128)S(1)}, f32[7,1,8,128]{3,2,1,0:T(8,128)S(1)}, u32[]{:S(2)}, u32[]{:S(2)}) collective-permute-start(f32[7,1,8,128]{3,2,1,0:T(8,128)S(1)} %get-tuple-element.20), channel_id=1, source_target_pairs={{4,0},{8,4},{12,8},{16,12},{20,16},{24,20},{28,24},{32,28},{36,32}... | collective-permute-start | bytes 86024 | tf_op jit(solution)/shard_map/ppermute | solution.py:31
  12.1 1.9 collective-permute-start
  14.0 6.9 %collective-permute-done = f32[7,1,8,128]{3,2,1,0:T(8,128)S(1)} collective-permute-done((f32[7,1,8,128]{3,2,1,0:T(8,128)S(1)}, f32[7,1,8,128]{3,2,1,0:T(8,128)S(1)}, u32[]{:S(2)}, u32[]{:S(2)}) %collective-permute-start) | collective-permute-done | bytes 28704 | tf_op jit(solution)/shard_map/ppermute | solution.py:30
  20.9 4.0 %collective-permute-start.3 = (f32[7,4,1,128]{3,2,1,0:T(1,128)S(1)}, f32[7,4,1,128]{3,2,1,0:T(1,128)S(1)}, u32[]{:S(2)}, u32[]{:S(2)}) collective-permute-start(f32[7,4,1,128]{3,2,1,0:T(1,128)S(1)} %get-tuple-element.14), channel_id=1, source_target_pairs={{1,0},{2,1},{3,2},{5,4},{6,5},{7,6},{9,8},{10,9},{11,10},{13,12},{... | collective-permute-start | bytes 43016 | tf_op jit(solution)/shard_map/ppermute | solution.py:31
  25.0 3.9 %collective-permute-start.2 = (f32[7,4,1,128]{3,2,1,0:T(1,128)S(1)}, f32[7,4,1,128]{3,2,1,0:T(1,128)S(1)}, u32[]{:S(2)}, u32[]{:S(2)}) collective-permute-start(f32[7,4,1,128]{3,2,1,0:T(1,128)S(1)} %get-tuple-element.13), channel_id=1, source_target_pairs={{0,1},{1,2},{2,3},{4,5},{5,6},{6,7},{8,9},{9,10},{10,11},{12,13},{... | collective-permute-start | bytes 43016 | tf_op jit(solution)/shard_map/ppermute | solution.py:30
  29.0 1.3 copy.51
  31.2 31.4 %shard_map.86 = f32[16,128,2]{2,1,0:T(8,128)} custom-call(f32[16,128,6]{2,1,0:T(8,128)} %bitcast.83, f32[6,40,128]{2,1,0:T(8,128)} %copy.53.source_ref), custom_call_target="tpu_custom_call" | custom-call | tf_op jit(solution)/shard_map/pallas_call | solution.py:129
  62.6 2.5 %fusion.3 = (f32[16,128]{1,0:T(8,128)S(1)}, f32[16,128]{1,0:T(8,128)S(1)}, f32[1,16,128]{0,2,1:T(8,128)S(1)}) fusion(f32[2,16,128]{0,2,1:T(8,128)} %bitcast.81, s32[16]{0:T(128)S(1)} %lt.80), kind=kLoop, calls=%fused_computation.9 | loop fusion | flops 16384 | bytes 41024 | tf_op jit(solution)/shard_map/mul | solution.py:181
  66.2 1.9 collective-permute-start.5
  68.2 3.3 %collective-permute-start.4 = (f32[3,1,8,128]{3,2,1,0:T(8,128)S(1)}, f32[3,1,8,128]{3,2,1,0:T(8,128)S(1)}, u32[]{:S(2)}, u32[]{:S(2)}) collective-permute-start(f32[3,1,8,128]{3,2,1,0:T(8,128)S(1)} %get-tuple-element.37), channel_id=1, source_target_pairs={{0,4},{4,8},{8,12},{12,16},{16,20},{20,24},{24,28},{28,32},{32,36}... | collective-permute-start | bytes 36872 | tf_op jit(solution)/shard_map/ppermute | solution.py:30
  71.6 5.3 %collective-permute-done.4 = f32[3,1,8,128]{3,2,1,0:T(8,128)S(1)} collective-permute-done((f32[3,1,8,128]{3,2,1,0:T(8,128)S(1)}, f32[3,1,8,128]{3,2,1,0:T(8,128)S(1)}, u32[]{:S(2)}, u32[]{:S(2)}) %collective-permute-start.4) | collective-permute-done | bytes 12320 | tf_op jit(solution)/shard_map/ppermute | solution.py:30
  76.9 1.9 collective-permute-start.7
  78.8 6.2 %collective-permute-start.6 = (f32[3,4,1,128]{3,2,1,0:T(1,128)S(1)}, f32[3,4,1,128]{3,2,1,0:T(1,128)S(1)}, u32[]{:S(2)}, u32[]{:S(2)}) collective-permute-start(f32[3,4,1,128]{3,2,1,0:T(1,128)S(1)} %get-tuple-element.31), channel_id=1, source_target_pairs={{0,1},{1,2},{2,3},{4,5},{5,6},{6,7},{8,9},{9,10},{10,11},{12,13},{... | collective-permute-start | bytes 18440 | tf_op jit(solution)/shard_map/ppermute | solution.py:30
  85.0 1.3 copy.58
  86.3 1.3 copy.62
  88.5 30.7 %shard_map.87 = f32[16,128,4]{2,1,0:T(8,128)} custom-call(f32[16,128,5]{2,1,0:T(8,128)} %bitcast.82, f32[6,40,128]{2,1,0:T(8,128)} %copy.60.source_ref), custom_call_target="tpu_custom_call" | custom-call | tf_op jit(solution)/shard_map/pallas_call | solution.py:129
  121.4 2.0 collective-permute-start.9
  123.4 3.3 %collective-permute-start.8 = (f32[3,1,8,128]{3,2,1,0:T(8,128)S(1)}, f32[3,1,8,128]{3,2,1,0:T(8,128)S(1)}, u32[]{:S(2)}, u32[]{:S(2)}) collective-permute-start(f32[3,1,8,128]{3,2,1,0:T(8,128)S(1)} %get-tuple-element.35), channel_id=1, source_target_pairs={{0,4},{4,8},{8,12},{12,16},{16,20},{20,24},{24,28},{28,32},{32,36}... | collective-permute-start | bytes 36872 | tf_op jit(solution)/shard_map/ppermute | solution.py:30
  127.4 4.7 %collective-permute-done.8 = f32[3,1,8,128]{3,2,1,0:T(8,128)S(1)} collective-permute-done((f32[3,1,8,128]{3,2,1,0:T(8,128)S(1)}, f32[3,1,8,128]{3,2,1,0:T(8,128)S(1)}, u32[]{:S(2)}, u32[]{:S(2)}) %collective-permute-start.8) | collective-permute-done | bytes 12320 | tf_op jit(solution)/shard_map/ppermute | solution.py:30
  132.1 1.9 collective-permute-start.11
  134.0 5.1 %collective-permute-start.10 = (f32[3,4,1,128]{3,2,1,0:T(1,128)S(1)}, f32[3,4,1,128]{3,2,1,0:T(1,128)S(1)}, u32[]{:S(2)}, u32[]{:S(2)}) collective-permute-start(f32[3,4,1,128]{3,2,1,0:T(1,128)S(1)} %get-tuple-element.29), channel_id=1, source_target_pairs={{0,1},{1,2},{2,3},{4,5},{5,6},{6,7},{8,9},{9,10},{10,11},{12,13},{... | collective-permute-start | bytes 18440 | tf_op jit(solution)/shard_map/ppermute | solution.py:30
  140.7 29.3 %shard_map.88 = f32[16,128,3]{2,1,0:T(8,128)} custom-call(f32[16,128,4]{2,1,0:T(8,128)} %bitcast.77, f32[7,40,128]{2,1,0:T(8,128)} %copy.64.source_ref), custom_call_target="tpu_custom_call" | custom-call | tf_op jit(solution)/shard_map/pallas_call | solution.py:129
  170.1 1.6 copy.65
  171.7 1.9 collective-permute-start.13
  173.6 3.4 %collective-permute-start.12 = (f32[3,1,8,128]{3,2,1,0:T(8,128)S(1)}, f32[3,1,8,128]{3,2,1,0:T(8,128)S(1)}, u32[]{:S(2)}, u32[]{:S(2)}) collective-permute-start(f32[3,1,8,128]{3,2,1,0:T(8,128)S(1)} %get-tuple-element.33), channel_id=1, source_target_pairs={{0,4},{4,8},{8,12},{12,16},{16,20},{20,24},{24,28},{28,32},{32,36}... | collective-permute-start | bytes 36872 | tf_op jit(solution)/shard_map/ppermute | solution.py:30
  177.0 5.2 %collective-permute-done.12 = f32[3,1,8,128]{3,2,1,0:T(8,128)S(1)} collective-permute-done((f32[3,1,8,128]{3,2,1,0:T(8,128)S(1)}, f32[3,1,8,128]{3,2,1,0:T(8,128)S(1)}, u32[]{:S(2)}, u32[]{:S(2)}) %collective-permute-start.12) | collective-permute-done | bytes 12320 | tf_op jit(solution)/shard_map/ppermute | solution.py:30
  182.3 1.9 collective-permute-start.15
  184.2 6.8 %collective-permute-start.14 = (f32[3,4,1,128]{3,2,1,0:T(1,128)S(1)}, f32[3,4,1,128]{3,2,1,0:T(1,128)S(1)}, u32[]{:S(2)}, u32[]{:S(2)}) collective-permute-start(f32[3,4,1,128]{3,2,1,0:T(1,128)S(1)} %get-tuple-element.27), channel_id=1, source_target_pairs={{0,1},{1,2},{2,3},{4,5},{5,6},{6,7},{8,9},{9,10},{10,11},{12,13},{... | collective-permute-start | bytes 18440 | tf_op jit(solution)/shard_map/ppermute | solution.py:30
  192.6 29.3 %shard_map.89 = f32[16,128,3]{2,1,0:T(8,128)} custom-call(f32[16,128,4]{2,1,0:T(8,128)} %bitcast.78, f32[7,40,128]{2,1,0:T(8,128)} %copy.67.source_ref), custom_call_target="tpu_custom_call" | custom-call | tf_op jit(solution)/shard_map/pallas_call | solution.py:129
  222.0 1.6 copy.68
  223.7 1.9 collective-permute-start.16
  225.6 6.9 %collective-permute-done.16 = f32[8,8,128]{2,1,0:T(8,128)S(1)} collective-permute-done((f32[8,8,128]{2,1,0:T(8,128)S(1)}, f32[8,8,128]{2,1,0:T(8,128)S(1)}, u32[]{:S(2)}, u32[]{:S(2)}) %collective-permute-start.16) | collective-permute-done | bytes 32800 | tf_op jit(solution)/shard_map/ppermute | solution.py:39
  (104 shorter events, 12.6 us)
Async XLA Ops:
  2.1 18.8 %copy-start.1 = (f32[3,2,8,128]{3,2,1,0:T(8,128)S(1)}, f32[3,2,8,128]{3,2,1,0:T(8,128)}, u32[]{:S(2)}) copy-start(f32[3,2,8,128]{3,2,1,0:T(8,128)} %param.7) | copy-start | bytes 73732
  2.1 18.8 %copy-start.2 = (f32[3,2,8,128]{3,2,1,0:T(8,128)S(1)}, f32[3,2,8,128]{3,2,1,0:T(8,128)}, u32[]{:S(2)}) copy-start(f32[3,2,8,128]{3,2,1,0:T(8,128)} %param.8) | copy-start | bytes 73732
  2.2 11.8 %collective-permute-start.1 = (f32[7,1,8,128]{3,2,1,0:T(8,128)S(1)}, f32[7,1,8,128]{3,2,1,0:T(8,128)S(1)}, u32[]{:S(2)}, u32[]{:S(2)}) collective-permute-start(f32[7,1,8,128]{3,2,1,0:T(8,128)S(1)} %get-tuple-element.20), channel_id=1, source_target_pairs={{4,0},{8,4},{12,8},{16,12},{20,16},{24,20},{28,24},{32,28},{36,32}... | collective-permute-start | bytes 86024 | tf_op jit(solution)/shard_map/ppermute | solution.py:31
  12.1 8.8 %collective-permute-start = (f32[7,1,8,128]{3,2,1,0:T(8,128)S(1)}, f32[7,1,8,128]{3,2,1,0:T(8,128)S(1)}, u32[]{:S(2)}, u32[]{:S(2)}) collective-permute-start(f32[7,1,8,128]{3,2,1,0:T(8,128)S(1)} %get-tuple-element.19), channel_id=1, source_target_pairs={{0,4},{4,8},{8,12},{12,16},{16,20},{20,24},{24,28},{28,32},{32,36}... | collective-permute-start | bytes 86024 | tf_op jit(solution)/shard_map/ppermute | solution.py:30
  20.9 9.4 %collective-permute-start.3 = (f32[7,4,1,128]{3,2,1,0:T(1,128)S(1)}, f32[7,4,1,128]{3,2,1,0:T(1,128)S(1)}, u32[]{:S(2)}, u32[]{:S(2)}) collective-permute-start(f32[7,4,1,128]{3,2,1,0:T(1,128)S(1)} %get-tuple-element.14), channel_id=1, source_target_pairs={{1,0},{2,1},{3,2},{5,4},{6,5},{7,6},{9,8},{10,9},{11,10},{13,12},{... | collective-permute-start | bytes 43016 | tf_op jit(solution)/shard_map/ppermute | solution.py:31
  25.0 4.0 %copy-start.3 = (s32[2,8]{1,0:T(2,128)S(1)}, s32[2,8]{1,0:T(2,128)}, u32[]{:S(2)}) copy-start(s32[2,8]{1,0:T(2,128)} %param.11) | copy-start | bytes 196
  25.0 5.4 %collective-permute-start.2 = (f32[7,4,1,128]{3,2,1,0:T(1,128)S(1)}, f32[7,4,1,128]{3,2,1,0:T(1,128)S(1)}, u32[]{:S(2)}, u32[]{:S(2)}) collective-permute-start(f32[7,4,1,128]{3,2,1,0:T(1,128)S(1)} %get-tuple-element.13), channel_id=1, source_target_pairs={{0,1},{1,2},{2,3},{4,5},{5,6},{6,7},{8,9},{9,10},{10,11},{12,13},{... | collective-permute-start | bytes 43016 | tf_op jit(solution)/shard_map/ppermute | solution.py:30
  65.5 0.7 copy-start.4
  65.5 0.7 copy-start.5
  66.2 5.3 %collective-permute-start.5 = (f32[3,1,8,128]{3,2,1,0:T(8,128)S(1)}, f32[3,1,8,128]{3,2,1,0:T(8,128)S(1)}, u32[]{:S(2)}, u32[]{:S(2)}) collective-permute-start(f32[3,1,8,128]{3,2,1,0:T(8,128)S(1)} %get-tuple-element.38), channel_id=1, source_target_pairs={{4,0},{8,4},{12,8},{16,12},{20,16},{24,20},{28,24},{32,28},{36,32}... | collective-permute-start | bytes 36872 | tf_op jit(solution)/shard_map/ppermute | solution.py:31
  68.2 8.7 %collective-permute-start.4 = (f32[3,1,8,128]{3,2,1,0:T(8,128)S(1)}, f32[3,1,8,128]{3,2,1,0:T(8,128)S(1)}, u32[]{:S(2)}, u32[]{:S(2)}) collective-permute-start(f32[3,1,8,128]{3,2,1,0:T(8,128)S(1)} %get-tuple-element.37), channel_id=1, source_target_pairs={{0,4},{4,8},{8,12},{12,16},{16,20},{20,24},{24,28},{28,32},{32,36}... | collective-permute-start | bytes 36872 | tf_op jit(solution)/shard_map/ppermute | solution.py:30
  76.9 10.8 %collective-permute-start.7 = (f32[3,4,1,128]{3,2,1,0:T(1,128)S(1)}, f32[3,4,1,128]{3,2,1,0:T(1,128)S(1)}, u32[]{:S(2)}, u32[]{:S(2)}) collective-permute-start(f32[3,4,1,128]{3,2,1,0:T(1,128)S(1)} %get-tuple-element.32), channel_id=1, source_target_pairs={{1,0},{2,1},{3,2},{5,4},{6,5},{7,6},{9,8},{10,9},{11,10},{13,12},{... | collective-permute-start | bytes 18440 | tf_op jit(solution)/shard_map/ppermute | solution.py:31
  78.8 8.9 %collective-permute-start.6 = (f32[3,4,1,128]{3,2,1,0:T(1,128)S(1)}, f32[3,4,1,128]{3,2,1,0:T(1,128)S(1)}, u32[]{:S(2)}, u32[]{:S(2)}) collective-permute-start(f32[3,4,1,128]{3,2,1,0:T(1,128)S(1)} %get-tuple-element.31), channel_id=1, source_target_pairs={{0,1},{1,2},{2,3},{4,5},{5,6},{6,7},{8,9},{9,10},{10,11},{12,13},{... | collective-permute-start | bytes 18440 | tf_op jit(solution)/shard_map/ppermute | solution.py:30
  120.6 6.1 %copy-start = (f32[16,128,4]{2,1,0:T(8,128)S(1)}, f32[16,128,4]{2,1,0:T(8,128)}, u32[]{:S(2)}) copy-start(f32[16,128,4]{2,1,0:T(8,128)} %shard_map.87) | copy-start | bytes 98308
  120.6 0.7 copy-start.7
  121.4 5.9 %collective-permute-start.9 = (f32[3,1,8,128]{3,2,1,0:T(8,128)S(1)}, f32[3,1,8,128]{3,2,1,0:T(8,128)S(1)}, u32[]{:S(2)}, u32[]{:S(2)}) collective-permute-start(f32[3,1,8,128]{3,2,1,0:T(8,128)S(1)} %get-tuple-element.36), channel_id=1, source_target_pairs={{4,0},{8,4},{12,8},{16,12},{20,16},{24,20},{28,24},{32,28},{36,32}... | collective-permute-start | bytes 36872 | tf_op jit(solution)/shard_map/ppermute | solution.py:31
  123.4 8.7 %collective-permute-start.8 = (f32[3,1,8,128]{3,2,1,0:T(8,128)S(1)}, f32[3,1,8,128]{3,2,1,0:T(8,128)S(1)}, u32[]{:S(2)}, u32[]{:S(2)}) collective-permute-start(f32[3,1,8,128]{3,2,1,0:T(8,128)S(1)} %get-tuple-element.35), channel_id=1, source_target_pairs={{0,4},{4,8},{8,12},{12,16},{16,20},{20,24},{24,28},{28,32},{32,36}... | collective-permute-start | bytes 36872 | tf_op jit(solution)/shard_map/ppermute | solution.py:30
  132.1 7.2 %collective-permute-start.11 = (f32[3,4,1,128]{3,2,1,0:T(1,128)S(1)}, f32[3,4,1,128]{3,2,1,0:T(1,128)S(1)}, u32[]{:S(2)}, u32[]{:S(2)}) collective-permute-start(f32[3,4,1,128]{3,2,1,0:T(1,128)S(1)} %get-tuple-element.30), channel_id=1, source_target_pairs={{1,0},{2,1},{3,2},{5,4},{6,5},{7,6},{9,8},{10,9},{11,10},{13,12},{... | collective-permute-start | bytes 18440 | tf_op jit(solution)/shard_map/ppermute | solution.py:31
  134.0 5.9 %collective-permute-start.10 = (f32[3,4,1,128]{3,2,1,0:T(1,128)S(1)}, f32[3,4,1,128]{3,2,1,0:T(1,128)S(1)}, u32[]{:S(2)}, u32[]{:S(2)}) collective-permute-start(f32[3,4,1,128]{3,2,1,0:T(1,128)S(1)} %get-tuple-element.29), channel_id=1, source_target_pairs={{0,1},{1,2},{2,3},{4,5},{5,6},{6,7},{8,9},{9,10},{10,11},{12,13},{... | collective-permute-start | bytes 18440 | tf_op jit(solution)/shard_map/ppermute | solution.py:30
  171.7 5.3 %copy-start.6 = (s32[2,8]{1,0:T(2,128)S(1)}, s32[2,8]{1,0:T(2,128)}, u32[]{:S(2)}) copy-start(s32[2,8]{1,0:T(2,128)} %param.12) | copy-start | bytes 196
  171.7 5.3 %collective-permute-start.13 = (f32[3,1,8,128]{3,2,1,0:T(8,128)S(1)}, f32[3,1,8,128]{3,2,1,0:T(8,128)S(1)}, u32[]{:S(2)}, u32[]{:S(2)}) collective-permute-start(f32[3,1,8,128]{3,2,1,0:T(8,128)S(1)} %get-tuple-element.34), channel_id=1, source_target_pairs={{4,0},{8,4},{12,8},{16,12},{20,16},{24,20},{28,24},{32,28},{36,32}... | collective-permute-start | bytes 36872 | tf_op jit(solution)/shard_map/ppermute | solution.py:31
  173.6 8.7 %collective-permute-start.12 = (f32[3,1,8,128]{3,2,1,0:T(8,128)S(1)}, f32[3,1,8,128]{3,2,1,0:T(8,128)S(1)}, u32[]{:S(2)}, u32[]{:S(2)}) collective-permute-start(f32[3,1,8,128]{3,2,1,0:T(8,128)S(1)} %get-tuple-element.33), channel_id=1, source_target_pairs={{0,4},{4,8},{8,12},{12,16},{16,20},{20,24},{24,28},{28,32},{32,36}... | collective-permute-start | bytes 36872 | tf_op jit(solution)/shard_map/ppermute | solution.py:30
  182.3 8.8 %collective-permute-start.15 = (f32[3,4,1,128]{3,2,1,0:T(1,128)S(1)}, f32[3,4,1,128]{3,2,1,0:T(1,128)S(1)}, u32[]{:S(2)}, u32[]{:S(2)}) collective-permute-start(f32[3,4,1,128]{3,2,1,0:T(1,128)S(1)} %get-tuple-element.28), channel_id=1, source_target_pairs={{1,0},{2,1},{3,2},{5,4},{6,5},{7,6},{9,8},{10,9},{11,10},{13,12},{... | collective-permute-start | bytes 18440 | tf_op jit(solution)/shard_map/ppermute | solution.py:31
  184.2 7.6 %collective-permute-start.14 = (f32[3,4,1,128]{3,2,1,0:T(1,128)S(1)}, f32[3,4,1,128]{3,2,1,0:T(1,128)S(1)}, u32[]{:S(2)}, u32[]{:S(2)}) collective-permute-start(f32[3,4,1,128]{3,2,1,0:T(1,128)S(1)} %get-tuple-element.27), channel_id=1, source_target_pairs={{0,1},{1,2},{2,3},{4,5},{5,6},{6,7},{8,9},{9,10},{10,11},{12,13},{... | collective-permute-start | bytes 18440 | tf_op jit(solution)/shard_map/ppermute | solution.py:30
  223.7 8.9 %collective-permute-start.16 = (f32[8,8,128]{2,1,0:T(8,128)S(1)}, f32[8,8,128]{2,1,0:T(8,128)S(1)}, u32[]{:S(2)}, u32[]{:S(2)}) collective-permute-start(f32[8,8,128]{2,1,0:T(8,128)S(1)} %pad_maximum_fusion.12), channel_id=1, source_target_pairs={{0,4},{4,8},{8,12},{12,16},{16,20},{20,24},{24,28},{28,32},{32,36}... | collective-permute-start | bytes 98312 | tf_op jit(solution)/shard_map/ppermute | solution.py:39

commit v3 on v2

--- a/solution.py
+++ b/solution.py
@@ -20,17 +20,34 @@
 NEIGHBOUR_STEPS = [(-1, -1), (-1, 0), (-1, 1), (0, -1), (0, 0), (0, 1), (1, -1), (1, 0), (1, 1)]
 
 
-def with_halo(array, sides, width):
-    for axis, dim in sides:
-        count, length = (lax.axis_size(axis), array.shape[dim])
-        up = [(i, (i + 1) % count) for i in range(count - 1)]
-        down = [(j, i) for i, j in up]
-        last = lax.slice_in_dim(array, length - width, length, axis=dim)
-        initial = lax.slice_in_dim(array, 0, width, axis=dim)
-        before = lax.ppermute(last, axis, up)
-        after = lax.ppermute(initial, axis, down)
-        array = jnp.concatenate([before, array, after], axis=dim)
-    return array
+def with_halo(array):
+    down_count, cross_count = (lax.axis_size("down"), lax.axis_size("cross"))
+    row_count, col_count = array.shape[1:3]
+    spans = {-1: (row_count - 1, col_count - 1), 0: (0, 0), 1: (0, 0)}
+    sizes = {-1: (1, 1), 0: (row_count, col_count), 1: (1, 1)}
+
+    def fetch(step_down, step_cross):
+        piece = lax.slice_in_dim(
+            array, spans[step_down][0], spans[step_down][0] + sizes[step_down][0], axis=1
+        )
+        piece = lax.slice_in_dim(
+            piece, spans[step_cross][1], spans[step_cross][1] + sizes[step_cross][1], axis=2
+        )
+        route = []
+        for down_index in range(down_count):
+            for cross_index in range(cross_count):
+                source_down, source_cross = (down_index + step_down, cross_index + step_cross)
+                if 0 <= source_down < down_count and 0 <= source_cross < cross_count:
+                    route.append(
+                        (source_down * cross_count + source_cross, down_index * cross_count + cross_index)
+                    )
+        return lax.ppermute(piece, ("down", "cross"), route)
+
+    grid = [
+        [array if (step_down, step_cross) == (0, 0) else fetch(step_down, step_cross) for step_cross in (-1, 0, 1)]
+        for step_down in (-1, 0, 1)
+    ]
+    return jnp.concatenate([jnp.concatenate(row, axis=2) for row in grid], axis=1)
 
 
 def from_behind(block, axis, distance):
@@ -169,7 +186,7 @@
     slot_ids = lax.broadcasted_iota(jnp.int32, (row_count, col_count, slot_count), 2)
     live = (slot_ids < counts[:, :, None]).astype(jnp.float32)
     state = jnp.concatenate([positions, velocities, live[None]], axis=0)
-    state_pad = with_halo(state, (("down", 1), ("cross", 2)), 1)
+    state_pad = with_halo(state)
     far = jnp.where(state_pad[6:7] > 0.0, state_pad[:3], FAR_AWAY)
     sums = pair_pass(
         "density",
@@ -183,7 +200,7 @@
     inverse = 1.0 / density
     pressure = STIFFNESS * (density - REST_DENSITY) * inverse * inverse
     viscosity = plastic_viscosity + yield_stress / jnp.sqrt(1.0 + strain)
-    dens_pad = with_halo(jnp.stack([inverse, pressure, viscosity]), (("down", 1), ("cross", 2)), 1)
+    dens_pad = with_halo(jnp.stack([inverse, pressure, viscosity]))
     forces = pair_pass(
         "force",
         jnp.concatenate([positions, pressure[None], viscosity[None]], axis=0),
@@ -198,7 +215,7 @@
     target = jnp.concatenate([positions, viscosity[None]], axis=0)
     current = predicted
     for sweep_index in range(JACOBI):
-        speed_pad = with_halo(current, (("down", 1), ("cross", 2)), 1)
+        speed_pad = with_halo(current)
         pulled = pair_pass(
             "jacobi",
             target,

time: 238 us -> 288 us (1.21)
  starting transfers between devices: 61.5 us -> 114 us
    ppermute x16 -> x32, starting transfers between devices: 59.6 us -> 112 us  [fetch(): return lax.ppermute(piece, ('down', 'cross'), route)]
    ppermute x16 -> x32, waiting for transfers between devices: 23.5 us -> 22.5 us  [fetch(): return lax.ppermute(piece, ('down', 'cross'), route)]
  transfers between devices with their start and end apart: 17 -> 33, of which waited for: 7 -> 5; matrix products, arithmetic and copies ran while one was open for 2% -> 2% of each run, Pallas kernels for 0% -> 0%
where the time goes in v3:
time: 288 us; the launch traced here: 286 us
  Pallas kernels  121 us (42%)
  starting transfers between devices  114 us (40%)
  waiting for transfers between devices  29.4 us (10%)
  local copies, waits for them, and re-layouts  13.9 us (5%)
  other arithmetic  7.1 us (2%)
    pallas_call x4, Pallas kernels, pair_pass(): pl.pallas_call(kernel, out_shape=jax.ShapeDtypeStruct((block_count, slot_...  121 us
    ppermute x32, starting transfers between devices, fetch(): return lax.ppermute(piece, ('down', 'cross'), route)  112 us
    ppermute x32, waiting for transfers between devices, fetch(): return lax.ppermute(piece, ('down', 'cross'), route)  22.5 us
    ppermute x1, waiting for transfers between devices, from_behind(): return lax.ppermute(block, axis, route)  6.95 us
  transfers between devices with their start and end apart: 33, of which 5 were waited for; matrix products, arithmetic and copies ran while one was open for 2% of the time, Pallas kernels for 0%

profile of v3, /device:TPU:3, one launch (start us, length us, event | category | flops | bytes accessed | tf_op | source)
XLA Modules:
  0.0 286.4 jit_solution(17402837725868915279)
XLA Ops:
  2.3 10.5 %collective-permute-start.7 = (f32[7,1,1,128]{3,2,1,0:T(1,128)S(1)}, f32[7,1,1,128]{3,2,1,0:T(1,128)S(1)}, u32[]{:S(2)}, u32[]{:S(2)}) collective-permute-start(f32[7,1,1,128]{3,2,1,0:T(1,128)S(1)} %get-tuple-element.18), channel_id=1, source_target_pairs={{5,0},{6,1},{7,2},{9,4},{10,5},{11,6},{13,8},{14,9},{15,10},{17,12... | collective-permute-start | bytes 10760 | tf_op jit(solution)/shard_map/ppermute | solution.py:44
  12.8 2.6 collective-permute-start.6
  15.4 3.5 %collective-permute-start.5 = (f32[7,1,1,128]{3,2,1,0:T(1,128)S(1)}, f32[7,1,1,128]{3,2,1,0:T(1,128)S(1)}, u32[]{:S(2)}, u32[]{:S(2)}) collective-permute-start(f32[7,1,1,128]{3,2,1,0:T(1,128)S(1)} %get-tuple-element.19), channel_id=1, source_target_pairs={{4,1},{5,2},{6,3},{8,5},{9,6},{10,7},{12,9},{13,10},{14,11},{16,13... | collective-permute-start | bytes 10760 | tf_op jit(solution)/shard_map/ppermute | solution.py:44
  19.0 1.9 collective-permute-start.4
  20.9 1.9 collective-permute-start.2
  22.9 6.5 %collective-permute-start.3 = (f32[7,2,1,128]{3,2,1,0:T(1,128)S(1)}, f32[7,2,1,128]{3,2,1,0:T(1,128)S(1)}, u32[]{:S(2)}, u32[]{:S(2)}) collective-permute-start(f32[7,2,1,128]{3,2,1,0:T(1,128)S(1)} %get-tuple-element.23), channel_id=1, source_target_pairs={{0,1},{1,2},{2,3},{4,5},{5,6},{6,7},{8,9},{9,10},{10,11},{12,13},{... | collective-permute-start | bytes 21512 | tf_op jit(solution)/shard_map/ppermute | solution.py:44
  29.4 2.4 collective-permute-start.1
  31.8 2.3 collective-permute-start
  35.6 5.4 %collective-permute-done = f32[7,1,1,128]{3,2,1,0:T(1,128)S(1)} collective-permute-done((f32[7,1,1,128]{3,2,1,0:T(1,128)S(1)}, f32[7,1,1,128]{3,2,1,0:T(1,128)S(1)}, u32[]{:S(2)}, u32[]{:S(2)}) %collective-permute-start) | collective-permute-done | bytes 3616 | tf_op jit(solution)/shard_map/ppermute | solution.py:44
  41.8 31.4 %shard_map.86 = f32[16,128,2]{2,1,0:T(8,128)} custom-call(f32[16,128,6]{2,1,0:T(8,128)} %bitcast.83, f32[6,40,128]{2,1,0:T(8,128)} %copy.53.source_ref), custom_call_target="tpu_custom_call" | custom-call | tf_op jit(solution)/shard_map/pallas_call | solution.py:146
  73.2 2.5 fusion.3
  76.8 2.1 collective-permute-start.15
  79.0 2.9 %collective-permute-start.14 = (f32[3,1,8,128]{3,2,1,0:T(8,128)S(1)}, f32[3,1,8,128]{3,2,1,0:T(8,128)S(1)}, u32[]{:S(2)}, u32[]{:S(2)}) collective-permute-start(f32[3,1,8,128]{3,2,1,0:T(8,128)S(1)} %get-tuple-element.52), channel_id=1, source_target_pairs={{4,0},{5,1},{6,2},{7,3},{8,4},{9,5},{10,6},{11,7},{12,8},{13,9},{1... | collective-permute-start | bytes 36872 | tf_op jit(solution)/shard_map/ppermute | solution.py:44
  81.9 4.2 %collective-permute-start.13 = (f32[3,1,1,128]{3,2,1,0:T(1,128)S(1)}, f32[3,1,1,128]{3,2,1,0:T(1,128)S(1)}, u32[]{:S(2)}, u32[]{:S(2)}) collective-permute-start(f32[3,1,1,128]{3,2,1,0:T(1,128)S(1)} %get-tuple-element.49), channel_id=1, source_target_pairs={{4,1},{5,2},{6,3},{8,5},{9,6},{10,7},{12,9},{13,10},{14,11},{16,13... | collective-permute-start | bytes 4616 | tf_op jit(solution)/shard_map/ppermute | solution.py:44
  90.0 7.4 %collective-permute-start.11 = (f32[3,2,1,128]{3,2,1,0:T(1,128)S(1)}, f32[3,2,1,128]{3,2,1,0:T(1,128)S(1)}, u32[]{:S(2)}, u32[]{:S(2)}) collective-permute-start(f32[3,2,1,128]{3,2,1,0:T(1,128)S(1)} %get-tuple-element.53), channel_id=1, source_target_pairs={{0,1},{1,2},{2,3},{4,5},{5,6},{6,7},{8,9},{9,10},{10,11},{12,13},{... | collective-permute-start | bytes 9224 | tf_op jit(solution)/shard_map/ppermute | solution.py:44
  97.4 2.2 collective-permute-start.9
  99.6 3.6 %collective-permute-start.8 = (f32[3,1,1,128]{3,2,1,0:T(1,128)S(1)}, f32[3,1,1,128]{3,2,1,0:T(1,128)S(1)}, u32[]{:S(2)}, u32[]{:S(2)}) collective-permute-start(f32[3,1,1,128]{3,2,1,0:T(1,128)S(1)} %get-tuple-element.47), channel_id=1, source_target_pairs={{0,5},{1,6},{2,7},{4,9},{5,10},{6,11},{8,13},{9,14},{10,15},{12,17... | collective-permute-start | bytes 4616 | tf_op jit(solution)/shard_map/ppermute | solution.py:44
  106.0 2.8 collective-permute-done.8
  109.6 30.7 %shard_map.87 = f32[16,128,4]{2,1,0:T(8,128)} custom-call(f32[16,128,5]{2,1,0:T(8,128)} %bitcast.82, f32[6,40,128]{2,1,0:T(8,128)} %copy.60.source_ref), custom_call_target="tpu_custom_call" | custom-call | tf_op jit(solution)/shard_map/pallas_call | solution.py:146
  142.5 3.4 %collective-permute-start.23 = (f32[3,1,1,128]{3,2,1,0:T(1,128)S(1)}, f32[3,1,1,128]{3,2,1,0:T(1,128)S(1)}, u32[]{:S(2)}, u32[]{:S(2)}) collective-permute-start(f32[3,1,1,128]{3,2,1,0:T(1,128)S(1)} %get-tuple-element.40), channel_id=1, source_target_pairs={{5,0},{6,1},{7,2},{9,4},{10,5},{11,6},{13,8},{14,9},{15,10},{17,12... | collective-permute-start | bytes 4616 | tf_op jit(solution)/shard_map/ppermute | solution.py:44
  145.9 5.3 %collective-permute-start.21 = (f32[3,1,1,128]{3,2,1,0:T(1,128)S(1)}, f32[3,1,1,128]{3,2,1,0:T(1,128)S(1)}, u32[]{:S(2)}, u32[]{:S(2)}) collective-permute-start(f32[3,1,1,128]{3,2,1,0:T(1,128)S(1)} %get-tuple-element.41), channel_id=1, source_target_pairs={{4,1},{5,2},{6,3},{8,5},{9,6},{10,7},{12,9},{13,10},{14,11},{16,13... | collective-permute-start | bytes 4616 | tf_op jit(solution)/shard_map/ppermute | solution.py:44
  153.8 5.7 %collective-permute-start.22 = (f32[3,1,8,128]{3,2,1,0:T(8,128)S(1)}, f32[3,1,8,128]{3,2,1,0:T(8,128)S(1)}, u32[]{:S(2)}, u32[]{:S(2)}) collective-permute-start(f32[3,1,8,128]{3,2,1,0:T(8,128)S(1)} %get-tuple-element.44), channel_id=1, source_target_pairs={{4,0},{5,1},{6,2},{7,3},{8,4},{9,5},{10,6},{11,7},{12,8},{13,9},{1... | collective-permute-start | bytes 36872 | tf_op jit(solution)/shard_map/ppermute | solution.py:44
  161.4 5.5 %collective-permute-start.19 = (f32[3,2,1,128]{3,2,1,0:T(1,128)S(1)}, f32[3,2,1,128]{3,2,1,0:T(1,128)S(1)}, u32[]{:S(2)}, u32[]{:S(2)}) collective-permute-start(f32[3,2,1,128]{3,2,1,0:T(1,128)S(1)} %get-tuple-element.45), channel_id=1, source_target_pairs={{0,1},{1,2},{2,3},{4,5},{5,6},{6,7},{8,9},{9,10},{10,11},{12,13},{... | collective-permute-start | bytes 9224 | tf_op jit(solution)/shard_map/ppermute | solution.py:44
  170.9 7.1 %collective-permute-done.16 = f32[3,1,1,128]{3,2,1,0:T(1,128)S(1)} collective-permute-done((f32[3,1,1,128]{3,2,1,0:T(1,128)S(1)}, f32[3,1,1,128]{3,2,1,0:T(1,128)S(1)}, u32[]{:S(2)}, u32[]{:S(2)}) %collective-permute-start.16) | collective-permute-done | bytes 1568 | tf_op jit(solution)/shard_map/ppermute | solution.py:44
  178.9 29.4 %shard_map.88 = f32[16,128,3]{2,1,0:T(8,128)} custom-call(f32[16,128,4]{2,1,0:T(8,128)} %bitcast.77, f32[7,40,128]{2,1,0:T(8,128)} %copy.64.source_ref), custom_call_target="tpu_custom_call" | custom-call | tf_op jit(solution)/shard_map/pallas_call | solution.py:146
  209.9 2.0 collective-permute-start.31
  211.8 5.3 %collective-permute-start.29 = (f32[3,1,1,128]{3,2,1,0:T(1,128)S(1)}, f32[3,1,1,128]{3,2,1,0:T(1,128)S(1)}, u32[]{:S(2)}, u32[]{:S(2)}) collective-permute-start(f32[3,1,1,128]{3,2,1,0:T(1,128)S(1)} %get-tuple-element.33), channel_id=1, source_target_pairs={{4,1},{5,2},{6,3},{8,5},{9,6},{10,7},{12,9},{13,10},{14,11},{16,13... | collective-permute-start | bytes 4616 | tf_op jit(solution)/shard_map/ppermute | solution.py:44
  219.1 5.9 %collective-permute-start.30 = (f32[3,1,8,128]{3,2,1,0:T(8,128)S(1)}, f32[3,1,8,128]{3,2,1,0:T(8,128)S(1)}, u32[]{:S(2)}, u32[]{:S(2)}) collective-permute-start(f32[3,1,8,128]{3,2,1,0:T(8,128)S(1)} %get-tuple-element.36), channel_id=1, source_target_pairs={{4,0},{5,1},{6,2},{7,3},{8,4},{9,5},{10,6},{11,7},{12,8},{13,9},{1... | collective-permute-start | bytes 36872 | tf_op jit(solution)/shard_map/ppermute | solution.py:44
  226.9 5.3 %collective-permute-start.27 = (f32[3,2,1,128]{3,2,1,0:T(1,128)S(1)}, f32[3,2,1,128]{3,2,1,0:T(1,128)S(1)}, u32[]{:S(2)}, u32[]{:S(2)}) collective-permute-start(f32[3,2,1,128]{3,2,1,0:T(1,128)S(1)} %get-tuple-element.37), channel_id=1, source_target_pairs={{0,1},{1,2},{2,3},{4,5},{5,6},{6,7},{8,9},{9,10},{10,11},{12,13},{... | collective-permute-start | bytes 9224 | tf_op jit(solution)/shard_map/ppermute | solution.py:44
  236.2 7.2 %collective-permute-done.24 = f32[3,1,1,128]{3,2,1,0:T(1,128)S(1)} collective-permute-done((f32[3,1,1,128]{3,2,1,0:T(1,128)S(1)}, f32[3,1,1,128]{3,2,1,0:T(1,128)S(1)}, u32[]{:S(2)}, u32[]{:S(2)}) %collective-permute-start.24) | collective-permute-done | bytes 1568 | tf_op jit(solution)/shard_map/ppermute | solution.py:44
  244.2 29.4 %shard_map.89 = f32[16,128,3]{2,1,0:T(8,128)} custom-call(f32[16,128,4]{2,1,0:T(8,128)} %bitcast.78, f32[7,40,128]{2,1,0:T(8,128)} %copy.67.source_ref), custom_call_target="tpu_custom_call" | custom-call | tf_op jit(solution)/shard_map/pallas_call | solution.py:146
  277.2 6.9 %collective-permute-done.32 = f32[8,8,128]{2,1,0:T(8,128)S(1)} collective-permute-done((f32[8,8,128]{2,1,0:T(8,128)S(1)}, f32[8,8,128]{2,1,0:T(8,128)S(1)}, u32[]{:S(2)}, u32[]{:S(2)}) %collective-permute-start.32) | collective-permute-done | bytes 32800 | tf_op jit(solution)/shard_map/ppermute | solution.py:56
  (140 shorter events, 39.7 us)
Async XLA Ops:
  2.3 20.6 %collective-permute-start.7 = (f32[7,1,1,128]{3,2,1,0:T(1,128)S(1)}, f32[7,1,1,128]{3,2,1,0:T(1,128)S(1)}, u32[]{:S(2)}, u32[]{:S(2)}) collective-permute-start(f32[7,1,1,128]{3,2,1,0:T(1,128)S(1)} %get-tuple-element.18), channel_id=1, source_target_pairs={{5,0},{6,1},{7,2},{9,4},{10,5},{11,6},{13,8},{14,9},{15,10},{17,12... | collective-permute-start | bytes 10760 | tf_op jit(solution)/shard_map/ppermute | solution.py:44
  12.8 28.2 %collective-permute-start.6 = (f32[7,1,8,128]{3,2,1,0:T(8,128)S(1)}, f32[7,1,8,128]{3,2,1,0:T(8,128)S(1)}, u32[]{:S(2)}, u32[]{:S(2)}) collective-permute-start(f32[7,1,8,128]{3,2,1,0:T(8,128)S(1)} %get-tuple-element.22), channel_id=1, source_target_pairs={{4,0},{5,1},{6,2},{7,3},{8,4},{9,5},{10,6},{11,7},{12,8},{13,9},{1... | collective-permute-start | bytes 86024 | tf_op jit(solution)/shard_map/ppermute | solution.py:44
  15.4 14.0 %collective-permute-start.5 = (f32[7,1,1,128]{3,2,1,0:T(1,128)S(1)}, f32[7,1,1,128]{3,2,1,0:T(1,128)S(1)}, u32[]{:S(2)}, u32[]{:S(2)}) collective-permute-start(f32[7,1,1,128]{3,2,1,0:T(1,128)S(1)} %get-tuple-element.19), channel_id=1, source_target_pairs={{4,1},{5,2},{6,3},{8,5},{9,6},{10,7},{12,9},{13,10},{14,11},{16,13... | collective-permute-start | bytes 10760 | tf_op jit(solution)/shard_map/ppermute | solution.py:44
  19.0 21.9 %collective-permute-start.4 = (f32[7,2,1,128]{3,2,1,0:T(1,128)S(1)}, f32[7,2,1,128]{3,2,1,0:T(1,128)S(1)}, u32[]{:S(2)}, u32[]{:S(2)}) collective-permute-start(f32[7,2,1,128]{3,2,1,0:T(1,128)S(1)} %get-tuple-element.24), channel_id=1, source_target_pairs={{1,0},{2,1},{3,2},{5,4},{6,5},{7,6},{9,8},{10,9},{11,10},{13,12},{... | collective-permute-start | bytes 21512 | tf_op jit(solution)/shard_map/ppermute | solution.py:44
  20.9 10.8 %collective-permute-start.2 = (f32[7,1,1,128]{3,2,1,0:T(1,128)S(1)}, f32[7,1,1,128]{3,2,1,0:T(1,128)S(1)}, u32[]{:S(2)}, u32[]{:S(2)}) collective-permute-start(f32[7,1,1,128]{3,2,1,0:T(1,128)S(1)} %get-tuple-element.20), channel_id=1, source_target_pairs={{1,4},{2,5},{3,6},{5,8},{6,9},{7,10},{9,12},{10,13},{11,14},{13,16... | collective-permute-start | bytes 10760 | tf_op jit(solution)/shard_map/ppermute | solution.py:44
  22.9 18.0 %collective-permute-start.3 = (f32[7,2,1,128]{3,2,1,0:T(1,128)S(1)}, f32[7,2,1,128]{3,2,1,0:T(1,128)S(1)}, u32[]{:S(2)}, u32[]{:S(2)}) collective-permute-start(f32[7,2,1,128]{3,2,1,0:T(1,128)S(1)} %get-tuple-element.23), channel_id=1, source_target_pairs={{0,1},{1,2},{2,3},{4,5},{5,6},{6,7},{8,9},{9,10},{10,11},{12,13},{... | collective-permute-start | bytes 21512 | tf_op jit(solution)/shard_map/ppermute | solution.py:44
  29.4 11.5 %collective-permute-start.1 = (f32[7,1,8,128]{3,2,1,0:T(8,128)S(1)}, f32[7,1,8,128]{3,2,1,0:T(8,128)S(1)}, u32[]{:S(2)}, u32[]{:S(2)}) collective-permute-start(f32[7,1,8,128]{3,2,1,0:T(8,128)S(1)} %get-tuple-element.21), channel_id=1, source_target_pairs={{0,4},{1,5},{2,6},{3,7},{4,8},{5,9},{6,10},{7,11},{8,12},{9,13},{1... | collective-permute-start | bytes 86024 | tf_op jit(solution)/shard_map/ppermute | solution.py:44
  31.8 9.1 %collective-permute-start = (f32[7,1,1,128]{3,2,1,0:T(1,128)S(1)}, f32[7,1,1,128]{3,2,1,0:T(1,128)S(1)}, u32[]{:S(2)}, u32[]{:S(2)}) collective-permute-start(f32[7,1,1,128]{3,2,1,0:T(1,128)S(1)} %get-tuple-element.17), channel_id=1, source_target_pairs={{0,5},{1,6},{2,7},{4,9},{5,10},{6,11},{8,13},{9,14},{10,15},{12,17... | collective-permute-start | bytes 10760 | tf_op jit(solution)/shard_map/ppermute | solution.py:44
  76.8 13.2 %collective-permute-start.15 = (f32[3,1,1,128]{3,2,1,0:T(1,128)S(1)}, f32[3,1,1,128]{3,2,1,0:T(1,128)S(1)}, u32[]{:S(2)}, u32[]{:S(2)}) collective-permute-start(f32[3,1,1,128]{3,2,1,0:T(1,128)S(1)} %get-tuple-element.48), channel_id=1, source_target_pairs={{5,0},{6,1},{7,2},{9,4},{10,5},{11,6},{13,8},{14,9},{15,10},{17,12... | collective-permute-start | bytes 4616 | tf_op jit(solution)/shard_map/ppermute | solution.py:44
  79.0 29.8 %collective-permute-start.14 = (f32[3,1,8,128]{3,2,1,0:T(8,128)S(1)}, f32[3,1,8,128]{3,2,1,0:T(8,128)S(1)}, u32[]{:S(2)}, u32[]{:S(2)}) collective-permute-start(f32[3,1,8,128]{3,2,1,0:T(8,128)S(1)} %get-tuple-element.52), channel_id=1, source_target_pairs={{4,0},{5,1},{6,2},{7,3},{8,4},{9,5},{10,6},{11,7},{12,8},{13,9},{1... | collective-permute-start | bytes 36872 | tf_op jit(solution)/shard_map/ppermute | solution.py:44
  81.9 15.5 %collective-permute-start.13 = (f32[3,1,1,128]{3,2,1,0:T(1,128)S(1)}, f32[3,1,1,128]{3,2,1,0:T(1,128)S(1)}, u32[]{:S(2)}, u32[]{:S(2)}) collective-permute-start(f32[3,1,1,128]{3,2,1,0:T(1,128)S(1)} %get-tuple-element.49), channel_id=1, source_target_pairs={{4,1},{5,2},{6,3},{8,5},{9,6},{10,7},{12,9},{13,10},{14,11},{16,13... | collective-permute-start | bytes 4616 | tf_op jit(solution)/shard_map/ppermute | solution.py:44
  86.1 22.6 %collective-permute-start.12 = (f32[3,2,1,128]{3,2,1,0:T(1,128)S(1)}, f32[3,2,1,128]{3,2,1,0:T(1,128)S(1)}, u32[]{:S(2)}, u32[]{:S(2)}) collective-permute-start(f32[3,2,1,128]{3,2,1,0:T(1,128)S(1)} %get-tuple-element.54), channel_id=1, source_target_pairs={{1,0},{2,1},{3,2},{5,4},{6,5},{7,6},{9,8},{10,9},{11,10},{13,12},{... | collective-permute-start | bytes 9224 | tf_op jit(solution)/shard_map/ppermute | solution.py:44
  88.0 11.6 %collective-permute-start.10 = (f32[3,1,1,128]{3,2,1,0:T(1,128)S(1)}, f32[3,1,1,128]{3,2,1,0:T(1,128)S(1)}, u32[]{:S(2)}, u32[]{:S(2)}) collective-permute-start(f32[3,1,1,128]{3,2,1,0:T(1,128)S(1)} %get-tuple-element.50), channel_id=1, source_target_pairs={{1,4},{2,5},{3,6},{5,8},{6,9},{7,10},{9,12},{10,13},{11,14},{13,16... | collective-permute-start | bytes 4616 | tf_op jit(solution)/shard_map/ppermute | solution.py:44
  90.0 18.8 %collective-permute-start.11 = (f32[3,2,1,128]{3,2,1,0:T(1,128)S(1)}, f32[3,2,1,128]{3,2,1,0:T(1,128)S(1)}, u32[]{:S(2)}, u32[]{:S(2)}) collective-permute-start(f32[3,2,1,128]{3,2,1,0:T(1,128)S(1)} %get-tuple-element.53), channel_id=1, source_target_pairs={{0,1},{1,2},{2,3},{4,5},{5,6},{6,7},{8,9},{9,10},{10,11},{12,13},{... | collective-permute-start | bytes 9224 | tf_op jit(solution)/shard_map/ppermute | solution.py:44
  97.4 11.3 %collective-permute-start.9 = (f32[3,1,8,128]{3,2,1,0:T(8,128)S(1)}, f32[3,1,8,128]{3,2,1,0:T(8,128)S(1)}, u32[]{:S(2)}, u32[]{:S(2)}) collective-permute-start(f32[3,1,8,128]{3,2,1,0:T(8,128)S(1)} %get-tuple-element.51), channel_id=1, source_target_pairs={{0,4},{1,5},{2,6},{3,7},{4,8},{5,9},{6,10},{7,11},{8,12},{9,13},{1... | collective-permute-start | bytes 36872 | tf_op jit(solution)/shard_map/ppermute | solution.py:44
  99.6 9.1 %collective-permute-start.8 = (f32[3,1,1,128]{3,2,1,0:T(1,128)S(1)}, f32[3,1,1,128]{3,2,1,0:T(1,128)S(1)}, u32[]{:S(2)}, u32[]{:S(2)}) collective-permute-start(f32[3,1,1,128]{3,2,1,0:T(1,128)S(1)} %get-tuple-element.47), channel_id=1, source_target_pairs={{0,5},{1,6},{2,7},{4,9},{5,10},{6,11},{8,13},{9,14},{10,15},{12,17... | collective-permute-start | bytes 4616 | tf_op jit(solution)/shard_map/ppermute | solution.py:44
  142.5 18.9 %collective-permute-start.23 = (f32[3,1,1,128]{3,2,1,0:T(1,128)S(1)}, f32[3,1,1,128]{3,2,1,0:T(1,128)S(1)}, u32[]{:S(2)}, u32[]{:S(2)}) collective-permute-start(f32[3,1,1,128]{3,2,1,0:T(1,128)S(1)} %get-tuple-element.40), channel_id=1, source_target_pairs={{5,0},{6,1},{7,2},{9,4},{10,5},{11,6},{13,8},{14,9},{15,10},{17,12... | collective-permute-start | bytes 4616 | tf_op jit(solution)/shard_map/ppermute | solution.py:44
  145.9 21.0 %collective-permute-start.21 = (f32[3,1,1,128]{3,2,1,0:T(1,128)S(1)}, f32[3,1,1,128]{3,2,1,0:T(1,128)S(1)}, u32[]{:S(2)}, u32[]{:S(2)}) collective-permute-start(f32[3,1,1,128]{3,2,1,0:T(1,128)S(1)} %get-tuple-element.41), channel_id=1, source_target_pairs={{4,1},{5,2},{6,3},{8,5},{9,6},{10,7},{12,9},{13,10},{14,11},{16,13... | collective-permute-start | bytes 4616 | tf_op jit(solution)/shard_map/ppermute | solution.py:44
  151.2 17.7 %collective-permute-start.18 = (f32[3,1,1,128]{3,2,1,0:T(1,128)S(1)}, f32[3,1,1,128]{3,2,1,0:T(1,128)S(1)}, u32[]{:S(2)}, u32[]{:S(2)}) collective-permute-start(f32[3,1,1,128]{3,2,1,0:T(1,128)S(1)} %get-tuple-element.42), channel_id=1, source_target_pairs={{1,4},{2,5},{3,6},{5,8},{6,9},{7,10},{9,12},{10,13},{11,14},{13,16... | collective-permute-start | bytes 4616 | tf_op jit(solution)/shard_map/ppermute | solution.py:44
  153.8 24.3 %collective-permute-start.22 = (f32[3,1,8,128]{3,2,1,0:T(8,128)S(1)}, f32[3,1,8,128]{3,2,1,0:T(8,128)S(1)}, u32[]{:S(2)}, u32[]{:S(2)}) collective-permute-start(f32[3,1,8,128]{3,2,1,0:T(8,128)S(1)} %get-tuple-element.44), channel_id=1, source_target_pairs={{4,0},{5,1},{6,2},{7,3},{8,4},{9,5},{10,6},{11,7},{12,8},{13,9},{1... | collective-permute-start | bytes 36872 | tf_op jit(solution)/shard_map/ppermute | solution.py:44
  159.5 18.6 %collective-permute-start.20 = (f32[3,2,1,128]{3,2,1,0:T(1,128)S(1)}, f32[3,2,1,128]{3,2,1,0:T(1,128)S(1)}, u32[]{:S(2)}, u32[]{:S(2)}) collective-permute-start(f32[3,2,1,128]{3,2,1,0:T(1,128)S(1)} %get-tuple-element.46), channel_id=1, source_target_pairs={{1,0},{2,1},{3,2},{5,4},{6,5},{7,6},{9,8},{10,9},{11,10},{13,12},{... | collective-permute-start | bytes 9224 | tf_op jit(solution)/shard_map/ppermute | solution.py:44
  161.4 16.6 %collective-permute-start.19 = (f32[3,2,1,128]{3,2,1,0:T(1,128)S(1)}, f32[3,2,1,128]{3,2,1,0:T(1,128)S(1)}, u32[]{:S(2)}, u32[]{:S(2)}) collective-permute-start(f32[3,2,1,128]{3,2,1,0:T(1,128)S(1)} %get-tuple-element.45), channel_id=1, source_target_pairs={{0,1},{1,2},{2,3},{4,5},{5,6},{6,7},{8,9},{9,10},{10,11},{12,13},{... | collective-permute-start | bytes 9224 | tf_op jit(solution)/shard_map/ppermute | solution.py:44
  167.0 11.1 %collective-permute-start.17 = (f32[3,1,8,128]{3,2,1,0:T(8,128)S(1)}, f32[3,1,8,128]{3,2,1,0:T(8,128)S(1)}, u32[]{:S(2)}, u32[]{:S(2)}) collective-permute-start(f32[3,1,8,128]{3,2,1,0:T(8,128)S(1)} %get-tuple-element.43), channel_id=1, source_target_pairs={{0,4},{1,5},{2,6},{3,7},{4,8},{5,9},{6,10},{7,11},{8,12},{9,13},{1... | collective-permute-start | bytes 36872 | tf_op jit(solution)/shard_map/ppermute | solution.py:44
  168.9 9.1 %collective-permute-start.16 = (f32[3,1,1,128]{3,2,1,0:T(1,128)S(1)}, f32[3,1,1,128]{3,2,1,0:T(1,128)S(1)}, u32[]{:S(2)}, u32[]{:S(2)}) collective-permute-start(f32[3,1,1,128]{3,2,1,0:T(1,128)S(1)} %get-tuple-element.39), channel_id=1, source_target_pairs={{0,5},{1,6},{2,7},{4,9},{5,10},{6,11},{8,13},{9,14},{10,15},{12,17... | collective-permute-start | bytes 4616 | tf_op jit(solution)/shard_map/ppermute | solution.py:44
  209.9 17.1 %collective-permute-start.31 = (f32[3,1,1,128]{3,2,1,0:T(1,128)S(1)}, f32[3,1,1,128]{3,2,1,0:T(1,128)S(1)}, u32[]{:S(2)}, u32[]{:S(2)}) collective-permute-start(f32[3,1,1,128]{3,2,1,0:T(1,128)S(1)} %get-tuple-element.32), channel_id=1, source_target_pairs={{5,0},{6,1},{7,2},{9,4},{10,5},{11,6},{13,8},{14,9},{15,10},{17,12... | collective-permute-start | bytes 4616 | tf_op jit(solution)/shard_map/ppermute | solution.py:44
  211.8 20.5 %collective-permute-start.29 = (f32[3,1,1,128]{3,2,1,0:T(1,128)S(1)}, f32[3,1,1,128]{3,2,1,0:T(1,128)S(1)}, u32[]{:S(2)}, u32[]{:S(2)}) collective-permute-start(f32[3,1,1,128]{3,2,1,0:T(1,128)S(1)} %get-tuple-element.33), channel_id=1, source_target_pairs={{4,1},{5,2},{6,3},{8,5},{9,6},{10,7},{12,9},{13,10},{14,11},{16,13... | collective-permute-start | bytes 4616 | tf_op jit(solution)/shard_map/ppermute | solution.py:44
  217.2 17.1 %collective-permute-start.26 = (f32[3,1,1,128]{3,2,1,0:T(1,128)S(1)}, f32[3,1,1,128]{3,2,1,0:T(1,128)S(1)}, u32[]{:S(2)}, u32[]{:S(2)}) collective-permute-start(f32[3,1,1,128]{3,2,1,0:T(1,128)S(1)} %get-tuple-element.34), channel_id=1, source_target_pairs={{1,4},{2,5},{3,6},{5,8},{6,9},{7,10},{9,12},{10,13},{11,14},{13,16... | collective-permute-start | bytes 4616 | tf_op jit(solution)/shard_map/ppermute | solution.py:44
  219.1 24.3 %collective-permute-start.30 = (f32[3,1,8,128]{3,2,1,0:T(8,128)S(1)}, f32[3,1,8,128]{3,2,1,0:T(8,128)S(1)}, u32[]{:S(2)}, u32[]{:S(2)}) collective-permute-start(f32[3,1,8,128]{3,2,1,0:T(8,128)S(1)} %get-tuple-element.36), channel_id=1, source_target_pairs={{4,0},{5,1},{6,2},{7,3},{8,4},{9,5},{10,6},{11,7},{12,8},{13,9},{1... | collective-permute-start | bytes 36872 | tf_op jit(solution)/shard_map/ppermute | solution.py:44
  225.0 18.4 %collective-permute-start.28 = (f32[3,2,1,128]{3,2,1,0:T(1,128)S(1)}, f32[3,2,1,128]{3,2,1,0:T(1,128)S(1)}, u32[]{:S(2)}, u32[]{:S(2)}) collective-permute-start(f32[3,2,1,128]{3,2,1,0:T(1,128)S(1)} %get-tuple-element.38), channel_id=1, source_target_pairs={{1,0},{2,1},{3,2},{5,4},{6,5},{7,6},{9,8},{10,9},{11,10},{13,12},{... | collective-permute-start | bytes 9224 | tf_op jit(solution)/shard_map/ppermute | solution.py:44
  226.9 16.4 %collective-permute-start.27 = (f32[3,2,1,128]{3,2,1,0:T(1,128)S(1)}, f32[3,2,1,128]{3,2,1,0:T(1,128)S(1)}, u32[]{:S(2)}, u32[]{:S(2)}) collective-permute-start(f32[3,2,1,128]{3,2,1,0:T(1,128)S(1)} %get-tuple-element.37), channel_id=1, source_target_pairs={{0,1},{1,2},{2,3},{4,5},{5,6},{6,7},{8,9},{9,10},{10,11},{12,13},{... | collective-permute-start | bytes 9224 | tf_op jit(solution)/shard_map/ppermute | solution.py:44
  232.3 11.1 %collective-permute-start.25 = (f32[3,1,8,128]{3,2,1,0:T(8,128)S(1)}, f32[3,1,8,128]{3,2,1,0:T(8,128)S(1)}, u32[]{:S(2)}, u32[]{:S(2)}) collective-permute-start(f32[3,1,8,128]{3,2,1,0:T(8,128)S(1)} %get-tuple-element.35), channel_id=1, source_target_pairs={{0,4},{1,5},{2,6},{3,7},{4,8},{5,9},{6,10},{7,11},{8,12},{9,13},{1... | collective-permute-start | bytes 36872 | tf_op jit(solution)/shard_map/ppermute | solution.py:44
  234.2 9.1 %collective-permute-start.24 = (f32[3,1,1,128]{3,2,1,0:T(1,128)S(1)}, f32[3,1,1,128]{3,2,1,0:T(1,128)S(1)}, u32[]{:S(2)}, u32[]{:S(2)}) collective-permute-start(f32[3,1,1,128]{3,2,1,0:T(1,128)S(1)} %get-tuple-element.31), channel_id=1, source_target_pairs={{0,5},{1,6},{2,7},{4,9},{5,10},{6,11},{8,13},{9,14},{10,15},{12,17... | collective-permute-start | bytes 4616 | tf_op jit(solution)/shard_map/ppermute | solution.py:44
  (9 other events, 51.4 us)

commit v4 on v2

--- a/solution.py
+++ b/solution.py
@@ -65,7 +65,7 @@
 
 
 FAR_AWAY = 1.0e4
-CHUNK = 16
+CHUNK = 32
 
 
 def pair_pass(kind, target, source, row_count, col_count):
@@ -98,7 +98,8 @@
                     other[1] + float(step_cross) - mine[1],
                     other[2] - mine[2],
                 ]
-                distance = jnp.sqrt(gaps[0] * gaps[0] + gaps[1] * gaps[1] + gaps[2] * gaps[2])
+                squared = gaps[0] * gaps[0] + gaps[1] * gaps[1] + gaps[2] * gaps[2]
+                distance = squared * lax.rsqrt(jnp.maximum(squared, 1.0e-30))
                 falloff = jnp.maximum(1.0 - distance, 0.0)
                 cubed = falloff * falloff * falloff
                 if kind == "density":

time: 238 us -> 196 us (0.82)
  Pallas kernels: 121 us -> 78.5 us
    pallas_call x4, Pallas kernels: 121 us -> 78.5 us  [pair_pass(): pl.pallas_call(kernel, out_shape=jax.ShapeDtypeStruct((block_count, slot_...]
  transfers between devices with their start and end apart: 17 -> 17, of which waited for: 7 -> 7; matrix products, arithmetic and copies ran while one was open for 2% -> 3% of each run, Pallas kernels for 0% -> 0%
where the time goes in v4:
time: 196 us; the launch traced here: 192 us
  Pallas kernels  78.5 us (40%)
  starting transfers between devices  61.5 us (31%)
  waiting for transfers between devices  30.5 us (16%)
  local copies, waits for them, and re-layouts  13.8 us (7%)
  other arithmetic  7 us (4%)
    pallas_call x4, Pallas kernels, pair_pass(): pl.pallas_call(kernel, out_shape=jax.ShapeDtypeStruct((block_count, slot_...  78.5 us
    ppermute x8, starting transfers between devices, with_halo(): before = lax.ppermute(last, axis, up)  34.1 us
    ppermute x8, starting transfers between devices, with_halo(): after = lax.ppermute(initial, axis, down)  25.5 us
    ppermute x8, waiting for transfers between devices, with_halo(): before = lax.ppermute(last, axis, up)  23.5 us
    ppermute x1, waiting for transfers between devices, from_behind(): return lax.ppermute(block, axis, route)  6.95 us
  transfers between devices with their start and end apart: 17, of which 7 were waited for; matrix products, arithmetic and copies ran while one was open for 3% of the time, Pallas kernels for 0%

profile of v4, /device:TPU:3, one launch (start us, length us, event | category | flops | bytes accessed | tf_op | source)
XLA Modules:
  0.0 192.4 jit_solution(11268309907043639258)
XLA Ops:
  2.2 9.9 %collective-permute-start.1 = (f32[7,1,8,128]{3,2,1,0:T(8,128)S(1)}, f32[7,1,8,128]{3,2,1,0:T(8,128)S(1)}, u32[]{:S(2)}, u32[]{:S(2)}) collective-permute-start(f32[7,1,8,128]{3,2,1,0:T(8,128)S(1)} %get-tuple-element.20), channel_id=1, source_target_pairs={{4,0},{8,4},{12,8},{16,12},{20,16},{24,20},{28,24},{32,28},{36,32}... | collective-permute-start | bytes 86024 | tf_op jit(solution)/shard_map/ppermute | solution.py:31
  12.1 1.9 collective-permute-start
  14.0 6.9 %collective-permute-done = f32[7,1,8,128]{3,2,1,0:T(8,128)S(1)} collective-permute-done((f32[7,1,8,128]{3,2,1,0:T(8,128)S(1)}, f32[7,1,8,128]{3,2,1,0:T(8,128)S(1)}, u32[]{:S(2)}, u32[]{:S(2)}) %collective-permute-start) | collective-permute-done | bytes 28704 | tf_op jit(solution)/shard_map/ppermute | solution.py:30
  20.9 4.0 %collective-permute-start.3 = (f32[7,4,1,128]{3,2,1,0:T(1,128)S(1)}, f32[7,4,1,128]{3,2,1,0:T(1,128)S(1)}, u32[]{:S(2)}, u32[]{:S(2)}) collective-permute-start(f32[7,4,1,128]{3,2,1,0:T(1,128)S(1)} %get-tuple-element.14), channel_id=1, source_target_pairs={{1,0},{2,1},{3,2},{5,4},{6,5},{7,6},{9,8},{10,9},{11,10},{13,12},{... | collective-permute-start | bytes 43016 | tf_op jit(solution)/shard_map/ppermute | solution.py:31
  25.0 3.9 %collective-permute-start.2 = (f32[7,4,1,128]{3,2,1,0:T(1,128)S(1)}, f32[7,4,1,128]{3,2,1,0:T(1,128)S(1)}, u32[]{:S(2)}, u32[]{:S(2)}) collective-permute-start(f32[7,4,1,128]{3,2,1,0:T(1,128)S(1)} %get-tuple-element.13), channel_id=1, source_target_pairs={{0,1},{1,2},{2,3},{4,5},{5,6},{6,7},{8,9},{9,10},{10,11},{12,13},{... | collective-permute-start | bytes 43016 | tf_op jit(solution)/shard_map/ppermute | solution.py:30
  29.0 1.3 copy.51
  31.2 20.8 %shard_map.86 = f32[16,128,2]{2,1,0:T(8,128)} custom-call(f32[16,128,6]{2,1,0:T(8,128)} %bitcast.83, f32[6,40,128]{2,1,0:T(8,128)} %copy.53.source_ref), custom_call_target="tpu_custom_call" | custom-call | tf_op jit(solution)/shard_map/pallas_call | solution.py:130
  52.0 2.5 %fusion.3 = (f32[16,128]{1,0:T(8,128)S(1)}, f32[16,128]{1,0:T(8,128)S(1)}, f32[1,16,128]{0,2,1:T(8,128)S(1)}) fusion(f32[2,16,128]{0,2,1:T(8,128)} %bitcast.81, s32[16]{0:T(128)S(1)} %lt.80), kind=kLoop, calls=%fused_computation.9 | loop fusion | flops 16384 | bytes 41024 | tf_op jit(solution)/shard_map/mul | solution.py:182
  55.6 1.9 %collective-permute-start.5 = (f32[3,1,8,128]{3,2,1,0:T(8,128)S(1)}, f32[3,1,8,128]{3,2,1,0:T(8,128)S(1)}, u32[]{:S(2)}, u32[]{:S(2)}) collective-permute-start(f32[3,1,8,128]{3,2,1,0:T(8,128)S(1)} %get-tuple-element.38), channel_id=1, source_target_pairs={{4,0},{8,4},{12,8},{16,12},{20,16},{24,20},{28,24},{32,28},{36,32}... | collective-permute-start | bytes 36872 | tf_op jit(solution)/shard_map/ppermute | solution.py:31
  57.6 3.3 %collective-permute-start.4 = (f32[3,1,8,128]{3,2,1,0:T(8,128)S(1)}, f32[3,1,8,128]{3,2,1,0:T(8,128)S(1)}, u32[]{:S(2)}, u32[]{:S(2)}) collective-permute-start(f32[3,1,8,128]{3,2,1,0:T(8,128)S(1)} %get-tuple-element.37), channel_id=1, source_target_pairs={{0,4},{4,8},{8,12},{12,16},{16,20},{20,24},{24,28},{28,32},{32,36}... | collective-permute-start | bytes 36872 | tf_op jit(solution)/shard_map/ppermute | solution.py:30
  61.0 5.3 %collective-permute-done.4 = f32[3,1,8,128]{3,2,1,0:T(8,128)S(1)} collective-permute-done((f32[3,1,8,128]{3,2,1,0:T(8,128)S(1)}, f32[3,1,8,128]{3,2,1,0:T(8,128)S(1)}, u32[]{:S(2)}, u32[]{:S(2)}) %collective-permute-start.4) | collective-permute-done | bytes 12320 | tf_op jit(solution)/shard_map/ppermute | solution.py:30
  66.3 1.9 collective-permute-start.7
  68.2 6.2 %collective-permute-start.6 = (f32[3,4,1,128]{3,2,1,0:T(1,128)S(1)}, f32[3,4,1,128]{3,2,1,0:T(1,128)S(1)}, u32[]{:S(2)}, u32[]{:S(2)}) collective-permute-start(f32[3,4,1,128]{3,2,1,0:T(1,128)S(1)} %get-tuple-element.31), channel_id=1, source_target_pairs={{0,1},{1,2},{2,3},{4,5},{5,6},{6,7},{8,9},{9,10},{10,11},{12,13},{... | collective-permute-start | bytes 18440 | tf_op jit(solution)/shard_map/ppermute | solution.py:30
  74.4 1.3 copy.58
  75.8 1.3 copy.62
  77.9 20.3 %shard_map.87 = f32[16,128,4]{2,1,0:T(8,128)} custom-call(f32[16,128,5]{2,1,0:T(8,128)} %bitcast.82, f32[6,40,128]{2,1,0:T(8,128)} %copy.60.source_ref), custom_call_target="tpu_custom_call" | custom-call | tf_op jit(solution)/shard_map/pallas_call | solution.py:130
  100.3 2.0 %collective-permute-start.9 = (f32[3,1,8,128]{3,2,1,0:T(8,128)S(1)}, f32[3,1,8,128]{3,2,1,0:T(8,128)S(1)}, u32[]{:S(2)}, u32[]{:S(2)}) collective-permute-start(f32[3,1,8,128]{3,2,1,0:T(8,128)S(1)} %get-tuple-element.36), channel_id=1, source_target_pairs={{4,0},{8,4},{12,8},{16,12},{20,16},{24,20},{28,24},{32,28},{36,32}... | collective-permute-start | bytes 36872 | tf_op jit(solution)/shard_map/ppermute | solution.py:31
  102.3 3.3 %collective-permute-start.8 = (f32[3,1,8,128]{3,2,1,0:T(8,128)S(1)}, f32[3,1,8,128]{3,2,1,0:T(8,128)S(1)}, u32[]{:S(2)}, u32[]{:S(2)}) collective-permute-start(f32[3,1,8,128]{3,2,1,0:T(8,128)S(1)} %get-tuple-element.35), channel_id=1, source_target_pairs={{0,4},{4,8},{8,12},{12,16},{16,20},{20,24},{24,28},{28,32},{32,36}... | collective-permute-start | bytes 36872 | tf_op jit(solution)/shard_map/ppermute | solution.py:30
  106.3 4.7 %collective-permute-done.8 = f32[3,1,8,128]{3,2,1,0:T(8,128)S(1)} collective-permute-done((f32[3,1,8,128]{3,2,1,0:T(8,128)S(1)}, f32[3,1,8,128]{3,2,1,0:T(8,128)S(1)}, u32[]{:S(2)}, u32[]{:S(2)}) %collective-permute-start.8) | collective-permute-done | bytes 12320 | tf_op jit(solution)/shard_map/ppermute | solution.py:30
  111.0 1.9 collective-permute-start.11
  112.9 5.1 %collective-permute-start.10 = (f32[3,4,1,128]{3,2,1,0:T(1,128)S(1)}, f32[3,4,1,128]{3,2,1,0:T(1,128)S(1)}, u32[]{:S(2)}, u32[]{:S(2)}) collective-permute-start(f32[3,4,1,128]{3,2,1,0:T(1,128)S(1)} %get-tuple-element.29), channel_id=1, source_target_pairs={{0,1},{1,2},{2,3},{4,5},{5,6},{6,7},{8,9},{9,10},{10,11},{12,13},{... | collective-permute-start | bytes 18440 | tf_op jit(solution)/shard_map/ppermute | solution.py:30
  119.6 18.7 %shard_map.88 = f32[16,128,3]{2,1,0:T(8,128)} custom-call(f32[16,128,4]{2,1,0:T(8,128)} %bitcast.77, f32[7,40,128]{2,1,0:T(8,128)} %copy.64.source_ref), custom_call_target="tpu_custom_call" | custom-call | tf_op jit(solution)/shard_map/pallas_call | solution.py:130
  138.4 1.6 copy.65
  140.0 1.9 collective-permute-start.13
  141.9 3.4 %collective-permute-start.12 = (f32[3,1,8,128]{3,2,1,0:T(8,128)S(1)}, f32[3,1,8,128]{3,2,1,0:T(8,128)S(1)}, u32[]{:S(2)}, u32[]{:S(2)}) collective-permute-start(f32[3,1,8,128]{3,2,1,0:T(8,128)S(1)} %get-tuple-element.33), channel_id=1, source_target_pairs={{0,4},{4,8},{8,12},{12,16},{16,20},{20,24},{24,28},{28,32},{32,36}... | collective-permute-start | bytes 36872 | tf_op jit(solution)/shard_map/ppermute | solution.py:30
  145.3 5.2 %collective-permute-done.12 = f32[3,1,8,128]{3,2,1,0:T(8,128)S(1)} collective-permute-done((f32[3,1,8,128]{3,2,1,0:T(8,128)S(1)}, f32[3,1,8,128]{3,2,1,0:T(8,128)S(1)}, u32[]{:S(2)}, u32[]{:S(2)}) %collective-permute-start.12) | collective-permute-done | bytes 12320 | tf_op jit(solution)/shard_map/ppermute | solution.py:30
  150.6 1.9 collective-permute-start.15
  152.5 6.8 %collective-permute-start.14 = (f32[3,4,1,128]{3,2,1,0:T(1,128)S(1)}, f32[3,4,1,128]{3,2,1,0:T(1,128)S(1)}, u32[]{:S(2)}, u32[]{:S(2)}) collective-permute-start(f32[3,4,1,128]{3,2,1,0:T(1,128)S(1)} %get-tuple-element.27), channel_id=1, source_target_pairs={{0,1},{1,2},{2,3},{4,5},{5,6},{6,7},{8,9},{9,10},{10,11},{12,13},{... | collective-permute-start | bytes 18440 | tf_op jit(solution)/shard_map/ppermute | solution.py:30
  160.9 18.7 %shard_map.89 = f32[16,128,3]{2,1,0:T(8,128)} custom-call(f32[16,128,4]{2,1,0:T(8,128)} %bitcast.78, f32[7,40,128]{2,1,0:T(8,128)} %copy.67.source_ref), custom_call_target="tpu_custom_call" | custom-call | tf_op jit(solution)/shard_map/pallas_call | solution.py:130
  179.6 1.6 copy.68
  181.4 1.9 collective-permute-start.16
  183.3 6.9 %collective-permute-done.16 = f32[8,8,128]{2,1,0:T(8,128)S(1)} collective-permute-done((f32[8,8,128]{2,1,0:T(8,128)S(1)}, f32[8,8,128]{2,1,0:T(8,128)S(1)}, u32[]{:S(2)}, u32[]{:S(2)}) %collective-permute-start.16) | collective-permute-done | bytes 32800 | tf_op jit(solution)/shard_map/ppermute | solution.py:39
  (104 shorter events, 12.6 us)
Async XLA Ops:
  2.1 18.8 %copy-start.1 = (f32[3,2,8,128]{3,2,1,0:T(8,128)S(1)}, f32[3,2,8,128]{3,2,1,0:T(8,128)}, u32[]{:S(2)}) copy-start(f32[3,2,8,128]{3,2,1,0:T(8,128)} %param.7) | copy-start | bytes 73732
  2.1 18.8 %copy-start.2 = (f32[3,2,8,128]{3,2,1,0:T(8,128)S(1)}, f32[3,2,8,128]{3,2,1,0:T(8,128)}, u32[]{:S(2)}) copy-start(f32[3,2,8,128]{3,2,1,0:T(8,128)} %param.8) | copy-start | bytes 73732
  2.2 11.8 %collective-permute-start.1 = (f32[7,1,8,128]{3,2,1,0:T(8,128)S(1)}, f32[7,1,8,128]{3,2,1,0:T(8,128)S(1)}, u32[]{:S(2)}, u32[]{:S(2)}) collective-permute-start(f32[7,1,8,128]{3,2,1,0:T(8,128)S(1)} %get-tuple-element.20), channel_id=1, source_target_pairs={{4,0},{8,4},{12,8},{16,12},{20,16},{24,20},{28,24},{32,28},{36,32}... | collective-permute-start | bytes 86024 | tf_op jit(solution)/shard_map/ppermute | solution.py:31
  12.1 8.8 %collective-permute-start = (f32[7,1,8,128]{3,2,1,0:T(8,128)S(1)}, f32[7,1,8,128]{3,2,1,0:T(8,128)S(1)}, u32[]{:S(2)}, u32[]{:S(2)}) collective-permute-start(f32[7,1,8,128]{3,2,1,0:T(8,128)S(1)} %get-tuple-element.19), channel_id=1, source_target_pairs={{0,4},{4,8},{8,12},{12,16},{16,20},{20,24},{24,28},{28,32},{32,36}... | collective-permute-start | bytes 86024 | tf_op jit(solution)/shard_map/ppermute | solution.py:30
  20.9 9.4 %collective-permute-start.3 = (f32[7,4,1,128]{3,2,1,0:T(1,128)S(1)}, f32[7,4,1,128]{3,2,1,0:T(1,128)S(1)}, u32[]{:S(2)}, u32[]{:S(2)}) collective-permute-start(f32[7,4,1,128]{3,2,1,0:T(1,128)S(1)} %get-tuple-element.14), channel_id=1, source_target_pairs={{1,0},{2,1},{3,2},{5,4},{6,5},{7,6},{9,8},{10,9},{11,10},{13,12},{... | collective-permute-start | bytes 43016 | tf_op jit(solution)/shard_map/ppermute | solution.py:31
  25.0 4.0 %copy-start.3 = (s32[2,8]{1,0:T(2,128)S(1)}, s32[2,8]{1,0:T(2,128)}, u32[]{:S(2)}) copy-start(s32[2,8]{1,0:T(2,128)} %param.11) | copy-start | bytes 196
  25.0 5.4 %collective-permute-start.2 = (f32[7,4,1,128]{3,2,1,0:T(1,128)S(1)}, f32[7,4,1,128]{3,2,1,0:T(1,128)S(1)}, u32[]{:S(2)}, u32[]{:S(2)}) collective-permute-start(f32[7,4,1,128]{3,2,1,0:T(1,128)S(1)} %get-tuple-element.13), channel_id=1, source_target_pairs={{0,1},{1,2},{2,3},{4,5},{5,6},{6,7},{8,9},{9,10},{10,11},{12,13},{... | collective-permute-start | bytes 43016 | tf_op jit(solution)/shard_map/ppermute | solution.py:30
  54.9 0.7 copy-start.4
  54.9 0.7 copy-start.5
  55.6 5.3 %collective-permute-start.5 = (f32[3,1,8,128]{3,2,1,0:T(8,128)S(1)}, f32[3,1,8,128]{3,2,1,0:T(8,128)S(1)}, u32[]{:S(2)}, u32[]{:S(2)}) collective-permute-start(f32[3,1,8,128]{3,2,1,0:T(8,128)S(1)} %get-tuple-element.38), channel_id=1, source_target_pairs={{4,0},{8,4},{12,8},{16,12},{20,16},{24,20},{28,24},{32,28},{36,32}... | collective-permute-start | bytes 36872 | tf_op jit(solution)/shard_map/ppermute | solution.py:31
  57.6 8.7 %collective-permute-start.4 = (f32[3,1,8,128]{3,2,1,0:T(8,128)S(1)}, f32[3,1,8,128]{3,2,1,0:T(8,128)S(1)}, u32[]{:S(2)}, u32[]{:S(2)}) collective-permute-start(f32[3,1,8,128]{3,2,1,0:T(8,128)S(1)} %get-tuple-element.37), channel_id=1, source_target_pairs={{0,4},{4,8},{8,12},{12,16},{16,20},{20,24},{24,28},{28,32},{32,36}... | collective-permute-start | bytes 36872 | tf_op jit(solution)/shard_map/ppermute | solution.py:30
  66.3 10.8 %collective-permute-start.7 = (f32[3,4,1,128]{3,2,1,0:T(1,128)S(1)}, f32[3,4,1,128]{3,2,1,0:T(1,128)S(1)}, u32[]{:S(2)}, u32[]{:S(2)}) collective-permute-start(f32[3,4,1,128]{3,2,1,0:T(1,128)S(1)} %get-tuple-element.32), channel_id=1, source_target_pairs={{1,0},{2,1},{3,2},{5,4},{6,5},{7,6},{9,8},{10,9},{11,10},{13,12},{... | collective-permute-start | bytes 18440 | tf_op jit(solution)/shard_map/ppermute | solution.py:31
  68.2 8.9 %collective-permute-start.6 = (f32[3,4,1,128]{3,2,1,0:T(1,128)S(1)}, f32[3,4,1,128]{3,2,1,0:T(1,128)S(1)}, u32[]{:S(2)}, u32[]{:S(2)}) collective-permute-start(f32[3,4,1,128]{3,2,1,0:T(1,128)S(1)} %get-tuple-element.31), channel_id=1, source_target_pairs={{0,1},{1,2},{2,3},{4,5},{5,6},{6,7},{8,9},{9,10},{10,11},{12,13},{... | collective-permute-start | bytes 18440 | tf_op jit(solution)/shard_map/ppermute | solution.py:30
  99.5 6.1 %copy-start = (f32[16,128,4]{2,1,0:T(8,128)S(1)}, f32[16,128,4]{2,1,0:T(8,128)}, u32[]{:S(2)}) copy-start(f32[16,128,4]{2,1,0:T(8,128)} %shard_map.87) | copy-start | bytes 98308
  99.5 0.7 copy-start.7
  100.3 5.9 %collective-permute-start.9 = (f32[3,1,8,128]{3,2,1,0:T(8,128)S(1)}, f32[3,1,8,128]{3,2,1,0:T(8,128)S(1)}, u32[]{:S(2)}, u32[]{:S(2)}) collective-permute-start(f32[3,1,8,128]{3,2,1,0:T(8,128)S(1)} %get-tuple-element.36), channel_id=1, source_target_pairs={{4,0},{8,4},{12,8},{16,12},{20,16},{24,20},{28,24},{32,28},{36,32}... | collective-permute-start | bytes 36872 | tf_op jit(solution)/shard_map/ppermute | solution.py:31
  102.3 8.7 %collective-permute-start.8 = (f32[3,1,8,128]{3,2,1,0:T(8,128)S(1)}, f32[3,1,8,128]{3,2,1,0:T(8,128)S(1)}, u32[]{:S(2)}, u32[]{:S(2)}) collective-permute-start(f32[3,1,8,128]{3,2,1,0:T(8,128)S(1)} %get-tuple-element.35), channel_id=1, source_target_pairs={{0,4},{4,8},{8,12},{12,16},{16,20},{20,24},{24,28},{28,32},{32,36}... | collective-permute-start | bytes 36872 | tf_op jit(solution)/shard_map/ppermute | solution.py:30
  111.0 7.2 %collective-permute-start.11 = (f32[3,4,1,128]{3,2,1,0:T(1,128)S(1)}, f32[3,4,1,128]{3,2,1,0:T(1,128)S(1)}, u32[]{:S(2)}, u32[]{:S(2)}) collective-permute-start(f32[3,4,1,128]{3,2,1,0:T(1,128)S(1)} %get-tuple-element.30), channel_id=1, source_target_pairs={{1,0},{2,1},{3,2},{5,4},{6,5},{7,6},{9,8},{10,9},{11,10},{13,12},{... | collective-permute-start | bytes 18440 | tf_op jit(solution)/shard_map/ppermute | solution.py:31
  112.9 5.9 %collective-permute-start.10 = (f32[3,4,1,128]{3,2,1,0:T(1,128)S(1)}, f32[3,4,1,128]{3,2,1,0:T(1,128)S(1)}, u32[]{:S(2)}, u32[]{:S(2)}) collective-permute-start(f32[3,4,1,128]{3,2,1,0:T(1,128)S(1)} %get-tuple-element.29), channel_id=1, source_target_pairs={{0,1},{1,2},{2,3},{4,5},{5,6},{6,7},{8,9},{9,10},{10,11},{12,13},{... | collective-permute-start | bytes 18440 | tf_op jit(solution)/shard_map/ppermute | solution.py:30
  140.0 5.3 %copy-start.6 = (s32[2,8]{1,0:T(2,128)S(1)}, s32[2,8]{1,0:T(2,128)}, u32[]{:S(2)}) copy-start(s32[2,8]{1,0:T(2,128)} %param.12) | copy-start | bytes 196
  140.0 5.3 %collective-permute-start.13 = (f32[3,1,8,128]{3,2,1,0:T(8,128)S(1)}, f32[3,1,8,128]{3,2,1,0:T(8,128)S(1)}, u32[]{:S(2)}, u32[]{:S(2)}) collective-permute-start(f32[3,1,8,128]{3,2,1,0:T(8,128)S(1)} %get-tuple-element.34), channel_id=1, source_target_pairs={{4,0},{8,4},{12,8},{16,12},{20,16},{24,20},{28,24},{32,28},{36,32}... | collective-permute-start | bytes 36872 | tf_op jit(solution)/shard_map/ppermute | solution.py:31
  141.9 8.7 %collective-permute-start.12 = (f32[3,1,8,128]{3,2,1,0:T(8,128)S(1)}, f32[3,1,8,128]{3,2,1,0:T(8,128)S(1)}, u32[]{:S(2)}, u32[]{:S(2)}) collective-permute-start(f32[3,1,8,128]{3,2,1,0:T(8,128)S(1)} %get-tuple-element.33), channel_id=1, source_target_pairs={{0,4},{4,8},{8,12},{12,16},{16,20},{20,24},{24,28},{28,32},{32,36}... | collective-permute-start | bytes 36872 | tf_op jit(solution)/shard_map/ppermute | solution.py:30
  150.6 8.8 %collective-permute-start.15 = (f32[3,4,1,128]{3,2,1,0:T(1,128)S(1)}, f32[3,4,1,128]{3,2,1,0:T(1,128)S(1)}, u32[]{:S(2)}, u32[]{:S(2)}) collective-permute-start(f32[3,4,1,128]{3,2,1,0:T(1,128)S(1)} %get-tuple-element.28), channel_id=1, source_target_pairs={{1,0},{2,1},{3,2},{5,4},{6,5},{7,6},{9,8},{10,9},{11,10},{13,12},{... | collective-permute-start | bytes 18440 | tf_op jit(solution)/shard_map/ppermute | solution.py:31
  152.5 7.6 %collective-permute-start.14 = (f32[3,4,1,128]{3,2,1,0:T(1,128)S(1)}, f32[3,4,1,128]{3,2,1,0:T(1,128)S(1)}, u32[]{:S(2)}, u32[]{:S(2)}) collective-permute-start(f32[3,4,1,128]{3,2,1,0:T(1,128)S(1)} %get-tuple-element.27), channel_id=1, source_target_pairs={{0,1},{1,2},{2,3},{4,5},{5,6},{6,7},{8,9},{9,10},{10,11},{12,13},{... | collective-permute-start | bytes 18440 | tf_op jit(solution)/shard_map/ppermute | solution.py:30
  181.4 8.9 %collective-permute-start.16 = (f32[8,8,128]{2,1,0:T(8,128)S(1)}, f32[8,8,128]{2,1,0:T(8,128)S(1)}, u32[]{:S(2)}, u32[]{:S(2)}) collective-permute-start(f32[8,8,128]{2,1,0:T(8,128)S(1)} %pad_maximum_fusion.12), channel_id=1, source_target_pairs={{0,4},{4,8},{8,12},{12,16},{16,20},{20,24},{24,28},{28,32},{32,36}... | collective-permute-start | bytes 98312 | tf_op jit(solution)/shard_map/ppermute | solution.py:39

commit v5 on v4

--- a/solution.py
+++ b/solution.py
@@ -68,7 +68,7 @@
 CHUNK = 32
 
 
-def pair_pass(kind, target, source, row_count, col_count):
+def pair_pass(kind, target, source, row_count, col_count, weights=None):
     slot_count = target.shape[-1]
     block_count = row_count * col_count
     chunk_count = slot_count // CHUNK
@@ -79,7 +79,14 @@
     target_cols = jnp.moveaxis(target.reshape(target_count, block_count, slot_count), 0, 2)
     source_rows = source.reshape(source_count, (row_count + 2) * padded_cols, slot_count)
 
-    def kernel(target_ref, source_ref, out_ref):
+    def kernel(target_ref, source_ref, *refs):
+        if kind == "force":
+            out_ref, weight_ref = refs
+        elif kind == "jacobi":
+            weight_ref, out_ref = refs
+        else:
+            (out_ref,) = refs
+
         def body(step, carry):
             block = step // chunk_count
             first = pl.multiple_of((step % chunk_count) * CHUNK, CHUNK)
@@ -90,9 +97,14 @@
                 jnp.broadcast_to(own[:, k : k + 1], (CHUNK, slot_count)) for k in range(target_count)
             ]
             totals = [jnp.zeros((CHUNK, slot_count), jnp.float32) for k in range(output_count)]
-            for step_down, step_cross in NEIGHBOUR_STEPS:
+            for neighbour, (step_down, step_cross) in enumerate(NEIGHBOUR_STEPS):
                 near = (row + 1 + step_down) * padded_cols + (col + 1 + step_cross)
                 other = [source_ref[k, pl.ds(near, 1), :] for k in range(source_count)]
+                if kind == "jacobi":
+                    pull = weight_ref[step * 9 + neighbour]
+                    for k in range(3):
+                        totals[k] = totals[k] + pull * other[k]
+                    continue
                 gaps = [
                     other[0] + float(step_down) - mine[0],
                     other[1] + float(step_cross) - mine[1],
@@ -114,11 +126,9 @@
                     push = (mine[3] + other[3]) * cubed
                     for k in range(3):
                         totals[k] = totals[k] + push * gaps[k]
-                    totals[3] = totals[3] + (mine[4] + other[5]) * other[4] * cubed
-                else:
-                    pull = (mine[3] + other[3]) * cubed
-                    for k in range(3):
-                        totals[k] = totals[k] + pull * other[4 + k]
+                    pull = (mine[4] + other[5]) * cubed
+                    weight_ref[step * 9 + neighbour] = pull
+                    totals[3] = totals[3] + pull * other[4]
             for k in range(output_count):
                 out_ref[block, pl.ds(first, CHUNK), pl.ds(k, 1)] = jnp.sum(
                     totals[k], axis=1, keepdims=True
@@ -127,11 +137,22 @@
 
         lax.fori_loop(0, block_count * chunk_count, body, 0)
 
-    result = pl.pallas_call(
-        kernel,
-        out_shape=jax.ShapeDtypeStruct((block_count, slot_count, output_count), jnp.float32),
-    )(target_cols, source_rows)
-    return jnp.moveaxis(result, 2, 0).reshape(output_count, row_count, col_count, slot_count)
+    out_shape = jax.ShapeDtypeStruct((block_count, slot_count, output_count), jnp.float32)
+    if kind == "force":
+        weight_shape = jax.ShapeDtypeStruct(
+            (block_count * chunk_count * 9, CHUNK, slot_count), jnp.float32
+        )
+        result, weights = pl.pallas_call(kernel, out_shape=(out_shape, weight_shape))(
+            target_cols, source_rows
+        )
+    elif kind == "jacobi":
+        result = pl.pallas_call(kernel, out_shape=out_shape)(target_cols, source_rows, weights)
+    else:
+        result = pl.pallas_call(kernel, out_shape=out_shape)(target_cols, source_rows)
+    result = jnp.moveaxis(result, 2, 0).reshape(output_count, row_count, col_count, slot_count)
+    if kind == "force":
+        return result, weights
+    return result
 
 
 def shift_lanes(field, distance):
@@ -185,7 +206,7 @@
     pressure = STIFFNESS * (density - REST_DENSITY) * inverse * inverse
     viscosity = plastic_viscosity + yield_stress / jnp.sqrt(1.0 + strain)
     dens_pad = with_halo(jnp.stack([inverse, pressure, viscosity]), (("down", 1), ("cross", 2)), 1)
-    forces = pair_pass(
+    forces, weights = pair_pass(
         "force",
         jnp.concatenate([positions, pressure[None], viscosity[None]], axis=0),
         jnp.concatenate([far, dens_pad[1:2], dens_pad[0:1], dens_pad[2:3]], axis=0),
@@ -203,9 +224,10 @@
         pulled = pair_pass(
             "jacobi",
             target,
-            jnp.concatenate([far, dens_pad[2:3], speed_pad * dens_pad[0:1]], axis=0),
+            speed_pad * dens_pad[0:1],
             row_count,
             col_count,
+            weights,
         )
         current = (predicted + TIME_STEP * (scale * inverse * pulled)) / diagonal
     moved_positions = positions + TIME_STEP * current

time: 196 us -> 188 us (0.959)
  Pallas kernels: 78.5 us -> 68.8 us
  other arithmetic: 7 us -> 11.3 us
    pallas_call x4, Pallas kernels: 78.5 us -> 68.8 us  [the longest x2 24.7 us: pair_pass(): pl.pallas_call(kernel, out_shape=out_shape)]
    ppermute x8, starting transfers between devices: 34.1 us -> 31.9 us  [with_halo(): before = lax.ppermute(last, axis, up)]
  transfers between devices with their start and end apart: 17 -> 17, of which waited for: 7 -> 7; matrix products, arithmetic and copies ran while one was open for 3% -> 4% of each run, Pallas kernels for 0% -> 0%
where the time goes in v5:
time: 188 us; the launch traced here: 185 us
  Pallas kernels  68.8 us (37%)
  starting transfers between devices  60.1 us (32%)
  waiting for transfers between devices  30 us (16%)
  local copies, waits for them, and re-layouts  13.3 us (7%)
  other arithmetic  11.3 us (6%)
    ppermute x8, starting transfers between devices, with_halo(): before = lax.ppermute(last, axis, up)  31.9 us
    ppermute x8, starting transfers between devices, with_halo(): after = lax.ppermute(initial, axis, down)  26.3 us
    pallas_call x2, Pallas kernels, pair_pass(): pl.pallas_call(kernel, out_shape=out_shape)  24.7 us
    pallas_call x1, Pallas kernels, pair_pass(): pl.pallas_call(kernel, out_shape=(out_shape, weight_shape))  23.3 us
    ppermute x8, waiting for transfers between devices, with_halo(): before = lax.ppermute(last, axis, up)  23 us
    pallas_call x1, Pallas kernels, pair_pass(): pl.pallas_call(kernel, out_shape=out_shape)(target_cols, source_rows)  20.8 us
    ppermute x1, waiting for transfers between devices, from_behind(): return lax.ppermute(block, axis, route)  6.95 us
  transfers between devices with their start and end apart: 17, of which 7 were waited for; matrix products, arithmetic and copies ran while one was open for 4% of the time, Pallas kernels for 0%

profile of v5, /device:TPU:3, one launch (start us, length us, event | category | flops | bytes accessed | tf_op | source)
XLA Modules:
  0.0 184.7 jit_solution(11598656598740153035)
XLA Ops:
  2.2 9.9 %collective-permute-start.1 = (f32[7,1,8,128]{3,2,1,0:T(8,128)S(1)}, f32[7,1,8,128]{3,2,1,0:T(8,128)S(1)}, u32[]{:S(2)}, u32[]{:S(2)}) collective-permute-start(f32[7,1,8,128]{3,2,1,0:T(8,128)S(1)} %get-tuple-element.23), channel_id=1, source_target_pairs={{4,0},{8,4},{12,8},{16,12},{20,16},{24,20},{28,24},{32,28},{36,32}... | collective-permute-start | bytes 86024 | tf_op jit(solution)/shard_map/ppermute | solution.py:31
  12.2 1.9 %collective-permute-start = (f32[7,1,8,128]{3,2,1,0:T(8,128)S(1)}, f32[7,1,8,128]{3,2,1,0:T(8,128)S(1)}, u32[]{:S(2)}, u32[]{:S(2)}) collective-permute-start(f32[7,1,8,128]{3,2,1,0:T(8,128)S(1)} %get-tuple-element.22), channel_id=1, source_target_pairs={{0,4},{4,8},{8,12},{12,16},{16,20},{20,24},{24,28},{28,32},{32,36}... | collective-permute-start | bytes 86024 | tf_op jit(solution)/shard_map/ppermute | solution.py:30
  14.1 6.9 %collective-permute-done = f32[7,1,8,128]{3,2,1,0:T(8,128)S(1)} collective-permute-done((f32[7,1,8,128]{3,2,1,0:T(8,128)S(1)}, f32[7,1,8,128]{3,2,1,0:T(8,128)S(1)}, u32[]{:S(2)}, u32[]{:S(2)}) %collective-permute-start) | collective-permute-done | bytes 28704 | tf_op jit(solution)/shard_map/ppermute | solution.py:30
  21.8 4.0 %collective-permute-start.3 = (f32[7,4,1,128]{3,2,1,0:T(1,128)S(1)}, f32[7,4,1,128]{3,2,1,0:T(1,128)S(1)}, u32[]{:S(2)}, u32[]{:S(2)}) collective-permute-start(f32[7,4,1,128]{3,2,1,0:T(1,128)S(1)} %get-tuple-element.18), channel_id=1, source_target_pairs={{1,0},{2,1},{3,2},{5,4},{6,5},{7,6},{9,8},{10,9},{11,10},{13,12},{... | collective-permute-start | bytes 43016 | tf_op jit(solution)/shard_map/ppermute | solution.py:31
  25.8 3.9 %collective-permute-start.2 = (f32[7,4,1,128]{3,2,1,0:T(1,128)S(1)}, f32[7,4,1,128]{3,2,1,0:T(1,128)S(1)}, u32[]{:S(2)}, u32[]{:S(2)}) collective-permute-start(f32[7,4,1,128]{3,2,1,0:T(1,128)S(1)} %get-tuple-element.17), channel_id=1, source_target_pairs={{0,1},{1,2},{2,3},{4,5},{5,6},{6,7},{8,9},{9,10},{10,11},{12,13},{... | collective-permute-start | bytes 43016 | tf_op jit(solution)/shard_map/ppermute | solution.py:30
  35.0 20.8 %shard_map.86 = f32[16,128,2]{2,1,0:T(8,128)} custom-call(f32[16,128,6]{2,1,0:T(8,128)} %bitcast.79, f32[6,40,128]{2,1,0:T(8,128)} %copy.57.source_ref), custom_call_target="tpu_custom_call" | custom-call | tf_op jit(solution)/shard_map/pallas_call | solution.py:151
  55.8 2.5 %fusion.3 = (f32[16,128]{1,0:T(8,128)S(1)}, f32[16,128]{1,0:T(8,128)S(1)}, f32[1,16,128]{0,2,1:T(8,128)S(1)}) fusion(f32[2,16,128]{0,2,1:T(8,128)} %bitcast.75, s32[16]{0:T(128)S(1)} %lt.80), kind=kLoop, calls=%fused_computation.9 | loop fusion | flops 16384 | bytes 41024 | tf_op jit(solution)/shard_map/mul | solution.py:203
  58.8 1.9 %collective-permute-start.5 = (f32[3,1,8,128]{3,2,1,0:T(8,128)S(1)}, f32[3,1,8,128]{3,2,1,0:T(8,128)S(1)}, u32[]{:S(2)}, u32[]{:S(2)}) collective-permute-start(f32[3,1,8,128]{3,2,1,0:T(8,128)S(1)} %get-tuple-element.41), channel_id=1, source_target_pairs={{4,0},{8,4},{12,8},{16,12},{20,16},{24,20},{28,24},{32,28},{36,32}... | collective-permute-start | bytes 36872 | tf_op jit(solution)/shard_map/ppermute | solution.py:31
  60.8 3.3 %collective-permute-start.4 = (f32[3,1,8,128]{3,2,1,0:T(8,128)S(1)}, f32[3,1,8,128]{3,2,1,0:T(8,128)S(1)}, u32[]{:S(2)}, u32[]{:S(2)}) collective-permute-start(f32[3,1,8,128]{3,2,1,0:T(8,128)S(1)} %get-tuple-element.40), channel_id=1, source_target_pairs={{0,4},{4,8},{8,12},{12,16},{16,20},{20,24},{24,28},{28,32},{32,36}... | collective-permute-start | bytes 36872 | tf_op jit(solution)/shard_map/ppermute | solution.py:30
  64.2 5.3 %collective-permute-done.4 = f32[3,1,8,128]{3,2,1,0:T(8,128)S(1)} collective-permute-done((f32[3,1,8,128]{3,2,1,0:T(8,128)S(1)}, f32[3,1,8,128]{3,2,1,0:T(8,128)S(1)}, u32[]{:S(2)}, u32[]{:S(2)}) %collective-permute-start.4) | collective-permute-done | bytes 12320 | tf_op jit(solution)/shard_map/ppermute | solution.py:30
  69.5 1.9 %collective-permute-start.7 = (f32[3,4,1,128]{3,2,1,0:T(1,128)S(1)}, f32[3,4,1,128]{3,2,1,0:T(1,128)S(1)}, u32[]{:S(2)}, u32[]{:S(2)}) collective-permute-start(f32[3,4,1,128]{3,2,1,0:T(1,128)S(1)} %get-tuple-element.35), channel_id=1, source_target_pairs={{1,0},{2,1},{3,2},{5,4},{6,5},{7,6},{9,8},{10,9},{11,10},{13,12},{... | collective-permute-start | bytes 18440 | tf_op jit(solution)/shard_map/ppermute | solution.py:31
  71.4 5.1 %collective-permute-start.6 = (f32[3,4,1,128]{3,2,1,0:T(1,128)S(1)}, f32[3,4,1,128]{3,2,1,0:T(1,128)S(1)}, u32[]{:S(2)}, u32[]{:S(2)}) collective-permute-start(f32[3,4,1,128]{3,2,1,0:T(1,128)S(1)} %get-tuple-element.34), channel_id=1, source_target_pairs={{0,1},{1,2},{2,3},{4,5},{5,6},{6,7},{8,9},{9,10},{10,11},{12,13},{... | collective-permute-start | bytes 18440 | tf_op jit(solution)/shard_map/ppermute | solution.py:30
  76.6 1.4 copy.62
  77.9 1.4 copy.66
  80.1 23.3 %shard_map.87 = (f32[16,128,4]{2,1,0:T(8,128)}, f32[576,32,128]{2,1,0:T(8,128)}) custom-call(f32[16,128,5]{2,1,0:T(8,128)} %bitcast.78, f32[6,40,128]{2,1,0:T(8,128)} %copy.64.source_ref), custom_call_target="tpu_custom_call" | custom-call | tf_op jit(solution)/shard_map/pallas_call | solution.py:145
  105.2 1.9 %collective-permute-start.9 = (f32[3,1,8,128]{3,2,1,0:T(8,128)S(1)}, f32[3,1,8,128]{3,2,1,0:T(8,128)S(1)}, u32[]{:S(2)}, u32[]{:S(2)}) collective-permute-start(f32[3,1,8,128]{3,2,1,0:T(8,128)S(1)} %get-tuple-element.39), channel_id=1, source_target_pairs={{4,0},{8,4},{12,8},{16,12},{20,16},{24,20},{28,24},{32,28},{36,32}... | collective-permute-start | bytes 36872 | tf_op jit(solution)/shard_map/ppermute | solution.py:31
  107.1 3.4 %collective-permute-start.8 = (f32[3,1,8,128]{3,2,1,0:T(8,128)S(1)}, f32[3,1,8,128]{3,2,1,0:T(8,128)S(1)}, u32[]{:S(2)}, u32[]{:S(2)}) collective-permute-start(f32[3,1,8,128]{3,2,1,0:T(8,128)S(1)} %get-tuple-element.38), channel_id=1, source_target_pairs={{0,4},{4,8},{8,12},{12,16},{16,20},{20,24},{24,28},{28,32},{32,36}... | collective-permute-start | bytes 36872 | tf_op jit(solution)/shard_map/ppermute | solution.py:30
  110.5 1.9 %slice_reduce_fusion = f32[16,128]{1,0:T(8,128)S(1)} fusion(f32[4,16,128]{0,2,1:T(8,128)} %bitcast.81), kind=kLoop, calls=%fused_computation | loop fusion | bytes 16384 | tf_op jit(solution)/shard_map/slice | solution.py:219
  112.4 3.4 %collective-permute-done.8 = f32[3,1,8,128]{3,2,1,0:T(8,128)S(1)} collective-permute-done((f32[3,1,8,128]{3,2,1,0:T(8,128)S(1)}, f32[3,1,8,128]{3,2,1,0:T(8,128)S(1)}, u32[]{:S(2)}, u32[]{:S(2)}) %collective-permute-start.8) | collective-permute-done | bytes 12320 | tf_op jit(solution)/shard_map/ppermute | solution.py:30
  115.8 1.9 %collective-permute-start.11 = (f32[3,4,1,128]{3,2,1,0:T(1,128)S(1)}, f32[3,4,1,128]{3,2,1,0:T(1,128)S(1)}, u32[]{:S(2)}, u32[]{:S(2)}) collective-permute-start(f32[3,4,1,128]{3,2,1,0:T(1,128)S(1)} %get-tuple-element.33), channel_id=1, source_target_pairs={{1,0},{2,1},{3,2},{5,4},{6,5},{7,6},{9,8},{10,9},{11,10},{13,12},{... | collective-permute-start | bytes 18440 | tf_op jit(solution)/shard_map/ppermute | solution.py:31
  117.7 5.1 %collective-permute-start.10 = (f32[3,4,1,128]{3,2,1,0:T(1,128)S(1)}, f32[3,4,1,128]{3,2,1,0:T(1,128)S(1)}, u32[]{:S(2)}, u32[]{:S(2)}) collective-permute-start(f32[3,4,1,128]{3,2,1,0:T(1,128)S(1)} %get-tuple-element.32), channel_id=1, source_target_pairs={{0,1},{1,2},{2,3},{4,5},{5,6},{6,7},{8,9},{9,10},{10,11},{12,13},{... | collective-permute-start | bytes 18440 | tf_op jit(solution)/shard_map/ppermute | solution.py:30
  124.3 12.4 %shard_map.88 = f32[16,128,3]{2,1,0:T(8,128)} custom-call(f32[16,128,4]{2,1,0:T(8,128)} %bitcast.73, f32[3,40,128]{2,1,0:T(8,128)} %broadcast_multiply_fusion.1.source_ref, f32[576,32,128]{2,1,0:T(8,128)} %get-tuple-element.5.refs_0_), custom_call_target="tpu_custom_call" | custom-call | tf_op jit(solution)/shard_map/pallas_call | solution.py:149
  136.6 1.6 copy.67
  138.2 2.7 %collective-permute-start.13 = (f32[3,1,8,128]{3,2,1,0:T(8,128)S(1)}, f32[3,1,8,128]{3,2,1,0:T(8,128)S(1)}, u32[]{:S(2)}, u32[]{:S(2)}) collective-permute-start(f32[3,1,8,128]{3,2,1,0:T(8,128)S(1)} %get-tuple-element.37), channel_id=1, source_target_pairs={{4,0},{8,4},{12,8},{16,12},{20,16},{24,20},{28,24},{32,28},{36,32}... | collective-permute-start | bytes 36872 | tf_op jit(solution)/shard_map/ppermute | solution.py:31
  141.0 2.5 %collective-permute-start.12 = (f32[3,1,8,128]{3,2,1,0:T(8,128)S(1)}, f32[3,1,8,128]{3,2,1,0:T(8,128)S(1)}, u32[]{:S(2)}, u32[]{:S(2)}) collective-permute-start(f32[3,1,8,128]{3,2,1,0:T(8,128)S(1)} %get-tuple-element.36), channel_id=1, source_target_pairs={{0,4},{4,8},{8,12},{12,16},{16,20},{20,24},{24,28},{28,32},{32,36}... | collective-permute-start | bytes 36872 | tf_op jit(solution)/shard_map/ppermute | solution.py:30
  143.6 6.1 %collective-permute-done.12 = f32[3,1,8,128]{3,2,1,0:T(8,128)S(1)} collective-permute-done((f32[3,1,8,128]{3,2,1,0:T(8,128)S(1)}, f32[3,1,8,128]{3,2,1,0:T(8,128)S(1)}, u32[]{:S(2)}, u32[]{:S(2)}) %collective-permute-start.12) | collective-permute-done | bytes 12320 | tf_op jit(solution)/shard_map/ppermute | solution.py:30
  149.7 1.9 %collective-permute-start.15 = (f32[3,4,1,128]{3,2,1,0:T(1,128)S(1)}, f32[3,4,1,128]{3,2,1,0:T(1,128)S(1)}, u32[]{:S(2)}, u32[]{:S(2)}) collective-permute-start(f32[3,4,1,128]{3,2,1,0:T(1,128)S(1)} %get-tuple-element.31), channel_id=1, source_target_pairs={{1,0},{2,1},{3,2},{5,4},{6,5},{7,6},{9,8},{10,9},{11,10},{13,12},{... | collective-permute-start | bytes 18440 | tf_op jit(solution)/shard_map/ppermute | solution.py:31
  151.6 6.5 %collective-permute-start.14 = (f32[3,4,1,128]{3,2,1,0:T(1,128)S(1)}, f32[3,4,1,128]{3,2,1,0:T(1,128)S(1)}, u32[]{:S(2)}, u32[]{:S(2)}) collective-permute-start(f32[3,4,1,128]{3,2,1,0:T(1,128)S(1)} %get-tuple-element.30), channel_id=1, source_target_pairs={{0,1},{1,2},{2,3},{4,5},{5,6},{6,7},{8,9},{9,10},{10,11},{12,13},{... | collective-permute-start | bytes 18440 | tf_op jit(solution)/shard_map/ppermute | solution.py:30
  159.5 12.4 %shard_map.89 = f32[16,128,3]{2,1,0:T(8,128)} custom-call(f32[16,128,4]{2,1,0:T(8,128)} %bitcast.74, f32[3,40,128]{2,1,0:T(8,128)} %broadcast_multiply_fusion.source_ref, f32[576,32,128]{2,1,0:T(8,128)} %get-tuple-element.5.refs_0_), custom_call_target="tpu_custom_call" | custom-call | tf_op jit(solution)/shard_map/pallas_call | solution.py:149
  171.9 1.6 copy.68
  173.6 1.9 %collective-permute-start.16 = (f32[8,8,128]{2,1,0:T(8,128)S(1)}, f32[8,8,128]{2,1,0:T(8,128)S(1)}, u32[]{:S(2)}, u32[]{:S(2)}) collective-permute-start(f32[8,8,128]{2,1,0:T(8,128)S(1)} %pad_maximum_fusion.11), channel_id=1, source_target_pairs={{0,4},{4,8},{8,12},{12,16},{16,20},{20,24},{24,28},{28,32},{32,36}... | collective-permute-start | bytes 98312 | tf_op jit(solution)/shard_map/ppermute | solution.py:39
  175.6 6.9 %collective-permute-done.16 = f32[8,8,128]{2,1,0:T(8,128)S(1)} collective-permute-done((f32[8,8,128]{2,1,0:T(8,128)S(1)}, f32[8,8,128]{2,1,0:T(8,128)S(1)}, u32[]{:S(2)}, u32[]{:S(2)}) %collective-permute-start.16) | collective-permute-done | bytes 32800 | tf_op jit(solution)/shard_map/ppermute | solution.py:39
  (101 shorter events, 15.7 us)
Async XLA Ops:
  0.6 104.5 %copy-start.6 = (f32[3]{0:T(128)S(1)}, f32[3]{0:T(128)}, u32[]{:S(2)}) copy-start(f32[3]{0:T(128)} %constant.56.clone) | copy-start | bytes 40
  0.6 58.1 %copy-start.2 = (s32[2,8]{1,0:T(2,128)S(1)}, s32[2,8]{1,0:T(2,128)}, u32[]{:S(2)}) copy-start(s32[2,8]{1,0:T(2,128)} %param.11) | copy-start | bytes 196
  0.7 63.5 %copy-start = (f32[3,2,8,128]{3,2,1,0:T(8,128)S(1)}, f32[3,2,8,128]{3,2,1,0:T(8,128)}, u32[]{:S(2)}) copy-start(f32[3,2,8,128]{3,2,1,0:T(8,128)} %param.7) | copy-start | bytes 73732
  0.7 104.4 %copy-start.1 = (f32[3,2,8,128]{3,2,1,0:T(8,128)S(1)}, f32[3,2,8,128]{3,2,1,0:T(8,128)}, u32[]{:S(2)}) copy-start(f32[3,2,8,128]{3,2,1,0:T(8,128)} %param.8) | copy-start | bytes 73732
  0.7 58.1 %copy-start.3 = (f32[2,8,128]{2,1,0:T(8,128)S(1)}, f32[2,8,128]{2,1,0:T(8,128)}, u32[]{:S(2)}) copy-start(f32[2,8,128]{2,1,0:T(8,128)} %param.9) | copy-start | bytes 24580
  0.7 58.1 %copy-start.4 = (f32[2,8,128]{2,1,0:T(8,128)S(1)}, f32[2,8,128]{2,1,0:T(8,128)}, u32[]{:S(2)}) copy-start(f32[2,8,128]{2,1,0:T(8,128)} %param.10) | copy-start | bytes 24580
  2.2 11.8 %collective-permute-start.1 = (f32[7,1,8,128]{3,2,1,0:T(8,128)S(1)}, f32[7,1,8,128]{3,2,1,0:T(8,128)S(1)}, u32[]{:S(2)}, u32[]{:S(2)}) collective-permute-start(f32[7,1,8,128]{3,2,1,0:T(8,128)S(1)} %get-tuple-element.23), channel_id=1, source_target_pairs={{4,0},{8,4},{12,8},{16,12},{20,16},{24,20},{28,24},{32,28},{36,32}... | collective-permute-start | bytes 86024 | tf_op jit(solution)/shard_map/ppermute | solution.py:31
  12.2 8.8 %collective-permute-start = (f32[7,1,8,128]{3,2,1,0:T(8,128)S(1)}, f32[7,1,8,128]{3,2,1,0:T(8,128)S(1)}, u32[]{:S(2)}, u32[]{:S(2)}) collective-permute-start(f32[7,1,8,128]{3,2,1,0:T(8,128)S(1)} %get-tuple-element.22), channel_id=1, source_target_pairs={{0,4},{4,8},{8,12},{12,16},{16,20},{20,24},{24,28},{28,32},{32,36}... | collective-permute-start | bytes 86024 | tf_op jit(solution)/shard_map/ppermute | solution.py:30
  21.8 10.8 %collective-permute-start.3 = (f32[7,4,1,128]{3,2,1,0:T(1,128)S(1)}, f32[7,4,1,128]{3,2,1,0:T(1,128)S(1)}, u32[]{:S(2)}, u32[]{:S(2)}) collective-permute-start(f32[7,4,1,128]{3,2,1,0:T(1,128)S(1)} %get-tuple-element.18), channel_id=1, source_target_pairs={{1,0},{2,1},{3,2},{5,4},{6,5},{7,6},{9,8},{10,9},{11,10},{13,12},{... | collective-permute-start | bytes 43016 | tf_op jit(solution)/shard_map/ppermute | solution.py:31
  25.8 6.8 %collective-permute-start.2 = (f32[7,4,1,128]{3,2,1,0:T(1,128)S(1)}, f32[7,4,1,128]{3,2,1,0:T(1,128)S(1)}, u32[]{:S(2)}, u32[]{:S(2)}) collective-permute-start(f32[7,4,1,128]{3,2,1,0:T(1,128)S(1)} %get-tuple-element.17), channel_id=1, source_target_pairs={{0,1},{1,2},{2,3},{4,5},{5,6},{6,7},{8,9},{9,10},{10,11},{12,13},{... | collective-permute-start | bytes 43016 | tf_op jit(solution)/shard_map/ppermute | solution.py:30
  58.8 5.3 %collective-permute-start.5 = (f32[3,1,8,128]{3,2,1,0:T(8,128)S(1)}, f32[3,1,8,128]{3,2,1,0:T(8,128)S(1)}, u32[]{:S(2)}, u32[]{:S(2)}) collective-permute-start(f32[3,1,8,128]{3,2,1,0:T(8,128)S(1)} %get-tuple-element.41), channel_id=1, source_target_pairs={{4,0},{8,4},{12,8},{16,12},{20,16},{24,20},{28,24},{32,28},{36,32}... | collective-permute-start | bytes 36872 | tf_op jit(solution)/shard_map/ppermute | solution.py:31
  60.8 8.7 %collective-permute-start.4 = (f32[3,1,8,128]{3,2,1,0:T(8,128)S(1)}, f32[3,1,8,128]{3,2,1,0:T(8,128)S(1)}, u32[]{:S(2)}, u32[]{:S(2)}) collective-permute-start(f32[3,1,8,128]{3,2,1,0:T(8,128)S(1)} %get-tuple-element.40), channel_id=1, source_target_pairs={{0,4},{4,8},{8,12},{12,16},{16,20},{20,24},{24,28},{28,32},{32,36}... | collective-permute-start | bytes 36872 | tf_op jit(solution)/shard_map/ppermute | solution.py:30
  69.5 9.8 %collective-permute-start.7 = (f32[3,4,1,128]{3,2,1,0:T(1,128)S(1)}, f32[3,4,1,128]{3,2,1,0:T(1,128)S(1)}, u32[]{:S(2)}, u32[]{:S(2)}) collective-permute-start(f32[3,4,1,128]{3,2,1,0:T(1,128)S(1)} %get-tuple-element.35), channel_id=1, source_target_pairs={{1,0},{2,1},{3,2},{5,4},{6,5},{7,6},{9,8},{10,9},{11,10},{13,12},{... | collective-permute-start | bytes 18440 | tf_op jit(solution)/shard_map/ppermute | solution.py:31
  71.4 7.9 %collective-permute-start.6 = (f32[3,4,1,128]{3,2,1,0:T(1,128)S(1)}, f32[3,4,1,128]{3,2,1,0:T(1,128)S(1)}, u32[]{:S(2)}, u32[]{:S(2)}) collective-permute-start(f32[3,4,1,128]{3,2,1,0:T(1,128)S(1)} %get-tuple-element.34), channel_id=1, source_target_pairs={{0,1},{1,2},{2,3},{4,5},{5,6},{6,7},{8,9},{9,10},{10,11},{12,13},{... | collective-permute-start | bytes 18440 | tf_op jit(solution)/shard_map/ppermute | solution.py:30
  80.1 63.4 %copy-start.5 = (s32[2,8]{1,0:T(2,128)S(1)}, s32[2,8]{1,0:T(2,128)}, u32[]{:S(2)}) copy-start(s32[2,8]{1,0:T(2,128)} %param.12) | copy-start | bytes 196
  105.2 7.2 %collective-permute-start.9 = (f32[3,1,8,128]{3,2,1,0:T(8,128)S(1)}, f32[3,1,8,128]{3,2,1,0:T(8,128)S(1)}, u32[]{:S(2)}, u32[]{:S(2)}) collective-permute-start(f32[3,1,8,128]{3,2,1,0:T(8,128)S(1)} %get-tuple-element.39), channel_id=1, source_target_pairs={{4,0},{8,4},{12,8},{16,12},{20,16},{24,20},{28,24},{32,28},{36,32}... | collective-permute-start | bytes 36872 | tf_op jit(solution)/shard_map/ppermute | solution.py:31
  107.1 8.7 %collective-permute-start.8 = (f32[3,1,8,128]{3,2,1,0:T(8,128)S(1)}, f32[3,1,8,128]{3,2,1,0:T(8,128)S(1)}, u32[]{:S(2)}, u32[]{:S(2)}) collective-permute-start(f32[3,1,8,128]{3,2,1,0:T(8,128)S(1)} %get-tuple-element.38), channel_id=1, source_target_pairs={{0,4},{4,8},{8,12},{12,16},{16,20},{20,24},{24,28},{28,32},{32,36}... | collective-permute-start | bytes 36872 | tf_op jit(solution)/shard_map/ppermute | solution.py:30
  115.8 7.2 %collective-permute-start.11 = (f32[3,4,1,128]{3,2,1,0:T(1,128)S(1)}, f32[3,4,1,128]{3,2,1,0:T(1,128)S(1)}, u32[]{:S(2)}, u32[]{:S(2)}) collective-permute-start(f32[3,4,1,128]{3,2,1,0:T(1,128)S(1)} %get-tuple-element.33), channel_id=1, source_target_pairs={{1,0},{2,1},{3,2},{5,4},{6,5},{7,6},{9,8},{10,9},{11,10},{13,12},{... | collective-permute-start | bytes 18440 | tf_op jit(solution)/shard_map/ppermute | solution.py:31
  117.7 5.9 %collective-permute-start.10 = (f32[3,4,1,128]{3,2,1,0:T(1,128)S(1)}, f32[3,4,1,128]{3,2,1,0:T(1,128)S(1)}, u32[]{:S(2)}, u32[]{:S(2)}) collective-permute-start(f32[3,4,1,128]{3,2,1,0:T(1,128)S(1)} %get-tuple-element.32), channel_id=1, source_target_pairs={{0,1},{1,2},{2,3},{4,5},{5,6},{6,7},{8,9},{9,10},{10,11},{12,13},{... | collective-permute-start | bytes 18440 | tf_op jit(solution)/shard_map/ppermute | solution.py:30
  138.2 5.3 %collective-permute-start.13 = (f32[3,1,8,128]{3,2,1,0:T(8,128)S(1)}, f32[3,1,8,128]{3,2,1,0:T(8,128)S(1)}, u32[]{:S(2)}, u32[]{:S(2)}) collective-permute-start(f32[3,1,8,128]{3,2,1,0:T(8,128)S(1)} %get-tuple-element.37), channel_id=1, source_target_pairs={{4,0},{8,4},{12,8},{16,12},{20,16},{24,20},{28,24},{32,28},{36,32}... | collective-permute-start | bytes 36872 | tf_op jit(solution)/shard_map/ppermute | solution.py:31
  141.0 8.7 %collective-permute-start.12 = (f32[3,1,8,128]{3,2,1,0:T(8,128)S(1)}, f32[3,1,8,128]{3,2,1,0:T(8,128)S(1)}, u32[]{:S(2)}, u32[]{:S(2)}) collective-permute-start(f32[3,1,8,128]{3,2,1,0:T(8,128)S(1)} %get-tuple-element.36), channel_id=1, source_target_pairs={{0,4},{4,8},{8,12},{12,16},{16,20},{20,24},{24,28},{28,32},{32,36}... | collective-permute-start | bytes 36872 | tf_op jit(solution)/shard_map/ppermute | solution.py:30
  149.7 8.5 %collective-permute-start.15 = (f32[3,4,1,128]{3,2,1,0:T(1,128)S(1)}, f32[3,4,1,128]{3,2,1,0:T(1,128)S(1)}, u32[]{:S(2)}, u32[]{:S(2)}) collective-permute-start(f32[3,4,1,128]{3,2,1,0:T(1,128)S(1)} %get-tuple-element.31), channel_id=1, source_target_pairs={{1,0},{2,1},{3,2},{5,4},{6,5},{7,6},{9,8},{10,9},{11,10},{13,12},{... | collective-permute-start | bytes 18440 | tf_op jit(solution)/shard_map/ppermute | solution.py:31
  151.6 7.3 %collective-permute-start.14 = (f32[3,4,1,128]{3,2,1,0:T(1,128)S(1)}, f32[3,4,1,128]{3,2,1,0:T(1,128)S(1)}, u32[]{:S(2)}, u32[]{:S(2)}) collective-permute-start(f32[3,4,1,128]{3,2,1,0:T(1,128)S(1)} %get-tuple-element.30), channel_id=1, source_target_pairs={{0,1},{1,2},{2,3},{4,5},{5,6},{6,7},{8,9},{9,10},{10,11},{12,13},{... | collective-permute-start | bytes 18440 | tf_op jit(solution)/shard_map/ppermute | solution.py:30
  173.6 8.9 %collective-permute-start.16 = (f32[8,8,128]{2,1,0:T(8,128)S(1)}, f32[8,8,128]{2,1,0:T(8,128)S(1)}, u32[]{:S(2)}, u32[]{:S(2)}) collective-permute-start(f32[8,8,128]{2,1,0:T(8,128)S(1)} %pad_maximum_fusion.11), channel_id=1, source_target_pairs={{0,4},{4,8},{8,12},{12,16},{16,20},{20,24},{24,28},{28,32},{32,36}... | collective-permute-start | bytes 98312 | tf_op jit(solution)/shard_map/ppermute | solution.py:39

commit v6 on v5

--- a/solution.py
+++ b/solution.py
@@ -87,9 +87,10 @@
         else:
             (out_ref,) = refs
 
+        block = pl.program_id(0)
+
         def body(step, carry):
-            block = step // chunk_count
-            first = pl.multiple_of((step % chunk_count) * CHUNK, CHUNK)
+            first = pl.multiple_of(step * CHUNK, CHUNK)
             row = block // col_count
             col = block % col_count
             own = target_ref[block, pl.ds(first, CHUNK), :]
@@ -135,20 +136,39 @@
                 )
             return carry
 
-        lax.fori_loop(0, block_count * chunk_count, body, 0)
+        lax.fori_loop(0, chunk_count, body, 0)
 
     out_shape = jax.ShapeDtypeStruct((block_count, slot_count, output_count), jnp.float32)
+    whole = [
+        pl.BlockSpec(target_cols.shape, lambda block: (0, 0, 0)),
+        pl.BlockSpec(source_rows.shape, lambda block: (0, 0, 0)),
+    ]
+    out_spec = pl.BlockSpec(out_shape.shape, lambda block: (0, 0, 0))
+    weight_spec = pl.BlockSpec((chunk_count * 9, CHUNK, slot_count), lambda block: (block, 0, 0))
+    grid = (block_count,)
     if kind == "force":
         weight_shape = jax.ShapeDtypeStruct(
             (block_count * chunk_count * 9, CHUNK, slot_count), jnp.float32
         )
-        result, weights = pl.pallas_call(kernel, out_shape=(out_shape, weight_shape))(
-            target_cols, source_rows
-        )
+        result, weights = pl.pallas_call(
+            kernel,
+            out_shape=(out_shape, weight_shape),
+            grid=grid,
+            in_specs=whole,
+            out_specs=(out_spec, weight_spec),
+        )(target_cols, source_rows)
     elif kind == "jacobi":
-        result = pl.pallas_call(kernel, out_shape=out_shape)(target_cols, source_rows, weights)
+        result = pl.pallas_call(
+            kernel,
+            out_shape=out_shape,
+            grid=grid,
+            in_specs=whole + [weight_spec],
+            out_specs=out_spec,
+        )(target_cols, source_rows, weights)
     else:
-        result = pl.pallas_call(kernel, out_shape=out_shape)(target_cols, source_rows)
+        result = pl.pallas_call(
+            kernel, out_shape=out_shape, grid=grid, in_specs=whole, out_specs=out_spec
+        )(target_cols, source_rows)
     result = jnp.moveaxis(result, 2, 0).reshape(output_count, row_count, col_count, slot_count)
     if kind == "force":
         return result, weights

time: 188 us -> 190 us (1.011)
  the two profiles are of different devices: /device:TPU:3 before, /device:TPU:6 now
where the time goes in v6:
time: 190 us; the launch traced here: 189 us
  Pallas kernels  70.1 us (37%)
  starting transfers between devices  49.1 us (26%)
  waiting for transfers between devices  43.5 us (23%)
  local copies, waits for them, and re-layouts  13.3 us (7%)
  other arithmetic  11.3 us (6%)
    ppermute x8, waiting for transfers between devices, with_halo(): before = lax.ppermute(last, axis, up)  35.4 us
    pallas_call x2, Pallas kernels, pair_pass(): pl.pallas_call(kernel, out_shape=out_shape, grid=grid, in_specs=whole + [...  28.5 us
    ppermute x8, starting transfers between devices, with_halo(): after = lax.ppermute(initial, axis, down)  25.1 us
    ppermute x8, starting transfers between devices, with_halo(): before = lax.ppermute(last, axis, up)  22.1 us
    pallas_call x1, Pallas kernels, pair_pass(): pl.pallas_call(kernel, out_shape=out_shape, grid=grid, in_specs=whole, ou...  20.9 us
    pallas_call x1, Pallas kernels, pair_pass(): pl.pallas_call(kernel, out_shape=(out_shape, weight_shape), grid=grid, in...  20.7 us
    ppermute x1, waiting for transfers between devices, from_behind(): return lax.ppermute(block, axis, route)  8.1 us
  transfers between devices with their start and end apart: 17, of which 9 were waited for; matrix products, arithmetic and copies ran while one was open for 4% of the time, Pallas kernels for 0%

profile of v6, /device:TPU:6, one launch (start us, length us, event | category | flops | bytes accessed | tf_op | source)
XLA Modules:
  0.0 188.5 jit_solution(17095867027113309196)
XLA Ops:
  2.2 10.5 %collective-permute-start.1 = (f32[7,1,8,128]{3,2,1,0:T(8,128)S(1)}, f32[7,1,8,128]{3,2,1,0:T(8,128)S(1)}, u32[]{:S(2)}, u32[]{:S(2)}) collective-permute-start(f32[7,1,8,128]{3,2,1,0:T(8,128)S(1)} %get-tuple-element.23), channel_id=1, source_target_pairs={{4,0},{8,4},{12,8},{16,12},{20,16},{24,20},{28,24},{32,28},{36,32}... | collective-permute-start | bytes 86024 | tf_op jit(solution)/shard_map/ppermute | solution.py:31
  12.7 1.9 %collective-permute-start = (f32[7,1,8,128]{3,2,1,0:T(8,128)S(1)}, f32[7,1,8,128]{3,2,1,0:T(8,128)S(1)}, u32[]{:S(2)}, u32[]{:S(2)}) collective-permute-start(f32[7,1,8,128]{3,2,1,0:T(8,128)S(1)} %get-tuple-element.22), channel_id=1, source_target_pairs={{0,4},{4,8},{8,12},{12,16},{16,20},{20,24},{24,28},{28,32},{32,36}... | collective-permute-start | bytes 86024 | tf_op jit(solution)/shard_map/ppermute | solution.py:30
  14.7 8.0 %collective-permute-done = f32[7,1,8,128]{3,2,1,0:T(8,128)S(1)} collective-permute-done((f32[7,1,8,128]{3,2,1,0:T(8,128)S(1)}, f32[7,1,8,128]{3,2,1,0:T(8,128)S(1)}, u32[]{:S(2)}, u32[]{:S(2)}) %collective-permute-start) | collective-permute-done | bytes 28704 | tf_op jit(solution)/shard_map/ppermute | solution.py:30
  23.6 1.9 %collective-permute-start.3 = (f32[7,4,1,128]{3,2,1,0:T(1,128)S(1)}, f32[7,4,1,128]{3,2,1,0:T(1,128)S(1)}, u32[]{:S(2)}, u32[]{:S(2)}) collective-permute-start(f32[7,4,1,128]{3,2,1,0:T(1,128)S(1)} %get-tuple-element.18), channel_id=1, source_target_pairs={{1,0},{2,1},{3,2},{5,4},{6,5},{7,6},{9,8},{10,9},{11,10},{13,12},{... | collective-permute-start | bytes 43016 | tf_op jit(solution)/shard_map/ppermute | solution.py:31
  25.5 2.4 %collective-permute-start.2 = (f32[7,4,1,128]{3,2,1,0:T(1,128)S(1)}, f32[7,4,1,128]{3,2,1,0:T(1,128)S(1)}, u32[]{:S(2)}, u32[]{:S(2)}) collective-permute-start(f32[7,4,1,128]{3,2,1,0:T(1,128)S(1)} %get-tuple-element.17), channel_id=1, source_target_pairs={{0,1},{1,2},{2,3},{4,5},{5,6},{6,7},{8,9},{9,10},{10,11},{12,13},{... | collective-permute-start | bytes 43016 | tf_op jit(solution)/shard_map/ppermute | solution.py:30
  34.4 20.9 %shard_map.86 = f32[16,128,2]{2,1,0:T(8,128)} custom-call(f32[16,128,6]{2,1,0:T(8,128)} %bitcast.79, f32[6,40,128]{2,1,0:T(8,128)} %copy.57.source_ref), custom_call_target="tpu_custom_call" | custom-call | tf_op jit(solution)/shard_map/pallas_call | solution.py:169
  55.2 2.5 %fusion.3 = (f32[16,128]{1,0:T(8,128)S(1)}, f32[16,128]{1,0:T(8,128)S(1)}, f32[1,16,128]{0,2,1:T(8,128)S(1)}) fusion(f32[2,16,128]{0,2,1:T(8,128)} %bitcast.75, s32[16]{0:T(128)S(1)} %lt.80), kind=kLoop, calls=%fused_computation.9 | loop fusion | flops 16384 | bytes 41024 | tf_op jit(solution)/shard_map/mul | solution.py:223
  58.3 1.9 %collective-permute-start.5 = (f32[3,1,8,128]{3,2,1,0:T(8,128)S(1)}, f32[3,1,8,128]{3,2,1,0:T(8,128)S(1)}, u32[]{:S(2)}, u32[]{:S(2)}) collective-permute-start(f32[3,1,8,128]{3,2,1,0:T(8,128)S(1)} %get-tuple-element.41), channel_id=1, source_target_pairs={{4,0},{8,4},{12,8},{16,12},{20,16},{24,20},{28,24},{32,28},{36,32}... | collective-permute-start | bytes 36872 | tf_op jit(solution)/shard_map/ppermute | solution.py:31
  60.2 3.9 %collective-permute-start.4 = (f32[3,1,8,128]{3,2,1,0:T(8,128)S(1)}, f32[3,1,8,128]{3,2,1,0:T(8,128)S(1)}, u32[]{:S(2)}, u32[]{:S(2)}) collective-permute-start(f32[3,1,8,128]{3,2,1,0:T(8,128)S(1)} %get-tuple-element.40), channel_id=1, source_target_pairs={{0,4},{4,8},{8,12},{12,16},{16,20},{20,24},{24,28},{28,32},{32,36}... | collective-permute-start | bytes 36872 | tf_op jit(solution)/shard_map/ppermute | solution.py:30
  64.2 5.8 %collective-permute-done.4 = f32[3,1,8,128]{3,2,1,0:T(8,128)S(1)} collective-permute-done((f32[3,1,8,128]{3,2,1,0:T(8,128)S(1)}, f32[3,1,8,128]{3,2,1,0:T(8,128)S(1)}, u32[]{:S(2)}, u32[]{:S(2)}) %collective-permute-start.4) | collective-permute-done | bytes 12320 | tf_op jit(solution)/shard_map/ppermute | solution.py:30
  70.0 2.3 %collective-permute-start.7 = (f32[3,4,1,128]{3,2,1,0:T(1,128)S(1)}, f32[3,4,1,128]{3,2,1,0:T(1,128)S(1)}, u32[]{:S(2)}, u32[]{:S(2)}) collective-permute-start(f32[3,4,1,128]{3,2,1,0:T(1,128)S(1)} %get-tuple-element.35), channel_id=1, source_target_pairs={{1,0},{2,1},{3,2},{5,4},{6,5},{7,6},{9,8},{10,9},{11,10},{13,12},{... | collective-permute-start | bytes 18440 | tf_op jit(solution)/shard_map/ppermute | solution.py:31
  72.3 2.0 %collective-permute-start.6 = (f32[3,4,1,128]{3,2,1,0:T(1,128)S(1)}, f32[3,4,1,128]{3,2,1,0:T(1,128)S(1)}, u32[]{:S(2)}, u32[]{:S(2)}) collective-permute-start(f32[3,4,1,128]{3,2,1,0:T(1,128)S(1)} %get-tuple-element.34), channel_id=1, source_target_pairs={{0,1},{1,2},{2,3},{4,5},{5,6},{6,7},{8,9},{9,10},{10,11},{12,13},{... | collective-permute-start | bytes 18440 | tf_op jit(solution)/shard_map/ppermute | solution.py:30
  77.1 1.7 collective-permute-done.6
  79.6 20.7 %shard_map.87 = (f32[16,128,4]{2,1,0:T(8,128)}, f32[576,32,128]{2,1,0:T(8,128)}) custom-call(f32[16,128,5]{2,1,0:T(8,128)} %bitcast.78, f32[6,40,128]{2,1,0:T(8,128)} %copy.64.source_ref), custom_call_target="tpu_custom_call" | custom-call | tf_op jit(solution)/shard_map/pallas_call | solution.py:153
  102.1 1.9 %collective-permute-start.9 = (f32[3,1,8,128]{3,2,1,0:T(8,128)S(1)}, f32[3,1,8,128]{3,2,1,0:T(8,128)S(1)}, u32[]{:S(2)}, u32[]{:S(2)}) collective-permute-start(f32[3,1,8,128]{3,2,1,0:T(8,128)S(1)} %get-tuple-element.39), channel_id=1, source_target_pairs={{4,0},{8,4},{12,8},{16,12},{20,16},{24,20},{28,24},{32,28},{36,32}... | collective-permute-start | bytes 36872 | tf_op jit(solution)/shard_map/ppermute | solution.py:31
  104.0 3.9 %collective-permute-start.8 = (f32[3,1,8,128]{3,2,1,0:T(8,128)S(1)}, f32[3,1,8,128]{3,2,1,0:T(8,128)S(1)}, u32[]{:S(2)}, u32[]{:S(2)}) collective-permute-start(f32[3,1,8,128]{3,2,1,0:T(8,128)S(1)} %get-tuple-element.38), channel_id=1, source_target_pairs={{0,4},{4,8},{8,12},{12,16},{16,20},{20,24},{24,28},{28,32},{32,36}... | collective-permute-start | bytes 36872 | tf_op jit(solution)/shard_map/ppermute | solution.py:30
  107.9 1.9 slice_reduce_fusion
  109.8 4.0 %collective-permute-done.8 = f32[3,1,8,128]{3,2,1,0:T(8,128)S(1)} collective-permute-done((f32[3,1,8,128]{3,2,1,0:T(8,128)S(1)}, f32[3,1,8,128]{3,2,1,0:T(8,128)S(1)}, u32[]{:S(2)}, u32[]{:S(2)}) %collective-permute-start.8) | collective-permute-done | bytes 12320 | tf_op jit(solution)/shard_map/ppermute | solution.py:30
  113.8 2.2 %collective-permute-start.11 = (f32[3,4,1,128]{3,2,1,0:T(1,128)S(1)}, f32[3,4,1,128]{3,2,1,0:T(1,128)S(1)}, u32[]{:S(2)}, u32[]{:S(2)}) collective-permute-start(f32[3,4,1,128]{3,2,1,0:T(1,128)S(1)} %get-tuple-element.33), channel_id=1, source_target_pairs={{1,0},{2,1},{3,2},{5,4},{6,5},{7,6},{9,8},{10,9},{11,10},{13,12},{... | collective-permute-start | bytes 18440 | tf_op jit(solution)/shard_map/ppermute | solution.py:31
  116.1 2.1 %collective-permute-start.10 = (f32[3,4,1,128]{3,2,1,0:T(1,128)S(1)}, f32[3,4,1,128]{3,2,1,0:T(1,128)S(1)}, u32[]{:S(2)}, u32[]{:S(2)}) collective-permute-start(f32[3,4,1,128]{3,2,1,0:T(1,128)S(1)} %get-tuple-element.32), channel_id=1, source_target_pairs={{0,1},{1,2},{2,3},{4,5},{5,6},{6,7},{8,9},{9,10},{10,11},{12,13},{... | collective-permute-start | bytes 18440 | tf_op jit(solution)/shard_map/ppermute | solution.py:30
  118.3 4.2 %collective-permute-done.10 = f32[3,4,1,128]{3,2,1,0:T(1,128)S(1)} collective-permute-done((f32[3,4,1,128]{3,2,1,0:T(1,128)S(1)}, f32[3,4,1,128]{3,2,1,0:T(1,128)S(1)}, u32[]{:S(2)}, u32[]{:S(2)}) %collective-permute-start.10) | collective-permute-done | bytes 6176 | tf_op jit(solution)/shard_map/ppermute | solution.py:30
  123.2 14.2 %shard_map.88 = f32[16,128,3]{2,1,0:T(8,128)} custom-call(f32[16,128,4]{2,1,0:T(8,128)} %bitcast.73, f32[3,40,128]{2,1,0:T(8,128)} %broadcast_multiply_fusion.1.source_ref, f32[576,32,128]{2,1,0:T(8,128)} %get-tuple-element.5.refs_0_), custom_call_target="tpu_custom_call" | custom-call | tf_op jit(solution)/shard_map/pallas_call | solution.py:161
  137.4 1.6 copy.67
  139.0 2.4 %collective-permute-start.13 = (f32[3,1,8,128]{3,2,1,0:T(8,128)S(1)}, f32[3,1,8,128]{3,2,1,0:T(8,128)S(1)}, u32[]{:S(2)}, u32[]{:S(2)}) collective-permute-start(f32[3,1,8,128]{3,2,1,0:T(8,128)S(1)} %get-tuple-element.37), channel_id=1, source_target_pairs={{4,0},{8,4},{12,8},{16,12},{20,16},{24,20},{28,24},{32,28},{36,32}... | collective-permute-start | bytes 36872 | tf_op jit(solution)/shard_map/ppermute | solution.py:31
  141.4 3.4 %collective-permute-start.12 = (f32[3,1,8,128]{3,2,1,0:T(8,128)S(1)}, f32[3,1,8,128]{3,2,1,0:T(8,128)S(1)}, u32[]{:S(2)}, u32[]{:S(2)}) collective-permute-start(f32[3,1,8,128]{3,2,1,0:T(8,128)S(1)} %get-tuple-element.36), channel_id=1, source_target_pairs={{0,4},{4,8},{8,12},{12,16},{16,20},{20,24},{24,28},{28,32},{32,36}... | collective-permute-start | bytes 36872 | tf_op jit(solution)/shard_map/ppermute | solution.py:30
  144.9 6.3 %collective-permute-done.12 = f32[3,1,8,128]{3,2,1,0:T(8,128)S(1)} collective-permute-done((f32[3,1,8,128]{3,2,1,0:T(8,128)S(1)}, f32[3,1,8,128]{3,2,1,0:T(8,128)S(1)}, u32[]{:S(2)}, u32[]{:S(2)}) %collective-permute-start.12) | collective-permute-done | bytes 12320 | tf_op jit(solution)/shard_map/ppermute | solution.py:30
  151.3 1.9 %collective-permute-start.15 = (f32[3,4,1,128]{3,2,1,0:T(1,128)S(1)}, f32[3,4,1,128]{3,2,1,0:T(1,128)S(1)}, u32[]{:S(2)}, u32[]{:S(2)}) collective-permute-start(f32[3,4,1,128]{3,2,1,0:T(1,128)S(1)} %get-tuple-element.31), channel_id=1, source_target_pairs={{1,0},{2,1},{3,2},{5,4},{6,5},{7,6},{9,8},{10,9},{11,10},{13,12},{... | collective-permute-start | bytes 18440 | tf_op jit(solution)/shard_map/ppermute | solution.py:31
  153.2 2.4 %collective-permute-start.14 = (f32[3,4,1,128]{3,2,1,0:T(1,128)S(1)}, f32[3,4,1,128]{3,2,1,0:T(1,128)S(1)}, u32[]{:S(2)}, u32[]{:S(2)}) collective-permute-start(f32[3,4,1,128]{3,2,1,0:T(1,128)S(1)} %get-tuple-element.30), channel_id=1, source_target_pairs={{0,1},{1,2},{2,3},{4,5},{5,6},{6,7},{8,9},{9,10},{10,11},{12,13},{... | collective-permute-start | bytes 18440 | tf_op jit(solution)/shard_map/ppermute | solution.py:30
  155.6 4.0 %collective-permute-done.14 = f32[3,4,1,128]{3,2,1,0:T(1,128)S(1)} collective-permute-done((f32[3,4,1,128]{3,2,1,0:T(1,128)S(1)}, f32[3,4,1,128]{3,2,1,0:T(1,128)S(1)}, u32[]{:S(2)}, u32[]{:S(2)}) %collective-permute-start.14) | collective-permute-done | bytes 6176 | tf_op jit(solution)/shard_map/ppermute | solution.py:30
  160.3 14.2 %shard_map.89 = f32[16,128,3]{2,1,0:T(8,128)} custom-call(f32[16,128,4]{2,1,0:T(8,128)} %bitcast.74, f32[3,40,128]{2,1,0:T(8,128)} %broadcast_multiply_fusion.source_ref, f32[576,32,128]{2,1,0:T(8,128)} %get-tuple-element.5.refs_0_), custom_call_target="tpu_custom_call" | custom-call | tf_op jit(solution)/shard_map/pallas_call | solution.py:161
  176.3 1.9 %collective-permute-start.16 = (f32[8,8,128]{2,1,0:T(8,128)S(1)}, f32[8,8,128]{2,1,0:T(8,128)S(1)}, u32[]{:S(2)}, u32[]{:S(2)}) collective-permute-start(f32[8,8,128]{2,1,0:T(8,128)S(1)} %pad_maximum_fusion.11), channel_id=1, source_target_pairs={{0,4},{4,8},{8,12},{12,16},{16,20},{20,24},{24,28},{28,32},{32,36}... | collective-permute-start | bytes 98312 | tf_op jit(solution)/shard_map/ppermute | solution.py:39
  178.2 8.1 %collective-permute-done.16 = f32[8,8,128]{2,1,0:T(8,128)S(1)} collective-permute-done((f32[8,8,128]{2,1,0:T(8,128)S(1)}, f32[8,8,128]{2,1,0:T(8,128)S(1)}, u32[]{:S(2)}, u32[]{:S(2)}) %collective-permute-start.16) | collective-permute-done | bytes 32800 | tf_op jit(solution)/shard_map/ppermute | solution.py:39
  (101 shorter events, 19.9 us)
Async XLA Ops:
  0.6 101.4 %copy-start.6 = (f32[3]{0:T(128)S(1)}, f32[3]{0:T(128)}, u32[]{:S(2)}) copy-start(f32[3]{0:T(128)} %constant.56.clone) | copy-start | bytes 40
  0.6 57.5 %copy-start.2 = (s32[2,8]{1,0:T(2,128)S(1)}, s32[2,8]{1,0:T(2,128)}, u32[]{:S(2)}) copy-start(s32[2,8]{1,0:T(2,128)} %param.11) | copy-start | bytes 196
  0.7 63.5 %copy-start = (f32[3,2,8,128]{3,2,1,0:T(8,128)S(1)}, f32[3,2,8,128]{3,2,1,0:T(8,128)}, u32[]{:S(2)}) copy-start(f32[3,2,8,128]{3,2,1,0:T(8,128)} %param.7) | copy-start | bytes 73732
  0.7 101.3 %copy-start.1 = (f32[3,2,8,128]{3,2,1,0:T(8,128)S(1)}, f32[3,2,8,128]{3,2,1,0:T(8,128)}, u32[]{:S(2)}) copy-start(f32[3,2,8,128]{3,2,1,0:T(8,128)} %param.8) | copy-start | bytes 73732
  0.7 57.5 %copy-start.3 = (f32[2,8,128]{2,1,0:T(8,128)S(1)}, f32[2,8,128]{2,1,0:T(8,128)}, u32[]{:S(2)}) copy-start(f32[2,8,128]{2,1,0:T(8,128)} %param.9) | copy-start | bytes 24580
  0.7 57.5 %copy-start.4 = (f32[2,8,128]{2,1,0:T(8,128)S(1)}, f32[2,8,128]{2,1,0:T(8,128)}, u32[]{:S(2)}) copy-start(f32[2,8,128]{2,1,0:T(8,128)} %param.10) | copy-start | bytes 24580
  2.2 12.4 %collective-permute-start.1 = (f32[7,1,8,128]{3,2,1,0:T(8,128)S(1)}, f32[7,1,8,128]{3,2,1,0:T(8,128)S(1)}, u32[]{:S(2)}, u32[]{:S(2)}) collective-permute-start(f32[7,1,8,128]{3,2,1,0:T(8,128)S(1)} %get-tuple-element.23), channel_id=1, source_target_pairs={{4,0},{8,4},{12,8},{16,12},{20,16},{24,20},{28,24},{32,28},{36,32}... | collective-permute-start | bytes 86024 | tf_op jit(solution)/shard_map/ppermute | solution.py:31
  12.7 10.0 %collective-permute-start = (f32[7,1,8,128]{3,2,1,0:T(8,128)S(1)}, f32[7,1,8,128]{3,2,1,0:T(8,128)S(1)}, u32[]{:S(2)}, u32[]{:S(2)}) collective-permute-start(f32[7,1,8,128]{3,2,1,0:T(8,128)S(1)} %get-tuple-element.22), channel_id=1, source_target_pairs={{0,4},{4,8},{8,12},{12,16},{16,20},{20,24},{24,28},{28,32},{32,36}... | collective-permute-start | bytes 86024 | tf_op jit(solution)/shard_map/ppermute | solution.py:30
  23.6 7.2 %collective-permute-start.3 = (f32[7,4,1,128]{3,2,1,0:T(1,128)S(1)}, f32[7,4,1,128]{3,2,1,0:T(1,128)S(1)}, u32[]{:S(2)}, u32[]{:S(2)}) collective-permute-start(f32[7,4,1,128]{3,2,1,0:T(1,128)S(1)} %get-tuple-element.18), channel_id=1, source_target_pairs={{1,0},{2,1},{3,2},{5,4},{6,5},{7,6},{9,8},{10,9},{11,10},{13,12},{... | collective-permute-start | bytes 43016 | tf_op jit(solution)/shard_map/ppermute | solution.py:31
  25.5 6.5 %collective-permute-start.2 = (f32[7,4,1,128]{3,2,1,0:T(1,128)S(1)}, f32[7,4,1,128]{3,2,1,0:T(1,128)S(1)}, u32[]{:S(2)}, u32[]{:S(2)}) collective-permute-start(f32[7,4,1,128]{3,2,1,0:T(1,128)S(1)} %get-tuple-element.17), channel_id=1, source_target_pairs={{0,1},{1,2},{2,3},{4,5},{5,6},{6,7},{8,9},{9,10},{10,11},{12,13},{... | collective-permute-start | bytes 43016 | tf_op jit(solution)/shard_map/ppermute | solution.py:30
  58.3 5.9 %collective-permute-start.5 = (f32[3,1,8,128]{3,2,1,0:T(8,128)S(1)}, f32[3,1,8,128]{3,2,1,0:T(8,128)S(1)}, u32[]{:S(2)}, u32[]{:S(2)}) collective-permute-start(f32[3,1,8,128]{3,2,1,0:T(8,128)S(1)} %get-tuple-element.41), channel_id=1, source_target_pairs={{4,0},{8,4},{12,8},{16,12},{20,16},{24,20},{28,24},{32,28},{36,32}... | collective-permute-start | bytes 36872 | tf_op jit(solution)/shard_map/ppermute | solution.py:31
  60.2 9.8 %collective-permute-start.4 = (f32[3,1,8,128]{3,2,1,0:T(8,128)S(1)}, f32[3,1,8,128]{3,2,1,0:T(8,128)S(1)}, u32[]{:S(2)}, u32[]{:S(2)}) collective-permute-start(f32[3,1,8,128]{3,2,1,0:T(8,128)S(1)} %get-tuple-element.40), channel_id=1, source_target_pairs={{0,4},{4,8},{8,12},{12,16},{16,20},{20,24},{24,28},{28,32},{32,36}... | collective-permute-start | bytes 36872 | tf_op jit(solution)/shard_map/ppermute | solution.py:30
  70.0 7.1 %collective-permute-start.7 = (f32[3,4,1,128]{3,2,1,0:T(1,128)S(1)}, f32[3,4,1,128]{3,2,1,0:T(1,128)S(1)}, u32[]{:S(2)}, u32[]{:S(2)}) collective-permute-start(f32[3,4,1,128]{3,2,1,0:T(1,128)S(1)} %get-tuple-element.35), channel_id=1, source_target_pairs={{1,0},{2,1},{3,2},{5,4},{6,5},{7,6},{9,8},{10,9},{11,10},{13,12},{... | collective-permute-start | bytes 18440 | tf_op jit(solution)/shard_map/ppermute | solution.py:31
  72.3 6.5 %collective-permute-start.6 = (f32[3,4,1,128]{3,2,1,0:T(1,128)S(1)}, f32[3,4,1,128]{3,2,1,0:T(1,128)S(1)}, u32[]{:S(2)}, u32[]{:S(2)}) collective-permute-start(f32[3,4,1,128]{3,2,1,0:T(1,128)S(1)} %get-tuple-element.34), channel_id=1, source_target_pairs={{0,1},{1,2},{2,3},{4,5},{5,6},{6,7},{8,9},{9,10},{10,11},{12,13},{... | collective-permute-start | bytes 18440 | tf_op jit(solution)/shard_map/ppermute | solution.py:30
  79.6 65.3 %copy-start.5 = (s32[2,8]{1,0:T(2,128)S(1)}, s32[2,8]{1,0:T(2,128)}, u32[]{:S(2)}) copy-start(s32[2,8]{1,0:T(2,128)} %param.12) | copy-start | bytes 196
  102.1 7.7 %collective-permute-start.9 = (f32[3,1,8,128]{3,2,1,0:T(8,128)S(1)}, f32[3,1,8,128]{3,2,1,0:T(8,128)S(1)}, u32[]{:S(2)}, u32[]{:S(2)}) collective-permute-start(f32[3,1,8,128]{3,2,1,0:T(8,128)S(1)} %get-tuple-element.39), channel_id=1, source_target_pairs={{4,0},{8,4},{12,8},{16,12},{20,16},{24,20},{28,24},{32,28},{36,32}... | collective-permute-start | bytes 36872 | tf_op jit(solution)/shard_map/ppermute | solution.py:31
  104.0 9.8 %collective-permute-start.8 = (f32[3,1,8,128]{3,2,1,0:T(8,128)S(1)}, f32[3,1,8,128]{3,2,1,0:T(8,128)S(1)}, u32[]{:S(2)}, u32[]{:S(2)}) collective-permute-start(f32[3,1,8,128]{3,2,1,0:T(8,128)S(1)} %get-tuple-element.38), channel_id=1, source_target_pairs={{0,4},{4,8},{8,12},{12,16},{16,20},{20,24},{24,28},{28,32},{32,36}... | collective-permute-start | bytes 36872 | tf_op jit(solution)/shard_map/ppermute | solution.py:30
  113.8 4.4 %collective-permute-start.11 = (f32[3,4,1,128]{3,2,1,0:T(1,128)S(1)}, f32[3,4,1,128]{3,2,1,0:T(1,128)S(1)}, u32[]{:S(2)}, u32[]{:S(2)}) collective-permute-start(f32[3,4,1,128]{3,2,1,0:T(1,128)S(1)} %get-tuple-element.33), channel_id=1, source_target_pairs={{1,0},{2,1},{3,2},{5,4},{6,5},{7,6},{9,8},{10,9},{11,10},{13,12},{... | collective-permute-start | bytes 18440 | tf_op jit(solution)/shard_map/ppermute | solution.py:31
  116.1 6.5 %collective-permute-start.10 = (f32[3,4,1,128]{3,2,1,0:T(1,128)S(1)}, f32[3,4,1,128]{3,2,1,0:T(1,128)S(1)}, u32[]{:S(2)}, u32[]{:S(2)}) collective-permute-start(f32[3,4,1,128]{3,2,1,0:T(1,128)S(1)} %get-tuple-element.32), channel_id=1, source_target_pairs={{0,1},{1,2},{2,3},{4,5},{5,6},{6,7},{8,9},{9,10},{10,11},{12,13},{... | collective-permute-start | bytes 18440 | tf_op jit(solution)/shard_map/ppermute | solution.py:30
  139.0 5.9 %collective-permute-start.13 = (f32[3,1,8,128]{3,2,1,0:T(8,128)S(1)}, f32[3,1,8,128]{3,2,1,0:T(8,128)S(1)}, u32[]{:S(2)}, u32[]{:S(2)}) collective-permute-start(f32[3,1,8,128]{3,2,1,0:T(8,128)S(1)} %get-tuple-element.37), channel_id=1, source_target_pairs={{4,0},{8,4},{12,8},{16,12},{20,16},{24,20},{28,24},{32,28},{36,32}... | collective-permute-start | bytes 36872 | tf_op jit(solution)/shard_map/ppermute | solution.py:31
  141.4 9.8 %collective-permute-start.12 = (f32[3,1,8,128]{3,2,1,0:T(8,128)S(1)}, f32[3,1,8,128]{3,2,1,0:T(8,128)S(1)}, u32[]{:S(2)}, u32[]{:S(2)}) collective-permute-start(f32[3,1,8,128]{3,2,1,0:T(8,128)S(1)} %get-tuple-element.36), channel_id=1, source_target_pairs={{0,4},{4,8},{8,12},{12,16},{16,20},{20,24},{24,28},{28,32},{32,36}... | collective-permute-start | bytes 36872 | tf_op jit(solution)/shard_map/ppermute | solution.py:30
  151.3 4.4 %collective-permute-start.15 = (f32[3,4,1,128]{3,2,1,0:T(1,128)S(1)}, f32[3,4,1,128]{3,2,1,0:T(1,128)S(1)}, u32[]{:S(2)}, u32[]{:S(2)}) collective-permute-start(f32[3,4,1,128]{3,2,1,0:T(1,128)S(1)} %get-tuple-element.31), channel_id=1, source_target_pairs={{1,0},{2,1},{3,2},{5,4},{6,5},{7,6},{9,8},{10,9},{11,10},{13,12},{... | collective-permute-start | bytes 18440 | tf_op jit(solution)/shard_map/ppermute | solution.py:31
  153.2 6.5 %collective-permute-start.14 = (f32[3,4,1,128]{3,2,1,0:T(1,128)S(1)}, f32[3,4,1,128]{3,2,1,0:T(1,128)S(1)}, u32[]{:S(2)}, u32[]{:S(2)}) collective-permute-start(f32[3,4,1,128]{3,2,1,0:T(1,128)S(1)} %get-tuple-element.30), channel_id=1, source_target_pairs={{0,1},{1,2},{2,3},{4,5},{5,6},{6,7},{8,9},{9,10},{10,11},{12,13},{... | collective-permute-start | bytes 18440 | tf_op jit(solution)/shard_map/ppermute | solution.py:30
  176.3 10.0 %collective-permute-start.16 = (f32[8,8,128]{2,1,0:T(8,128)S(1)}, f32[8,8,128]{2,1,0:T(8,128)S(1)}, u32[]{:S(2)}, u32[]{:S(2)}) collective-permute-start(f32[8,8,128]{2,1,0:T(8,128)S(1)} %pad_maximum_fusion.11), channel_id=1, source_target_pairs={{0,4},{4,8},{8,12},{12,16},{16,20},{20,24},{24,28},{28,32},{32,36}... | collective-permute-start | bytes 98312 | tf_op jit(solution)/shard_map/ppermute | solution.py:39

commit v7 on v6

--- a/solution.py
+++ b/solution.py
@@ -87,10 +87,15 @@
         else:
             (out_ref,) = refs
 
-        block = pl.program_id(0)
+        grid_block = None if kind == "jacobi" else pl.program_id(0)
 
         def body(step, carry):
-            first = pl.multiple_of(step * CHUNK, CHUNK)
+            if kind == "jacobi":
+                block = step // chunk_count
+                first = pl.multiple_of((step % chunk_count) * CHUNK, CHUNK)
+            else:
+                block = grid_block
+                first = pl.multiple_of(step * CHUNK, CHUNK)
             row = block // col_count
             col = block % col_count
             own = target_ref[block, pl.ds(first, CHUNK), :]
@@ -136,7 +141,7 @@
                 )
             return carry
 
-        lax.fori_loop(0, chunk_count, body, 0)
+        lax.fori_loop(0, block_count * chunk_count if kind == "jacobi" else chunk_count, body, 0)
 
     out_shape = jax.ShapeDtypeStruct((block_count, slot_count, output_count), jnp.float32)
     whole = [
@@ -158,13 +163,7 @@
             out_specs=(out_spec, weight_spec),
         )(target_cols, source_rows)
     elif kind == "jacobi":
-        result = pl.pallas_call(
-            kernel,
-            out_shape=out_shape,
-            grid=grid,
-            in_specs=whole + [weight_spec],
-            out_specs=out_spec,
-        )(target_cols, source_rows, weights)
+        result = pl.pallas_call(kernel, out_shape=out_shape)(target_cols, source_rows, weights)
     else:
         result = pl.pallas_call(
             kernel, out_shape=out_shape, grid=grid, in_specs=whole, out_specs=out_spec
@@ -237,7 +236,7 @@
     gravity = jnp.array([GRAVITY_DOWN, 0.0, GRAVITY_UP], jnp.float32)[:, None, None, None]
     predicted = velocities + TIME_STEP * (-scale * forces[:3] + gravity)
     diagonal = 1.0 + TIME_STEP * (scale * inverse * forces[3])
-    target = jnp.concatenate([positions, viscosity[None]], axis=0)
+    target = viscosity[None]
     current = predicted
     for sweep_index in range(JACOBI):
         speed_pad = with_halo(current, (("down", 1), ("cross", 2)), 1)

time: 190 us -> 186 us (0.979)
  the two profiles are of different devices: /device:TPU:6 before, /device:TPU:3 now
where the time goes in v7:
time: 186 us; the launch traced here: 182 us
  Pallas kernels  66.3 us (36%)
  starting transfers between devices  60.1 us (32%)
  waiting for transfers between devices  30 us (16%)
  local copies, waits for them, and re-layouts  13.3 us (7%)
  other arithmetic  11.3 us (6%)
    ppermute x8, starting transfers between devices, with_halo(): before = lax.ppermute(last, axis, up)  31.9 us
    ppermute x8, starting transfers between devices, with_halo(): after = lax.ppermute(initial, axis, down)  26.3 us
    pallas_call x2, Pallas kernels, pair_pass(): pl.pallas_call(kernel, out_shape=out_shape)  24.7 us
    ppermute x8, waiting for transfers between devices, with_halo(): before = lax.ppermute(last, axis, up)  23 us
    pallas_call x1, Pallas kernels, pair_pass(): pl.pallas_call(kernel, out_shape=out_shape, grid=grid, in_specs=whole, ou...  20.9 us
    pallas_call x1, Pallas kernels, pair_pass(): pl.pallas_call(kernel, out_shape=(out_shape, weight_shape), grid=grid, in...  20.8 us
    ppermute x1, waiting for transfers between devices, from_behind(): return lax.ppermute(block, axis, route)  6.95 us
  transfers between devices with their start and end apart: 17, of which 7 were waited for; matrix products, arithmetic and copies ran while one was open for 4% of the time, Pallas kernels for 0%

profile of v7, /device:TPU:3, one launch (start us, length us, event | category | flops | bytes accessed | tf_op | source)
XLA Modules:
  0.0 182.3 jit_solution(18409614315262406243)
XLA Ops:
  2.2 9.9 %collective-permute-start.1 = (f32[7,1,8,128]{3,2,1,0:T(8,128)S(1)}, f32[7,1,8,128]{3,2,1,0:T(8,128)S(1)}, u32[]{:S(2)}, u32[]{:S(2)}) collective-permute-start(f32[7,1,8,128]{3,2,1,0:T(8,128)S(1)} %get-tuple-element.23), channel_id=1, source_target_pairs={{4,0},{8,4},{12,8},{16,12},{20,16},{24,20},{28,24},{32,28},{36,32}... | collective-permute-start | bytes 86024 | tf_op jit(solution)/shard_map/ppermute | solution.py:31
  12.2 1.9 %collective-permute-start = (f32[7,1,8,128]{3,2,1,0:T(8,128)S(1)}, f32[7,1,8,128]{3,2,1,0:T(8,128)S(1)}, u32[]{:S(2)}, u32[]{:S(2)}) collective-permute-start(f32[7,1,8,128]{3,2,1,0:T(8,128)S(1)} %get-tuple-element.22), channel_id=1, source_target_pairs={{0,4},{4,8},{8,12},{12,16},{16,20},{20,24},{24,28},{28,32},{32,36}... | collective-permute-start | bytes 86024 | tf_op jit(solution)/shard_map/ppermute | solution.py:30
  14.1 6.9 %collective-permute-done = f32[7,1,8,128]{3,2,1,0:T(8,128)S(1)} collective-permute-done((f32[7,1,8,128]{3,2,1,0:T(8,128)S(1)}, f32[7,1,8,128]{3,2,1,0:T(8,128)S(1)}, u32[]{:S(2)}, u32[]{:S(2)}) %collective-permute-start) | collective-permute-done | bytes 28704 | tf_op jit(solution)/shard_map/ppermute | solution.py:30
  21.8 4.0 %collective-permute-start.3 = (f32[7,4,1,128]{3,2,1,0:T(1,128)S(1)}, f32[7,4,1,128]{3,2,1,0:T(1,128)S(1)}, u32[]{:S(2)}, u32[]{:S(2)}) collective-permute-start(f32[7,4,1,128]{3,2,1,0:T(1,128)S(1)} %get-tuple-element.18), channel_id=1, source_target_pairs={{1,0},{2,1},{3,2},{5,4},{6,5},{7,6},{9,8},{10,9},{11,10},{13,12},{... | collective-permute-start | bytes 43016 | tf_op jit(solution)/shard_map/ppermute | solution.py:31
  25.8 3.9 %collective-permute-start.2 = (f32[7,4,1,128]{3,2,1,0:T(1,128)S(1)}, f32[7,4,1,128]{3,2,1,0:T(1,128)S(1)}, u32[]{:S(2)}, u32[]{:S(2)}) collective-permute-start(f32[7,4,1,128]{3,2,1,0:T(1,128)S(1)} %get-tuple-element.17), channel_id=1, source_target_pairs={{0,1},{1,2},{2,3},{4,5},{5,6},{6,7},{8,9},{9,10},{10,11},{12,13},{... | collective-permute-start | bytes 43016 | tf_op jit(solution)/shard_map/ppermute | solution.py:30
  35.0 20.9 %shard_map.86 = f32[16,128,2]{2,1,0:T(8,128)} custom-call(f32[16,128,6]{2,1,0:T(8,128)} %bitcast.71, f32[6,40,128]{2,1,0:T(8,128)} %copy.60.source_ref), custom_call_target="tpu_custom_call" | custom-call | tf_op jit(solution)/shard_map/pallas_call | solution.py:168
  55.9 2.5 %fusion.3 = (f32[16,128]{1,0:T(8,128)S(1)}, f32[16,128]{1,0:T(8,128)S(1)}, f32[1,16,128]{0,2,1:T(8,128)S(1)}) fusion(f32[2,16,128]{0,2,1:T(8,128)} %bitcast.67, s32[16]{0:T(128)S(1)} %lt.80), kind=kLoop, calls=%fused_computation.9 | loop fusion | flops 16384 | bytes 41024 | tf_op jit(solution)/shard_map/mul | solution.py:222
  58.9 1.9 %collective-permute-start.5 = (f32[3,1,8,128]{3,2,1,0:T(8,128)S(1)}, f32[3,1,8,128]{3,2,1,0:T(8,128)S(1)}, u32[]{:S(2)}, u32[]{:S(2)}) collective-permute-start(f32[3,1,8,128]{3,2,1,0:T(8,128)S(1)} %get-tuple-element.41), channel_id=1, source_target_pairs={{4,0},{8,4},{12,8},{16,12},{20,16},{24,20},{28,24},{32,28},{36,32}... | collective-permute-start | bytes 36872 | tf_op jit(solution)/shard_map/ppermute | solution.py:31
  60.9 3.3 %collective-permute-start.4 = (f32[3,1,8,128]{3,2,1,0:T(8,128)S(1)}, f32[3,1,8,128]{3,2,1,0:T(8,128)S(1)}, u32[]{:S(2)}, u32[]{:S(2)}) collective-permute-start(f32[3,1,8,128]{3,2,1,0:T(8,128)S(1)} %get-tuple-element.40), channel_id=1, source_target_pairs={{0,4},{4,8},{8,12},{12,16},{16,20},{20,24},{24,28},{28,32},{32,36}... | collective-permute-start | bytes 36872 | tf_op jit(solution)/shard_map/ppermute | solution.py:30
  64.2 5.3 %collective-permute-done.4 = f32[3,1,8,128]{3,2,1,0:T(8,128)S(1)} collective-permute-done((f32[3,1,8,128]{3,2,1,0:T(8,128)S(1)}, f32[3,1,8,128]{3,2,1,0:T(8,128)S(1)}, u32[]{:S(2)}, u32[]{:S(2)}) %collective-permute-start.4) | collective-permute-done | bytes 12320 | tf_op jit(solution)/shard_map/ppermute | solution.py:30
  69.5 1.9 %collective-permute-start.7 = (f32[3,4,1,128]{3,2,1,0:T(1,128)S(1)}, f32[3,4,1,128]{3,2,1,0:T(1,128)S(1)}, u32[]{:S(2)}, u32[]{:S(2)}) collective-permute-start(f32[3,4,1,128]{3,2,1,0:T(1,128)S(1)} %get-tuple-element.35), channel_id=1, source_target_pairs={{1,0},{2,1},{3,2},{5,4},{6,5},{7,6},{9,8},{10,9},{11,10},{13,12},{... | collective-permute-start | bytes 18440 | tf_op jit(solution)/shard_map/ppermute | solution.py:31
  71.5 5.1 %collective-permute-start.6 = (f32[3,4,1,128]{3,2,1,0:T(1,128)S(1)}, f32[3,4,1,128]{3,2,1,0:T(1,128)S(1)}, u32[]{:S(2)}, u32[]{:S(2)}) collective-permute-start(f32[3,4,1,128]{3,2,1,0:T(1,128)S(1)} %get-tuple-element.34), channel_id=1, source_target_pairs={{0,1},{1,2},{2,3},{4,5},{5,6},{6,7},{8,9},{9,10},{10,11},{12,13},{... | collective-permute-start | bytes 18440 | tf_op jit(solution)/shard_map/ppermute | solution.py:30
  76.6 1.4 copy.65
  78.0 1.4 copy.71.target_ref
  80.2 20.8 %shard_map.87 = (f32[16,128,4]{2,1,0:T(8,128)}, f32[576,32,128]{2,1,0:T(8,128)}) custom-call(f32[16,128,5]{2,1,0:T(8,128)} %bitcast.70, f32[6,40,128]{2,1,0:T(8,128)} %copy.67.source_ref), custom_call_target="tpu_custom_call" | custom-call | tf_op jit(solution)/shard_map/pallas_call | solution.py:158
  102.7 1.9 %collective-permute-start.9 = (f32[3,1,8,128]{3,2,1,0:T(8,128)S(1)}, f32[3,1,8,128]{3,2,1,0:T(8,128)S(1)}, u32[]{:S(2)}, u32[]{:S(2)}) collective-permute-start(f32[3,1,8,128]{3,2,1,0:T(8,128)S(1)} %get-tuple-element.39), channel_id=1, source_target_pairs={{4,0},{8,4},{12,8},{16,12},{20,16},{24,20},{28,24},{32,28},{36,32}... | collective-permute-start | bytes 36872 | tf_op jit(solution)/shard_map/ppermute | solution.py:31
  104.7 3.4 %collective-permute-start.8 = (f32[3,1,8,128]{3,2,1,0:T(8,128)S(1)}, f32[3,1,8,128]{3,2,1,0:T(8,128)S(1)}, u32[]{:S(2)}, u32[]{:S(2)}) collective-permute-start(f32[3,1,8,128]{3,2,1,0:T(8,128)S(1)} %get-tuple-element.38), channel_id=1, source_target_pairs={{0,4},{4,8},{8,12},{12,16},{16,20},{20,24},{24,28},{28,32},{32,36}... | collective-permute-start | bytes 36872 | tf_op jit(solution)/shard_map/ppermute | solution.py:30
  108.0 1.9 %slice_reduce_fusion = f32[16,128]{1,0:T(8,128)S(1)} fusion(f32[4,16,128]{0,2,1:T(8,128)} %bitcast.73), kind=kLoop, calls=%fused_computation | loop fusion | bytes 16384 | tf_op jit(solution)/shard_map/slice | solution.py:238
  109.9 3.4 %collective-permute-done.8 = f32[3,1,8,128]{3,2,1,0:T(8,128)S(1)} collective-permute-done((f32[3,1,8,128]{3,2,1,0:T(8,128)S(1)}, f32[3,1,8,128]{3,2,1,0:T(8,128)S(1)}, u32[]{:S(2)}, u32[]{:S(2)}) %collective-permute-start.8) | collective-permute-done | bytes 12320 | tf_op jit(solution)/shard_map/ppermute | solution.py:30
  113.3 1.9 %collective-permute-start.11 = (f32[3,4,1,128]{3,2,1,0:T(1,128)S(1)}, f32[3,4,1,128]{3,2,1,0:T(1,128)S(1)}, u32[]{:S(2)}, u32[]{:S(2)}) collective-permute-start(f32[3,4,1,128]{3,2,1,0:T(1,128)S(1)} %get-tuple-element.33), channel_id=1, source_target_pairs={{1,0},{2,1},{3,2},{5,4},{6,5},{7,6},{9,8},{10,9},{11,10},{13,12},{... | collective-permute-start | bytes 18440 | tf_op jit(solution)/shard_map/ppermute | solution.py:31
  115.3 5.1 %collective-permute-start.10 = (f32[3,4,1,128]{3,2,1,0:T(1,128)S(1)}, f32[3,4,1,128]{3,2,1,0:T(1,128)S(1)}, u32[]{:S(2)}, u32[]{:S(2)}) collective-permute-start(f32[3,4,1,128]{3,2,1,0:T(1,128)S(1)} %get-tuple-element.32), channel_id=1, source_target_pairs={{0,1},{1,2},{2,3},{4,5},{5,6},{6,7},{8,9},{9,10},{10,11},{12,13},{... | collective-permute-start | bytes 18440 | tf_op jit(solution)/shard_map/ppermute | solution.py:30
  121.9 12.4 %shard_map.88 = f32[16,128,3]{2,1,0:T(8,128)} custom-call(f32[16,128,1]{2,1,0:T(8,128)} %copy.71.target_ref, f32[3,40,128]{2,1,0:T(8,128)} %broadcast_multiply_fusion.1.source_ref, f32[576,32,128]{2,1,0:T(8,128)} %get-tuple-element.5.refs_0_), custom_call_target="tpu_custom_call" | custom-call | tf_op jit(solution)/shard_map/pallas_call | solution.py:166
  134.2 1.6 copy.70
  135.8 2.7 %collective-permute-start.13 = (f32[3,1,8,128]{3,2,1,0:T(8,128)S(1)}, f32[3,1,8,128]{3,2,1,0:T(8,128)S(1)}, u32[]{:S(2)}, u32[]{:S(2)}) collective-permute-start(f32[3,1,8,128]{3,2,1,0:T(8,128)S(1)} %get-tuple-element.37), channel_id=1, source_target_pairs={{4,0},{8,4},{12,8},{16,12},{20,16},{24,20},{28,24},{32,28},{36,32}... | collective-permute-start | bytes 36872 | tf_op jit(solution)/shard_map/ppermute | solution.py:31
  138.6 2.5 %collective-permute-start.12 = (f32[3,1,8,128]{3,2,1,0:T(8,128)S(1)}, f32[3,1,8,128]{3,2,1,0:T(8,128)S(1)}, u32[]{:S(2)}, u32[]{:S(2)}) collective-permute-start(f32[3,1,8,128]{3,2,1,0:T(8,128)S(1)} %get-tuple-element.36), channel_id=1, source_target_pairs={{0,4},{4,8},{8,12},{12,16},{16,20},{20,24},{24,28},{28,32},{32,36}... | collective-permute-start | bytes 36872 | tf_op jit(solution)/shard_map/ppermute | solution.py:30
  141.2 6.1 %collective-permute-done.12 = f32[3,1,8,128]{3,2,1,0:T(8,128)S(1)} collective-permute-done((f32[3,1,8,128]{3,2,1,0:T(8,128)S(1)}, f32[3,1,8,128]{3,2,1,0:T(8,128)S(1)}, u32[]{:S(2)}, u32[]{:S(2)}) %collective-permute-start.12) | collective-permute-done | bytes 12320 | tf_op jit(solution)/shard_map/ppermute | solution.py:30
  147.2 1.9 %collective-permute-start.15 = (f32[3,4,1,128]{3,2,1,0:T(1,128)S(1)}, f32[3,4,1,128]{3,2,1,0:T(1,128)S(1)}, u32[]{:S(2)}, u32[]{:S(2)}) collective-permute-start(f32[3,4,1,128]{3,2,1,0:T(1,128)S(1)} %get-tuple-element.31), channel_id=1, source_target_pairs={{1,0},{2,1},{3,2},{5,4},{6,5},{7,6},{9,8},{10,9},{11,10},{13,12},{... | collective-permute-start | bytes 18440 | tf_op jit(solution)/shard_map/ppermute | solution.py:31
  149.2 6.5 %collective-permute-start.14 = (f32[3,4,1,128]{3,2,1,0:T(1,128)S(1)}, f32[3,4,1,128]{3,2,1,0:T(1,128)S(1)}, u32[]{:S(2)}, u32[]{:S(2)}) collective-permute-start(f32[3,4,1,128]{3,2,1,0:T(1,128)S(1)} %get-tuple-element.30), channel_id=1, source_target_pairs={{0,1},{1,2},{2,3},{4,5},{5,6},{6,7},{8,9},{9,10},{10,11},{12,13},{... | collective-permute-start | bytes 18440 | tf_op jit(solution)/shard_map/ppermute | solution.py:30
  157.1 12.4 %shard_map.89 = f32[16,128,3]{2,1,0:T(8,128)} custom-call(f32[16,128,1]{2,1,0:T(8,128)} %copy.71.target_ref, f32[3,40,128]{2,1,0:T(8,128)} %broadcast_multiply_fusion.source_ref, f32[576,32,128]{2,1,0:T(8,128)} %get-tuple-element.5.refs_0_), custom_call_target="tpu_custom_call" | custom-call | tf_op jit(solution)/shard_map/pallas_call | solution.py:166
  169.5 1.6 copy.72
  171.2 1.9 %collective-permute-start.16 = (f32[8,8,128]{2,1,0:T(8,128)S(1)}, f32[8,8,128]{2,1,0:T(8,128)S(1)}, u32[]{:S(2)}, u32[]{:S(2)}) collective-permute-start(f32[8,8,128]{2,1,0:T(8,128)S(1)} %pad_maximum_fusion.10), channel_id=1, source_target_pairs={{0,4},{4,8},{8,12},{12,16},{16,20},{20,24},{24,28},{28,32},{32,36}... | collective-permute-start | bytes 98312 | tf_op jit(solution)/shard_map/ppermute | solution.py:39
  173.1 6.9 %collective-permute-done.16 = f32[8,8,128]{2,1,0:T(8,128)S(1)} collective-permute-done((f32[8,8,128]{2,1,0:T(8,128)S(1)}, f32[8,8,128]{2,1,0:T(8,128)S(1)}, u32[]{:S(2)}, u32[]{:S(2)}) %collective-permute-start.16) | collective-permute-done | bytes 32800 | tf_op jit(solution)/shard_map/ppermute | solution.py:39
  (100 shorter events, 15.8 us)
Async XLA Ops:
  0.6 102.0 %copy-start.6 = (f32[3]{0:T(128)S(1)}, f32[3]{0:T(128)}, u32[]{:S(2)}) copy-start(f32[3]{0:T(128)} %constant.56.clone) | copy-start | bytes 40
  0.6 58.1 %copy-start.2 = (s32[2,8]{1,0:T(2,128)S(1)}, s32[2,8]{1,0:T(2,128)}, u32[]{:S(2)}) copy-start(s32[2,8]{1,0:T(2,128)} %param.11) | copy-start | bytes 196
  0.7 76.0 %copy-start = (f32[3,2,8,128]{3,2,1,0:T(8,128)S(1)}, f32[3,2,8,128]{3,2,1,0:T(8,128)}, u32[]{:S(2)}) copy-start(f32[3,2,8,128]{3,2,1,0:T(8,128)} %param.7) | copy-start | bytes 73732
  0.7 102.0 %copy-start.1 = (f32[3,2,8,128]{3,2,1,0:T(8,128)S(1)}, f32[3,2,8,128]{3,2,1,0:T(8,128)}, u32[]{:S(2)}) copy-start(f32[3,2,8,128]{3,2,1,0:T(8,128)} %param.8) | copy-start | bytes 73732
  0.7 58.2 %copy-start.3 = (f32[2,8,128]{2,1,0:T(8,128)S(1)}, f32[2,8,128]{2,1,0:T(8,128)}, u32[]{:S(2)}) copy-start(f32[2,8,128]{2,1,0:T(8,128)} %param.9) | copy-start | bytes 24580
  0.7 58.2 %copy-start.4 = (f32[2,8,128]{2,1,0:T(8,128)S(1)}, f32[2,8,128]{2,1,0:T(8,128)}, u32[]{:S(2)}) copy-start(f32[2,8,128]{2,1,0:T(8,128)} %param.10) | copy-start | bytes 24580
  2.2 11.8 %collective-permute-start.1 = (f32[7,1,8,128]{3,2,1,0:T(8,128)S(1)}, f32[7,1,8,128]{3,2,1,0:T(8,128)S(1)}, u32[]{:S(2)}, u32[]{:S(2)}) collective-permute-start(f32[7,1,8,128]{3,2,1,0:T(8,128)S(1)} %get-tuple-element.23), channel_id=1, source_target_pairs={{4,0},{8,4},{12,8},{16,12},{20,16},{24,20},{28,24},{32,28},{36,32}... | collective-permute-start | bytes 86024 | tf_op jit(solution)/shard_map/ppermute | solution.py:31
  12.2 8.8 %collective-permute-start = (f32[7,1,8,128]{3,2,1,0:T(8,128)S(1)}, f32[7,1,8,128]{3,2,1,0:T(8,128)S(1)}, u32[]{:S(2)}, u32[]{:S(2)}) collective-permute-start(f32[7,1,8,128]{3,2,1,0:T(8,128)S(1)} %get-tuple-element.22), channel_id=1, source_target_pairs={{0,4},{4,8},{8,12},{12,16},{16,20},{20,24},{24,28},{28,32},{32,36}... | collective-permute-start | bytes 86024 | tf_op jit(solution)/shard_map/ppermute | solution.py:30
  21.8 10.8 %collective-permute-start.3 = (f32[7,4,1,128]{3,2,1,0:T(1,128)S(1)}, f32[7,4,1,128]{3,2,1,0:T(1,128)S(1)}, u32[]{:S(2)}, u32[]{:S(2)}) collective-permute-start(f32[7,4,1,128]{3,2,1,0:T(1,128)S(1)} %get-tuple-element.18), channel_id=1, source_target_pairs={{1,0},{2,1},{3,2},{5,4},{6,5},{7,6},{9,8},{10,9},{11,10},{13,12},{... | collective-permute-start | bytes 43016 | tf_op jit(solution)/shard_map/ppermute | solution.py:31
  25.8 6.8 %collective-permute-start.2 = (f32[7,4,1,128]{3,2,1,0:T(1,128)S(1)}, f32[7,4,1,128]{3,2,1,0:T(1,128)S(1)}, u32[]{:S(2)}, u32[]{:S(2)}) collective-permute-start(f32[7,4,1,128]{3,2,1,0:T(1,128)S(1)} %get-tuple-element.17), channel_id=1, source_target_pairs={{0,1},{1,2},{2,3},{4,5},{5,6},{6,7},{8,9},{9,10},{10,11},{12,13},{... | collective-permute-start | bytes 43016 | tf_op jit(solution)/shard_map/ppermute | solution.py:30
  58.9 5.3 %collective-permute-start.5 = (f32[3,1,8,128]{3,2,1,0:T(8,128)S(1)}, f32[3,1,8,128]{3,2,1,0:T(8,128)S(1)}, u32[]{:S(2)}, u32[]{:S(2)}) collective-permute-start(f32[3,1,8,128]{3,2,1,0:T(8,128)S(1)} %get-tuple-element.41), channel_id=1, source_target_pairs={{4,0},{8,4},{12,8},{16,12},{20,16},{24,20},{28,24},{32,28},{36,32}... | collective-permute-start | bytes 36872 | tf_op jit(solution)/shard_map/ppermute | solution.py:31
  60.9 8.7 %collective-permute-start.4 = (f32[3,1,8,128]{3,2,1,0:T(8,128)S(1)}, f32[3,1,8,128]{3,2,1,0:T(8,128)S(1)}, u32[]{:S(2)}, u32[]{:S(2)}) collective-permute-start(f32[3,1,8,128]{3,2,1,0:T(8,128)S(1)} %get-tuple-element.40), channel_id=1, source_target_pairs={{0,4},{4,8},{8,12},{12,16},{16,20},{20,24},{24,28},{28,32},{32,36}... | collective-permute-start | bytes 36872 | tf_op jit(solution)/shard_map/ppermute | solution.py:30
  69.5 9.8 %collective-permute-start.7 = (f32[3,4,1,128]{3,2,1,0:T(1,128)S(1)}, f32[3,4,1,128]{3,2,1,0:T(1,128)S(1)}, u32[]{:S(2)}, u32[]{:S(2)}) collective-permute-start(f32[3,4,1,128]{3,2,1,0:T(1,128)S(1)} %get-tuple-element.35), channel_id=1, source_target_pairs={{1,0},{2,1},{3,2},{5,4},{6,5},{7,6},{9,8},{10,9},{11,10},{13,12},{... | collective-permute-start | bytes 18440 | tf_op jit(solution)/shard_map/ppermute | solution.py:31
  71.5 7.9 %collective-permute-start.6 = (f32[3,4,1,128]{3,2,1,0:T(1,128)S(1)}, f32[3,4,1,128]{3,2,1,0:T(1,128)S(1)}, u32[]{:S(2)}, u32[]{:S(2)}) collective-permute-start(f32[3,4,1,128]{3,2,1,0:T(1,128)S(1)} %get-tuple-element.34), channel_id=1, source_target_pairs={{0,1},{1,2},{2,3},{4,5},{5,6},{6,7},{8,9},{9,10},{10,11},{12,13},{... | collective-permute-start | bytes 18440 | tf_op jit(solution)/shard_map/ppermute | solution.py:30
  80.2 60.9 %copy-start.5 = (s32[2,8]{1,0:T(2,128)S(1)}, s32[2,8]{1,0:T(2,128)}, u32[]{:S(2)}) copy-start(s32[2,8]{1,0:T(2,128)} %param.12) | copy-start | bytes 196
  102.7 7.2 %collective-permute-start.9 = (f32[3,1,8,128]{3,2,1,0:T(8,128)S(1)}, f32[3,1,8,128]{3,2,1,0:T(8,128)S(1)}, u32[]{:S(2)}, u32[]{:S(2)}) collective-permute-start(f32[3,1,8,128]{3,2,1,0:T(8,128)S(1)} %get-tuple-element.39), channel_id=1, source_target_pairs={{4,0},{8,4},{12,8},{16,12},{20,16},{24,20},{28,24},{32,28},{36,32}... | collective-permute-start | bytes 36872 | tf_op jit(solution)/shard_map/ppermute | solution.py:31
  104.7 8.7 %collective-permute-start.8 = (f32[3,1,8,128]{3,2,1,0:T(8,128)S(1)}, f32[3,1,8,128]{3,2,1,0:T(8,128)S(1)}, u32[]{:S(2)}, u32[]{:S(2)}) collective-permute-start(f32[3,1,8,128]{3,2,1,0:T(8,128)S(1)} %get-tuple-element.38), channel_id=1, source_target_pairs={{0,4},{4,8},{8,12},{12,16},{16,20},{20,24},{24,28},{28,32},{32,36}... | collective-permute-start | bytes 36872 | tf_op jit(solution)/shard_map/ppermute | solution.py:30
  113.3 7.2 %collective-permute-start.11 = (f32[3,4,1,128]{3,2,1,0:T(1,128)S(1)}, f32[3,4,1,128]{3,2,1,0:T(1,128)S(1)}, u32[]{:S(2)}, u32[]{:S(2)}) collective-permute-start(f32[3,4,1,128]{3,2,1,0:T(1,128)S(1)} %get-tuple-element.33), channel_id=1, source_target_pairs={{1,0},{2,1},{3,2},{5,4},{6,5},{7,6},{9,8},{10,9},{11,10},{13,12},{... | collective-permute-start | bytes 18440 | tf_op jit(solution)/shard_map/ppermute | solution.py:31
  115.3 5.9 %collective-permute-start.10 = (f32[3,4,1,128]{3,2,1,0:T(1,128)S(1)}, f32[3,4,1,128]{3,2,1,0:T(1,128)S(1)}, u32[]{:S(2)}, u32[]{:S(2)}) collective-permute-start(f32[3,4,1,128]{3,2,1,0:T(1,128)S(1)} %get-tuple-element.32), channel_id=1, source_target_pairs={{0,1},{1,2},{2,3},{4,5},{5,6},{6,7},{8,9},{9,10},{10,11},{12,13},{... | collective-permute-start | bytes 18440 | tf_op jit(solution)/shard_map/ppermute | solution.py:30
  135.8 5.3 %collective-permute-start.13 = (f32[3,1,8,128]{3,2,1,0:T(8,128)S(1)}, f32[3,1,8,128]{3,2,1,0:T(8,128)S(1)}, u32[]{:S(2)}, u32[]{:S(2)}) collective-permute-start(f32[3,1,8,128]{3,2,1,0:T(8,128)S(1)} %get-tuple-element.37), channel_id=1, source_target_pairs={{4,0},{8,4},{12,8},{16,12},{20,16},{24,20},{28,24},{32,28},{36,32}... | collective-permute-start | bytes 36872 | tf_op jit(solution)/shard_map/ppermute | solution.py:31
  138.6 8.7 %collective-permute-start.12 = (f32[3,1,8,128]{3,2,1,0:T(8,128)S(1)}, f32[3,1,8,128]{3,2,1,0:T(8,128)S(1)}, u32[]{:S(2)}, u32[]{:S(2)}) collective-permute-start(f32[3,1,8,128]{3,2,1,0:T(8,128)S(1)} %get-tuple-element.36), channel_id=1, source_target_pairs={{0,4},{4,8},{8,12},{12,16},{16,20},{20,24},{24,28},{28,32},{32,36}... | collective-permute-start | bytes 36872 | tf_op jit(solution)/shard_map/ppermute | solution.py:30
  147.2 8.5 %collective-permute-start.15 = (f32[3,4,1,128]{3,2,1,0:T(1,128)S(1)}, f32[3,4,1,128]{3,2,1,0:T(1,128)S(1)}, u32[]{:S(2)}, u32[]{:S(2)}) collective-permute-start(f32[3,4,1,128]{3,2,1,0:T(1,128)S(1)} %get-tuple-element.31), channel_id=1, source_target_pairs={{1,0},{2,1},{3,2},{5,4},{6,5},{7,6},{9,8},{10,9},{11,10},{13,12},{... | collective-permute-start | bytes 18440 | tf_op jit(solution)/shard_map/ppermute | solution.py:31
  149.2 7.3 %collective-permute-start.14 = (f32[3,4,1,128]{3,2,1,0:T(1,128)S(1)}, f32[3,4,1,128]{3,2,1,0:T(1,128)S(1)}, u32[]{:S(2)}, u32[]{:S(2)}) collective-permute-start(f32[3,4,1,128]{3,2,1,0:T(1,128)S(1)} %get-tuple-element.30), channel_id=1, source_target_pairs={{0,1},{1,2},{2,3},{4,5},{5,6},{6,7},{8,9},{9,10},{10,11},{12,13},{... | collective-permute-start | bytes 18440 | tf_op jit(solution)/shard_map/ppermute | solution.py:30
  171.2 8.9 %collective-permute-start.16 = (f32[8,8,128]{2,1,0:T(8,128)S(1)}, f32[8,8,128]{2,1,0:T(8,128)S(1)}, u32[]{:S(2)}, u32[]{:S(2)}) collective-permute-start(f32[8,8,128]{2,1,0:T(8,128)S(1)} %pad_maximum_fusion.10), channel_id=1, source_target_pairs={{0,4},{4,8},{8,12},{12,16},{16,20},{20,24},{24,28},{28,32},{32,36}... | collective-permute-start | bytes 98312 | tf_op jit(solution)/shard_map/ppermute | solution.py:39

commit v8 on v7

--- a/solution.py
+++ b/solution.py
@@ -65,7 +65,7 @@
 
 
 FAR_AWAY = 1.0e4
-CHUNK = 32
+CHUNK = 128
 
 
 def pair_pass(kind, target, source, row_count, col_count, weights=None):

time: 186 us -> 164 us (0.88)
  the two profiles are of different devices: /device:TPU:3 before, /device:TPU:6 now
where the time goes in v8:
time: 164 us; the launch traced here: 163 us
  starting transfers between devices  49.1 us (30%)
  Pallas kernels  44.5 us (27%)
  waiting for transfers between devices  43.5 us (27%)
  local copies, waits for them, and re-layouts  13.3 us (8%)
  other arithmetic  11.3 us (7%)
    ppermute x8, waiting for transfers between devices, with_halo(): before = lax.ppermute(last, axis, up)  35.4 us
    ppermute x8, starting transfers between devices, with_halo(): after = lax.ppermute(initial, axis, down)  25.1 us
    ppermute x8, starting transfers between devices, with_halo(): before = lax.ppermute(last, axis, up)  22.1 us
    pallas_call x2, Pallas kernels, pair_pass(): pl.pallas_call(kernel, out_shape=out_shape)  16.5 us
    pallas_call x1, Pallas kernels, pair_pass(): pl.pallas_call(kernel, out_shape=(out_shape, weight_shape), grid=grid, in...  14.1 us
    pallas_call x1, Pallas kernels, pair_pass(): pl.pallas_call(kernel, out_shape=out_shape, grid=grid, in_specs=whole, ou...  13.9 us
    ppermute x1, waiting for transfers between devices, from_behind(): return lax.ppermute(block, axis, route)  8.1 us
  transfers between devices with their start and end apart: 17, of which 9 were waited for; matrix products, arithmetic and copies ran while one was open for 5% of the time, Pallas kernels for 0%

profile of v8, /device:TPU:6, one launch (start us, length us, event | category | flops | bytes accessed | tf_op | source)
XLA Modules:
  0.0 163.0 jit_solution(15559524860490042824)
XLA Ops:
  2.2 10.5 %collective-permute-start.1 = (f32[7,1,8,128]{3,2,1,0:T(8,128)S(1)}, f32[7,1,8,128]{3,2,1,0:T(8,128)S(1)}, u32[]{:S(2)}, u32[]{:S(2)}) collective-permute-start(f32[7,1,8,128]{3,2,1,0:T(8,128)S(1)} %get-tuple-element.23), channel_id=1, source_target_pairs={{4,0},{8,4},{12,8},{16,12},{20,16},{24,20},{28,24},{32,28},{36,32}... | collective-permute-start | bytes 86024 | tf_op jit(solution)/shard_map/ppermute | solution.py:31
  12.7 1.9 %collective-permute-start = (f32[7,1,8,128]{3,2,1,0:T(8,128)S(1)}, f32[7,1,8,128]{3,2,1,0:T(8,128)S(1)}, u32[]{:S(2)}, u32[]{:S(2)}) collective-permute-start(f32[7,1,8,128]{3,2,1,0:T(8,128)S(1)} %get-tuple-element.22), channel_id=1, source_target_pairs={{0,4},{4,8},{8,12},{12,16},{16,20},{20,24},{24,28},{28,32},{32,36}... | collective-permute-start | bytes 86024 | tf_op jit(solution)/shard_map/ppermute | solution.py:30
  14.7 8.0 %collective-permute-done = f32[7,1,8,128]{3,2,1,0:T(8,128)S(1)} collective-permute-done((f32[7,1,8,128]{3,2,1,0:T(8,128)S(1)}, f32[7,1,8,128]{3,2,1,0:T(8,128)S(1)}, u32[]{:S(2)}, u32[]{:S(2)}) %collective-permute-start) | collective-permute-done | bytes 28704 | tf_op jit(solution)/shard_map/ppermute | solution.py:30
  23.6 1.9 %collective-permute-start.3 = (f32[7,4,1,128]{3,2,1,0:T(1,128)S(1)}, f32[7,4,1,128]{3,2,1,0:T(1,128)S(1)}, u32[]{:S(2)}, u32[]{:S(2)}) collective-permute-start(f32[7,4,1,128]{3,2,1,0:T(1,128)S(1)} %get-tuple-element.18), channel_id=1, source_target_pairs={{1,0},{2,1},{3,2},{5,4},{6,5},{7,6},{9,8},{10,9},{11,10},{13,12},{... | collective-permute-start | bytes 43016 | tf_op jit(solution)/shard_map/ppermute | solution.py:31
  25.5 2.4 %collective-permute-start.2 = (f32[7,4,1,128]{3,2,1,0:T(1,128)S(1)}, f32[7,4,1,128]{3,2,1,0:T(1,128)S(1)}, u32[]{:S(2)}, u32[]{:S(2)}) collective-permute-start(f32[7,4,1,128]{3,2,1,0:T(1,128)S(1)} %get-tuple-element.17), channel_id=1, source_target_pairs={{0,1},{1,2},{2,3},{4,5},{5,6},{6,7},{8,9},{9,10},{10,11},{12,13},{... | collective-permute-start | bytes 43016 | tf_op jit(solution)/shard_map/ppermute | solution.py:30
  34.4 13.9 %shard_map.86 = f32[16,128,2]{2,1,0:T(8,128)} custom-call(f32[16,128,6]{2,1,0:T(8,128)} %bitcast.71, f32[6,40,128]{2,1,0:T(8,128)} %copy.60.source_ref), custom_call_target="tpu_custom_call" | custom-call | tf_op jit(solution)/shard_map/pallas_call | solution.py:168
  48.2 2.5 %fusion.3 = (f32[16,128]{1,0:T(8,128)S(1)}, f32[16,128]{1,0:T(8,128)S(1)}, f32[1,16,128]{0,2,1:T(8,128)S(1)}) fusion(f32[2,16,128]{0,2,1:T(8,128)} %bitcast.67, s32[16]{0:T(128)S(1)} %lt.80), kind=kLoop, calls=%fused_computation.9 | loop fusion | flops 16384 | bytes 41024 | tf_op jit(solution)/shard_map/mul | solution.py:222
  51.3 1.9 %collective-permute-start.5 = (f32[3,1,8,128]{3,2,1,0:T(8,128)S(1)}, f32[3,1,8,128]{3,2,1,0:T(8,128)S(1)}, u32[]{:S(2)}, u32[]{:S(2)}) collective-permute-start(f32[3,1,8,128]{3,2,1,0:T(8,128)S(1)} %get-tuple-element.41), channel_id=1, source_target_pairs={{4,0},{8,4},{12,8},{16,12},{20,16},{24,20},{28,24},{32,28},{36,32}... | collective-permute-start | bytes 36872 | tf_op jit(solution)/shard_map/ppermute | solution.py:31
  53.2 3.9 %collective-permute-start.4 = (f32[3,1,8,128]{3,2,1,0:T(8,128)S(1)}, f32[3,1,8,128]{3,2,1,0:T(8,128)S(1)}, u32[]{:S(2)}, u32[]{:S(2)}) collective-permute-start(f32[3,1,8,128]{3,2,1,0:T(8,128)S(1)} %get-tuple-element.40), channel_id=1, source_target_pairs={{0,4},{4,8},{8,12},{12,16},{16,20},{20,24},{24,28},{28,32},{32,36}... | collective-permute-start | bytes 36872 | tf_op jit(solution)/shard_map/ppermute | solution.py:30
  57.2 5.9 %collective-permute-done.4 = f32[3,1,8,128]{3,2,1,0:T(8,128)S(1)} collective-permute-done((f32[3,1,8,128]{3,2,1,0:T(8,128)S(1)}, f32[3,1,8,128]{3,2,1,0:T(8,128)S(1)}, u32[]{:S(2)}, u32[]{:S(2)}) %collective-permute-start.4) | collective-permute-done | bytes 12320 | tf_op jit(solution)/shard_map/ppermute | solution.py:30
  63.0 2.3 %collective-permute-start.7 = (f32[3,4,1,128]{3,2,1,0:T(1,128)S(1)}, f32[3,4,1,128]{3,2,1,0:T(1,128)S(1)}, u32[]{:S(2)}, u32[]{:S(2)}) collective-permute-start(f32[3,4,1,128]{3,2,1,0:T(1,128)S(1)} %get-tuple-element.35), channel_id=1, source_target_pairs={{1,0},{2,1},{3,2},{5,4},{6,5},{7,6},{9,8},{10,9},{11,10},{13,12},{... | collective-permute-start | bytes 18440 | tf_op jit(solution)/shard_map/ppermute | solution.py:31
  65.3 2.0 %collective-permute-start.6 = (f32[3,4,1,128]{3,2,1,0:T(1,128)S(1)}, f32[3,4,1,128]{3,2,1,0:T(1,128)S(1)}, u32[]{:S(2)}, u32[]{:S(2)}) collective-permute-start(f32[3,4,1,128]{3,2,1,0:T(1,128)S(1)} %get-tuple-element.34), channel_id=1, source_target_pairs={{0,1},{1,2},{2,3},{4,5},{5,6},{6,7},{8,9},{9,10},{10,11},{12,13},{... | collective-permute-start | bytes 18440 | tf_op jit(solution)/shard_map/ppermute | solution.py:30
  70.1 1.6 %collective-permute-done.6 = f32[3,4,1,128]{3,2,1,0:T(1,128)S(1)} collective-permute-done((f32[3,4,1,128]{3,2,1,0:T(1,128)S(1)}, f32[3,4,1,128]{3,2,1,0:T(1,128)S(1)}, u32[]{:S(2)}, u32[]{:S(2)}) %collective-permute-start.6) | collective-permute-done | bytes 6176 | tf_op jit(solution)/shard_map/ppermute | solution.py:30
  72.6 14.1 %shard_map.87 = (f32[16,128,4]{2,1,0:T(8,128)}, f32[144,128,128]{2,1,0:T(8,128)}) custom-call(f32[16,128,5]{2,1,0:T(8,128)} %bitcast.70, f32[6,40,128]{2,1,0:T(8,128)} %copy.67.source_ref), custom_call_target="tpu_custom_call" | custom-call | tf_op jit(solution)/shard_map/pallas_call | solution.py:158
  88.5 1.9 %collective-permute-start.9 = (f32[3,1,8,128]{3,2,1,0:T(8,128)S(1)}, f32[3,1,8,128]{3,2,1,0:T(8,128)S(1)}, u32[]{:S(2)}, u32[]{:S(2)}) collective-permute-start(f32[3,1,8,128]{3,2,1,0:T(8,128)S(1)} %get-tuple-element.39), channel_id=1, source_target_pairs={{4,0},{8,4},{12,8},{16,12},{20,16},{24,20},{28,24},{32,28},{36,32}... | collective-permute-start | bytes 36872 | tf_op jit(solution)/shard_map/ppermute | solution.py:31
  90.4 3.9 %collective-permute-start.8 = (f32[3,1,8,128]{3,2,1,0:T(8,128)S(1)}, f32[3,1,8,128]{3,2,1,0:T(8,128)S(1)}, u32[]{:S(2)}, u32[]{:S(2)}) collective-permute-start(f32[3,1,8,128]{3,2,1,0:T(8,128)S(1)} %get-tuple-element.38), channel_id=1, source_target_pairs={{0,4},{4,8},{8,12},{12,16},{16,20},{20,24},{24,28},{28,32},{32,36}... | collective-permute-start | bytes 36872 | tf_op jit(solution)/shard_map/ppermute | solution.py:30
  94.4 1.9 %slice_reduce_fusion = f32[16,128]{1,0:T(8,128)S(1)} fusion(f32[4,16,128]{0,2,1:T(8,128)} %bitcast.73), kind=kLoop, calls=%fused_computation | loop fusion | bytes 16384 | tf_op jit(solution)/shard_map/slice | solution.py:238
  96.2 4.0 %collective-permute-done.8 = f32[3,1,8,128]{3,2,1,0:T(8,128)S(1)} collective-permute-done((f32[3,1,8,128]{3,2,1,0:T(8,128)S(1)}, f32[3,1,8,128]{3,2,1,0:T(8,128)S(1)}, u32[]{:S(2)}, u32[]{:S(2)}) %collective-permute-start.8) | collective-permute-done | bytes 12320 | tf_op jit(solution)/shard_map/ppermute | solution.py:30
  100.3 2.2 %collective-permute-start.11 = (f32[3,4,1,128]{3,2,1,0:T(1,128)S(1)}, f32[3,4,1,128]{3,2,1,0:T(1,128)S(1)}, u32[]{:S(2)}, u32[]{:S(2)}) collective-permute-start(f32[3,4,1,128]{3,2,1,0:T(1,128)S(1)} %get-tuple-element.33), channel_id=1, source_target_pairs={{1,0},{2,1},{3,2},{5,4},{6,5},{7,6},{9,8},{10,9},{11,10},{13,12},{... | collective-permute-start | bytes 18440 | tf_op jit(solution)/shard_map/ppermute | solution.py:31
  102.5 2.1 %collective-permute-start.10 = (f32[3,4,1,128]{3,2,1,0:T(1,128)S(1)}, f32[3,4,1,128]{3,2,1,0:T(1,128)S(1)}, u32[]{:S(2)}, u32[]{:S(2)}) collective-permute-start(f32[3,4,1,128]{3,2,1,0:T(1,128)S(1)} %get-tuple-element.32), channel_id=1, source_target_pairs={{0,1},{1,2},{2,3},{4,5},{5,6},{6,7},{8,9},{9,10},{10,11},{12,13},{... | collective-permute-start | bytes 18440 | tf_op jit(solution)/shard_map/ppermute | solution.py:30
  104.7 4.3 %collective-permute-done.10 = f32[3,4,1,128]{3,2,1,0:T(1,128)S(1)} collective-permute-done((f32[3,4,1,128]{3,2,1,0:T(1,128)S(1)}, f32[3,4,1,128]{3,2,1,0:T(1,128)S(1)}, u32[]{:S(2)}, u32[]{:S(2)}) %collective-permute-start.10) | collective-permute-done | bytes 6176 | tf_op jit(solution)/shard_map/ppermute | solution.py:30
  109.6 8.2 %shard_map.88 = f32[16,128,3]{2,1,0:T(8,128)} custom-call(f32[16,128,1]{2,1,0:T(8,128)} %copy.71.target_ref, f32[3,40,128]{2,1,0:T(8,128)} %broadcast_multiply_fusion.1.source_ref, f32[144,128,128]{2,1,0:T(8,128)} %get-tuple-element.5.refs_0_), custom_call_target="tpu_custom_call" | custom-call | tf_op jit(solution)/shard_map/pallas_call | solution.py:166
  119.5 2.4 %collective-permute-start.13 = (f32[3,1,8,128]{3,2,1,0:T(8,128)S(1)}, f32[3,1,8,128]{3,2,1,0:T(8,128)S(1)}, u32[]{:S(2)}, u32[]{:S(2)}) collective-permute-start(f32[3,1,8,128]{3,2,1,0:T(8,128)S(1)} %get-tuple-element.37), channel_id=1, source_target_pairs={{4,0},{8,4},{12,8},{16,12},{20,16},{24,20},{28,24},{32,28},{36,32}... | collective-permute-start | bytes 36872 | tf_op jit(solution)/shard_map/ppermute | solution.py:31
  121.9 3.4 %collective-permute-start.12 = (f32[3,1,8,128]{3,2,1,0:T(8,128)S(1)}, f32[3,1,8,128]{3,2,1,0:T(8,128)S(1)}, u32[]{:S(2)}, u32[]{:S(2)}) collective-permute-start(f32[3,1,8,128]{3,2,1,0:T(8,128)S(1)} %get-tuple-element.36), channel_id=1, source_target_pairs={{0,4},{4,8},{8,12},{12,16},{16,20},{20,24},{24,28},{28,32},{32,36}... | collective-permute-start | bytes 36872 | tf_op jit(solution)/shard_map/ppermute | solution.py:30
  125.4 6.3 %collective-permute-done.12 = f32[3,1,8,128]{3,2,1,0:T(8,128)S(1)} collective-permute-done((f32[3,1,8,128]{3,2,1,0:T(8,128)S(1)}, f32[3,1,8,128]{3,2,1,0:T(8,128)S(1)}, u32[]{:S(2)}, u32[]{:S(2)}) %collective-permute-start.12) | collective-permute-done | bytes 12320 | tf_op jit(solution)/shard_map/ppermute | solution.py:30
  131.7 1.9 %collective-permute-start.15 = (f32[3,4,1,128]{3,2,1,0:T(1,128)S(1)}, f32[3,4,1,128]{3,2,1,0:T(1,128)S(1)}, u32[]{:S(2)}, u32[]{:S(2)}) collective-permute-start(f32[3,4,1,128]{3,2,1,0:T(1,128)S(1)} %get-tuple-element.31), channel_id=1, source_target_pairs={{1,0},{2,1},{3,2},{5,4},{6,5},{7,6},{9,8},{10,9},{11,10},{13,12},{... | collective-permute-start | bytes 18440 | tf_op jit(solution)/shard_map/ppermute | solution.py:31
  133.6 2.4 %collective-permute-start.14 = (f32[3,4,1,128]{3,2,1,0:T(1,128)S(1)}, f32[3,4,1,128]{3,2,1,0:T(1,128)S(1)}, u32[]{:S(2)}, u32[]{:S(2)}) collective-permute-start(f32[3,4,1,128]{3,2,1,0:T(1,128)S(1)} %get-tuple-element.30), channel_id=1, source_target_pairs={{0,1},{1,2},{2,3},{4,5},{5,6},{6,7},{8,9},{9,10},{10,11},{12,13},{... | collective-permute-start | bytes 18440 | tf_op jit(solution)/shard_map/ppermute | solution.py:30
  136.1 4.0 %collective-permute-done.14 = f32[3,4,1,128]{3,2,1,0:T(1,128)S(1)} collective-permute-done((f32[3,4,1,128]{3,2,1,0:T(1,128)S(1)}, f32[3,4,1,128]{3,2,1,0:T(1,128)S(1)}, u32[]{:S(2)}, u32[]{:S(2)}) %collective-permute-start.14) | collective-permute-done | bytes 6176 | tf_op jit(solution)/shard_map/ppermute | solution.py:30
  140.8 8.2 %shard_map.89 = f32[16,128,3]{2,1,0:T(8,128)} custom-call(f32[16,128,1]{2,1,0:T(8,128)} %copy.71.target_ref, f32[3,40,128]{2,1,0:T(8,128)} %broadcast_multiply_fusion.source_ref, f32[144,128,128]{2,1,0:T(8,128)} %get-tuple-element.5.refs_0_), custom_call_target="tpu_custom_call" | custom-call | tf_op jit(solution)/shard_map/pallas_call | solution.py:166
  149.0 1.6 copy.72
  150.8 1.9 %collective-permute-start.16 = (f32[8,8,128]{2,1,0:T(8,128)S(1)}, f32[8,8,128]{2,1,0:T(8,128)S(1)}, u32[]{:S(2)}, u32[]{:S(2)}) collective-permute-start(f32[8,8,128]{2,1,0:T(8,128)S(1)} %pad_maximum_fusion.10), channel_id=1, source_target_pairs={{0,4},{4,8},{8,12},{12,16},{16,20},{20,24},{24,28},{28,32},{32,36}... | collective-permute-start | bytes 98312 | tf_op jit(solution)/shard_map/ppermute | solution.py:39
  152.7 8.1 %collective-permute-done.16 = f32[8,8,128]{2,1,0:T(8,128)S(1)} collective-permute-done((f32[8,8,128]{2,1,0:T(8,128)S(1)}, f32[8,8,128]{2,1,0:T(8,128)S(1)}, u32[]{:S(2)}, u32[]{:S(2)}) %collective-permute-start.16) | collective-permute-done | bytes 32800 | tf_op jit(solution)/shard_map/ppermute | solution.py:39
  (100 shorter events, 19.9 us)
Async XLA Ops:
  0.6 87.8 %copy-start.6 = (f32[3]{0:T(128)S(1)}, f32[3]{0:T(128)}, u32[]{:S(2)}) copy-start(f32[3]{0:T(128)} %constant.56.clone) | copy-start | bytes 40
  0.6 50.5 %copy-start.2 = (s32[2,8]{1,0:T(2,128)S(1)}, s32[2,8]{1,0:T(2,128)}, u32[]{:S(2)}) copy-start(s32[2,8]{1,0:T(2,128)} %param.11) | copy-start | bytes 196
  0.7 66.7 %copy-start = (f32[3,2,8,128]{3,2,1,0:T(8,128)S(1)}, f32[3,2,8,128]{3,2,1,0:T(8,128)}, u32[]{:S(2)}) copy-start(f32[3,2,8,128]{3,2,1,0:T(8,128)} %param.7) | copy-start | bytes 73732
  0.7 87.7 %copy-start.1 = (f32[3,2,8,128]{3,2,1,0:T(8,128)S(1)}, f32[3,2,8,128]{3,2,1,0:T(8,128)}, u32[]{:S(2)}) copy-start(f32[3,2,8,128]{3,2,1,0:T(8,128)} %param.8) | copy-start | bytes 73732
  0.7 50.5 %copy-start.3 = (f32[2,8,128]{2,1,0:T(8,128)S(1)}, f32[2,8,128]{2,1,0:T(8,128)}, u32[]{:S(2)}) copy-start(f32[2,8,128]{2,1,0:T(8,128)} %param.9) | copy-start | bytes 24580
  0.7 50.5 %copy-start.4 = (f32[2,8,128]{2,1,0:T(8,128)S(1)}, f32[2,8,128]{2,1,0:T(8,128)}, u32[]{:S(2)}) copy-start(f32[2,8,128]{2,1,0:T(8,128)} %param.10) | copy-start | bytes 24580
  2.2 12.4 %collective-permute-start.1 = (f32[7,1,8,128]{3,2,1,0:T(8,128)S(1)}, f32[7,1,8,128]{3,2,1,0:T(8,128)S(1)}, u32[]{:S(2)}, u32[]{:S(2)}) collective-permute-start(f32[7,1,8,128]{3,2,1,0:T(8,128)S(1)} %get-tuple-element.23), channel_id=1, source_target_pairs={{4,0},{8,4},{12,8},{16,12},{20,16},{24,20},{28,24},{32,28},{36,32}... | collective-permute-start | bytes 86024 | tf_op jit(solution)/shard_map/ppermute | solution.py:31
  12.7 10.0 %collective-permute-start = (f32[7,1,8,128]{3,2,1,0:T(8,128)S(1)}, f32[7,1,8,128]{3,2,1,0:T(8,128)S(1)}, u32[]{:S(2)}, u32[]{:S(2)}) collective-permute-start(f32[7,1,8,128]{3,2,1,0:T(8,128)S(1)} %get-tuple-element.22), channel_id=1, source_target_pairs={{0,4},{4,8},{8,12},{12,16},{16,20},{20,24},{24,28},{28,32},{32,36}... | collective-permute-start | bytes 86024 | tf_op jit(solution)/shard_map/ppermute | solution.py:30
  23.6 7.2 %collective-permute-start.3 = (f32[7,4,1,128]{3,2,1,0:T(1,128)S(1)}, f32[7,4,1,128]{3,2,1,0:T(1,128)S(1)}, u32[]{:S(2)}, u32[]{:S(2)}) collective-permute-start(f32[7,4,1,128]{3,2,1,0:T(1,128)S(1)} %get-tuple-element.18), channel_id=1, source_target_pairs={{1,0},{2,1},{3,2},{5,4},{6,5},{7,6},{9,8},{10,9},{11,10},{13,12},{... | collective-permute-start | bytes 43016 | tf_op jit(solution)/shard_map/ppermute | solution.py:31
  25.5 6.5 %collective-permute-start.2 = (f32[7,4,1,128]{3,2,1,0:T(1,128)S(1)}, f32[7,4,1,128]{3,2,1,0:T(1,128)S(1)}, u32[]{:S(2)}, u32[]{:S(2)}) collective-permute-start(f32[7,4,1,128]{3,2,1,0:T(1,128)S(1)} %get-tuple-element.17), channel_id=1, source_target_pairs={{0,1},{1,2},{2,3},{4,5},{5,6},{6,7},{8,9},{9,10},{10,11},{12,13},{... | collective-permute-start | bytes 43016 | tf_op jit(solution)/shard_map/ppermute | solution.py:30
  51.3 5.9 %collective-permute-start.5 = (f32[3,1,8,128]{3,2,1,0:T(8,128)S(1)}, f32[3,1,8,128]{3,2,1,0:T(8,128)S(1)}, u32[]{:S(2)}, u32[]{:S(2)}) collective-permute-start(f32[3,1,8,128]{3,2,1,0:T(8,128)S(1)} %get-tuple-element.41), channel_id=1, source_target_pairs={{4,0},{8,4},{12,8},{16,12},{20,16},{24,20},{28,24},{32,28},{36,32}... | collective-permute-start | bytes 36872 | tf_op jit(solution)/shard_map/ppermute | solution.py:31
  53.2 9.8 %collective-permute-start.4 = (f32[3,1,8,128]{3,2,1,0:T(8,128)S(1)}, f32[3,1,8,128]{3,2,1,0:T(8,128)S(1)}, u32[]{:S(2)}, u32[]{:S(2)}) collective-permute-start(f32[3,1,8,128]{3,2,1,0:T(8,128)S(1)} %get-tuple-element.40), channel_id=1, source_target_pairs={{0,4},{4,8},{8,12},{12,16},{16,20},{20,24},{24,28},{28,32},{32,36}... | collective-permute-start | bytes 36872 | tf_op jit(solution)/shard_map/ppermute | solution.py:30
  63.0 7.1 %collective-permute-start.7 = (f32[3,4,1,128]{3,2,1,0:T(1,128)S(1)}, f32[3,4,1,128]{3,2,1,0:T(1,128)S(1)}, u32[]{:S(2)}, u32[]{:S(2)}) collective-permute-start(f32[3,4,1,128]{3,2,1,0:T(1,128)S(1)} %get-tuple-element.35), channel_id=1, source_target_pairs={{1,0},{2,1},{3,2},{5,4},{6,5},{7,6},{9,8},{10,9},{11,10},{13,12},{... | collective-permute-start | bytes 18440 | tf_op jit(solution)/shard_map/ppermute | solution.py:31
  65.3 6.5 %collective-permute-start.6 = (f32[3,4,1,128]{3,2,1,0:T(1,128)S(1)}, f32[3,4,1,128]{3,2,1,0:T(1,128)S(1)}, u32[]{:S(2)}, u32[]{:S(2)}) collective-permute-start(f32[3,4,1,128]{3,2,1,0:T(1,128)S(1)} %get-tuple-element.34), channel_id=1, source_target_pairs={{0,1},{1,2},{2,3},{4,5},{5,6},{6,7},{8,9},{9,10},{10,11},{12,13},{... | collective-permute-start | bytes 18440 | tf_op jit(solution)/shard_map/ppermute | solution.py:30
  72.6 52.7 %copy-start.5 = (s32[2,8]{1,0:T(2,128)S(1)}, s32[2,8]{1,0:T(2,128)}, u32[]{:S(2)}) copy-start(s32[2,8]{1,0:T(2,128)} %param.12) | copy-start | bytes 196
  88.5 7.7 %collective-permute-start.9 = (f32[3,1,8,128]{3,2,1,0:T(8,128)S(1)}, f32[3,1,8,128]{3,2,1,0:T(8,128)S(1)}, u32[]{:S(2)}, u32[]{:S(2)}) collective-permute-start(f32[3,1,8,128]{3,2,1,0:T(8,128)S(1)} %get-tuple-element.39), channel_id=1, source_target_pairs={{4,0},{8,4},{12,8},{16,12},{20,16},{24,20},{28,24},{32,28},{36,32}... | collective-permute-start | bytes 36872 | tf_op jit(solution)/shard_map/ppermute | solution.py:31
  90.4 9.8 %collective-permute-start.8 = (f32[3,1,8,128]{3,2,1,0:T(8,128)S(1)}, f32[3,1,8,128]{3,2,1,0:T(8,128)S(1)}, u32[]{:S(2)}, u32[]{:S(2)}) collective-permute-start(f32[3,1,8,128]{3,2,1,0:T(8,128)S(1)} %get-tuple-element.38), channel_id=1, source_target_pairs={{0,4},{4,8},{8,12},{12,16},{16,20},{20,24},{24,28},{28,32},{32,36}... | collective-permute-start | bytes 36872 | tf_op jit(solution)/shard_map/ppermute | solution.py:30
  100.3 4.4 %collective-permute-start.11 = (f32[3,4,1,128]{3,2,1,0:T(1,128)S(1)}, f32[3,4,1,128]{3,2,1,0:T(1,128)S(1)}, u32[]{:S(2)}, u32[]{:S(2)}) collective-permute-start(f32[3,4,1,128]{3,2,1,0:T(1,128)S(1)} %get-tuple-element.33), channel_id=1, source_target_pairs={{1,0},{2,1},{3,2},{5,4},{6,5},{7,6},{9,8},{10,9},{11,10},{13,12},{... | collective-permute-start | bytes 18440 | tf_op jit(solution)/shard_map/ppermute | solution.py:31
  102.5 6.5 %collective-permute-start.10 = (f32[3,4,1,128]{3,2,1,0:T(1,128)S(1)}, f32[3,4,1,128]{3,2,1,0:T(1,128)S(1)}, u32[]{:S(2)}, u32[]{:S(2)}) collective-permute-start(f32[3,4,1,128]{3,2,1,0:T(1,128)S(1)} %get-tuple-element.32), channel_id=1, source_target_pairs={{0,1},{1,2},{2,3},{4,5},{5,6},{6,7},{8,9},{9,10},{10,11},{12,13},{... | collective-permute-start | bytes 18440 | tf_op jit(solution)/shard_map/ppermute | solution.py:30
  119.5 5.9 %collective-permute-start.13 = (f32[3,1,8,128]{3,2,1,0:T(8,128)S(1)}, f32[3,1,8,128]{3,2,1,0:T(8,128)S(1)}, u32[]{:S(2)}, u32[]{:S(2)}) collective-permute-start(f32[3,1,8,128]{3,2,1,0:T(8,128)S(1)} %get-tuple-element.37), channel_id=1, source_target_pairs={{4,0},{8,4},{12,8},{16,12},{20,16},{24,20},{28,24},{32,28},{36,32}... | collective-permute-start | bytes 36872 | tf_op jit(solution)/shard_map/ppermute | solution.py:31
  121.9 9.8 %collective-permute-start.12 = (f32[3,1,8,128]{3,2,1,0:T(8,128)S(1)}, f32[3,1,8,128]{3,2,1,0:T(8,128)S(1)}, u32[]{:S(2)}, u32[]{:S(2)}) collective-permute-start(f32[3,1,8,128]{3,2,1,0:T(8,128)S(1)} %get-tuple-element.36), channel_id=1, source_target_pairs={{0,4},{4,8},{8,12},{12,16},{16,20},{20,24},{24,28},{28,32},{32,36}... | collective-permute-start | bytes 36872 | tf_op jit(solution)/shard_map/ppermute | solution.py:30
  131.7 4.4 %collective-permute-start.15 = (f32[3,4,1,128]{3,2,1,0:T(1,128)S(1)}, f32[3,4,1,128]{3,2,1,0:T(1,128)S(1)}, u32[]{:S(2)}, u32[]{:S(2)}) collective-permute-start(f32[3,4,1,128]{3,2,1,0:T(1,128)S(1)} %get-tuple-element.31), channel_id=1, source_target_pairs={{1,0},{2,1},{3,2},{5,4},{6,5},{7,6},{9,8},{10,9},{11,10},{13,12},{... | collective-permute-start | bytes 18440 | tf_op jit(solution)/shard_map/ppermute | solution.py:31
  133.6 6.5 %collective-permute-start.14 = (f32[3,4,1,128]{3,2,1,0:T(1,128)S(1)}, f32[3,4,1,128]{3,2,1,0:T(1,128)S(1)}, u32[]{:S(2)}, u32[]{:S(2)}) collective-permute-start(f32[3,4,1,128]{3,2,1,0:T(1,128)S(1)} %get-tuple-element.30), channel_id=1, source_target_pairs={{0,1},{1,2},{2,3},{4,5},{5,6},{6,7},{8,9},{9,10},{10,11},{12,13},{... | collective-permute-start | bytes 18440 | tf_op jit(solution)/shard_map/ppermute | solution.py:30
  150.8 10.0 %collective-permute-start.16 = (f32[8,8,128]{2,1,0:T(8,128)S(1)}, f32[8,8,128]{2,1,0:T(8,128)S(1)}, u32[]{:S(2)}, u32[]{:S(2)}) collective-permute-start(f32[8,8,128]{2,1,0:T(8,128)S(1)} %pad_maximum_fusion.10), channel_id=1, source_target_pairs={{0,4},{4,8},{8,12},{12,16},{16,20},{20,24},{24,28},{28,32},{32,36}... | collective-permute-start | bytes 98312 | tf_op jit(solution)/shard_map/ppermute | solution.py:39

commit v9 on v8

--- a/solution.py
+++ b/solution.py
@@ -135,15 +135,18 @@
                     pull = (mine[4] + other[5]) * cubed
                     weight_ref[step * 9 + neighbour] = pull
                     totals[3] = totals[3] + pull * other[4]
+            lanes = lax.broadcasted_iota(jnp.int32, (CHUNK, slot_count), 1)
+            table = jnp.zeros((CHUNK, slot_count), jnp.float32)
             for k in range(output_count):
-                out_ref[block, pl.ds(first, CHUNK), pl.ds(k, 1)] = jnp.sum(
-                    totals[k], axis=1, keepdims=True
-                )
+                table = jnp.where(lanes == k, jnp.sum(totals[k], axis=1, keepdims=True), table)
+            flipped = table.T
+            for k in range(output_count):
+                out_ref[k, pl.ds(block, 1), pl.ds(first, CHUNK)] = flipped[k : k + 1, :]
             return carry
 
         lax.fori_loop(0, block_count * chunk_count if kind == "jacobi" else chunk_count, body, 0)
 
-    out_shape = jax.ShapeDtypeStruct((block_count, slot_count, output_count), jnp.float32)
+    out_shape = jax.ShapeDtypeStruct((output_count, block_count, slot_count), jnp.float32)
     whole = [
         pl.BlockSpec(target_cols.shape, lambda block: (0, 0, 0)),
         pl.BlockSpec(source_rows.shape, lambda block: (0, 0, 0)),
@@ -168,7 +171,7 @@
         result = pl.pallas_call(
             kernel, out_shape=out_shape, grid=grid, in_specs=whole, out_specs=out_spec
         )(target_cols, source_rows)
-    result = jnp.moveaxis(result, 2, 0).reshape(output_count, row_count, col_count, slot_count)
+    result = result.reshape(output_count, row_count, col_count, slot_count)
     if kind == "force":
         return result, weights
     return result

time: 164 us -> 158 us (0.963)
  the two profiles are of different devices: /device:TPU:6 before, /device:TPU:3 now
where the time goes in v9:
time: 158 us; the launch traced here: 156 us
  starting transfers between devices  67.4 us (43%)
  Pallas kernels  44.7 us (28%)
  waiting for transfers between devices  22 us (14%)
  other arithmetic  13.6 us (9%)
  local copies, waits for them, and re-layouts  7.65 us (5%)
    ppermute x8, starting transfers between devices, with_halo(): after = lax.ppermute(initial, axis, down)  42.4 us
    ppermute x8, starting transfers between devices, with_halo(): before = lax.ppermute(last, axis, up)  23 us
    pallas_call x2, Pallas kernels, pair_pass(): pl.pallas_call(kernel, out_shape=out_shape)  16.9 us
    pallas_call x1, Pallas kernels, pair_pass(): pl.pallas_call(kernel, out_shape=out_shape, grid=grid, in_specs=whole, ou...  14.1 us
    ppermute x8, waiting for transfers between devices, with_halo(): after = lax.ppermute(initial, axis, down)  13.9 us
    pallas_call x1, Pallas kernels, pair_pass(): pl.pallas_call(kernel, out_shape=(out_shape, weight_shape), grid=grid, in...  13.6 us
    ppermute x1, waiting for transfers between devices, from_behind(): return lax.ppermute(block, axis, route)  8.11 us
  transfers between devices with their start and end apart: 17, of which 7 were waited for; matrix products, arithmetic and copies ran while one was open for 5% of the time, Pallas kernels for 0%

profile of v9, /device:TPU:3, one launch (start us, length us, event | category | flops | bytes accessed | tf_op | source)
XLA Modules:
  0.0 156.4 jit_solution(9382197108563023490)
XLA Ops:
  2.2 3.5 %collective-permute-start = (f32[7,1,8,128]{3,2,1,0:T(8,128)S(1)}, f32[7,1,8,128]{3,2,1,0:T(8,128)S(1)}, u32[]{:S(2)}, u32[]{:S(2)}) collective-permute-start(f32[7,1,8,128]{3,2,1,0:T(8,128)S(1)} %get-tuple-element.19), channel_id=1, source_target_pairs={{0,4},{4,8},{8,12},{12,16},{16,20},{20,24},{24,28},{28,32},{32,36}... | collective-permute-start | bytes 86024 | tf_op jit(solution)/shard_map/ppermute | solution.py:30
  5.8 8.3 %collective-permute-start.1 = (f32[7,1,8,128]{3,2,1,0:T(8,128)S(1)}, f32[7,1,8,128]{3,2,1,0:T(8,128)S(1)}, u32[]{:S(2)}, u32[]{:S(2)}) collective-permute-start(f32[7,1,8,128]{3,2,1,0:T(8,128)S(1)} %get-tuple-element.20), channel_id=1, source_target_pairs={{4,0},{8,4},{12,8},{16,12},{20,16},{24,20},{28,24},{32,28},{36,32}... | collective-permute-start | bytes 86024 | tf_op jit(solution)/shard_map/ppermute | solution.py:31
  14.1 1.0 collective-permute-done.1
  15.0 0.8 pad_maximum_fusion.16
  15.9 5.5 %collective-permute-start.2 = (f32[7,4,1,128]{3,2,1,0:T(1,128)S(1)}, f32[7,4,1,128]{3,2,1,0:T(1,128)S(1)}, u32[]{:S(2)}, u32[]{:S(2)}) collective-permute-start(f32[7,4,1,128]{3,2,1,0:T(1,128)S(1)} %get-tuple-element.14), channel_id=1, source_target_pairs={{0,1},{1,2},{2,3},{4,5},{5,6},{6,7},{8,9},{9,10},{10,11},{12,13},{... | collective-permute-start | bytes 43016 | tf_op jit(solution)/shard_map/ppermute | solution.py:30
  21.3 1.9 %collective-permute-start.3 = (f32[7,4,1,128]{3,2,1,0:T(1,128)S(1)}, f32[7,4,1,128]{3,2,1,0:T(1,128)S(1)}, u32[]{:S(2)}, u32[]{:S(2)}) collective-permute-start(f32[7,4,1,128]{3,2,1,0:T(1,128)S(1)} %get-tuple-element.15), channel_id=1, source_target_pairs={{1,0},{2,1},{3,2},{5,4},{6,5},{7,6},{9,8},{10,9},{11,10},{13,12},{... | collective-permute-start | bytes 43016 | tf_op jit(solution)/shard_map/ppermute | solution.py:31
  24.8 1.4 copy.44
  26.1 1.7 %collective-permute-done.3 = f32[7,4,1,128]{3,2,1,0:T(1,128)S(1)} collective-permute-done((f32[7,4,1,128]{3,2,1,0:T(1,128)S(1)}, f32[7,4,1,128]{3,2,1,0:T(1,128)S(1)}, u32[]{:S(2)}, u32[]{:S(2)}) %collective-permute-start.3) | collective-permute-done | bytes 14368 | tf_op jit(solution)/shard_map/ppermute | solution.py:31
  30.3 14.1 %shard_map.86 = f32[2,16,128]{2,1,0:T(8,128)} custom-call(f32[16,128,6]{2,1,0:T(8,128)} %bitcast.88, f32[6,40,128]{2,1,0:T(8,128)} %copy.46.source_ref), custom_call_target="tpu_custom_call" | custom-call | tf_op jit(solution)/shard_map/pallas_call | solution.py:171
  45.9 1.9 %collective-permute-start.4 = (f32[3,1,8,128]{3,2,1,0:T(8,128)S(1)}, f32[3,1,8,128]{3,2,1,0:T(8,128)S(1)}, u32[]{:S(2)}, u32[]{:S(2)}) collective-permute-start(f32[3,1,8,128]{3,2,1,0:T(8,128)S(1)} %get-tuple-element.37), channel_id=1, source_target_pairs={{0,4},{4,8},{8,12},{12,16},{16,20},{20,24},{24,28},{28,32},{32,36}... | collective-permute-start | bytes 36872 | tf_op jit(solution)/shard_map/ppermute | solution.py:30
  47.9 8.8 %collective-permute-start.5 = (f32[3,1,8,128]{3,2,1,0:T(8,128)S(1)}, f32[3,1,8,128]{3,2,1,0:T(8,128)S(1)}, u32[]{:S(2)}, u32[]{:S(2)}) collective-permute-start(f32[3,1,8,128]{3,2,1,0:T(8,128)S(1)} %get-tuple-element.38), channel_id=1, source_target_pairs={{4,0},{8,4},{12,8},{16,12},{20,16},{24,20},{28,24},{32,28},{36,32}... | collective-permute-start | bytes 36872 | tf_op jit(solution)/shard_map/ppermute | solution.py:31
  57.5 3.7 %collective-permute-start.6 = (f32[3,4,1,128]{3,2,1,0:T(1,128)S(1)}, f32[3,4,1,128]{3,2,1,0:T(1,128)S(1)}, u32[]{:S(2)}, u32[]{:S(2)}) collective-permute-start(f32[3,4,1,128]{3,2,1,0:T(1,128)S(1)} %get-tuple-element.31), channel_id=1, source_target_pairs={{0,1},{1,2},{2,3},{4,5},{5,6},{6,7},{8,9},{9,10},{10,11},{12,13},{... | collective-permute-start | bytes 18440 | tf_op jit(solution)/shard_map/ppermute | solution.py:30
  61.1 1.9 %collective-permute-start.7 = (f32[3,4,1,128]{3,2,1,0:T(1,128)S(1)}, f32[3,4,1,128]{3,2,1,0:T(1,128)S(1)}, u32[]{:S(2)}, u32[]{:S(2)}) collective-permute-start(f32[3,4,1,128]{3,2,1,0:T(1,128)S(1)} %get-tuple-element.32), channel_id=1, source_target_pairs={{1,0},{2,1},{3,2},{5,4},{6,5},{7,6},{9,8},{10,9},{11,10},{13,12},{... | collective-permute-start | bytes 18440 | tf_op jit(solution)/shard_map/ppermute | solution.py:31
  63.8 1.4 copy.47
  65.2 2.4 %collective-permute-done.7 = f32[3,4,1,128]{3,2,1,0:T(1,128)S(1)} collective-permute-done((f32[3,4,1,128]{3,2,1,0:T(1,128)S(1)}, f32[3,4,1,128]{3,2,1,0:T(1,128)S(1)}, u32[]{:S(2)}, u32[]{:S(2)}) %collective-permute-start.7) | collective-permute-done | bytes 6176 | tf_op jit(solution)/shard_map/ppermute | solution.py:31
  68.4 13.6 %shard_map.87 = (f32[4,16,128]{2,1,0:T(8,128)}, f32[144,128,128]{2,1,0:T(8,128)}) custom-call(f32[16,128,5]{2,1,0:T(8,128)} %bitcast.87, f32[6,40,128]{2,1,0:T(8,128)} %copy.49.source_ref), custom_call_target="tpu_custom_call" | custom-call | tf_op jit(solution)/shard_map/pallas_call | solution.py:161
  82.1 0.9 fusion.24
  83.0 1.9 %collective-permute-start.8 = (f32[3,1,8,128]{3,2,1,0:T(8,128)S(1)}, f32[3,1,8,128]{3,2,1,0:T(8,128)S(1)}, u32[]{:S(2)}, u32[]{:S(2)}) collective-permute-start(f32[3,1,8,128]{3,2,1,0:T(8,128)S(1)} %get-tuple-element.35), channel_id=1, source_target_pairs={{0,4},{4,8},{8,12},{12,16},{16,20},{20,24},{24,28},{28,32},{32,36}... | collective-permute-start | bytes 36872 | tf_op jit(solution)/shard_map/ppermute | solution.py:30
  84.9 8.7 %collective-permute-start.9 = (f32[3,1,8,128]{3,2,1,0:T(8,128)S(1)}, f32[3,1,8,128]{3,2,1,0:T(8,128)S(1)}, u32[]{:S(2)}, u32[]{:S(2)}) collective-permute-start(f32[3,1,8,128]{3,2,1,0:T(8,128)S(1)} %get-tuple-element.36), channel_id=1, source_target_pairs={{4,0},{8,4},{12,8},{16,12},{20,16},{24,20},{28,24},{32,28},{36,32}... | collective-permute-start | bytes 36872 | tf_op jit(solution)/shard_map/ppermute | solution.py:31
  93.6 1.4 copy.51.target_ref
  95.0 2.4 %collective-permute-start.10 = (f32[3,4,1,128]{3,2,1,0:T(1,128)S(1)}, f32[3,4,1,128]{3,2,1,0:T(1,128)S(1)}, u32[]{:S(2)}, u32[]{:S(2)}) collective-permute-start(f32[3,4,1,128]{3,2,1,0:T(1,128)S(1)} %get-tuple-element.29), channel_id=1, source_target_pairs={{0,1},{1,2},{2,3},{4,5},{5,6},{6,7},{8,9},{9,10},{10,11},{12,13},{... | collective-permute-start | bytes 18440 | tf_op jit(solution)/shard_map/ppermute | solution.py:30
  97.5 1.9 %collective-permute-start.11 = (f32[3,4,1,128]{3,2,1,0:T(1,128)S(1)}, f32[3,4,1,128]{3,2,1,0:T(1,128)S(1)}, u32[]{:S(2)}, u32[]{:S(2)}) collective-permute-start(f32[3,4,1,128]{3,2,1,0:T(1,128)S(1)} %get-tuple-element.30), channel_id=1, source_target_pairs={{1,0},{2,1},{3,2},{5,4},{6,5},{7,6},{9,8},{10,9},{11,10},{13,12},{... | collective-permute-start | bytes 18440 | tf_op jit(solution)/shard_map/ppermute | solution.py:31
  100.2 3.7 %collective-permute-done.11 = f32[3,4,1,128]{3,2,1,0:T(1,128)S(1)} collective-permute-done((f32[3,4,1,128]{3,2,1,0:T(1,128)S(1)}, f32[3,4,1,128]{3,2,1,0:T(1,128)S(1)}, u32[]{:S(2)}, u32[]{:S(2)}) %collective-permute-start.11) | collective-permute-done | bytes 6176 | tf_op jit(solution)/shard_map/ppermute | solution.py:31
  104.6 8.5 %shard_map.88 = f32[3,16,128]{2,1,0:T(8,128)} custom-call(f32[16,128,1]{2,1,0:T(8,128)} %copy.51.target_ref, f32[3,40,128]{2,1,0:T(8,128)} %broadcast_multiply_fusion.1.source_ref, f32[144,128,128]{2,1,0:T(8,128)} %get-tuple-element.5.refs_0_), custom_call_target="tpu_custom_call" | custom-call | tf_op jit(solution)/shard_map/pallas_call | solution.py:169
  113.9 1.9 %collective-permute-start.12 = (f32[3,1,8,128]{3,2,1,0:T(8,128)S(1)}, f32[3,1,8,128]{3,2,1,0:T(8,128)S(1)}, u32[]{:S(2)}, u32[]{:S(2)}) collective-permute-start(f32[3,1,8,128]{3,2,1,0:T(8,128)S(1)} %get-tuple-element.33), channel_id=1, source_target_pairs={{0,4},{4,8},{8,12},{12,16},{16,20},{20,24},{24,28},{28,32},{32,36}... | collective-permute-start | bytes 36872 | tf_op jit(solution)/shard_map/ppermute | solution.py:30
  115.8 8.7 %collective-permute-start.13 = (f32[3,1,8,128]{3,2,1,0:T(8,128)S(1)}, f32[3,1,8,128]{3,2,1,0:T(8,128)S(1)}, u32[]{:S(2)}, u32[]{:S(2)}) collective-permute-start(f32[3,1,8,128]{3,2,1,0:T(8,128)S(1)} %get-tuple-element.34), channel_id=1, source_target_pairs={{4,0},{8,4},{12,8},{16,12},{20,16},{24,20},{28,24},{32,28},{36,32}... | collective-permute-start | bytes 36872 | tf_op jit(solution)/shard_map/ppermute | solution.py:31
  125.4 2.2 %collective-permute-start.14 = (f32[3,4,1,128]{3,2,1,0:T(1,128)S(1)}, f32[3,4,1,128]{3,2,1,0:T(1,128)S(1)}, u32[]{:S(2)}, u32[]{:S(2)}) collective-permute-start(f32[3,4,1,128]{3,2,1,0:T(1,128)S(1)} %get-tuple-element.27), channel_id=1, source_target_pairs={{0,1},{1,2},{2,3},{4,5},{5,6},{6,7},{8,9},{9,10},{10,11},{12,13},{... | collective-permute-start | bytes 18440 | tf_op jit(solution)/shard_map/ppermute | solution.py:30
  127.6 2.1 %collective-permute-start.15 = (f32[3,4,1,128]{3,2,1,0:T(1,128)S(1)}, f32[3,4,1,128]{3,2,1,0:T(1,128)S(1)}, u32[]{:S(2)}, u32[]{:S(2)}) collective-permute-start(f32[3,4,1,128]{3,2,1,0:T(1,128)S(1)} %get-tuple-element.28), channel_id=1, source_target_pairs={{1,0},{2,1},{3,2},{5,4},{6,5},{7,6},{9,8},{10,9},{11,10},{13,12},{... | collective-permute-start | bytes 18440 | tf_op jit(solution)/shard_map/ppermute | solution.py:31
  129.8 4.3 %collective-permute-done.15 = f32[3,4,1,128]{3,2,1,0:T(1,128)S(1)} collective-permute-done((f32[3,4,1,128]{3,2,1,0:T(1,128)S(1)}, f32[3,4,1,128]{3,2,1,0:T(1,128)S(1)}, u32[]{:S(2)}, u32[]{:S(2)}) %collective-permute-start.15) | collective-permute-done | bytes 6176 | tf_op jit(solution)/shard_map/ppermute | solution.py:31
  134.7 8.5 %shard_map.89 = f32[3,16,128]{2,1,0:T(8,128)} custom-call(f32[16,128,1]{2,1,0:T(8,128)} %copy.51.target_ref, f32[3,40,128]{2,1,0:T(8,128)} %broadcast_multiply_fusion.source_ref, f32[144,128,128]{2,1,0:T(8,128)} %get-tuple-element.5.refs_0_), custom_call_target="tpu_custom_call" | custom-call | tf_op jit(solution)/shard_map/pallas_call | solution.py:169
  144.2 1.9 %collective-permute-start.16 = (f32[8,8,128]{2,1,0:T(8,128)S(1)}, f32[8,8,128]{2,1,0:T(8,128)S(1)}, u32[]{:S(2)}, u32[]{:S(2)}) collective-permute-start(f32[8,8,128]{2,1,0:T(8,128)S(1)} %pad_maximum_fusion.10), channel_id=1, source_target_pairs={{0,4},{4,8},{8,12},{12,16},{16,20},{20,24},{24,28},{28,32},{32,36}... | collective-permute-start | bytes 98312 | tf_op jit(solution)/shard_map/ppermute | solution.py:39
  146.1 8.1 %collective-permute-done.16 = f32[8,8,128]{2,1,0:T(8,128)S(1)} collective-permute-done((f32[8,8,128]{2,1,0:T(8,128)S(1)}, f32[8,8,128]{2,1,0:T(8,128)S(1)}, u32[]{:S(2)}, u32[]{:S(2)}) %collective-permute-start.16) | collective-permute-done | bytes 32800 | tf_op jit(solution)/shard_map/ppermute | solution.py:39
  (91 shorter events, 16.2 us)
Async XLA Ops:
  0.6 98.8 %copy-start.3 = (s32[2,8]{1,0:T(2,128)S(1)}, s32[2,8]{1,0:T(2,128)}, u32[]{:S(2)}) copy-start(s32[2,8]{1,0:T(2,128)} %param.11) | copy-start | bytes 196
  2.2 11.8 %collective-permute-start = (f32[7,1,8,128]{3,2,1,0:T(8,128)S(1)}, f32[7,1,8,128]{3,2,1,0:T(8,128)S(1)}, u32[]{:S(2)}, u32[]{:S(2)}) collective-permute-start(f32[7,1,8,128]{3,2,1,0:T(8,128)S(1)} %get-tuple-element.19), channel_id=1, source_target_pairs={{0,4},{4,8},{8,12},{12,16},{16,20},{20,24},{24,28},{28,32},{32,36}... | collective-permute-start | bytes 86024 | tf_op jit(solution)/shard_map/ppermute | solution.py:30
  5.8 9.3 %collective-permute-start.1 = (f32[7,1,8,128]{3,2,1,0:T(8,128)S(1)}, f32[7,1,8,128]{3,2,1,0:T(8,128)S(1)}, u32[]{:S(2)}, u32[]{:S(2)}) collective-permute-start(f32[7,1,8,128]{3,2,1,0:T(8,128)S(1)} %get-tuple-element.20), channel_id=1, source_target_pairs={{4,0},{8,4},{12,8},{16,12},{20,16},{24,20},{28,24},{32,28},{36,32}... | collective-permute-start | bytes 86024 | tf_op jit(solution)/shard_map/ppermute | solution.py:31
  15.9 10.3 %collective-permute-start.2 = (f32[7,4,1,128]{3,2,1,0:T(1,128)S(1)}, f32[7,4,1,128]{3,2,1,0:T(1,128)S(1)}, u32[]{:S(2)}, u32[]{:S(2)}) collective-permute-start(f32[7,4,1,128]{3,2,1,0:T(1,128)S(1)} %get-tuple-element.14), channel_id=1, source_target_pairs={{0,1},{1,2},{2,3},{4,5},{5,6},{6,7},{8,9},{9,10},{10,11},{12,13},{... | collective-permute-start | bytes 43016 | tf_op jit(solution)/shard_map/ppermute | solution.py:30
  21.3 6.5 %collective-permute-start.3 = (f32[7,4,1,128]{3,2,1,0:T(1,128)S(1)}, f32[7,4,1,128]{3,2,1,0:T(1,128)S(1)}, u32[]{:S(2)}, u32[]{:S(2)}) collective-permute-start(f32[7,4,1,128]{3,2,1,0:T(1,128)S(1)} %get-tuple-element.15), channel_id=1, source_target_pairs={{1,0},{2,1},{3,2},{5,4},{6,5},{7,6},{9,8},{10,9},{11,10},{13,12},{... | collective-permute-start | bytes 43016 | tf_op jit(solution)/shard_map/ppermute | solution.py:31
  27.9 85.1 %copy-start = (f32[3,2,8,128]{3,2,1,0:T(8,128)S(1)}, f32[3,2,8,128]{3,2,1,0:T(8,128)}, u32[]{:S(2)}) copy-start(f32[3,2,8,128]{3,2,1,0:T(8,128)} %param.8) | copy-start | bytes 73732
  27.9 85.1 %copy-start.4 = (f32[3]{0:T(128)S(1)}, f32[3]{0:T(128)}, u32[]{:S(2)}) copy-start(f32[3]{0:T(128)} %constant.56.clone) | copy-start | bytes 40
  28.7 95.9 %copy-start.5 = (s32[2,8]{1,0:T(2,128)S(1)}, s32[2,8]{1,0:T(2,128)}, u32[]{:S(2)}) copy-start(s32[2,8]{1,0:T(2,128)} %param.12) | copy-start | bytes 196
  45.9 11.5 %collective-permute-start.4 = (f32[3,1,8,128]{3,2,1,0:T(8,128)S(1)}, f32[3,1,8,128]{3,2,1,0:T(8,128)S(1)}, u32[]{:S(2)}, u32[]{:S(2)}) collective-permute-start(f32[3,1,8,128]{3,2,1,0:T(8,128)S(1)} %get-tuple-element.37), channel_id=1, source_target_pairs={{0,4},{4,8},{8,12},{12,16},{16,20},{20,24},{24,28},{28,32},{32,36}... | collective-permute-start | bytes 36872 | tf_op jit(solution)/shard_map/ppermute | solution.py:30
  47.9 9.6 %collective-permute-start.5 = (f32[3,1,8,128]{3,2,1,0:T(8,128)S(1)}, f32[3,1,8,128]{3,2,1,0:T(8,128)S(1)}, u32[]{:S(2)}, u32[]{:S(2)}) collective-permute-start(f32[3,1,8,128]{3,2,1,0:T(8,128)S(1)} %get-tuple-element.38), channel_id=1, source_target_pairs={{4,0},{8,4},{12,8},{16,12},{20,16},{24,20},{28,24},{32,28},{36,32}... | collective-permute-start | bytes 36872 | tf_op jit(solution)/shard_map/ppermute | solution.py:31
  57.5 7.7 %collective-permute-start.6 = (f32[3,4,1,128]{3,2,1,0:T(1,128)S(1)}, f32[3,4,1,128]{3,2,1,0:T(1,128)S(1)}, u32[]{:S(2)}, u32[]{:S(2)}) collective-permute-start(f32[3,4,1,128]{3,2,1,0:T(1,128)S(1)} %get-tuple-element.31), channel_id=1, source_target_pairs={{0,1},{1,2},{2,3},{4,5},{5,6},{6,7},{8,9},{9,10},{10,11},{12,13},{... | collective-permute-start | bytes 18440 | tf_op jit(solution)/shard_map/ppermute | solution.py:30
  61.1 6.5 %collective-permute-start.7 = (f32[3,4,1,128]{3,2,1,0:T(1,128)S(1)}, f32[3,4,1,128]{3,2,1,0:T(1,128)S(1)}, u32[]{:S(2)}, u32[]{:S(2)}) collective-permute-start(f32[3,4,1,128]{3,2,1,0:T(1,128)S(1)} %get-tuple-element.32), channel_id=1, source_target_pairs={{1,0},{2,1},{3,2},{5,4},{6,5},{7,6},{9,8},{10,9},{11,10},{13,12},{... | collective-permute-start | bytes 18440 | tf_op jit(solution)/shard_map/ppermute | solution.py:31
  82.1 31.0 %copy-start.2 = (f32[4,16,128]{2,1,0:T(8,128)S(1)}, f32[4,16,128]{2,1,0:T(8,128)}, u32[]{:S(2)}) copy-start(f32[4,16,128]{2,1,0:T(8,128)} %get-tuple-element.4) | copy-start | bytes 98308
  83.0 12.0 %collective-permute-start.8 = (f32[3,1,8,128]{3,2,1,0:T(8,128)S(1)}, f32[3,1,8,128]{3,2,1,0:T(8,128)S(1)}, u32[]{:S(2)}, u32[]{:S(2)}) collective-permute-start(f32[3,1,8,128]{3,2,1,0:T(8,128)S(1)} %get-tuple-element.35), channel_id=1, source_target_pairs={{0,4},{4,8},{8,12},{12,16},{16,20},{20,24},{24,28},{28,32},{32,36}... | collective-permute-start | bytes 36872 | tf_op jit(solution)/shard_map/ppermute | solution.py:30
  84.9 10.1 %collective-permute-start.9 = (f32[3,1,8,128]{3,2,1,0:T(8,128)S(1)}, f32[3,1,8,128]{3,2,1,0:T(8,128)S(1)}, u32[]{:S(2)}, u32[]{:S(2)}) collective-permute-start(f32[3,1,8,128]{3,2,1,0:T(8,128)S(1)} %get-tuple-element.36), channel_id=1, source_target_pairs={{4,0},{8,4},{12,8},{16,12},{20,16},{24,20},{28,24},{32,28},{36,32}... | collective-permute-start | bytes 36872 | tf_op jit(solution)/shard_map/ppermute | solution.py:31
  95.0 5.2 %collective-permute-start.10 = (f32[3,4,1,128]{3,2,1,0:T(1,128)S(1)}, f32[3,4,1,128]{3,2,1,0:T(1,128)S(1)}, u32[]{:S(2)}, u32[]{:S(2)}) collective-permute-start(f32[3,4,1,128]{3,2,1,0:T(1,128)S(1)} %get-tuple-element.29), channel_id=1, source_target_pairs={{0,1},{1,2},{2,3},{4,5},{5,6},{6,7},{8,9},{9,10},{10,11},{12,13},{... | collective-permute-start | bytes 18440 | tf_op jit(solution)/shard_map/ppermute | solution.py:30
  97.5 6.5 %collective-permute-start.11 = (f32[3,4,1,128]{3,2,1,0:T(1,128)S(1)}, f32[3,4,1,128]{3,2,1,0:T(1,128)S(1)}, u32[]{:S(2)}, u32[]{:S(2)}) collective-permute-start(f32[3,4,1,128]{3,2,1,0:T(1,128)S(1)} %get-tuple-element.30), channel_id=1, source_target_pairs={{1,0},{2,1},{3,2},{5,4},{6,5},{7,6},{9,8},{10,9},{11,10},{13,12},{... | collective-permute-start | bytes 18440 | tf_op jit(solution)/shard_map/ppermute | solution.py:31
  104.6 38.6 %copy-start.1 = (f32[3,2,8,128]{3,2,1,0:T(8,128)S(1)}, f32[3,2,8,128]{3,2,1,0:T(8,128)}, u32[]{:S(2)}) copy-start(f32[3,2,8,128]{3,2,1,0:T(8,128)} %param.7) | copy-start | bytes 73732
  113.9 10.7 %collective-permute-start.12 = (f32[3,1,8,128]{3,2,1,0:T(8,128)S(1)}, f32[3,1,8,128]{3,2,1,0:T(8,128)S(1)}, u32[]{:S(2)}, u32[]{:S(2)}) collective-permute-start(f32[3,1,8,128]{3,2,1,0:T(8,128)S(1)} %get-tuple-element.33), channel_id=1, source_target_pairs={{0,4},{4,8},{8,12},{12,16},{16,20},{20,24},{24,28},{28,32},{32,36}... | collective-permute-start | bytes 36872 | tf_op jit(solution)/shard_map/ppermute | solution.py:30
  115.8 9.6 %collective-permute-start.13 = (f32[3,1,8,128]{3,2,1,0:T(8,128)S(1)}, f32[3,1,8,128]{3,2,1,0:T(8,128)S(1)}, u32[]{:S(2)}, u32[]{:S(2)}) collective-permute-start(f32[3,1,8,128]{3,2,1,0:T(8,128)S(1)} %get-tuple-element.34), channel_id=1, source_target_pairs={{4,0},{8,4},{12,8},{16,12},{20,16},{24,20},{28,24},{32,28},{36,32}... | collective-permute-start | bytes 36872 | tf_op jit(solution)/shard_map/ppermute | solution.py:31
  125.4 4.4 %collective-permute-start.14 = (f32[3,4,1,128]{3,2,1,0:T(1,128)S(1)}, f32[3,4,1,128]{3,2,1,0:T(1,128)S(1)}, u32[]{:S(2)}, u32[]{:S(2)}) collective-permute-start(f32[3,4,1,128]{3,2,1,0:T(1,128)S(1)} %get-tuple-element.27), channel_id=1, source_target_pairs={{0,1},{1,2},{2,3},{4,5},{5,6},{6,7},{8,9},{9,10},{10,11},{12,13},{... | collective-permute-start | bytes 18440 | tf_op jit(solution)/shard_map/ppermute | solution.py:30
  127.6 6.5 %collective-permute-start.15 = (f32[3,4,1,128]{3,2,1,0:T(1,128)S(1)}, f32[3,4,1,128]{3,2,1,0:T(1,128)S(1)}, u32[]{:S(2)}, u32[]{:S(2)}) collective-permute-start(f32[3,4,1,128]{3,2,1,0:T(1,128)S(1)} %get-tuple-element.28), channel_id=1, source_target_pairs={{1,0},{2,1},{3,2},{5,4},{6,5},{7,6},{9,8},{10,9},{11,10},{13,12},{... | collective-permute-start | bytes 18440 | tf_op jit(solution)/shard_map/ppermute | solution.py:31
  144.2 10.0 %collective-permute-start.16 = (f32[8,8,128]{2,1,0:T(8,128)S(1)}, f32[8,8,128]{2,1,0:T(8,128)S(1)}, u32[]{:S(2)}, u32[]{:S(2)}) collective-permute-start(f32[8,8,128]{2,1,0:T(8,128)S(1)} %pad_maximum_fusion.10), channel_id=1, source_target_pairs={{0,4},{4,8},{8,12},{12,16},{16,20},{20,24},{24,28},{28,32},{32,36}... | collective-permute-start | bytes 98312 | tf_op jit(solution)/shard_map/ppermute | solution.py:39

commit v10 on v9

--- a/solution.py
+++ b/solution.py
@@ -76,7 +76,7 @@
     target_count = target.shape[0]
     source_count = source.shape[0]
     output_count = {"density": 2, "force": 4, "jacobi": 3}[kind]
-    target_cols = jnp.moveaxis(target.reshape(target_count, block_count, slot_count), 0, 2)
+    target_cols = target.reshape(target_count, block_count, slot_count)
     source_rows = source.reshape(source_count, (row_count + 2) * padded_cols, slot_count)
 
     def kernel(target_ref, source_ref, *refs):
@@ -98,7 +98,11 @@
                 first = pl.multiple_of(step * CHUNK, CHUNK)
             row = block // col_count
             col = block % col_count
-            own = target_ref[block, pl.ds(first, CHUNK), :]
+            stacked = jnp.zeros((slot_count, slot_count), jnp.float32)
+            planes = lax.broadcasted_iota(jnp.int32, (slot_count, slot_count), 0)
+            for k in range(target_count):
+                stacked = jnp.where(planes == k, target_ref[k, pl.ds(block, 1), :], stacked)
+            own = stacked.T
             mine = [
                 jnp.broadcast_to(own[:, k : k + 1], (CHUNK, slot_count)) for k in range(target_count)
             ]

time: 158 us -> 157 us (level)
  local copies, waits for them, and re-layouts: 7.65 us -> 3.57 us
  waiting for transfers between devices: 22 us -> 24.1 us
    concatenate x2 -> x0, local copies, waits for them, and re-layouts: 2.71 us -> none  [the longest x1 1.36 us: per_device(): jnp.concatenate([positions, pressure[None], viscosity[None]], axis=0)]
    ppermute x8, waiting for transfers between devices: 13.9 us -> 16 us  [with_halo(): after = lax.ppermute(initial, axis, down)]
  transfers between devices with their start and end apart: 17 -> 17, of which waited for: 7 -> 8; matrix products, arithmetic and copies ran while one was open for 5% -> 3% of each run, Pallas kernels for 0% -> 0%
where the time goes in v10:
time: 157 us; the launch traced here: 156 us
  starting transfers between devices  66.6 us (42%)
  Pallas kernels  45.5 us (29%)
  waiting for transfers between devices  24.1 us (15%)
  other arithmetic  14.8 us (9%)
  local copies, waits for them, and re-layouts  3.57 us (2%)
    ppermute x8, starting transfers between devices, with_halo(): after = lax.ppermute(initial, axis, down)  42.6 us
    ppermute x8, starting transfers between devices, with_halo(): before = lax.ppermute(last, axis, up)  22.1 us
    pallas_call x2, Pallas kernels, pair_pass(): pl.pallas_call(kernel, out_shape=out_shape)  16.3 us
    ppermute x8, waiting for transfers between devices, with_halo(): after = lax.ppermute(initial, axis, down)  16 us
    pallas_call x1, Pallas kernels, pair_pass(): pl.pallas_call(kernel, out_shape=out_shape, grid=grid, in_specs=whole, ou...  14.8 us
    pallas_call x1, Pallas kernels, pair_pass(): pl.pallas_call(kernel, out_shape=(out_shape, weight_shape), grid=grid, in...  14.4 us
    ppermute x1, waiting for transfers between devices, from_behind(): return lax.ppermute(block, axis, route)  8.11 us
  transfers between devices with their start and end apart: 17, of which 8 were waited for; matrix products, arithmetic and copies ran while one was open for 3% of the time, Pallas kernels for 0%

profile of v10, /device:TPU:3, one launch (start us, length us, event | category | flops | bytes accessed | tf_op | source)
XLA Modules:
  0.0 155.7 jit_solution(14542154054207288525)
XLA Ops:
  2.2 3.5 %collective-permute-start = (f32[7,1,8,128]{3,2,1,0:T(8,128)S(1)}, f32[7,1,8,128]{3,2,1,0:T(8,128)S(1)}, u32[]{:S(2)}, u32[]{:S(2)}) collective-permute-start(f32[7,1,8,128]{3,2,1,0:T(8,128)S(1)} %get-tuple-element.19), channel_id=1, source_target_pairs={{0,4},{4,8},{8,12},{12,16},{16,20},{20,24},{24,28},{28,32},{32,36}... | collective-permute-start | bytes 86024 | tf_op jit(solution)/shard_map/ppermute | solution.py:30
  5.8 8.3 %collective-permute-start.1 = (f32[7,1,8,128]{3,2,1,0:T(8,128)S(1)}, f32[7,1,8,128]{3,2,1,0:T(8,128)S(1)}, u32[]{:S(2)}, u32[]{:S(2)}) collective-permute-start(f32[7,1,8,128]{3,2,1,0:T(8,128)S(1)} %get-tuple-element.20), channel_id=1, source_target_pairs={{4,0},{8,4},{12,8},{16,12},{20,16},{24,20},{28,24},{32,28},{36,32}... | collective-permute-start | bytes 86024 | tf_op jit(solution)/shard_map/ppermute | solution.py:31
  14.1 1.0 collective-permute-done.1
  15.0 0.8 pad_maximum_fusion.15
  15.9 5.5 %collective-permute-start.2 = (f32[7,4,1,128]{3,2,1,0:T(1,128)S(1)}, f32[7,4,1,128]{3,2,1,0:T(1,128)S(1)}, u32[]{:S(2)}, u32[]{:S(2)}) collective-permute-start(f32[7,4,1,128]{3,2,1,0:T(1,128)S(1)} %get-tuple-element.14), channel_id=1, source_target_pairs={{0,1},{1,2},{2,3},{4,5},{5,6},{6,7},{8,9},{9,10},{10,11},{12,13},{... | collective-permute-start | bytes 43016 | tf_op jit(solution)/shard_map/ppermute | solution.py:30
  21.4 1.9 %collective-permute-start.3 = (f32[7,4,1,128]{3,2,1,0:T(1,128)S(1)}, f32[7,4,1,128]{3,2,1,0:T(1,128)S(1)}, u32[]{:S(2)}, u32[]{:S(2)}) collective-permute-start(f32[7,4,1,128]{3,2,1,0:T(1,128)S(1)} %get-tuple-element.15), channel_id=1, source_target_pairs={{1,0},{2,1},{3,2},{5,4},{6,5},{7,6},{9,8},{10,9},{11,10},{13,12},{... | collective-permute-start | bytes 43016 | tf_op jit(solution)/shard_map/ppermute | solution.py:31
  23.3 1.4 maximum_bitcast_fusion.target_ref
  25.4 2.5 %collective-permute-done.3 = f32[7,4,1,128]{3,2,1,0:T(1,128)S(1)} collective-permute-done((f32[7,4,1,128]{3,2,1,0:T(1,128)S(1)}, f32[7,4,1,128]{3,2,1,0:T(1,128)S(1)}, u32[]{:S(2)}, u32[]{:S(2)}) %collective-permute-start.3) | collective-permute-done | bytes 14368 | tf_op jit(solution)/shard_map/ppermute | solution.py:31
  30.2 14.8 %shard_map.86 = f32[2,16,128]{2,1,0:T(8,128)} custom-call(f32[6,16,128]{2,1,0:T(8,128)} %maximum_bitcast_fusion.target_ref, f32[6,40,128]{2,1,0:T(8,128)} %copy.11.source_ref), custom_call_target="tpu_custom_call" | custom-call | tf_op jit(solution)/shard_map/pallas_call | solution.py:175
  46.6 1.9 %collective-permute-start.4 = (f32[3,1,8,128]{3,2,1,0:T(8,128)S(1)}, f32[3,1,8,128]{3,2,1,0:T(8,128)S(1)}, u32[]{:S(2)}, u32[]{:S(2)}) collective-permute-start(f32[3,1,8,128]{3,2,1,0:T(8,128)S(1)} %get-tuple-element.39), channel_id=1, source_target_pairs={{0,4},{4,8},{8,12},{12,16},{16,20},{20,24},{24,28},{28,32},{32,36}... | collective-permute-start | bytes 36872 | tf_op jit(solution)/shard_map/ppermute | solution.py:30
  48.6 8.8 %collective-permute-start.5 = (f32[3,1,8,128]{3,2,1,0:T(8,128)S(1)}, f32[3,1,8,128]{3,2,1,0:T(8,128)S(1)}, u32[]{:S(2)}, u32[]{:S(2)}) collective-permute-start(f32[3,1,8,128]{3,2,1,0:T(8,128)S(1)} %get-tuple-element.40), channel_id=1, source_target_pairs={{4,0},{8,4},{12,8},{16,12},{20,16},{24,20},{28,24},{32,28},{36,32}... | collective-permute-start | bytes 36872 | tf_op jit(solution)/shard_map/ppermute | solution.py:31
  58.2 2.9 %collective-permute-start.6 = (f32[3,4,1,128]{3,2,1,0:T(1,128)S(1)}, f32[3,4,1,128]{3,2,1,0:T(1,128)S(1)}, u32[]{:S(2)}, u32[]{:S(2)}) collective-permute-start(f32[3,4,1,128]{3,2,1,0:T(1,128)S(1)} %get-tuple-element.31), channel_id=1, source_target_pairs={{0,1},{1,2},{2,3},{4,5},{5,6},{6,7},{8,9},{9,10},{10,11},{12,13},{... | collective-permute-start | bytes 18440 | tf_op jit(solution)/shard_map/ppermute | solution.py:30
  61.1 1.9 %collective-permute-start.7 = (f32[3,4,1,128]{3,2,1,0:T(1,128)S(1)}, f32[3,4,1,128]{3,2,1,0:T(1,128)S(1)}, u32[]{:S(2)}, u32[]{:S(2)}) collective-permute-start(f32[3,4,1,128]{3,2,1,0:T(1,128)S(1)} %get-tuple-element.32), channel_id=1, source_target_pairs={{1,0},{2,1},{3,2},{5,4},{6,5},{7,6},{9,8},{10,9},{11,10},{13,12},{... | collective-permute-start | bytes 18440 | tf_op jit(solution)/shard_map/ppermute | solution.py:31
  63.0 1.4 pad_maximum_fusion.8.target_ref
  64.4 3.2 %collective-permute-done.7 = f32[3,4,1,128]{3,2,1,0:T(1,128)S(1)} collective-permute-done((f32[3,4,1,128]{3,2,1,0:T(1,128)S(1)}, f32[3,4,1,128]{3,2,1,0:T(1,128)S(1)}, u32[]{:S(2)}, u32[]{:S(2)}) %collective-permute-start.7) | collective-permute-done | bytes 6176 | tf_op jit(solution)/shard_map/ppermute | solution.py:31
  68.4 14.4 %shard_map.87 = (f32[4,16,128]{2,1,0:T(8,128)}, f32[144,128,128]{2,1,0:T(8,128)}) custom-call(f32[5,16,128]{2,1,0:T(8,128)} %pad_maximum_fusion.8.target_ref, f32[6,40,128]{2,1,0:T(8,128)} %copy.13.source_ref), custom_call_target="tpu_custom_call" | custom-call | tf_op jit(solution)/shard_map/pallas_call | solution.py:165
  82.8 0.9 fusion.24
  83.7 1.9 %collective-permute-start.8 = (f32[3,1,8,128]{3,2,1,0:T(8,128)S(1)}, f32[3,1,8,128]{3,2,1,0:T(8,128)S(1)}, u32[]{:S(2)}, u32[]{:S(2)}) collective-permute-start(f32[3,1,8,128]{3,2,1,0:T(8,128)S(1)} %get-tuple-element.37), channel_id=1, source_target_pairs={{0,4},{4,8},{8,12},{12,16},{16,20},{20,24},{24,28},{28,32},{32,36}... | collective-permute-start | bytes 36872 | tf_op jit(solution)/shard_map/ppermute | solution.py:30
  85.6 8.7 %collective-permute-start.9 = (f32[3,1,8,128]{3,2,1,0:T(8,128)S(1)}, f32[3,1,8,128]{3,2,1,0:T(8,128)S(1)}, u32[]{:S(2)}, u32[]{:S(2)}) collective-permute-start(f32[3,1,8,128]{3,2,1,0:T(8,128)S(1)} %get-tuple-element.38), channel_id=1, source_target_pairs={{4,0},{8,4},{12,8},{16,12},{20,16},{24,20},{28,24},{32,28},{36,32}... | collective-permute-start | bytes 36872 | tf_op jit(solution)/shard_map/ppermute | solution.py:31
  95.2 2.2 %collective-permute-start.10 = (f32[3,4,1,128]{3,2,1,0:T(1,128)S(1)}, f32[3,4,1,128]{3,2,1,0:T(1,128)S(1)}, u32[]{:S(2)}, u32[]{:S(2)}) collective-permute-start(f32[3,4,1,128]{3,2,1,0:T(1,128)S(1)} %get-tuple-element.29), channel_id=1, source_target_pairs={{0,1},{1,2},{2,3},{4,5},{5,6},{6,7},{8,9},{9,10},{10,11},{12,13},{... | collective-permute-start | bytes 18440 | tf_op jit(solution)/shard_map/ppermute | solution.py:30
  97.4 2.1 %collective-permute-start.11 = (f32[3,4,1,128]{3,2,1,0:T(1,128)S(1)}, f32[3,4,1,128]{3,2,1,0:T(1,128)S(1)}, u32[]{:S(2)}, u32[]{:S(2)}) collective-permute-start(f32[3,4,1,128]{3,2,1,0:T(1,128)S(1)} %get-tuple-element.30), channel_id=1, source_target_pairs={{1,0},{2,1},{3,2},{5,4},{6,5},{7,6},{9,8},{10,9},{11,10},{13,12},{... | collective-permute-start | bytes 18440 | tf_op jit(solution)/shard_map/ppermute | solution.py:31
  100.4 3.5 %collective-permute-done.11 = f32[3,4,1,128]{3,2,1,0:T(1,128)S(1)} collective-permute-done((f32[3,4,1,128]{3,2,1,0:T(1,128)S(1)}, f32[3,4,1,128]{3,2,1,0:T(1,128)S(1)}, u32[]{:S(2)}, u32[]{:S(2)}) %collective-permute-start.11) | collective-permute-done | bytes 6176 | tf_op jit(solution)/shard_map/ppermute | solution.py:31
  104.6 8.1 %shard_map.88 = f32[3,16,128]{2,1,0:T(8,128)} custom-call(f32[1,16,128]{2,1,0:T(8,128)} %copy-done.3, f32[3,40,128]{2,1,0:T(8,128)} %broadcast_multiply_fusion.1.source_ref, f32[144,128,128]{2,1,0:T(8,128)} %get-tuple-element.5.refs_0_), custom_call_target="tpu_custom_call" | custom-call | tf_op jit(solution)/shard_map/pallas_call | solution.py:173
  112.7 0.8 fusion.22
  113.5 1.9 %collective-permute-start.12 = (f32[3,1,8,128]{3,2,1,0:T(8,128)S(1)}, f32[3,1,8,128]{3,2,1,0:T(8,128)S(1)}, u32[]{:S(2)}, u32[]{:S(2)}) collective-permute-start(f32[3,1,8,128]{3,2,1,0:T(8,128)S(1)} %get-tuple-element.35), channel_id=1, source_target_pairs={{0,4},{4,8},{8,12},{12,16},{16,20},{20,24},{24,28},{28,32},{32,36}... | collective-permute-start | bytes 36872 | tf_op jit(solution)/shard_map/ppermute | solution.py:30
  115.5 8.7 %collective-permute-start.13 = (f32[3,1,8,128]{3,2,1,0:T(8,128)S(1)}, f32[3,1,8,128]{3,2,1,0:T(8,128)S(1)}, u32[]{:S(2)}, u32[]{:S(2)}) collective-permute-start(f32[3,1,8,128]{3,2,1,0:T(8,128)S(1)} %get-tuple-element.36), channel_id=1, source_target_pairs={{4,0},{8,4},{12,8},{16,12},{20,16},{24,20},{28,24},{32,28},{36,32}... | collective-permute-start | bytes 36872 | tf_op jit(solution)/shard_map/ppermute | solution.py:31
  125.0 2.2 %collective-permute-start.14 = (f32[3,4,1,128]{3,2,1,0:T(1,128)S(1)}, f32[3,4,1,128]{3,2,1,0:T(1,128)S(1)}, u32[]{:S(2)}, u32[]{:S(2)}) collective-permute-start(f32[3,4,1,128]{3,2,1,0:T(1,128)S(1)} %get-tuple-element.27), channel_id=1, source_target_pairs={{0,1},{1,2},{2,3},{4,5},{5,6},{6,7},{8,9},{9,10},{10,11},{12,13},{... | collective-permute-start | bytes 18440 | tf_op jit(solution)/shard_map/ppermute | solution.py:30
  127.2 2.1 %collective-permute-start.15 = (f32[3,4,1,128]{3,2,1,0:T(1,128)S(1)}, f32[3,4,1,128]{3,2,1,0:T(1,128)S(1)}, u32[]{:S(2)}, u32[]{:S(2)}) collective-permute-start(f32[3,4,1,128]{3,2,1,0:T(1,128)S(1)} %get-tuple-element.28), channel_id=1, source_target_pairs={{1,0},{2,1},{3,2},{5,4},{6,5},{7,6},{9,8},{10,9},{11,10},{13,12},{... | collective-permute-start | bytes 18440 | tf_op jit(solution)/shard_map/ppermute | solution.py:31
  129.4 4.3 %collective-permute-done.15 = f32[3,4,1,128]{3,2,1,0:T(1,128)S(1)} collective-permute-done((f32[3,4,1,128]{3,2,1,0:T(1,128)S(1)}, f32[3,4,1,128]{3,2,1,0:T(1,128)S(1)}, u32[]{:S(2)}, u32[]{:S(2)}) %collective-permute-start.15) | collective-permute-done | bytes 6176 | tf_op jit(solution)/shard_map/ppermute | solution.py:31
  134.4 8.1 %shard_map.89 = f32[3,16,128]{2,1,0:T(8,128)} custom-call(f32[1,16,128]{2,1,0:T(8,128)} %copy-done.3, f32[3,40,128]{2,1,0:T(8,128)} %broadcast_multiply_fusion.source_ref, f32[144,128,128]{2,1,0:T(8,128)} %get-tuple-element.5.refs_0_), custom_call_target="tpu_custom_call" | custom-call | tf_op jit(solution)/shard_map/pallas_call | solution.py:173
  143.5 1.9 %collective-permute-start.16 = (f32[8,8,128]{2,1,0:T(8,128)S(1)}, f32[8,8,128]{2,1,0:T(8,128)S(1)}, u32[]{:S(2)}, u32[]{:S(2)}) collective-permute-start(f32[8,8,128]{2,1,0:T(8,128)S(1)} %pad_maximum_fusion.9), channel_id=1, source_target_pairs={{0,4},{4,8},{8,12},{12,16},{16,20},{20,24},{24,28},{28,32},{32,36}... | collective-permute-start | bytes 98312 | tf_op jit(solution)/shard_map/ppermute | solution.py:39
  145.4 8.1 %collective-permute-done.16 = f32[8,8,128]{2,1,0:T(8,128)S(1)} collective-permute-done((f32[8,8,128]{2,1,0:T(8,128)S(1)}, f32[8,8,128]{2,1,0:T(8,128)S(1)}, u32[]{:S(2)}, u32[]{:S(2)}) %collective-permute-start.16) | collective-permute-done | bytes 32800 | tf_op jit(solution)/shard_map/ppermute | solution.py:39
  (90 shorter events, 14.7 us)
Async XLA Ops:
  0.6 112.1 %copy-start.5 = (f32[3]{0:T(128)S(1)}, f32[3]{0:T(128)}, u32[]{:S(2)}) copy-start(f32[3]{0:T(128)} %constant.56.clone) | copy-start | bytes 40
  0.6 123.6 %copy-start.4 = (s32[2,8]{1,0:T(2,128)S(1)}, s32[2,8]{1,0:T(2,128)}, u32[]{:S(2)}) copy-start(s32[2,8]{1,0:T(2,128)} %param.11) | copy-start | bytes 196
  0.7 112.0 %copy-start = (f32[3,2,8,128]{3,2,1,0:T(8,128)S(1)}, f32[3,2,8,128]{3,2,1,0:T(8,128)}, u32[]{:S(2)}) copy-start(f32[3,2,8,128]{3,2,1,0:T(8,128)} %param.8) | copy-start | bytes 73732
  0.7 123.5 %copy-start.6 = (s32[2,8]{1,0:T(2,128)S(1)}, s32[2,8]{1,0:T(2,128)}, u32[]{:S(2)}) copy-start(s32[2,8]{1,0:T(2,128)} %param.12) | copy-start | bytes 196
  2.2 11.8 %collective-permute-start = (f32[7,1,8,128]{3,2,1,0:T(8,128)S(1)}, f32[7,1,8,128]{3,2,1,0:T(8,128)S(1)}, u32[]{:S(2)}, u32[]{:S(2)}) collective-permute-start(f32[7,1,8,128]{3,2,1,0:T(8,128)S(1)} %get-tuple-element.19), channel_id=1, source_target_pairs={{0,4},{4,8},{8,12},{12,16},{16,20},{20,24},{24,28},{28,32},{32,36}... | collective-permute-start | bytes 86024 | tf_op jit(solution)/shard_map/ppermute | solution.py:30
  5.8 9.3 %collective-permute-start.1 = (f32[7,1,8,128]{3,2,1,0:T(8,128)S(1)}, f32[7,1,8,128]{3,2,1,0:T(8,128)S(1)}, u32[]{:S(2)}, u32[]{:S(2)}) collective-permute-start(f32[7,1,8,128]{3,2,1,0:T(8,128)S(1)} %get-tuple-element.20), channel_id=1, source_target_pairs={{4,0},{8,4},{12,8},{16,12},{20,16},{24,20},{28,24},{32,28},{36,32}... | collective-permute-start | bytes 86024 | tf_op jit(solution)/shard_map/ppermute | solution.py:31
  15.9 9.5 %collective-permute-start.2 = (f32[7,4,1,128]{3,2,1,0:T(1,128)S(1)}, f32[7,4,1,128]{3,2,1,0:T(1,128)S(1)}, u32[]{:S(2)}, u32[]{:S(2)}) collective-permute-start(f32[7,4,1,128]{3,2,1,0:T(1,128)S(1)} %get-tuple-element.14), channel_id=1, source_target_pairs={{0,1},{1,2},{2,3},{4,5},{5,6},{6,7},{8,9},{9,10},{10,11},{12,13},{... | collective-permute-start | bytes 43016 | tf_op jit(solution)/shard_map/ppermute | solution.py:30
  21.4 6.5 %collective-permute-start.3 = (f32[7,4,1,128]{3,2,1,0:T(1,128)S(1)}, f32[7,4,1,128]{3,2,1,0:T(1,128)S(1)}, u32[]{:S(2)}, u32[]{:S(2)}) collective-permute-start(f32[7,4,1,128]{3,2,1,0:T(1,128)S(1)} %get-tuple-element.15), channel_id=1, source_target_pairs={{1,0},{2,1},{3,2},{5,4},{6,5},{7,6},{9,8},{10,9},{11,10},{13,12},{... | collective-permute-start | bytes 43016 | tf_op jit(solution)/shard_map/ppermute | solution.py:31
  46.6 57.9 %copy-start.3 = (f32[1,16,128]{2,1,0:T(8,128)}, f32[1,16,128]{2,1,0:T(8,128)S(1)}, u32[]{:S(2)}) copy-start(f32[1,16,128]{2,1,0:T(8,128)S(1)} %get-tuple-element.34.target_ref) | copy-start | bytes 24580
  46.6 11.5 %collective-permute-start.4 = (f32[3,1,8,128]{3,2,1,0:T(8,128)S(1)}, f32[3,1,8,128]{3,2,1,0:T(8,128)S(1)}, u32[]{:S(2)}, u32[]{:S(2)}) collective-permute-start(f32[3,1,8,128]{3,2,1,0:T(8,128)S(1)} %get-tuple-element.39), channel_id=1, source_target_pairs={{0,4},{4,8},{8,12},{12,16},{16,20},{20,24},{24,28},{28,32},{32,36}... | collective-permute-start | bytes 36872 | tf_op jit(solution)/shard_map/ppermute | solution.py:30
  48.6 9.6 %collective-permute-start.5 = (f32[3,1,8,128]{3,2,1,0:T(8,128)S(1)}, f32[3,1,8,128]{3,2,1,0:T(8,128)S(1)}, u32[]{:S(2)}, u32[]{:S(2)}) collective-permute-start(f32[3,1,8,128]{3,2,1,0:T(8,128)S(1)} %get-tuple-element.40), channel_id=1, source_target_pairs={{4,0},{8,4},{12,8},{16,12},{20,16},{24,20},{28,24},{32,28},{36,32}... | collective-permute-start | bytes 36872 | tf_op jit(solution)/shard_map/ppermute | solution.py:31
  58.2 6.2 %collective-permute-start.6 = (f32[3,4,1,128]{3,2,1,0:T(1,128)S(1)}, f32[3,4,1,128]{3,2,1,0:T(1,128)S(1)}, u32[]{:S(2)}, u32[]{:S(2)}) collective-permute-start(f32[3,4,1,128]{3,2,1,0:T(1,128)S(1)} %get-tuple-element.31), channel_id=1, source_target_pairs={{0,1},{1,2},{2,3},{4,5},{5,6},{6,7},{8,9},{9,10},{10,11},{12,13},{... | collective-permute-start | bytes 18440 | tf_op jit(solution)/shard_map/ppermute | solution.py:30
  61.1 6.5 %collective-permute-start.7 = (f32[3,4,1,128]{3,2,1,0:T(1,128)S(1)}, f32[3,4,1,128]{3,2,1,0:T(1,128)S(1)}, u32[]{:S(2)}, u32[]{:S(2)}) collective-permute-start(f32[3,4,1,128]{3,2,1,0:T(1,128)S(1)} %get-tuple-element.32), channel_id=1, source_target_pairs={{1,0},{2,1},{3,2},{5,4},{6,5},{7,6},{9,8},{10,9},{11,10},{13,12},{... | collective-permute-start | bytes 18440 | tf_op jit(solution)/shard_map/ppermute | solution.py:31
  82.8 29.9 %copy-start.2 = (f32[4,16,128]{2,1,0:T(8,128)S(1)}, f32[4,16,128]{2,1,0:T(8,128)}, u32[]{:S(2)}) copy-start(f32[4,16,128]{2,1,0:T(8,128)} %get-tuple-element.4) | copy-start | bytes 98308
  83.7 10.7 %collective-permute-start.8 = (f32[3,1,8,128]{3,2,1,0:T(8,128)S(1)}, f32[3,1,8,128]{3,2,1,0:T(8,128)S(1)}, u32[]{:S(2)}, u32[]{:S(2)}) collective-permute-start(f32[3,1,8,128]{3,2,1,0:T(8,128)S(1)} %get-tuple-element.37), channel_id=1, source_target_pairs={{0,4},{4,8},{8,12},{12,16},{16,20},{20,24},{24,28},{28,32},{32,36}... | collective-permute-start | bytes 36872 | tf_op jit(solution)/shard_map/ppermute | solution.py:30
  85.6 9.6 %collective-permute-start.9 = (f32[3,1,8,128]{3,2,1,0:T(8,128)S(1)}, f32[3,1,8,128]{3,2,1,0:T(8,128)S(1)}, u32[]{:S(2)}, u32[]{:S(2)}) collective-permute-start(f32[3,1,8,128]{3,2,1,0:T(8,128)S(1)} %get-tuple-element.38), channel_id=1, source_target_pairs={{4,0},{8,4},{12,8},{16,12},{20,16},{24,20},{28,24},{32,28},{36,32}... | collective-permute-start | bytes 36872 | tf_op jit(solution)/shard_map/ppermute | solution.py:31
  95.2 5.2 %collective-permute-start.10 = (f32[3,4,1,128]{3,2,1,0:T(1,128)S(1)}, f32[3,4,1,128]{3,2,1,0:T(1,128)S(1)}, u32[]{:S(2)}, u32[]{:S(2)}) collective-permute-start(f32[3,4,1,128]{3,2,1,0:T(1,128)S(1)} %get-tuple-element.29), channel_id=1, source_target_pairs={{0,1},{1,2},{2,3},{4,5},{5,6},{6,7},{8,9},{9,10},{10,11},{12,13},{... | collective-permute-start | bytes 18440 | tf_op jit(solution)/shard_map/ppermute | solution.py:30
  97.4 6.5 %collective-permute-start.11 = (f32[3,4,1,128]{3,2,1,0:T(1,128)S(1)}, f32[3,4,1,128]{3,2,1,0:T(1,128)S(1)}, u32[]{:S(2)}, u32[]{:S(2)}) collective-permute-start(f32[3,4,1,128]{3,2,1,0:T(1,128)S(1)} %get-tuple-element.30), channel_id=1, source_target_pairs={{1,0},{2,1},{3,2},{5,4},{6,5},{7,6},{9,8},{10,9},{11,10},{13,12},{... | collective-permute-start | bytes 18440 | tf_op jit(solution)/shard_map/ppermute | solution.py:31
  104.6 37.9 %copy-start.1 = (f32[3,2,8,128]{3,2,1,0:T(8,128)S(1)}, f32[3,2,8,128]{3,2,1,0:T(8,128)}, u32[]{:S(2)}) copy-start(f32[3,2,8,128]{3,2,1,0:T(8,128)} %param.7) | copy-start | bytes 73732
  113.5 10.7 %collective-permute-start.12 = (f32[3,1,8,128]{3,2,1,0:T(8,128)S(1)}, f32[3,1,8,128]{3,2,1,0:T(8,128)S(1)}, u32[]{:S(2)}, u32[]{:S(2)}) collective-permute-start(f32[3,1,8,128]{3,2,1,0:T(8,128)S(1)} %get-tuple-element.35), channel_id=1, source_target_pairs={{0,4},{4,8},{8,12},{12,16},{16,20},{20,24},{24,28},{28,32},{32,36}... | collective-permute-start | bytes 36872 | tf_op jit(solution)/shard_map/ppermute | solution.py:30
  115.5 9.6 %collective-permute-start.13 = (f32[3,1,8,128]{3,2,1,0:T(8,128)S(1)}, f32[3,1,8,128]{3,2,1,0:T(8,128)S(1)}, u32[]{:S(2)}, u32[]{:S(2)}) collective-permute-start(f32[3,1,8,128]{3,2,1,0:T(8,128)S(1)} %get-tuple-element.36), channel_id=1, source_target_pairs={{4,0},{8,4},{12,8},{16,12},{20,16},{24,20},{28,24},{32,28},{36,32}... | collective-permute-start | bytes 36872 | tf_op jit(solution)/shard_map/ppermute | solution.py:31
  125.0 4.4 %collective-permute-start.14 = (f32[3,4,1,128]{3,2,1,0:T(1,128)S(1)}, f32[3,4,1,128]{3,2,1,0:T(1,128)S(1)}, u32[]{:S(2)}, u32[]{:S(2)}) collective-permute-start(f32[3,4,1,128]{3,2,1,0:T(1,128)S(1)} %get-tuple-element.27), channel_id=1, source_target_pairs={{0,1},{1,2},{2,3},{4,5},{5,6},{6,7},{8,9},{9,10},{10,11},{12,13},{... | collective-permute-start | bytes 18440 | tf_op jit(solution)/shard_map/ppermute | solution.py:30
  127.2 6.5 %collective-permute-start.15 = (f32[3,4,1,128]{3,2,1,0:T(1,128)S(1)}, f32[3,4,1,128]{3,2,1,0:T(1,128)S(1)}, u32[]{:S(2)}, u32[]{:S(2)}) collective-permute-start(f32[3,4,1,128]{3,2,1,0:T(1,128)S(1)} %get-tuple-element.28), channel_id=1, source_target_pairs={{1,0},{2,1},{3,2},{5,4},{6,5},{7,6},{9,8},{10,9},{11,10},{13,12},{... | collective-permute-start | bytes 18440 | tf_op jit(solution)/shard_map/ppermute | solution.py:31
  143.5 10.0 %collective-permute-start.16 = (f32[8,8,128]{2,1,0:T(8,128)S(1)}, f32[8,8,128]{2,1,0:T(8,128)S(1)}, u32[]{:S(2)}, u32[]{:S(2)}) collective-permute-start(f32[8,8,128]{2,1,0:T(8,128)S(1)} %pad_maximum_fusion.9), channel_id=1, source_target_pairs={{0,4},{4,8},{8,12},{12,16},{16,20},{20,24},{24,28},{28,32},{32,36}... | collective-permute-start | bytes 98312 | tf_op jit(solution)/shard_map/ppermute | solution.py:39

commit v11 on v10

--- a/solution.py
+++ b/solution.py
@@ -87,15 +87,10 @@
         else:
             (out_ref,) = refs
 
-        grid_block = None if kind == "jacobi" else pl.program_id(0)
+        block = pl.program_id(0)
 
         def body(step, carry):
-            if kind == "jacobi":
-                block = step // chunk_count
-                first = pl.multiple_of((step % chunk_count) * CHUNK, CHUNK)
-            else:
-                block = grid_block
-                first = pl.multiple_of(step * CHUNK, CHUNK)
+            first = pl.multiple_of(step * CHUNK, CHUNK)
             row = block // col_count
             col = block % col_count
             stacked = jnp.zeros((slot_count, slot_count), jnp.float32)
@@ -148,7 +143,7 @@
                 out_ref[k, pl.ds(block, 1), pl.ds(first, CHUNK)] = flipped[k : k + 1, :]
             return carry
 
-        lax.fori_loop(0, block_count * chunk_count if kind == "jacobi" else chunk_count, body, 0)
+        lax.fori_loop(0, chunk_count, body, 0)
 
     out_shape = jax.ShapeDtypeStruct((output_count, block_count, slot_count), jnp.float32)
     whole = [
@@ -170,7 +165,13 @@
             out_specs=(out_spec, weight_spec),
         )(target_cols, source_rows)
     elif kind == "jacobi":
-        result = pl.pallas_call(kernel, out_shape=out_shape)(target_cols, source_rows, weights)
+        result = pl.pallas_call(
+            kernel,
+            out_shape=out_shape,
+            grid=grid,
+            in_specs=whole + [weight_spec],
+            out_specs=out_spec,
+        )(target_cols, source_rows, weights)
     else:
         result = pl.pallas_call(
             kernel, out_shape=out_shape, grid=grid, in_specs=whole, out_specs=out_spec

time: 157 us -> 164 us (1.045)
  Pallas kernels: 45.5 us -> 52.3 us
    pallas_call x2, Pallas kernels: 16.3 us -> 23.1 us  [pair_pass(): pl.pallas_call(kernel, out_shape=out_shape, grid=grid, in_specs=whole + [...]
where the time goes in v11:
time: 164 us; the launch traced here: 163 us
  starting transfers between devices  66.6 us (41%)
  Pallas kernels  52.3 us (32%)
  waiting for transfers between devices  24.1 us (15%)
  other arithmetic  14.8 us (9%)
  local copies, waits for them, and re-layouts  3.57 us (2%)
    ppermute x8, starting transfers between devices, with_halo(): after = lax.ppermute(initial, axis, down)  42.6 us
    pallas_call x2, Pallas kernels, pair_pass(): pl.pallas_call(kernel, out_shape=out_shape, grid=grid, in_specs=whole + [...  23.1 us
    ppermute x8, starting transfers between devices, with_halo(): before = lax.ppermute(last, axis, up)  22.1 us
    ppermute x8, waiting for transfers between devices, with_halo(): after = lax.ppermute(initial, axis, down)  16 us
    pallas_call x1, Pallas kernels, pair_pass(): pl.pallas_call(kernel, out_shape=out_shape, grid=grid, in_specs=whole, ou...  14.8 us
    pallas_call x1, Pallas kernels, pair_pass(): pl.pallas_call(kernel, out_shape=(out_shape, weight_shape), grid=grid, in...  14.4 us
    ppermute x1, waiting for transfers between devices, from_behind(): return lax.ppermute(block, axis, route)  8.11 us
  transfers between devices with their start and end apart: 17, of which 8 were waited for; matrix products, arithmetic and copies ran while one was open for 3% of the time, Pallas kernels for 0%

profile of v11, /device:TPU:3, one launch (start us, length us, event | category | flops | bytes accessed | tf_op | source)
XLA Modules:
  0.0 162.5 jit_solution(2315447416016959001)
XLA Ops:
  2.2 3.5 %collective-permute-start = (f32[7,1,8,128]{3,2,1,0:T(8,128)S(1)}, f32[7,1,8,128]{3,2,1,0:T(8,128)S(1)}, u32[]{:S(2)}, u32[]{:S(2)}) collective-permute-start(f32[7,1,8,128]{3,2,1,0:T(8,128)S(1)} %get-tuple-element.19), channel_id=1, source_target_pairs={{0,4},{4,8},{8,12},{12,16},{16,20},{20,24},{24,28},{28,32},{32,36}... | collective-permute-start | bytes 86024 | tf_op jit(solution)/shard_map/ppermute | solution.py:30
  5.8 8.3 %collective-permute-start.1 = (f32[7,1,8,128]{3,2,1,0:T(8,128)S(1)}, f32[7,1,8,128]{3,2,1,0:T(8,128)S(1)}, u32[]{:S(2)}, u32[]{:S(2)}) collective-permute-start(f32[7,1,8,128]{3,2,1,0:T(8,128)S(1)} %get-tuple-element.20), channel_id=1, source_target_pairs={{4,0},{8,4},{12,8},{16,12},{20,16},{24,20},{28,24},{32,28},{36,32}... | collective-permute-start | bytes 86024 | tf_op jit(solution)/shard_map/ppermute | solution.py:31
  14.1 1.0 collective-permute-done.1
  15.0 0.8 pad_maximum_fusion.15
  15.9 5.5 %collective-permute-start.2 = (f32[7,4,1,128]{3,2,1,0:T(1,128)S(1)}, f32[7,4,1,128]{3,2,1,0:T(1,128)S(1)}, u32[]{:S(2)}, u32[]{:S(2)}) collective-permute-start(f32[7,4,1,128]{3,2,1,0:T(1,128)S(1)} %get-tuple-element.14), channel_id=1, source_target_pairs={{0,1},{1,2},{2,3},{4,5},{5,6},{6,7},{8,9},{9,10},{10,11},{12,13},{... | collective-permute-start | bytes 43016 | tf_op jit(solution)/shard_map/ppermute | solution.py:30
  21.4 1.9 %collective-permute-start.3 = (f32[7,4,1,128]{3,2,1,0:T(1,128)S(1)}, f32[7,4,1,128]{3,2,1,0:T(1,128)S(1)}, u32[]{:S(2)}, u32[]{:S(2)}) collective-permute-start(f32[7,4,1,128]{3,2,1,0:T(1,128)S(1)} %get-tuple-element.15), channel_id=1, source_target_pairs={{1,0},{2,1},{3,2},{5,4},{6,5},{7,6},{9,8},{10,9},{11,10},{13,12},{... | collective-permute-start | bytes 43016 | tf_op jit(solution)/shard_map/ppermute | solution.py:31
  23.3 1.4 maximum_bitcast_fusion.target_ref
  25.4 2.5 %collective-permute-done.3 = f32[7,4,1,128]{3,2,1,0:T(1,128)S(1)} collective-permute-done((f32[7,4,1,128]{3,2,1,0:T(1,128)S(1)}, f32[7,4,1,128]{3,2,1,0:T(1,128)S(1)}, u32[]{:S(2)}, u32[]{:S(2)}) %collective-permute-start.3) | collective-permute-done | bytes 14368 | tf_op jit(solution)/shard_map/ppermute | solution.py:31
  30.2 14.8 %shard_map.86 = f32[2,16,128]{2,1,0:T(8,128)} custom-call(f32[6,16,128]{2,1,0:T(8,128)} %maximum_bitcast_fusion.target_ref, f32[6,40,128]{2,1,0:T(8,128)} %copy.11.source_ref), custom_call_target="tpu_custom_call" | custom-call | tf_op jit(solution)/shard_map/pallas_call | solution.py:176
  46.6 1.9 %collective-permute-start.4 = (f32[3,1,8,128]{3,2,1,0:T(8,128)S(1)}, f32[3,1,8,128]{3,2,1,0:T(8,128)S(1)}, u32[]{:S(2)}, u32[]{:S(2)}) collective-permute-start(f32[3,1,8,128]{3,2,1,0:T(8,128)S(1)} %get-tuple-element.39), channel_id=1, source_target_pairs={{0,4},{4,8},{8,12},{12,16},{16,20},{20,24},{24,28},{28,32},{32,36}... | collective-permute-start | bytes 36872 | tf_op jit(solution)/shard_map/ppermute | solution.py:30
  48.6 8.8 %collective-permute-start.5 = (f32[3,1,8,128]{3,2,1,0:T(8,128)S(1)}, f32[3,1,8,128]{3,2,1,0:T(8,128)S(1)}, u32[]{:S(2)}, u32[]{:S(2)}) collective-permute-start(f32[3,1,8,128]{3,2,1,0:T(8,128)S(1)} %get-tuple-element.40), channel_id=1, source_target_pairs={{4,0},{8,4},{12,8},{16,12},{20,16},{24,20},{28,24},{32,28},{36,32}... | collective-permute-start | bytes 36872 | tf_op jit(solution)/shard_map/ppermute | solution.py:31
  58.2 2.9 %collective-permute-start.6 = (f32[3,4,1,128]{3,2,1,0:T(1,128)S(1)}, f32[3,4,1,128]{3,2,1,0:T(1,128)S(1)}, u32[]{:S(2)}, u32[]{:S(2)}) collective-permute-start(f32[3,4,1,128]{3,2,1,0:T(1,128)S(1)} %get-tuple-element.31), channel_id=1, source_target_pairs={{0,1},{1,2},{2,3},{4,5},{5,6},{6,7},{8,9},{9,10},{10,11},{12,13},{... | collective-permute-start | bytes 18440 | tf_op jit(solution)/shard_map/ppermute | solution.py:30
  61.1 1.9 %collective-permute-start.7 = (f32[3,4,1,128]{3,2,1,0:T(1,128)S(1)}, f32[3,4,1,128]{3,2,1,0:T(1,128)S(1)}, u32[]{:S(2)}, u32[]{:S(2)}) collective-permute-start(f32[3,4,1,128]{3,2,1,0:T(1,128)S(1)} %get-tuple-element.32), channel_id=1, source_target_pairs={{1,0},{2,1},{3,2},{5,4},{6,5},{7,6},{9,8},{10,9},{11,10},{13,12},{... | collective-permute-start | bytes 18440 | tf_op jit(solution)/shard_map/ppermute | solution.py:31
  63.0 1.4 pad_maximum_fusion.8.target_ref
  64.4 3.2 %collective-permute-done.7 = f32[3,4,1,128]{3,2,1,0:T(1,128)S(1)} collective-permute-done((f32[3,4,1,128]{3,2,1,0:T(1,128)S(1)}, f32[3,4,1,128]{3,2,1,0:T(1,128)S(1)}, u32[]{:S(2)}, u32[]{:S(2)}) %collective-permute-start.7) | collective-permute-done | bytes 6176 | tf_op jit(solution)/shard_map/ppermute | solution.py:31
  68.4 14.4 %shard_map.87 = (f32[4,16,128]{2,1,0:T(8,128)}, f32[144,128,128]{2,1,0:T(8,128)}) custom-call(f32[5,16,128]{2,1,0:T(8,128)} %pad_maximum_fusion.8.target_ref, f32[6,40,128]{2,1,0:T(8,128)} %copy.13.source_ref), custom_call_target="tpu_custom_call" | custom-call | tf_op jit(solution)/shard_map/pallas_call | solution.py:160
  82.8 0.9 fusion.24
  83.7 1.9 %collective-permute-start.8 = (f32[3,1,8,128]{3,2,1,0:T(8,128)S(1)}, f32[3,1,8,128]{3,2,1,0:T(8,128)S(1)}, u32[]{:S(2)}, u32[]{:S(2)}) collective-permute-start(f32[3,1,8,128]{3,2,1,0:T(8,128)S(1)} %get-tuple-element.37), channel_id=1, source_target_pairs={{0,4},{4,8},{8,12},{12,16},{16,20},{20,24},{24,28},{28,32},{32,36}... | collective-permute-start | bytes 36872 | tf_op jit(solution)/shard_map/ppermute | solution.py:30
  85.6 8.7 %collective-permute-start.9 = (f32[3,1,8,128]{3,2,1,0:T(8,128)S(1)}, f32[3,1,8,128]{3,2,1,0:T(8,128)S(1)}, u32[]{:S(2)}, u32[]{:S(2)}) collective-permute-start(f32[3,1,8,128]{3,2,1,0:T(8,128)S(1)} %get-tuple-element.38), channel_id=1, source_target_pairs={{4,0},{8,4},{12,8},{16,12},{20,16},{24,20},{28,24},{32,28},{36,32}... | collective-permute-start | bytes 36872 | tf_op jit(solution)/shard_map/ppermute | solution.py:31
  95.2 2.2 %collective-permute-start.10 = (f32[3,4,1,128]{3,2,1,0:T(1,128)S(1)}, f32[3,4,1,128]{3,2,1,0:T(1,128)S(1)}, u32[]{:S(2)}, u32[]{:S(2)}) collective-permute-start(f32[3,4,1,128]{3,2,1,0:T(1,128)S(1)} %get-tuple-element.29), channel_id=1, source_target_pairs={{0,1},{1,2},{2,3},{4,5},{5,6},{6,7},{8,9},{9,10},{10,11},{12,13},{... | collective-permute-start | bytes 18440 | tf_op jit(solution)/shard_map/ppermute | solution.py:30
  97.4 2.1 %collective-permute-start.11 = (f32[3,4,1,128]{3,2,1,0:T(1,128)S(1)}, f32[3,4,1,128]{3,2,1,0:T(1,128)S(1)}, u32[]{:S(2)}, u32[]{:S(2)}) collective-permute-start(f32[3,4,1,128]{3,2,1,0:T(1,128)S(1)} %get-tuple-element.30), channel_id=1, source_target_pairs={{1,0},{2,1},{3,2},{5,4},{6,5},{7,6},{9,8},{10,9},{11,10},{13,12},{... | collective-permute-start | bytes 18440 | tf_op jit(solution)/shard_map/ppermute | solution.py:31
  100.4 3.5 %collective-permute-done.11 = f32[3,4,1,128]{3,2,1,0:T(1,128)S(1)} collective-permute-done((f32[3,4,1,128]{3,2,1,0:T(1,128)S(1)}, f32[3,4,1,128]{3,2,1,0:T(1,128)S(1)}, u32[]{:S(2)}, u32[]{:S(2)}) %collective-permute-start.11) | collective-permute-done | bytes 6176 | tf_op jit(solution)/shard_map/ppermute | solution.py:31
  104.6 11.5 %shard_map.88 = f32[3,16,128]{2,1,0:T(8,128)} custom-call(f32[1,16,128]{2,1,0:T(8,128)} %copy-done.3, f32[3,40,128]{2,1,0:T(8,128)} %broadcast_multiply_fusion.1.source_ref, f32[144,128,128]{2,1,0:T(8,128)} %get-tuple-element.5.refs_0_), custom_call_target="tpu_custom_call" | custom-call | tf_op jit(solution)/shard_map/pallas_call | solution.py:168
  116.1 0.8 fusion.22
  116.9 1.9 %collective-permute-start.12 = (f32[3,1,8,128]{3,2,1,0:T(8,128)S(1)}, f32[3,1,8,128]{3,2,1,0:T(8,128)S(1)}, u32[]{:S(2)}, u32[]{:S(2)}) collective-permute-start(f32[3,1,8,128]{3,2,1,0:T(8,128)S(1)} %get-tuple-element.35), channel_id=1, source_target_pairs={{0,4},{4,8},{8,12},{12,16},{16,20},{20,24},{24,28},{28,32},{32,36}... | collective-permute-start | bytes 36872 | tf_op jit(solution)/shard_map/ppermute | solution.py:30
  118.9 8.7 %collective-permute-start.13 = (f32[3,1,8,128]{3,2,1,0:T(8,128)S(1)}, f32[3,1,8,128]{3,2,1,0:T(8,128)S(1)}, u32[]{:S(2)}, u32[]{:S(2)}) collective-permute-start(f32[3,1,8,128]{3,2,1,0:T(8,128)S(1)} %get-tuple-element.36), channel_id=1, source_target_pairs={{4,0},{8,4},{12,8},{16,12},{20,16},{24,20},{28,24},{32,28},{36,32}... | collective-permute-start | bytes 36872 | tf_op jit(solution)/shard_map/ppermute | solution.py:31
  128.4 2.2 %collective-permute-start.14 = (f32[3,4,1,128]{3,2,1,0:T(1,128)S(1)}, f32[3,4,1,128]{3,2,1,0:T(1,128)S(1)}, u32[]{:S(2)}, u32[]{:S(2)}) collective-permute-start(f32[3,4,1,128]{3,2,1,0:T(1,128)S(1)} %get-tuple-element.27), channel_id=1, source_target_pairs={{0,1},{1,2},{2,3},{4,5},{5,6},{6,7},{8,9},{9,10},{10,11},{12,13},{... | collective-permute-start | bytes 18440 | tf_op jit(solution)/shard_map/ppermute | solution.py:30
  130.6 2.1 %collective-permute-start.15 = (f32[3,4,1,128]{3,2,1,0:T(1,128)S(1)}, f32[3,4,1,128]{3,2,1,0:T(1,128)S(1)}, u32[]{:S(2)}, u32[]{:S(2)}) collective-permute-start(f32[3,4,1,128]{3,2,1,0:T(1,128)S(1)} %get-tuple-element.28), channel_id=1, source_target_pairs={{1,0},{2,1},{3,2},{5,4},{6,5},{7,6},{9,8},{10,9},{11,10},{13,12},{... | collective-permute-start | bytes 18440 | tf_op jit(solution)/shard_map/ppermute | solution.py:31
  132.8 4.3 %collective-permute-done.15 = f32[3,4,1,128]{3,2,1,0:T(1,128)S(1)} collective-permute-done((f32[3,4,1,128]{3,2,1,0:T(1,128)S(1)}, f32[3,4,1,128]{3,2,1,0:T(1,128)S(1)}, u32[]{:S(2)}, u32[]{:S(2)}) %collective-permute-start.15) | collective-permute-done | bytes 6176 | tf_op jit(solution)/shard_map/ppermute | solution.py:31
  137.8 11.5 %shard_map.89 = f32[3,16,128]{2,1,0:T(8,128)} custom-call(f32[1,16,128]{2,1,0:T(8,128)} %copy-done.3, f32[3,40,128]{2,1,0:T(8,128)} %broadcast_multiply_fusion.source_ref, f32[144,128,128]{2,1,0:T(8,128)} %get-tuple-element.5.refs_0_), custom_call_target="tpu_custom_call" | custom-call | tf_op jit(solution)/shard_map/pallas_call | solution.py:168
  150.3 1.9 %collective-permute-start.16 = (f32[8,8,128]{2,1,0:T(8,128)S(1)}, f32[8,8,128]{2,1,0:T(8,128)S(1)}, u32[]{:S(2)}, u32[]{:S(2)}) collective-permute-start(f32[8,8,128]{2,1,0:T(8,128)S(1)} %pad_maximum_fusion.9), channel_id=1, source_target_pairs={{0,4},{4,8},{8,12},{12,16},{16,20},{20,24},{24,28},{28,32},{32,36}... | collective-permute-start | bytes 98312 | tf_op jit(solution)/shard_map/ppermute | solution.py:39
  152.2 8.1 %collective-permute-done.16 = f32[8,8,128]{2,1,0:T(8,128)S(1)} collective-permute-done((f32[8,8,128]{2,1,0:T(8,128)S(1)}, f32[8,8,128]{2,1,0:T(8,128)S(1)}, u32[]{:S(2)}, u32[]{:S(2)}) %collective-permute-start.16) | collective-permute-done | bytes 32800 | tf_op jit(solution)/shard_map/ppermute | solution.py:39
  (90 shorter events, 14.7 us)
Async XLA Ops:
  0.6 115.5 %copy-start.5 = (f32[3]{0:T(128)S(1)}, f32[3]{0:T(128)}, u32[]{:S(2)}) copy-start(f32[3]{0:T(128)} %constant.56.clone) | copy-start | bytes 40
  0.6 127.0 %copy-start.4 = (s32[2,8]{1,0:T(2,128)S(1)}, s32[2,8]{1,0:T(2,128)}, u32[]{:S(2)}) copy-start(s32[2,8]{1,0:T(2,128)} %param.11) | copy-start | bytes 196
  0.7 115.5 %copy-start = (f32[3,2,8,128]{3,2,1,0:T(8,128)S(1)}, f32[3,2,8,128]{3,2,1,0:T(8,128)}, u32[]{:S(2)}) copy-start(f32[3,2,8,128]{3,2,1,0:T(8,128)} %param.8) | copy-start | bytes 73732
  0.7 127.0 %copy-start.6 = (s32[2,8]{1,0:T(2,128)S(1)}, s32[2,8]{1,0:T(2,128)}, u32[]{:S(2)}) copy-start(s32[2,8]{1,0:T(2,128)} %param.12) | copy-start | bytes 196
  2.2 11.8 %collective-permute-start = (f32[7,1,8,128]{3,2,1,0:T(8,128)S(1)}, f32[7,1,8,128]{3,2,1,0:T(8,128)S(1)}, u32[]{:S(2)}, u32[]{:S(2)}) collective-permute-start(f32[7,1,8,128]{3,2,1,0:T(8,128)S(1)} %get-tuple-element.19), channel_id=1, source_target_pairs={{0,4},{4,8},{8,12},{12,16},{16,20},{20,24},{24,28},{28,32},{32,36}... | collective-permute-start | bytes 86024 | tf_op jit(solution)/shard_map/ppermute | solution.py:30
  5.8 9.3 %collective-permute-start.1 = (f32[7,1,8,128]{3,2,1,0:T(8,128)S(1)}, f32[7,1,8,128]{3,2,1,0:T(8,128)S(1)}, u32[]{:S(2)}, u32[]{:S(2)}) collective-permute-start(f32[7,1,8,128]{3,2,1,0:T(8,128)S(1)} %get-tuple-element.20), channel_id=1, source_target_pairs={{4,0},{8,4},{12,8},{16,12},{20,16},{24,20},{28,24},{32,28},{36,32}... | collective-permute-start | bytes 86024 | tf_op jit(solution)/shard_map/ppermute | solution.py:31
  15.9 9.5 %collective-permute-start.2 = (f32[7,4,1,128]{3,2,1,0:T(1,128)S(1)}, f32[7,4,1,128]{3,2,1,0:T(1,128)S(1)}, u32[]{:S(2)}, u32[]{:S(2)}) collective-permute-start(f32[7,4,1,128]{3,2,1,0:T(1,128)S(1)} %get-tuple-element.14), channel_id=1, source_target_pairs={{0,1},{1,2},{2,3},{4,5},{5,6},{6,7},{8,9},{9,10},{10,11},{12,13},{... | collective-permute-start | bytes 43016 | tf_op jit(solution)/shard_map/ppermute | solution.py:30
  21.4 6.5 %collective-permute-start.3 = (f32[7,4,1,128]{3,2,1,0:T(1,128)S(1)}, f32[7,4,1,128]{3,2,1,0:T(1,128)S(1)}, u32[]{:S(2)}, u32[]{:S(2)}) collective-permute-start(f32[7,4,1,128]{3,2,1,0:T(1,128)S(1)} %get-tuple-element.15), channel_id=1, source_target_pairs={{1,0},{2,1},{3,2},{5,4},{6,5},{7,6},{9,8},{10,9},{11,10},{13,12},{... | collective-permute-start | bytes 43016 | tf_op jit(solution)/shard_map/ppermute | solution.py:31
  46.6 57.9 %copy-start.3 = (f32[1,16,128]{2,1,0:T(8,128)}, f32[1,16,128]{2,1,0:T(8,128)S(1)}, u32[]{:S(2)}) copy-start(f32[1,16,128]{2,1,0:T(8,128)S(1)} %get-tuple-element.34.target_ref) | copy-start | bytes 24580
  46.6 11.5 %collective-permute-start.4 = (f32[3,1,8,128]{3,2,1,0:T(8,128)S(1)}, f32[3,1,8,128]{3,2,1,0:T(8,128)S(1)}, u32[]{:S(2)}, u32[]{:S(2)}) collective-permute-start(f32[3,1,8,128]{3,2,1,0:T(8,128)S(1)} %get-tuple-element.39), channel_id=1, source_target_pairs={{0,4},{4,8},{8,12},{12,16},{16,20},{20,24},{24,28},{28,32},{32,36}... | collective-permute-start | bytes 36872 | tf_op jit(solution)/shard_map/ppermute | solution.py:30
  48.6 9.6 %collective-permute-start.5 = (f32[3,1,8,128]{3,2,1,0:T(8,128)S(1)}, f32[3,1,8,128]{3,2,1,0:T(8,128)S(1)}, u32[]{:S(2)}, u32[]{:S(2)}) collective-permute-start(f32[3,1,8,128]{3,2,1,0:T(8,128)S(1)} %get-tuple-element.40), channel_id=1, source_target_pairs={{4,0},{8,4},{12,8},{16,12},{20,16},{24,20},{28,24},{32,28},{36,32}... | collective-permute-start | bytes 36872 | tf_op jit(solution)/shard_map/ppermute | solution.py:31
  58.2 6.2 %collective-permute-start.6 = (f32[3,4,1,128]{3,2,1,0:T(1,128)S(1)}, f32[3,4,1,128]{3,2,1,0:T(1,128)S(1)}, u32[]{:S(2)}, u32[]{:S(2)}) collective-permute-start(f32[3,4,1,128]{3,2,1,0:T(1,128)S(1)} %get-tuple-element.31), channel_id=1, source_target_pairs={{0,1},{1,2},{2,3},{4,5},{5,6},{6,7},{8,9},{9,10},{10,11},{12,13},{... | collective-permute-start | bytes 18440 | tf_op jit(solution)/shard_map/ppermute | solution.py:30
  61.1 6.5 %collective-permute-start.7 = (f32[3,4,1,128]{3,2,1,0:T(1,128)S(1)}, f32[3,4,1,128]{3,2,1,0:T(1,128)S(1)}, u32[]{:S(2)}, u32[]{:S(2)}) collective-permute-start(f32[3,4,1,128]{3,2,1,0:T(1,128)S(1)} %get-tuple-element.32), channel_id=1, source_target_pairs={{1,0},{2,1},{3,2},{5,4},{6,5},{7,6},{9,8},{10,9},{11,10},{13,12},{... | collective-permute-start | bytes 18440 | tf_op jit(solution)/shard_map/ppermute | solution.py:31
  82.8 33.3 %copy-start.2 = (f32[4,16,128]{2,1,0:T(8,128)S(1)}, f32[4,16,128]{2,1,0:T(8,128)}, u32[]{:S(2)}) copy-start(f32[4,16,128]{2,1,0:T(8,128)} %get-tuple-element.4) | copy-start | bytes 98308
  83.7 10.7 %collective-permute-start.8 = (f32[3,1,8,128]{3,2,1,0:T(8,128)S(1)}, f32[3,1,8,128]{3,2,1,0:T(8,128)S(1)}, u32[]{:S(2)}, u32[]{:S(2)}) collective-permute-start(f32[3,1,8,128]{3,2,1,0:T(8,128)S(1)} %get-tuple-element.37), channel_id=1, source_target_pairs={{0,4},{4,8},{8,12},{12,16},{16,20},{20,24},{24,28},{28,32},{32,36}... | collective-permute-start | bytes 36872 | tf_op jit(solution)/shard_map/ppermute | solution.py:30
  85.6 9.6 %collective-permute-start.9 = (f32[3,1,8,128]{3,2,1,0:T(8,128)S(1)}, f32[3,1,8,128]{3,2,1,0:T(8,128)S(1)}, u32[]{:S(2)}, u32[]{:S(2)}) collective-permute-start(f32[3,1,8,128]{3,2,1,0:T(8,128)S(1)} %get-tuple-element.38), channel_id=1, source_target_pairs={{4,0},{8,4},{12,8},{16,12},{20,16},{24,20},{28,24},{32,28},{36,32}... | collective-permute-start | bytes 36872 | tf_op jit(solution)/shard_map/ppermute | solution.py:31
  95.2 5.2 %collective-permute-start.10 = (f32[3,4,1,128]{3,2,1,0:T(1,128)S(1)}, f32[3,4,1,128]{3,2,1,0:T(1,128)S(1)}, u32[]{:S(2)}, u32[]{:S(2)}) collective-permute-start(f32[3,4,1,128]{3,2,1,0:T(1,128)S(1)} %get-tuple-element.29), channel_id=1, source_target_pairs={{0,1},{1,2},{2,3},{4,5},{5,6},{6,7},{8,9},{9,10},{10,11},{12,13},{... | collective-permute-start | bytes 18440 | tf_op jit(solution)/shard_map/ppermute | solution.py:30
  97.4 6.5 %collective-permute-start.11 = (f32[3,4,1,128]{3,2,1,0:T(1,128)S(1)}, f32[3,4,1,128]{3,2,1,0:T(1,128)S(1)}, u32[]{:S(2)}, u32[]{:S(2)}) collective-permute-start(f32[3,4,1,128]{3,2,1,0:T(1,128)S(1)} %get-tuple-element.30), channel_id=1, source_target_pairs={{1,0},{2,1},{3,2},{5,4},{6,5},{7,6},{9,8},{10,9},{11,10},{13,12},{... | collective-permute-start | bytes 18440 | tf_op jit(solution)/shard_map/ppermute | solution.py:31
  104.6 44.7 %copy-start.1 = (f32[3,2,8,128]{3,2,1,0:T(8,128)S(1)}, f32[3,2,8,128]{3,2,1,0:T(8,128)}, u32[]{:S(2)}) copy-start(f32[3,2,8,128]{3,2,1,0:T(8,128)} %param.7) | copy-start | bytes 73732
  116.9 10.7 %collective-permute-start.12 = (f32[3,1,8,128]{3,2,1,0:T(8,128)S(1)}, f32[3,1,8,128]{3,2,1,0:T(8,128)S(1)}, u32[]{:S(2)}, u32[]{:S(2)}) collective-permute-start(f32[3,1,8,128]{3,2,1,0:T(8,128)S(1)} %get-tuple-element.35), channel_id=1, source_target_pairs={{0,4},{4,8},{8,12},{12,16},{16,20},{20,24},{24,28},{28,32},{32,36}... | collective-permute-start | bytes 36872 | tf_op jit(solution)/shard_map/ppermute | solution.py:30
  118.9 9.6 %collective-permute-start.13 = (f32[3,1,8,128]{3,2,1,0:T(8,128)S(1)}, f32[3,1,8,128]{3,2,1,0:T(8,128)S(1)}, u32[]{:S(2)}, u32[]{:S(2)}) collective-permute-start(f32[3,1,8,128]{3,2,1,0:T(8,128)S(1)} %get-tuple-element.36), channel_id=1, source_target_pairs={{4,0},{8,4},{12,8},{16,12},{20,16},{24,20},{28,24},{32,28},{36,32}... | collective-permute-start | bytes 36872 | tf_op jit(solution)/shard_map/ppermute | solution.py:31
  128.4 4.4 %collective-permute-start.14 = (f32[3,4,1,128]{3,2,1,0:T(1,128)S(1)}, f32[3,4,1,128]{3,2,1,0:T(1,128)S(1)}, u32[]{:S(2)}, u32[]{:S(2)}) collective-permute-start(f32[3,4,1,128]{3,2,1,0:T(1,128)S(1)} %get-tuple-element.27), channel_id=1, source_target_pairs={{0,1},{1,2},{2,3},{4,5},{5,6},{6,7},{8,9},{9,10},{10,11},{12,13},{... | collective-permute-start | bytes 18440 | tf_op jit(solution)/shard_map/ppermute | solution.py:30
  130.6 6.5 %collective-permute-start.15 = (f32[3,4,1,128]{3,2,1,0:T(1,128)S(1)}, f32[3,4,1,128]{3,2,1,0:T(1,128)S(1)}, u32[]{:S(2)}, u32[]{:S(2)}) collective-permute-start(f32[3,4,1,128]{3,2,1,0:T(1,128)S(1)} %get-tuple-element.28), channel_id=1, source_target_pairs={{1,0},{2,1},{3,2},{5,4},{6,5},{7,6},{9,8},{10,9},{11,10},{13,12},{... | collective-permute-start | bytes 18440 | tf_op jit(solution)/shard_map/ppermute | solution.py:31
  150.3 10.0 %collective-permute-start.16 = (f32[8,8,128]{2,1,0:T(8,128)S(1)}, f32[8,8,128]{2,1,0:T(8,128)S(1)}, u32[]{:S(2)}, u32[]{:S(2)}) collective-permute-start(f32[8,8,128]{2,1,0:T(8,128)S(1)} %pad_maximum_fusion.9), channel_id=1, source_target_pairs={{0,4},{4,8},{8,12},{12,16},{16,20},{20,24},{24,28},{28,32},{32,36}... | collective-permute-start | bytes 98312 | tf_op jit(solution)/shard_map/ppermute | solution.py:39

commit v12 on v10

--- a/solution.py
+++ b/solution.py
@@ -75,7 +75,7 @@
     padded_cols = col_count + 2
     target_count = target.shape[0]
     source_count = source.shape[0]
-    output_count = {"density": 2, "force": 4, "jacobi": 3}[kind]
+    output_count = {"density": 2, "force": 3}.get(kind, source_count)
     target_cols = target.reshape(target_count, block_count, slot_count)
     source_rows = source.reshape(source_count, (row_count + 2) * padded_cols, slot_count)
 
@@ -112,7 +112,7 @@
                 other = [source_ref[k, pl.ds(near, 1), :] for k in range(source_count)]
                 if kind == "jacobi":
                     pull = weight_ref[step * 9 + neighbour]
-                    for k in range(3):
+                    for k in range(source_count):
                         totals[k] = totals[k] + pull * other[k]
                     continue
                 gaps = [
@@ -138,7 +138,6 @@
                         totals[k] = totals[k] + push * gaps[k]
                     pull = (mine[4] + other[5]) * cubed
                     weight_ref[step * 9 + neighbour] = pull
-                    totals[3] = totals[3] + pull * other[4]
             lanes = lax.broadcasted_iota(jnp.int32, (CHUNK, slot_count), 1)
             table = jnp.zeros((CHUNK, slot_count), jnp.float32)
             for k in range(output_count):
@@ -242,19 +241,18 @@
     scale = PARTICLE_MASS * 20.0 * KERNEL_NORM
     gravity = jnp.array([GRAVITY_DOWN, 0.0, GRAVITY_UP], jnp.float32)[:, None, None, None]
     predicted = velocities + TIME_STEP * (-scale * forces[:3] + gravity)
-    diagonal = 1.0 + TIME_STEP * (scale * inverse * forces[3])
     target = viscosity[None]
     current = predicted
+    diagonal = None
     for sweep_index in range(JACOBI):
         speed_pad = with_halo(current, (("down", 1), ("cross", 2)), 1)
-        pulled = pair_pass(
-            "jacobi",
-            target,
-            speed_pad * dens_pad[0:1],
-            row_count,
-            col_count,
-            weights,
-        )
+        source = speed_pad * dens_pad[0:1]
+        if diagonal is None:
+            source = jnp.concatenate([source, dens_pad[0:1]], axis=0)
+        pulled = pair_pass("jacobi", target, source, row_count, col_count, weights)
+        if diagonal is None:
+            diagonal = 1.0 + TIME_STEP * (scale * inverse * pulled[3])
+            pulled = pulled[:3]
         current = (predicted + TIME_STEP * (scale * inverse * pulled)) / diagonal
     moved_positions = positions + TIME_STEP * current
     field_six = jnp.concatenate([moved_positions, current], axis=0)

time: 157 us -> 158 us (level)
  no operation moved by 1% of the time
where the time goes in v12:
time: 158 us; the launch traced here: 156 us
  starting transfers between devices  66.6 us (42%)
  Pallas kernels  45.4 us (29%)
  waiting for transfers between devices  24.9 us (16%)
  other arithmetic  14.2 us (9%)
  local copies, waits for them, and re-layouts  4.21 us (3%)
    ppermute x8, starting transfers between devices, with_halo(): after = lax.ppermute(initial, axis, down)  42.6 us
    ppermute x8, starting transfers between devices, with_halo(): before = lax.ppermute(last, axis, up)  22.1 us
    pallas_call x2, Pallas kernels, pair_pass(): pl.pallas_call(kernel, out_shape=out_shape)  16.9 us
    ppermute x8, waiting for transfers between devices, with_halo(): after = lax.ppermute(initial, axis, down)  16.8 us
    pallas_call x1, Pallas kernels, pair_pass(): pl.pallas_call(kernel, out_shape=out_shape, grid=grid, in_specs=whole, ou...  14.8 us
    pallas_call x1, Pallas kernels, pair_pass(): pl.pallas_call(kernel, out_shape=(out_shape, weight_shape), grid=grid, in...  13.7 us
    ppermute x1, waiting for transfers between devices, from_behind(): return lax.ppermute(block, axis, route)  8.11 us
  transfers between devices with their start and end apart: 17, of which 8 were waited for; matrix products, arithmetic and copies ran while one was open for 3% of the time, Pallas kernels for 0%

profile of v12, /device:TPU:3, one launch (start us, length us, event | category | flops | bytes accessed | tf_op | source)
XLA Modules:
  0.0 156.4 jit_solution(657652188413324034)
XLA Ops:
  2.2 3.5 %collective-permute-start = (f32[7,1,8,128]{3,2,1,0:T(8,128)S(1)}, f32[7,1,8,128]{3,2,1,0:T(8,128)S(1)}, u32[]{:S(2)}, u32[]{:S(2)}) collective-permute-start(f32[7,1,8,128]{3,2,1,0:T(8,128)S(1)} %get-tuple-element.20), channel_id=1, source_target_pairs={{0,4},{4,8},{8,12},{12,16},{16,20},{20,24},{24,28},{28,32},{32,36}... | collective-permute-start | bytes 86024 | tf_op jit(solution)/shard_map/ppermute | solution.py:30
  5.8 8.3 %collective-permute-start.1 = (f32[7,1,8,128]{3,2,1,0:T(8,128)S(1)}, f32[7,1,8,128]{3,2,1,0:T(8,128)S(1)}, u32[]{:S(2)}, u32[]{:S(2)}) collective-permute-start(f32[7,1,8,128]{3,2,1,0:T(8,128)S(1)} %get-tuple-element.21), channel_id=1, source_target_pairs={{4,0},{8,4},{12,8},{16,12},{20,16},{24,20},{28,24},{32,28},{36,32}... | collective-permute-start | bytes 86024 | tf_op jit(solution)/shard_map/ppermute | solution.py:31
  14.1 1.0 collective-permute-done.1
  15.0 0.8 pad_maximum_fusion.15
  15.9 5.5 %collective-permute-start.2 = (f32[7,4,1,128]{3,2,1,0:T(1,128)S(1)}, f32[7,4,1,128]{3,2,1,0:T(1,128)S(1)}, u32[]{:S(2)}, u32[]{:S(2)}) collective-permute-start(f32[7,4,1,128]{3,2,1,0:T(1,128)S(1)} %get-tuple-element.14), channel_id=1, source_target_pairs={{0,1},{1,2},{2,3},{4,5},{5,6},{6,7},{8,9},{9,10},{10,11},{12,13},{... | collective-permute-start | bytes 43016 | tf_op jit(solution)/shard_map/ppermute | solution.py:30
  21.4 1.9 %collective-permute-start.3 = (f32[7,4,1,128]{3,2,1,0:T(1,128)S(1)}, f32[7,4,1,128]{3,2,1,0:T(1,128)S(1)}, u32[]{:S(2)}, u32[]{:S(2)}) collective-permute-start(f32[7,4,1,128]{3,2,1,0:T(1,128)S(1)} %get-tuple-element.15), channel_id=1, source_target_pairs={{1,0},{2,1},{3,2},{5,4},{6,5},{7,6},{9,8},{10,9},{11,10},{13,12},{... | collective-permute-start | bytes 43016 | tf_op jit(solution)/shard_map/ppermute | solution.py:31
  23.3 1.4 maximum_bitcast_fusion.target_ref
  25.4 2.5 %collective-permute-done.3 = f32[7,4,1,128]{3,2,1,0:T(1,128)S(1)} collective-permute-done((f32[7,4,1,128]{3,2,1,0:T(1,128)S(1)}, f32[7,4,1,128]{3,2,1,0:T(1,128)S(1)}, u32[]{:S(2)}, u32[]{:S(2)}) %collective-permute-start.3) | collective-permute-done | bytes 14368 | tf_op jit(solution)/shard_map/ppermute | solution.py:31
  30.2 14.8 %shard_map.86 = f32[2,16,128]{2,1,0:T(8,128)} custom-call(f32[6,16,128]{2,1,0:T(8,128)} %maximum_bitcast_fusion.target_ref, f32[6,40,128]{2,1,0:T(8,128)} %copy.11.source_ref), custom_call_target="tpu_custom_call" | custom-call | tf_op jit(solution)/shard_map/pallas_call | solution.py:174
  45.1 0.8 broadcast_divide_fusion
  46.7 1.9 %collective-permute-start.4 = (f32[3,1,8,128]{3,2,1,0:T(8,128)S(1)}, f32[3,1,8,128]{3,2,1,0:T(8,128)S(1)}, u32[]{:S(2)}, u32[]{:S(2)}) collective-permute-start(f32[3,1,8,128]{3,2,1,0:T(8,128)S(1)} %get-tuple-element.40), channel_id=1, source_target_pairs={{0,4},{4,8},{8,12},{12,16},{16,20},{20,24},{24,28},{28,32},{32,36}... | collective-permute-start | bytes 36872 | tf_op jit(solution)/shard_map/ppermute | solution.py:30
  48.6 8.8 %collective-permute-start.5 = (f32[3,1,8,128]{3,2,1,0:T(8,128)S(1)}, f32[3,1,8,128]{3,2,1,0:T(8,128)S(1)}, u32[]{:S(2)}, u32[]{:S(2)}) collective-permute-start(f32[3,1,8,128]{3,2,1,0:T(8,128)S(1)} %get-tuple-element.41), channel_id=1, source_target_pairs={{4,0},{8,4},{12,8},{16,12},{20,16},{24,20},{28,24},{32,28},{36,32}... | collective-permute-start | bytes 36872 | tf_op jit(solution)/shard_map/ppermute | solution.py:31
  58.2 2.9 %collective-permute-start.6 = (f32[3,4,1,128]{3,2,1,0:T(1,128)S(1)}, f32[3,4,1,128]{3,2,1,0:T(1,128)S(1)}, u32[]{:S(2)}, u32[]{:S(2)}) collective-permute-start(f32[3,4,1,128]{3,2,1,0:T(1,128)S(1)} %get-tuple-element.32), channel_id=1, source_target_pairs={{0,1},{1,2},{2,3},{4,5},{5,6},{6,7},{8,9},{9,10},{10,11},{12,13},{... | collective-permute-start | bytes 18440 | tf_op jit(solution)/shard_map/ppermute | solution.py:30
  61.2 1.9 %collective-permute-start.7 = (f32[3,4,1,128]{3,2,1,0:T(1,128)S(1)}, f32[3,4,1,128]{3,2,1,0:T(1,128)S(1)}, u32[]{:S(2)}, u32[]{:S(2)}) collective-permute-start(f32[3,4,1,128]{3,2,1,0:T(1,128)S(1)} %get-tuple-element.33), channel_id=1, source_target_pairs={{1,0},{2,1},{3,2},{5,4},{6,5},{7,6},{9,8},{10,9},{11,10},{13,12},{... | collective-permute-start | bytes 18440 | tf_op jit(solution)/shard_map/ppermute | solution.py:31
  63.1 1.4 pad_maximum_fusion.8.target_ref
  64.4 3.2 %collective-permute-done.7 = f32[3,4,1,128]{3,2,1,0:T(1,128)S(1)} collective-permute-done((f32[3,4,1,128]{3,2,1,0:T(1,128)S(1)}, f32[3,4,1,128]{3,2,1,0:T(1,128)S(1)}, u32[]{:S(2)}, u32[]{:S(2)}) %collective-permute-start.7) | collective-permute-done | bytes 6176 | tf_op jit(solution)/shard_map/ppermute | solution.py:31
  68.4 13.7 %shard_map.87 = (f32[3,16,128]{2,1,0:T(8,128)}, f32[144,128,128]{2,1,0:T(8,128)}) custom-call(f32[5,16,128]{2,1,0:T(8,128)} %pad_maximum_fusion.8.target_ref, f32[6,40,128]{2,1,0:T(8,128)} %copy.13.source_ref), custom_call_target="tpu_custom_call" | custom-call | tf_op jit(solution)/shard_map/pallas_call | solution.py:164
  82.1 0.9 fusion.25
  83.0 1.9 %collective-permute-start.8 = (f32[3,1,8,128]{3,2,1,0:T(8,128)S(1)}, f32[3,1,8,128]{3,2,1,0:T(8,128)S(1)}, u32[]{:S(2)}, u32[]{:S(2)}) collective-permute-start(f32[3,1,8,128]{3,2,1,0:T(8,128)S(1)} %get-tuple-element.38), channel_id=1, source_target_pairs={{0,4},{4,8},{8,12},{12,16},{16,20},{20,24},{24,28},{28,32},{32,36}... | collective-permute-start | bytes 36872 | tf_op jit(solution)/shard_map/ppermute | solution.py:30
  84.9 8.7 %collective-permute-start.9 = (f32[3,1,8,128]{3,2,1,0:T(8,128)S(1)}, f32[3,1,8,128]{3,2,1,0:T(8,128)S(1)}, u32[]{:S(2)}, u32[]{:S(2)}) collective-permute-start(f32[3,1,8,128]{3,2,1,0:T(8,128)S(1)} %get-tuple-element.39), channel_id=1, source_target_pairs={{4,0},{8,4},{12,8},{16,12},{20,16},{24,20},{28,24},{32,28},{36,32}... | collective-permute-start | bytes 36872 | tf_op jit(solution)/shard_map/ppermute | solution.py:31
  94.5 2.2 %collective-permute-start.10 = (f32[3,4,1,128]{3,2,1,0:T(1,128)S(1)}, f32[3,4,1,128]{3,2,1,0:T(1,128)S(1)}, u32[]{:S(2)}, u32[]{:S(2)}) collective-permute-start(f32[3,4,1,128]{3,2,1,0:T(1,128)S(1)} %get-tuple-element.30), channel_id=1, source_target_pairs={{0,1},{1,2},{2,3},{4,5},{5,6},{6,7},{8,9},{9,10},{10,11},{12,13},{... | collective-permute-start | bytes 18440 | tf_op jit(solution)/shard_map/ppermute | solution.py:30
  96.8 2.1 %collective-permute-start.11 = (f32[3,4,1,128]{3,2,1,0:T(1,128)S(1)}, f32[3,4,1,128]{3,2,1,0:T(1,128)S(1)}, u32[]{:S(2)}, u32[]{:S(2)}) collective-permute-start(f32[3,4,1,128]{3,2,1,0:T(1,128)S(1)} %get-tuple-element.31), channel_id=1, source_target_pairs={{1,0},{2,1},{3,2},{5,4},{6,5},{7,6},{9,8},{10,9},{11,10},{13,12},{... | collective-permute-start | bytes 18440 | tf_op jit(solution)/shard_map/ppermute | solution.py:31
  98.9 4.3 %collective-permute-done.11 = f32[3,4,1,128]{3,2,1,0:T(1,128)S(1)} collective-permute-done((f32[3,4,1,128]{3,2,1,0:T(1,128)S(1)}, f32[3,4,1,128]{3,2,1,0:T(1,128)S(1)}, u32[]{:S(2)}, u32[]{:S(2)}) %collective-permute-start.11) | collective-permute-done | bytes 6176 | tf_op jit(solution)/shard_map/ppermute | solution.py:31
  103.9 8.7 %shard_map.88 = f32[4,16,128]{2,1,0:T(8,128)} custom-call(f32[1,16,128]{2,1,0:T(8,128)} %copy-done.4, f32[4,40,128]{2,1,0:T(8,128)} %reshape.207.source_ref, f32[144,128,128]{2,1,0:T(8,128)} %get-tuple-element.5.refs_0_), custom_call_target="tpu_custom_call" | custom-call | tf_op jit(solution)/shard_map/pallas_call | solution.py:172
  114.3 1.9 %collective-permute-start.12 = (f32[3,1,8,128]{3,2,1,0:T(8,128)S(1)}, f32[3,1,8,128]{3,2,1,0:T(8,128)S(1)}, u32[]{:S(2)}, u32[]{:S(2)}) collective-permute-start(f32[3,1,8,128]{3,2,1,0:T(8,128)S(1)} %get-tuple-element.36), channel_id=1, source_target_pairs={{0,4},{4,8},{8,12},{12,16},{16,20},{20,24},{24,28},{28,32},{32,36}... | collective-permute-start | bytes 36872 | tf_op jit(solution)/shard_map/ppermute | solution.py:30
  116.2 8.7 %collective-permute-start.13 = (f32[3,1,8,128]{3,2,1,0:T(8,128)S(1)}, f32[3,1,8,128]{3,2,1,0:T(8,128)S(1)}, u32[]{:S(2)}, u32[]{:S(2)}) collective-permute-start(f32[3,1,8,128]{3,2,1,0:T(8,128)S(1)} %get-tuple-element.37), channel_id=1, source_target_pairs={{4,0},{8,4},{12,8},{16,12},{20,16},{24,20},{28,24},{32,28},{36,32}... | collective-permute-start | bytes 36872 | tf_op jit(solution)/shard_map/ppermute | solution.py:31
  125.8 2.2 %collective-permute-start.14 = (f32[3,4,1,128]{3,2,1,0:T(1,128)S(1)}, f32[3,4,1,128]{3,2,1,0:T(1,128)S(1)}, u32[]{:S(2)}, u32[]{:S(2)}) collective-permute-start(f32[3,4,1,128]{3,2,1,0:T(1,128)S(1)} %get-tuple-element.28), channel_id=1, source_target_pairs={{0,1},{1,2},{2,3},{4,5},{5,6},{6,7},{8,9},{9,10},{10,11},{12,13},{... | collective-permute-start | bytes 18440 | tf_op jit(solution)/shard_map/ppermute | solution.py:30
  128.0 2.1 %collective-permute-start.15 = (f32[3,4,1,128]{3,2,1,0:T(1,128)S(1)}, f32[3,4,1,128]{3,2,1,0:T(1,128)S(1)}, u32[]{:S(2)}, u32[]{:S(2)}) collective-permute-start(f32[3,4,1,128]{3,2,1,0:T(1,128)S(1)} %get-tuple-element.29), channel_id=1, source_target_pairs={{1,0},{2,1},{3,2},{5,4},{6,5},{7,6},{9,8},{10,9},{11,10},{13,12},{... | collective-permute-start | bytes 18440 | tf_op jit(solution)/shard_map/ppermute | solution.py:31
  130.1 4.3 %collective-permute-done.15 = f32[3,4,1,128]{3,2,1,0:T(1,128)S(1)} collective-permute-done((f32[3,4,1,128]{3,2,1,0:T(1,128)S(1)}, f32[3,4,1,128]{3,2,1,0:T(1,128)S(1)}, u32[]{:S(2)}, u32[]{:S(2)}) %collective-permute-start.15) | collective-permute-done | bytes 6176 | tf_op jit(solution)/shard_map/ppermute | solution.py:31
  135.1 8.1 %shard_map.89 = f32[3,16,128]{2,1,0:T(8,128)} custom-call(f32[1,16,128]{2,1,0:T(8,128)} %copy-done.4, f32[3,40,128]{2,1,0:T(8,128)} %broadcast_multiply_fusion.source_ref, f32[144,128,128]{2,1,0:T(8,128)} %get-tuple-element.5.refs_0_), custom_call_target="tpu_custom_call" | custom-call | tf_op jit(solution)/shard_map/pallas_call | solution.py:172
  144.2 1.9 %collective-permute-start.16 = (f32[8,8,128]{2,1,0:T(8,128)S(1)}, f32[8,8,128]{2,1,0:T(8,128)S(1)}, u32[]{:S(2)}, u32[]{:S(2)}) collective-permute-start(f32[8,8,128]{2,1,0:T(8,128)S(1)} %pad_maximum_fusion.9), channel_id=1, source_target_pairs={{0,4},{4,8},{8,12},{12,16},{16,20},{20,24},{24,28},{28,32},{32,36}... | collective-permute-start | bytes 98312 | tf_op jit(solution)/shard_map/ppermute | solution.py:39
  146.1 8.1 %collective-permute-done.16 = f32[8,8,128]{2,1,0:T(8,128)S(1)} collective-permute-done((f32[8,8,128]{2,1,0:T(8,128)S(1)}, f32[8,8,128]{2,1,0:T(8,128)S(1)}, u32[]{:S(2)}, u32[]{:S(2)}) %collective-permute-start.16) | collective-permute-done | bytes 32800 | tf_op jit(solution)/shard_map/ppermute | solution.py:39
  (92 shorter events, 14.7 us)
Async XLA Ops:
  0.6 112.8 %copy-start.6 = (f32[3]{0:T(128)S(1)}, f32[3]{0:T(128)}, u32[]{:S(2)}) copy-start(f32[3]{0:T(128)} %constant.56.clone) | copy-start | bytes 40
  0.6 112.0 %copy-start.5 = (s32[2,8]{1,0:T(2,128)S(1)}, s32[2,8]{1,0:T(2,128)}, u32[]{:S(2)}) copy-start(s32[2,8]{1,0:T(2,128)} %param.11) | copy-start | bytes 196
  0.7 112.8 %copy-start = (f32[3,2,8,128]{3,2,1,0:T(8,128)S(1)}, f32[3,2,8,128]{3,2,1,0:T(8,128)}, u32[]{:S(2)}) copy-start(f32[3,2,8,128]{3,2,1,0:T(8,128)} %param.8) | copy-start | bytes 73732
  0.7 124.3 %copy-start.7 = (s32[2,8]{1,0:T(2,128)S(1)}, s32[2,8]{1,0:T(2,128)}, u32[]{:S(2)}) copy-start(s32[2,8]{1,0:T(2,128)} %param.12) | copy-start | bytes 196
  2.2 11.8 %collective-permute-start = (f32[7,1,8,128]{3,2,1,0:T(8,128)S(1)}, f32[7,1,8,128]{3,2,1,0:T(8,128)S(1)}, u32[]{:S(2)}, u32[]{:S(2)}) collective-permute-start(f32[7,1,8,128]{3,2,1,0:T(8,128)S(1)} %get-tuple-element.20), channel_id=1, source_target_pairs={{0,4},{4,8},{8,12},{12,16},{16,20},{20,24},{24,28},{28,32},{32,36}... | collective-permute-start | bytes 86024 | tf_op jit(solution)/shard_map/ppermute | solution.py:30
  5.8 9.3 %collective-permute-start.1 = (f32[7,1,8,128]{3,2,1,0:T(8,128)S(1)}, f32[7,1,8,128]{3,2,1,0:T(8,128)S(1)}, u32[]{:S(2)}, u32[]{:S(2)}) collective-permute-start(f32[7,1,8,128]{3,2,1,0:T(8,128)S(1)} %get-tuple-element.21), channel_id=1, source_target_pairs={{4,0},{8,4},{12,8},{16,12},{20,16},{24,20},{28,24},{32,28},{36,32}... | collective-permute-start | bytes 86024 | tf_op jit(solution)/shard_map/ppermute | solution.py:31
  15.9 9.5 %collective-permute-start.2 = (f32[7,4,1,128]{3,2,1,0:T(1,128)S(1)}, f32[7,4,1,128]{3,2,1,0:T(1,128)S(1)}, u32[]{:S(2)}, u32[]{:S(2)}) collective-permute-start(f32[7,4,1,128]{3,2,1,0:T(1,128)S(1)} %get-tuple-element.14), channel_id=1, source_target_pairs={{0,1},{1,2},{2,3},{4,5},{5,6},{6,7},{8,9},{9,10},{10,11},{12,13},{... | collective-permute-start | bytes 43016 | tf_op jit(solution)/shard_map/ppermute | solution.py:30
  21.4 6.5 %collective-permute-start.3 = (f32[7,4,1,128]{3,2,1,0:T(1,128)S(1)}, f32[7,4,1,128]{3,2,1,0:T(1,128)S(1)}, u32[]{:S(2)}, u32[]{:S(2)}) collective-permute-start(f32[7,4,1,128]{3,2,1,0:T(1,128)S(1)} %get-tuple-element.15), channel_id=1, source_target_pairs={{1,0},{2,1},{3,2},{5,4},{6,5},{7,6},{9,8},{10,9},{11,10},{13,12},{... | collective-permute-start | bytes 43016 | tf_op jit(solution)/shard_map/ppermute | solution.py:31
  45.1 67.5 %copy-start.3 = (f32[2,16,128]{2,1,0:T(8,128)S(1)}, f32[2,16,128]{2,1,0:T(8,128)}, u32[]{:S(2)}) copy-start(f32[2,16,128]{2,1,0:T(8,128)} %shard_map.86) | copy-start | bytes 49156
  46.7 57.2 %copy-start.4 = (f32[1,16,128]{2,1,0:T(8,128)}, f32[1,16,128]{2,1,0:T(8,128)S(1)}, u32[]{:S(2)}) copy-start(f32[1,16,128]{2,1,0:T(8,128)S(1)} %get-tuple-element.35.target_ref) | copy-start | bytes 24580
  46.7 11.5 %collective-permute-start.4 = (f32[3,1,8,128]{3,2,1,0:T(8,128)S(1)}, f32[3,1,8,128]{3,2,1,0:T(8,128)S(1)}, u32[]{:S(2)}, u32[]{:S(2)}) collective-permute-start(f32[3,1,8,128]{3,2,1,0:T(8,128)S(1)} %get-tuple-element.40), channel_id=1, source_target_pairs={{0,4},{4,8},{8,12},{12,16},{16,20},{20,24},{24,28},{28,32},{32,36}... | collective-permute-start | bytes 36872 | tf_op jit(solution)/shard_map/ppermute | solution.py:30
  48.6 9.6 %collective-permute-start.5 = (f32[3,1,8,128]{3,2,1,0:T(8,128)S(1)}, f32[3,1,8,128]{3,2,1,0:T(8,128)S(1)}, u32[]{:S(2)}, u32[]{:S(2)}) collective-permute-start(f32[3,1,8,128]{3,2,1,0:T(8,128)S(1)} %get-tuple-element.41), channel_id=1, source_target_pairs={{4,0},{8,4},{12,8},{16,12},{20,16},{24,20},{28,24},{32,28},{36,32}... | collective-permute-start | bytes 36872 | tf_op jit(solution)/shard_map/ppermute | solution.py:31
  58.2 6.2 %collective-permute-start.6 = (f32[3,4,1,128]{3,2,1,0:T(1,128)S(1)}, f32[3,4,1,128]{3,2,1,0:T(1,128)S(1)}, u32[]{:S(2)}, u32[]{:S(2)}) collective-permute-start(f32[3,4,1,128]{3,2,1,0:T(1,128)S(1)} %get-tuple-element.32), channel_id=1, source_target_pairs={{0,1},{1,2},{2,3},{4,5},{5,6},{6,7},{8,9},{9,10},{10,11},{12,13},{... | collective-permute-start | bytes 18440 | tf_op jit(solution)/shard_map/ppermute | solution.py:30
  61.2 6.5 %collective-permute-start.7 = (f32[3,4,1,128]{3,2,1,0:T(1,128)S(1)}, f32[3,4,1,128]{3,2,1,0:T(1,128)S(1)}, u32[]{:S(2)}, u32[]{:S(2)}) collective-permute-start(f32[3,4,1,128]{3,2,1,0:T(1,128)S(1)} %get-tuple-element.33), channel_id=1, source_target_pairs={{1,0},{2,1},{3,2},{5,4},{6,5},{7,6},{9,8},{10,9},{11,10},{13,12},{... | collective-permute-start | bytes 18440 | tf_op jit(solution)/shard_map/ppermute | solution.py:31
  82.1 31.3 %copy-start.2 = (f32[3,16,128]{2,1,0:T(8,128)S(1)}, f32[3,16,128]{2,1,0:T(8,128)}, u32[]{:S(2)}) copy-start(f32[3,16,128]{2,1,0:T(8,128)} %get-tuple-element.4) | copy-start | bytes 73732
  83.0 10.7 %collective-permute-start.8 = (f32[3,1,8,128]{3,2,1,0:T(8,128)S(1)}, f32[3,1,8,128]{3,2,1,0:T(8,128)S(1)}, u32[]{:S(2)}, u32[]{:S(2)}) collective-permute-start(f32[3,1,8,128]{3,2,1,0:T(8,128)S(1)} %get-tuple-element.38), channel_id=1, source_target_pairs={{0,4},{4,8},{8,12},{12,16},{16,20},{20,24},{24,28},{28,32},{32,36}... | collective-permute-start | bytes 36872 | tf_op jit(solution)/shard_map/ppermute | solution.py:30
  84.9 9.6 %collective-permute-start.9 = (f32[3,1,8,128]{3,2,1,0:T(8,128)S(1)}, f32[3,1,8,128]{3,2,1,0:T(8,128)S(1)}, u32[]{:S(2)}, u32[]{:S(2)}) collective-permute-start(f32[3,1,8,128]{3,2,1,0:T(8,128)S(1)} %get-tuple-element.39), channel_id=1, source_target_pairs={{4,0},{8,4},{12,8},{16,12},{20,16},{24,20},{28,24},{32,28},{36,32}... | collective-permute-start | bytes 36872 | tf_op jit(solution)/shard_map/ppermute | solution.py:31
  94.5 4.3 %collective-permute-start.10 = (f32[3,4,1,128]{3,2,1,0:T(1,128)S(1)}, f32[3,4,1,128]{3,2,1,0:T(1,128)S(1)}, u32[]{:S(2)}, u32[]{:S(2)}) collective-permute-start(f32[3,4,1,128]{3,2,1,0:T(1,128)S(1)} %get-tuple-element.30), channel_id=1, source_target_pairs={{0,1},{1,2},{2,3},{4,5},{5,6},{6,7},{8,9},{9,10},{10,11},{12,13},{... | collective-permute-start | bytes 18440 | tf_op jit(solution)/shard_map/ppermute | solution.py:30
  96.8 6.5 %collective-permute-start.11 = (f32[3,4,1,128]{3,2,1,0:T(1,128)S(1)}, f32[3,4,1,128]{3,2,1,0:T(1,128)S(1)}, u32[]{:S(2)}, u32[]{:S(2)}) collective-permute-start(f32[3,4,1,128]{3,2,1,0:T(1,128)S(1)} %get-tuple-element.31), channel_id=1, source_target_pairs={{1,0},{2,1},{3,2},{5,4},{6,5},{7,6},{9,8},{10,9},{11,10},{13,12},{... | collective-permute-start | bytes 18440 | tf_op jit(solution)/shard_map/ppermute | solution.py:31
  103.9 39.3 %copy-start.1 = (f32[3,2,8,128]{3,2,1,0:T(8,128)S(1)}, f32[3,2,8,128]{3,2,1,0:T(8,128)}, u32[]{:S(2)}) copy-start(f32[3,2,8,128]{3,2,1,0:T(8,128)} %param.7) | copy-start | bytes 73732
  114.3 10.7 %collective-permute-start.12 = (f32[3,1,8,128]{3,2,1,0:T(8,128)S(1)}, f32[3,1,8,128]{3,2,1,0:T(8,128)S(1)}, u32[]{:S(2)}, u32[]{:S(2)}) collective-permute-start(f32[3,1,8,128]{3,2,1,0:T(8,128)S(1)} %get-tuple-element.36), channel_id=1, source_target_pairs={{0,4},{4,8},{8,12},{12,16},{16,20},{20,24},{24,28},{28,32},{32,36}... | collective-permute-start | bytes 36872 | tf_op jit(solution)/shard_map/ppermute | solution.py:30
  116.2 9.6 %collective-permute-start.13 = (f32[3,1,8,128]{3,2,1,0:T(8,128)S(1)}, f32[3,1,8,128]{3,2,1,0:T(8,128)S(1)}, u32[]{:S(2)}, u32[]{:S(2)}) collective-permute-start(f32[3,1,8,128]{3,2,1,0:T(8,128)S(1)} %get-tuple-element.37), channel_id=1, source_target_pairs={{4,0},{8,4},{12,8},{16,12},{20,16},{24,20},{28,24},{32,28},{36,32}... | collective-permute-start | bytes 36872 | tf_op jit(solution)/shard_map/ppermute | solution.py:31
  125.8 4.4 %collective-permute-start.14 = (f32[3,4,1,128]{3,2,1,0:T(1,128)S(1)}, f32[3,4,1,128]{3,2,1,0:T(1,128)S(1)}, u32[]{:S(2)}, u32[]{:S(2)}) collective-permute-start(f32[3,4,1,128]{3,2,1,0:T(1,128)S(1)} %get-tuple-element.28), channel_id=1, source_target_pairs={{0,1},{1,2},{2,3},{4,5},{5,6},{6,7},{8,9},{9,10},{10,11},{12,13},{... | collective-permute-start | bytes 18440 | tf_op jit(solution)/shard_map/ppermute | solution.py:30
  128.0 6.5 %collective-permute-start.15 = (f32[3,4,1,128]{3,2,1,0:T(1,128)S(1)}, f32[3,4,1,128]{3,2,1,0:T(1,128)S(1)}, u32[]{:S(2)}, u32[]{:S(2)}) collective-permute-start(f32[3,4,1,128]{3,2,1,0:T(1,128)S(1)} %get-tuple-element.29), channel_id=1, source_target_pairs={{1,0},{2,1},{3,2},{5,4},{6,5},{7,6},{9,8},{10,9},{11,10},{13,12},{... | collective-permute-start | bytes 18440 | tf_op jit(solution)/shard_map/ppermute | solution.py:31
  144.2 10.0 %collective-permute-start.16 = (f32[8,8,128]{2,1,0:T(8,128)S(1)}, f32[8,8,128]{2,1,0:T(8,128)S(1)}, u32[]{:S(2)}, u32[]{:S(2)}) collective-permute-start(f32[8,8,128]{2,1,0:T(8,128)S(1)} %pad_maximum_fusion.9), channel_id=1, source_target_pairs={{0,4},{4,8},{8,12},{12,16},{16,20},{20,24},{24,28},{28,32},{32,36}... | collective-permute-start | bytes 98312 | tf_op jit(solution)/shard_map/ppermute | solution.py:39

commit v13 on v10

--- a/solution.py
+++ b/solution.py
@@ -148,7 +148,9 @@
                 out_ref[k, pl.ds(block, 1), pl.ds(first, CHUNK)] = flipped[k : k + 1, :]
             return carry
 
-        lax.fori_loop(0, block_count * chunk_count if kind == "jacobi" else chunk_count, body, 0)
+        lax.fori_loop(
+            0, block_count * chunk_count if kind == "jacobi" else chunk_count, body, 0, unroll=True
+        )
 
     out_shape = jax.ShapeDtypeStruct((output_count, block_count, slot_count), jnp.float32)
     whole = [

time: 157 us -> 154 us (0.981)
  Pallas kernels: 45.5 us -> 42.2 us
    pallas_call x2, Pallas kernels: 16.3 us -> 12.9 us  [pair_pass(): pl.pallas_call(kernel, out_shape=out_shape)]
where the time goes in v13:
time: 154 us; the launch traced here: 152 us
  starting transfers between devices  66.6 us (43%)
  Pallas kernels  42.2 us (27%)
  waiting for transfers between devices  24.1 us (16%)
  other arithmetic  14.8 us (10%)
  local copies, waits for them, and re-layouts  3.57 us (2%)
    ppermute x8, starting transfers between devices, with_halo(): after = lax.ppermute(initial, axis, down)  42.6 us
    ppermute x8, starting transfers between devices, with_halo(): before = lax.ppermute(last, axis, up)  22.1 us
    ppermute x8, waiting for transfers between devices, with_halo(): after = lax.ppermute(initial, axis, down)  16 us
    pallas_call x1, Pallas kernels, pair_pass(): pl.pallas_call(kernel, out_shape=out_shape, grid=grid, in_specs=whole, ou...  14.8 us
    pallas_call x1, Pallas kernels, pair_pass(): pl.pallas_call(kernel, out_shape=(out_shape, weight_shape), grid=grid, in...  14.4 us
    pallas_call x2, Pallas kernels, pair_pass(): pl.pallas_call(kernel, out_shape=out_shape)  12.9 us
    ppermute x1, waiting for transfers between devices, from_behind(): return lax.ppermute(block, axis, route)  8.11 us
  transfers between devices with their start and end apart: 17, of which 8 were waited for; matrix products, arithmetic and copies ran while one was open for 3% of the time, Pallas kernels for 0%

profile of v13, /device:TPU:3, one launch (start us, length us, event | category | flops | bytes accessed | tf_op | source)
XLA Modules:
  0.0 152.4 jit_solution(1468884676344426455)
XLA Ops:
  2.2 3.5 %collective-permute-start = (f32[7,1,8,128]{3,2,1,0:T(8,128)S(1)}, f32[7,1,8,128]{3,2,1,0:T(8,128)S(1)}, u32[]{:S(2)}, u32[]{:S(2)}) collective-permute-start(f32[7,1,8,128]{3,2,1,0:T(8,128)S(1)} %get-tuple-element.19), channel_id=1, source_target_pairs={{0,4},{4,8},{8,12},{12,16},{16,20},{20,24},{24,28},{28,32},{32,36}... | collective-permute-start | bytes 86024 | tf_op jit(solution)/shard_map/ppermute | solution.py:30
  5.8 8.3 %collective-permute-start.1 = (f32[7,1,8,128]{3,2,1,0:T(8,128)S(1)}, f32[7,1,8,128]{3,2,1,0:T(8,128)S(1)}, u32[]{:S(2)}, u32[]{:S(2)}) collective-permute-start(f32[7,1,8,128]{3,2,1,0:T(8,128)S(1)} %get-tuple-element.20), channel_id=1, source_target_pairs={{4,0},{8,4},{12,8},{16,12},{20,16},{24,20},{28,24},{32,28},{36,32}... | collective-permute-start | bytes 86024 | tf_op jit(solution)/shard_map/ppermute | solution.py:31
  14.1 1.0 collective-permute-done.1
  15.0 0.8 pad_maximum_fusion.15
  15.9 5.5 %collective-permute-start.2 = (f32[7,4,1,128]{3,2,1,0:T(1,128)S(1)}, f32[7,4,1,128]{3,2,1,0:T(1,128)S(1)}, u32[]{:S(2)}, u32[]{:S(2)}) collective-permute-start(f32[7,4,1,128]{3,2,1,0:T(1,128)S(1)} %get-tuple-element.14), channel_id=1, source_target_pairs={{0,1},{1,2},{2,3},{4,5},{5,6},{6,7},{8,9},{9,10},{10,11},{12,13},{... | collective-permute-start | bytes 43016 | tf_op jit(solution)/shard_map/ppermute | solution.py:30
  21.4 1.9 %collective-permute-start.3 = (f32[7,4,1,128]{3,2,1,0:T(1,128)S(1)}, f32[7,4,1,128]{3,2,1,0:T(1,128)S(1)}, u32[]{:S(2)}, u32[]{:S(2)}) collective-permute-start(f32[7,4,1,128]{3,2,1,0:T(1,128)S(1)} %get-tuple-element.15), channel_id=1, source_target_pairs={{1,0},{2,1},{3,2},{5,4},{6,5},{7,6},{9,8},{10,9},{11,10},{13,12},{... | collective-permute-start | bytes 43016 | tf_op jit(solution)/shard_map/ppermute | solution.py:31
  23.3 1.4 maximum_bitcast_fusion.target_ref
  25.4 2.5 %collective-permute-done.3 = f32[7,4,1,128]{3,2,1,0:T(1,128)S(1)} collective-permute-done((f32[7,4,1,128]{3,2,1,0:T(1,128)S(1)}, f32[7,4,1,128]{3,2,1,0:T(1,128)S(1)}, u32[]{:S(2)}, u32[]{:S(2)}) %collective-permute-start.3) | collective-permute-done | bytes 14368 | tf_op jit(solution)/shard_map/ppermute | solution.py:31
  30.2 14.8 %shard_map.86 = f32[2,16,128]{2,1,0:T(8,128)} custom-call(f32[6,16,128]{2,1,0:T(8,128)} %maximum_bitcast_fusion.target_ref, f32[6,40,128]{2,1,0:T(8,128)} %copy.11.source_ref), custom_call_target="tpu_custom_call" | custom-call | tf_op jit(solution)/shard_map/pallas_call | solution.py:177
  46.6 1.9 %collective-permute-start.4 = (f32[3,1,8,128]{3,2,1,0:T(8,128)S(1)}, f32[3,1,8,128]{3,2,1,0:T(8,128)S(1)}, u32[]{:S(2)}, u32[]{:S(2)}) collective-permute-start(f32[3,1,8,128]{3,2,1,0:T(8,128)S(1)} %get-tuple-element.39), channel_id=1, source_target_pairs={{0,4},{4,8},{8,12},{12,16},{16,20},{20,24},{24,28},{28,32},{32,36}... | collective-permute-start | bytes 36872 | tf_op jit(solution)/shard_map/ppermute | solution.py:30
  48.6 8.8 %collective-permute-start.5 = (f32[3,1,8,128]{3,2,1,0:T(8,128)S(1)}, f32[3,1,8,128]{3,2,1,0:T(8,128)S(1)}, u32[]{:S(2)}, u32[]{:S(2)}) collective-permute-start(f32[3,1,8,128]{3,2,1,0:T(8,128)S(1)} %get-tuple-element.40), channel_id=1, source_target_pairs={{4,0},{8,4},{12,8},{16,12},{20,16},{24,20},{28,24},{32,28},{36,32}... | collective-permute-start | bytes 36872 | tf_op jit(solution)/shard_map/ppermute | solution.py:31
  58.2 2.9 %collective-permute-start.6 = (f32[3,4,1,128]{3,2,1,0:T(1,128)S(1)}, f32[3,4,1,128]{3,2,1,0:T(1,128)S(1)}, u32[]{:S(2)}, u32[]{:S(2)}) collective-permute-start(f32[3,4,1,128]{3,2,1,0:T(1,128)S(1)} %get-tuple-element.31), channel_id=1, source_target_pairs={{0,1},{1,2},{2,3},{4,5},{5,6},{6,7},{8,9},{9,10},{10,11},{12,13},{... | collective-permute-start | bytes 18440 | tf_op jit(solution)/shard_map/ppermute | solution.py:30
  61.1 1.9 %collective-permute-start.7 = (f32[3,4,1,128]{3,2,1,0:T(1,128)S(1)}, f32[3,4,1,128]{3,2,1,0:T(1,128)S(1)}, u32[]{:S(2)}, u32[]{:S(2)}) collective-permute-start(f32[3,4,1,128]{3,2,1,0:T(1,128)S(1)} %get-tuple-element.32), channel_id=1, source_target_pairs={{1,0},{2,1},{3,2},{5,4},{6,5},{7,6},{9,8},{10,9},{11,10},{13,12},{... | collective-permute-start | bytes 18440 | tf_op jit(solution)/shard_map/ppermute | solution.py:31
  63.0 1.4 pad_maximum_fusion.8.target_ref
  64.4 3.2 %collective-permute-done.7 = f32[3,4,1,128]{3,2,1,0:T(1,128)S(1)} collective-permute-done((f32[3,4,1,128]{3,2,1,0:T(1,128)S(1)}, f32[3,4,1,128]{3,2,1,0:T(1,128)S(1)}, u32[]{:S(2)}, u32[]{:S(2)}) %collective-permute-start.7) | collective-permute-done | bytes 6176 | tf_op jit(solution)/shard_map/ppermute | solution.py:31
  68.4 14.4 %shard_map.87 = (f32[4,16,128]{2,1,0:T(8,128)}, f32[144,128,128]{2,1,0:T(8,128)}) custom-call(f32[5,16,128]{2,1,0:T(8,128)} %pad_maximum_fusion.8.target_ref, f32[6,40,128]{2,1,0:T(8,128)} %copy.13.source_ref), custom_call_target="tpu_custom_call" | custom-call | tf_op jit(solution)/shard_map/pallas_call | solution.py:167
  82.8 0.9 fusion.24
  83.7 1.9 %collective-permute-start.8 = (f32[3,1,8,128]{3,2,1,0:T(8,128)S(1)}, f32[3,1,8,128]{3,2,1,0:T(8,128)S(1)}, u32[]{:S(2)}, u32[]{:S(2)}) collective-permute-start(f32[3,1,8,128]{3,2,1,0:T(8,128)S(1)} %get-tuple-element.37), channel_id=1, source_target_pairs={{0,4},{4,8},{8,12},{12,16},{16,20},{20,24},{24,28},{28,32},{32,36}... | collective-permute-start | bytes 36872 | tf_op jit(solution)/shard_map/ppermute | solution.py:30
  85.6 8.7 %collective-permute-start.9 = (f32[3,1,8,128]{3,2,1,0:T(8,128)S(1)}, f32[3,1,8,128]{3,2,1,0:T(8,128)S(1)}, u32[]{:S(2)}, u32[]{:S(2)}) collective-permute-start(f32[3,1,8,128]{3,2,1,0:T(8,128)S(1)} %get-tuple-element.38), channel_id=1, source_target_pairs={{4,0},{8,4},{12,8},{16,12},{20,16},{24,20},{28,24},{32,28},{36,32}... | collective-permute-start | bytes 36872 | tf_op jit(solution)/shard_map/ppermute | solution.py:31
  95.2 2.2 %collective-permute-start.10 = (f32[3,4,1,128]{3,2,1,0:T(1,128)S(1)}, f32[3,4,1,128]{3,2,1,0:T(1,128)S(1)}, u32[]{:S(2)}, u32[]{:S(2)}) collective-permute-start(f32[3,4,1,128]{3,2,1,0:T(1,128)S(1)} %get-tuple-element.29), channel_id=1, source_target_pairs={{0,1},{1,2},{2,3},{4,5},{5,6},{6,7},{8,9},{9,10},{10,11},{12,13},{... | collective-permute-start | bytes 18440 | tf_op jit(solution)/shard_map/ppermute | solution.py:30
  97.4 2.1 %collective-permute-start.11 = (f32[3,4,1,128]{3,2,1,0:T(1,128)S(1)}, f32[3,4,1,128]{3,2,1,0:T(1,128)S(1)}, u32[]{:S(2)}, u32[]{:S(2)}) collective-permute-start(f32[3,4,1,128]{3,2,1,0:T(1,128)S(1)} %get-tuple-element.30), channel_id=1, source_target_pairs={{1,0},{2,1},{3,2},{5,4},{6,5},{7,6},{9,8},{10,9},{11,10},{13,12},{... | collective-permute-start | bytes 18440 | tf_op jit(solution)/shard_map/ppermute | solution.py:31
  100.4 3.5 %collective-permute-done.11 = f32[3,4,1,128]{3,2,1,0:T(1,128)S(1)} collective-permute-done((f32[3,4,1,128]{3,2,1,0:T(1,128)S(1)}, f32[3,4,1,128]{3,2,1,0:T(1,128)S(1)}, u32[]{:S(2)}, u32[]{:S(2)}) %collective-permute-start.11) | collective-permute-done | bytes 6176 | tf_op jit(solution)/shard_map/ppermute | solution.py:31
  104.6 6.5 %shard_map.88 = f32[3,16,128]{2,1,0:T(8,128)} custom-call(f32[1,16,128]{2,1,0:T(8,128)} %copy-done.3, f32[3,40,128]{2,1,0:T(8,128)} %broadcast_multiply_fusion.1.source_ref, f32[144,128,128]{2,1,0:T(8,128)} %get-tuple-element.5.refs_0_), custom_call_target="tpu_custom_call" | custom-call | tf_op jit(solution)/shard_map/pallas_call | solution.py:175
  111.0 0.8 fusion.22
  111.9 1.9 %collective-permute-start.12 = (f32[3,1,8,128]{3,2,1,0:T(8,128)S(1)}, f32[3,1,8,128]{3,2,1,0:T(8,128)S(1)}, u32[]{:S(2)}, u32[]{:S(2)}) collective-permute-start(f32[3,1,8,128]{3,2,1,0:T(8,128)S(1)} %get-tuple-element.35), channel_id=1, source_target_pairs={{0,4},{4,8},{8,12},{12,16},{16,20},{20,24},{24,28},{28,32},{32,36}... | collective-permute-start | bytes 36872 | tf_op jit(solution)/shard_map/ppermute | solution.py:30
  113.8 8.7 %collective-permute-start.13 = (f32[3,1,8,128]{3,2,1,0:T(8,128)S(1)}, f32[3,1,8,128]{3,2,1,0:T(8,128)S(1)}, u32[]{:S(2)}, u32[]{:S(2)}) collective-permute-start(f32[3,1,8,128]{3,2,1,0:T(8,128)S(1)} %get-tuple-element.36), channel_id=1, source_target_pairs={{4,0},{8,4},{12,8},{16,12},{20,16},{24,20},{28,24},{32,28},{36,32}... | collective-permute-start | bytes 36872 | tf_op jit(solution)/shard_map/ppermute | solution.py:31
  123.4 2.2 %collective-permute-start.14 = (f32[3,4,1,128]{3,2,1,0:T(1,128)S(1)}, f32[3,4,1,128]{3,2,1,0:T(1,128)S(1)}, u32[]{:S(2)}, u32[]{:S(2)}) collective-permute-start(f32[3,4,1,128]{3,2,1,0:T(1,128)S(1)} %get-tuple-element.27), channel_id=1, source_target_pairs={{0,1},{1,2},{2,3},{4,5},{5,6},{6,7},{8,9},{9,10},{10,11},{12,13},{... | collective-permute-start | bytes 18440 | tf_op jit(solution)/shard_map/ppermute | solution.py:30
  125.6 2.1 %collective-permute-start.15 = (f32[3,4,1,128]{3,2,1,0:T(1,128)S(1)}, f32[3,4,1,128]{3,2,1,0:T(1,128)S(1)}, u32[]{:S(2)}, u32[]{:S(2)}) collective-permute-start(f32[3,4,1,128]{3,2,1,0:T(1,128)S(1)} %get-tuple-element.28), channel_id=1, source_target_pairs={{1,0},{2,1},{3,2},{5,4},{6,5},{7,6},{9,8},{10,9},{11,10},{13,12},{... | collective-permute-start | bytes 18440 | tf_op jit(solution)/shard_map/ppermute | solution.py:31
  127.7 4.3 %collective-permute-done.15 = f32[3,4,1,128]{3,2,1,0:T(1,128)S(1)} collective-permute-done((f32[3,4,1,128]{3,2,1,0:T(1,128)S(1)}, f32[3,4,1,128]{3,2,1,0:T(1,128)S(1)}, u32[]{:S(2)}, u32[]{:S(2)}) %collective-permute-start.15) | collective-permute-done | bytes 6176 | tf_op jit(solution)/shard_map/ppermute | solution.py:31
  132.7 6.5 %shard_map.89 = f32[3,16,128]{2,1,0:T(8,128)} custom-call(f32[1,16,128]{2,1,0:T(8,128)} %copy-done.3, f32[3,40,128]{2,1,0:T(8,128)} %broadcast_multiply_fusion.source_ref, f32[144,128,128]{2,1,0:T(8,128)} %get-tuple-element.5.refs_0_), custom_call_target="tpu_custom_call" | custom-call | tf_op jit(solution)/shard_map/pallas_call | solution.py:175
  140.1 1.9 %collective-permute-start.16 = (f32[8,8,128]{2,1,0:T(8,128)S(1)}, f32[8,8,128]{2,1,0:T(8,128)S(1)}, u32[]{:S(2)}, u32[]{:S(2)}) collective-permute-start(f32[8,8,128]{2,1,0:T(8,128)S(1)} %pad_maximum_fusion.9), channel_id=1, source_target_pairs={{0,4},{4,8},{8,12},{12,16},{16,20},{20,24},{24,28},{28,32},{32,36}... | collective-permute-start | bytes 98312 | tf_op jit(solution)/shard_map/ppermute | solution.py:39
  142.0 8.1 %collective-permute-done.16 = f32[8,8,128]{2,1,0:T(8,128)S(1)} collective-permute-done((f32[8,8,128]{2,1,0:T(8,128)S(1)}, f32[8,8,128]{2,1,0:T(8,128)S(1)}, u32[]{:S(2)}, u32[]{:S(2)}) %collective-permute-start.16) | collective-permute-done | bytes 32800 | tf_op jit(solution)/shard_map/ppermute | solution.py:39
  (90 shorter events, 14.7 us)
Async XLA Ops:
  0.6 110.4 %copy-start.5 = (f32[3]{0:T(128)S(1)}, f32[3]{0:T(128)}, u32[]{:S(2)}) copy-start(f32[3]{0:T(128)} %constant.56.clone) | copy-start | bytes 40
  0.6 121.9 %copy-start.4 = (s32[2,8]{1,0:T(2,128)S(1)}, s32[2,8]{1,0:T(2,128)}, u32[]{:S(2)}) copy-start(s32[2,8]{1,0:T(2,128)} %param.11) | copy-start | bytes 196
  0.7 110.4 %copy-start = (f32[3,2,8,128]{3,2,1,0:T(8,128)S(1)}, f32[3,2,8,128]{3,2,1,0:T(8,128)}, u32[]{:S(2)}) copy-start(f32[3,2,8,128]{3,2,1,0:T(8,128)} %param.8) | copy-start | bytes 73732
  0.7 121.9 %copy-start.6 = (s32[2,8]{1,0:T(2,128)S(1)}, s32[2,8]{1,0:T(2,128)}, u32[]{:S(2)}) copy-start(s32[2,8]{1,0:T(2,128)} %param.12) | copy-start | bytes 196
  2.2 11.8 %collective-permute-start = (f32[7,1,8,128]{3,2,1,0:T(8,128)S(1)}, f32[7,1,8,128]{3,2,1,0:T(8,128)S(1)}, u32[]{:S(2)}, u32[]{:S(2)}) collective-permute-start(f32[7,1,8,128]{3,2,1,0:T(8,128)S(1)} %get-tuple-element.19), channel_id=1, source_target_pairs={{0,4},{4,8},{8,12},{12,16},{16,20},{20,24},{24,28},{28,32},{32,36}... | collective-permute-start | bytes 86024 | tf_op jit(solution)/shard_map/ppermute | solution.py:30
  5.8 9.3 %collective-permute-start.1 = (f32[7,1,8,128]{3,2,1,0:T(8,128)S(1)}, f32[7,1,8,128]{3,2,1,0:T(8,128)S(1)}, u32[]{:S(2)}, u32[]{:S(2)}) collective-permute-start(f32[7,1,8,128]{3,2,1,0:T(8,128)S(1)} %get-tuple-element.20), channel_id=1, source_target_pairs={{4,0},{8,4},{12,8},{16,12},{20,16},{24,20},{28,24},{32,28},{36,32}... | collective-permute-start | bytes 86024 | tf_op jit(solution)/shard_map/ppermute | solution.py:31
  15.9 9.5 %collective-permute-start.2 = (f32[7,4,1,128]{3,2,1,0:T(1,128)S(1)}, f32[7,4,1,128]{3,2,1,0:T(1,128)S(1)}, u32[]{:S(2)}, u32[]{:S(2)}) collective-permute-start(f32[7,4,1,128]{3,2,1,0:T(1,128)S(1)} %get-tuple-element.14), channel_id=1, source_target_pairs={{0,1},{1,2},{2,3},{4,5},{5,6},{6,7},{8,9},{9,10},{10,11},{12,13},{... | collective-permute-start | bytes 43016 | tf_op jit(solution)/shard_map/ppermute | solution.py:30
  21.4 6.5 %collective-permute-start.3 = (f32[7,4,1,128]{3,2,1,0:T(1,128)S(1)}, f32[7,4,1,128]{3,2,1,0:T(1,128)S(1)}, u32[]{:S(2)}, u32[]{:S(2)}) collective-permute-start(f32[7,4,1,128]{3,2,1,0:T(1,128)S(1)} %get-tuple-element.15), channel_id=1, source_target_pairs={{1,0},{2,1},{3,2},{5,4},{6,5},{7,6},{9,8},{10,9},{11,10},{13,12},{... | collective-permute-start | bytes 43016 | tf_op jit(solution)/shard_map/ppermute | solution.py:31
  46.6 57.9 %copy-start.3 = (f32[1,16,128]{2,1,0:T(8,128)}, f32[1,16,128]{2,1,0:T(8,128)S(1)}, u32[]{:S(2)}) copy-start(f32[1,16,128]{2,1,0:T(8,128)S(1)} %get-tuple-element.34.target_ref) | copy-start | bytes 24580
  46.6 11.5 %collective-permute-start.4 = (f32[3,1,8,128]{3,2,1,0:T(8,128)S(1)}, f32[3,1,8,128]{3,2,1,0:T(8,128)S(1)}, u32[]{:S(2)}, u32[]{:S(2)}) collective-permute-start(f32[3,1,8,128]{3,2,1,0:T(8,128)S(1)} %get-tuple-element.39), channel_id=1, source_target_pairs={{0,4},{4,8},{8,12},{12,16},{16,20},{20,24},{24,28},{28,32},{32,36}... | collective-permute-start | bytes 36872 | tf_op jit(solution)/shard_map/ppermute | solution.py:30
  48.6 9.6 %collective-permute-start.5 = (f32[3,1,8,128]{3,2,1,0:T(8,128)S(1)}, f32[3,1,8,128]{3,2,1,0:T(8,128)S(1)}, u32[]{:S(2)}, u32[]{:S(2)}) collective-permute-start(f32[3,1,8,128]{3,2,1,0:T(8,128)S(1)} %get-tuple-element.40), channel_id=1, source_target_pairs={{4,0},{8,4},{12,8},{16,12},{20,16},{24,20},{28,24},{32,28},{36,32}... | collective-permute-start | bytes 36872 | tf_op jit(solution)/shard_map/ppermute | solution.py:31
  58.2 6.2 %collective-permute-start.6 = (f32[3,4,1,128]{3,2,1,0:T(1,128)S(1)}, f32[3,4,1,128]{3,2,1,0:T(1,128)S(1)}, u32[]{:S(2)}, u32[]{:S(2)}) collective-permute-start(f32[3,4,1,128]{3,2,1,0:T(1,128)S(1)} %get-tuple-element.31), channel_id=1, source_target_pairs={{0,1},{1,2},{2,3},{4,5},{5,6},{6,7},{8,9},{9,10},{10,11},{12,13},{... | collective-permute-start | bytes 18440 | tf_op jit(solution)/shard_map/ppermute | solution.py:30
  61.1 6.5 %collective-permute-start.7 = (f32[3,4,1,128]{3,2,1,0:T(1,128)S(1)}, f32[3,4,1,128]{3,2,1,0:T(1,128)S(1)}, u32[]{:S(2)}, u32[]{:S(2)}) collective-permute-start(f32[3,4,1,128]{3,2,1,0:T(1,128)S(1)} %get-tuple-element.32), channel_id=1, source_target_pairs={{1,0},{2,1},{3,2},{5,4},{6,5},{7,6},{9,8},{10,9},{11,10},{13,12},{... | collective-permute-start | bytes 18440 | tf_op jit(solution)/shard_map/ppermute | solution.py:31
  82.8 28.2 %copy-start.2 = (f32[4,16,128]{2,1,0:T(8,128)S(1)}, f32[4,16,128]{2,1,0:T(8,128)}, u32[]{:S(2)}) copy-start(f32[4,16,128]{2,1,0:T(8,128)} %get-tuple-element.4) | copy-start | bytes 98308
  83.7 10.7 %collective-permute-start.8 = (f32[3,1,8,128]{3,2,1,0:T(8,128)S(1)}, f32[3,1,8,128]{3,2,1,0:T(8,128)S(1)}, u32[]{:S(2)}, u32[]{:S(2)}) collective-permute-start(f32[3,1,8,128]{3,2,1,0:T(8,128)S(1)} %get-tuple-element.37), channel_id=1, source_target_pairs={{0,4},{4,8},{8,12},{12,16},{16,20},{20,24},{24,28},{28,32},{32,36}... | collective-permute-start | bytes 36872 | tf_op jit(solution)/shard_map/ppermute | solution.py:30
  85.6 9.6 %collective-permute-start.9 = (f32[3,1,8,128]{3,2,1,0:T(8,128)S(1)}, f32[3,1,8,128]{3,2,1,0:T(8,128)S(1)}, u32[]{:S(2)}, u32[]{:S(2)}) collective-permute-start(f32[3,1,8,128]{3,2,1,0:T(8,128)S(1)} %get-tuple-element.38), channel_id=1, source_target_pairs={{4,0},{8,4},{12,8},{16,12},{20,16},{24,20},{28,24},{32,28},{36,32}... | collective-permute-start | bytes 36872 | tf_op jit(solution)/shard_map/ppermute | solution.py:31
  95.2 5.2 %collective-permute-start.10 = (f32[3,4,1,128]{3,2,1,0:T(1,128)S(1)}, f32[3,4,1,128]{3,2,1,0:T(1,128)S(1)}, u32[]{:S(2)}, u32[]{:S(2)}) collective-permute-start(f32[3,4,1,128]{3,2,1,0:T(1,128)S(1)} %get-tuple-element.29), channel_id=1, source_target_pairs={{0,1},{1,2},{2,3},{4,5},{5,6},{6,7},{8,9},{9,10},{10,11},{12,13},{... | collective-permute-start | bytes 18440 | tf_op jit(solution)/shard_map/ppermute | solution.py:30
  97.4 6.5 %collective-permute-start.11 = (f32[3,4,1,128]{3,2,1,0:T(1,128)S(1)}, f32[3,4,1,128]{3,2,1,0:T(1,128)S(1)}, u32[]{:S(2)}, u32[]{:S(2)}) collective-permute-start(f32[3,4,1,128]{3,2,1,0:T(1,128)S(1)} %get-tuple-element.30), channel_id=1, source_target_pairs={{1,0},{2,1},{3,2},{5,4},{6,5},{7,6},{9,8},{10,9},{11,10},{13,12},{... | collective-permute-start | bytes 18440 | tf_op jit(solution)/shard_map/ppermute | solution.py:31
  104.6 34.6 %copy-start.1 = (f32[3,2,8,128]{3,2,1,0:T(8,128)S(1)}, f32[3,2,8,128]{3,2,1,0:T(8,128)}, u32[]{:S(2)}) copy-start(f32[3,2,8,128]{3,2,1,0:T(8,128)} %param.7) | copy-start | bytes 73732
  111.9 10.7 %collective-permute-start.12 = (f32[3,1,8,128]{3,2,1,0:T(8,128)S(1)}, f32[3,1,8,128]{3,2,1,0:T(8,128)S(1)}, u32[]{:S(2)}, u32[]{:S(2)}) collective-permute-start(f32[3,1,8,128]{3,2,1,0:T(8,128)S(1)} %get-tuple-element.35), channel_id=1, source_target_pairs={{0,4},{4,8},{8,12},{12,16},{16,20},{20,24},{24,28},{28,32},{32,36}... | collective-permute-start | bytes 36872 | tf_op jit(solution)/shard_map/ppermute | solution.py:30
  113.8 9.6 %collective-permute-start.13 = (f32[3,1,8,128]{3,2,1,0:T(8,128)S(1)}, f32[3,1,8,128]{3,2,1,0:T(8,128)S(1)}, u32[]{:S(2)}, u32[]{:S(2)}) collective-permute-start(f32[3,1,8,128]{3,2,1,0:T(8,128)S(1)} %get-tuple-element.36), channel_id=1, source_target_pairs={{4,0},{8,4},{12,8},{16,12},{20,16},{24,20},{28,24},{32,28},{36,32}... | collective-permute-start | bytes 36872 | tf_op jit(solution)/shard_map/ppermute | solution.py:31
  123.4 4.4 %collective-permute-start.14 = (f32[3,4,1,128]{3,2,1,0:T(1,128)S(1)}, f32[3,4,1,128]{3,2,1,0:T(1,128)S(1)}, u32[]{:S(2)}, u32[]{:S(2)}) collective-permute-start(f32[3,4,1,128]{3,2,1,0:T(1,128)S(1)} %get-tuple-element.27), channel_id=1, source_target_pairs={{0,1},{1,2},{2,3},{4,5},{5,6},{6,7},{8,9},{9,10},{10,11},{12,13},{... | collective-permute-start | bytes 18440 | tf_op jit(solution)/shard_map/ppermute | solution.py:30
  125.6 6.5 %collective-permute-start.15 = (f32[3,4,1,128]{3,2,1,0:T(1,128)S(1)}, f32[3,4,1,128]{3,2,1,0:T(1,128)S(1)}, u32[]{:S(2)}, u32[]{:S(2)}) collective-permute-start(f32[3,4,1,128]{3,2,1,0:T(1,128)S(1)} %get-tuple-element.28), channel_id=1, source_target_pairs={{1,0},{2,1},{3,2},{5,4},{6,5},{7,6},{9,8},{10,9},{11,10},{13,12},{... | collective-permute-start | bytes 18440 | tf_op jit(solution)/shard_map/ppermute | solution.py:31
  140.1 10.0 %collective-permute-start.16 = (f32[8,8,128]{2,1,0:T(8,128)S(1)}, f32[8,8,128]{2,1,0:T(8,128)S(1)}, u32[]{:S(2)}, u32[]{:S(2)}) collective-permute-start(f32[8,8,128]{2,1,0:T(8,128)S(1)} %pad_maximum_fusion.9), channel_id=1, source_target_pairs={{0,4},{4,8},{8,12},{12,16},{16,20},{20,24},{24,28},{28,32},{32,36}... | collective-permute-start | bytes 98312 | tf_op jit(solution)/shard_map/ppermute | solution.py:39

commit v14 on v13

--- a/solution.py
+++ b/solution.py
@@ -87,10 +87,10 @@
         else:
             (out_ref,) = refs
 
-        grid_block = None if kind == "jacobi" else pl.program_id(0)
+        grid_block = None if kind != "force" else pl.program_id(0)
 
         def body(step, carry):
-            if kind == "jacobi":
+            if kind != "force":
                 block = step // chunk_count
                 first = pl.multiple_of((step % chunk_count) * CHUNK, CHUNK)
             else:
@@ -149,7 +149,7 @@
             return carry
 
         lax.fori_loop(
-            0, block_count * chunk_count if kind == "jacobi" else chunk_count, body, 0, unroll=True
+            0, block_count * chunk_count if kind != "force" else chunk_count, body, 0, unroll=True
         )
 
     out_shape = jax.ShapeDtypeStruct((output_count, block_count, slot_count), jnp.float32)
@@ -174,9 +174,7 @@
     elif kind == "jacobi":
         result = pl.pallas_call(kernel, out_shape=out_shape)(target_cols, source_rows, weights)
     else:
-        result = pl.pallas_call(
-            kernel, out_shape=out_shape, grid=grid, in_specs=whole, out_specs=out_spec
-        )(target_cols, source_rows)
+        result = pl.pallas_call(kernel, out_shape=out_shape)(target_cols, source_rows)
     result = result.reshape(output_count, row_count, col_count, slot_count)
     if kind == "force":
         return result, weights

time: 154 us -> 152 us (0.987)
  Pallas kernels: 42.2 us -> 40.1 us
    pallas_call x1, Pallas kernels: 14.8 us -> 12.8 us  [pair_pass(): pl.pallas_call(kernel, out_shape=out_shape)(target_cols, source_rows)]
where the time goes in v14:
time: 152 us; the launch traced here: 150 us
  starting transfers between devices  66.8 us (44%)
  Pallas kernels  40.1 us (26%)
  waiting for transfers between devices  24.1 us (16%)
  other arithmetic  14.8 us (10%)
  local copies, waits for them, and re-layouts  3.57 us (2%)
    ppermute x8, starting transfers between devices, with_halo(): after = lax.ppermute(initial, axis, down)  42.8 us
    ppermute x8, starting transfers between devices, with_halo(): before = lax.ppermute(last, axis, up)  22.1 us
    ppermute x8, waiting for transfers between devices, with_halo(): after = lax.ppermute(initial, axis, down)  16 us
    pallas_call x1, Pallas kernels, pair_pass(): pl.pallas_call(kernel, out_shape=(out_shape, weight_shape), grid=grid, in...  14.4 us
    pallas_call x2, Pallas kernels, pair_pass(): pl.pallas_call(kernel, out_shape=out_shape)  12.9 us
    pallas_call x1, Pallas kernels, pair_pass(): pl.pallas_call(kernel, out_shape=out_shape)(target_cols, source_rows)  12.8 us
    ppermute x1, waiting for transfers between devices, from_behind(): return lax.ppermute(block, axis, route)  8.11 us
  transfers between devices with their start and end apart: 17, of which 8 were waited for; matrix products, arithmetic and copies ran while one was open for 3% of the time, Pallas kernels for 0%

profile of v14, /device:TPU:3, one launch (start us, length us, event | category | flops | bytes accessed | tf_op | source)
XLA Modules:
  0.0 150.5 jit_solution(11419356348958369206)
XLA Ops:
  2.2 3.5 %collective-permute-start = (f32[7,1,8,128]{3,2,1,0:T(8,128)S(1)}, f32[7,1,8,128]{3,2,1,0:T(8,128)S(1)}, u32[]{:S(2)}, u32[]{:S(2)}) collective-permute-start(f32[7,1,8,128]{3,2,1,0:T(8,128)S(1)} %get-tuple-element.19), channel_id=1, source_target_pairs={{0,4},{4,8},{8,12},{12,16},{16,20},{20,24},{24,28},{28,32},{32,36}... | collective-permute-start | bytes 86024 | tf_op jit(solution)/shard_map/ppermute | solution.py:30
  5.8 8.3 %collective-permute-start.1 = (f32[7,1,8,128]{3,2,1,0:T(8,128)S(1)}, f32[7,1,8,128]{3,2,1,0:T(8,128)S(1)}, u32[]{:S(2)}, u32[]{:S(2)}) collective-permute-start(f32[7,1,8,128]{3,2,1,0:T(8,128)S(1)} %get-tuple-element.20), channel_id=1, source_target_pairs={{4,0},{8,4},{12,8},{16,12},{20,16},{24,20},{28,24},{32,28},{36,32}... | collective-permute-start | bytes 86024 | tf_op jit(solution)/shard_map/ppermute | solution.py:31
  14.1 1.0 collective-permute-done.1
  15.0 0.8 pad_maximum_fusion.15
  15.9 5.5 %collective-permute-start.2 = (f32[7,4,1,128]{3,2,1,0:T(1,128)S(1)}, f32[7,4,1,128]{3,2,1,0:T(1,128)S(1)}, u32[]{:S(2)}, u32[]{:S(2)}) collective-permute-start(f32[7,4,1,128]{3,2,1,0:T(1,128)S(1)} %get-tuple-element.14), channel_id=1, source_target_pairs={{0,1},{1,2},{2,3},{4,5},{5,6},{6,7},{8,9},{9,10},{10,11},{12,13},{... | collective-permute-start | bytes 43016 | tf_op jit(solution)/shard_map/ppermute | solution.py:30
  21.4 1.9 %collective-permute-start.3 = (f32[7,4,1,128]{3,2,1,0:T(1,128)S(1)}, f32[7,4,1,128]{3,2,1,0:T(1,128)S(1)}, u32[]{:S(2)}, u32[]{:S(2)}) collective-permute-start(f32[7,4,1,128]{3,2,1,0:T(1,128)S(1)} %get-tuple-element.15), channel_id=1, source_target_pairs={{1,0},{2,1},{3,2},{5,4},{6,5},{7,6},{9,8},{10,9},{11,10},{13,12},{... | collective-permute-start | bytes 43016 | tf_op jit(solution)/shard_map/ppermute | solution.py:31
  23.3 1.4 maximum_bitcast_fusion.target_ref
  25.4 2.5 %collective-permute-done.3 = f32[7,4,1,128]{3,2,1,0:T(1,128)S(1)} collective-permute-done((f32[7,4,1,128]{3,2,1,0:T(1,128)S(1)}, f32[7,4,1,128]{3,2,1,0:T(1,128)S(1)}, u32[]{:S(2)}, u32[]{:S(2)}) %collective-permute-start.3) | collective-permute-done | bytes 14368 | tf_op jit(solution)/shard_map/ppermute | solution.py:31
  30.2 12.8 %shard_map.86 = f32[2,16,128]{2,1,0:T(8,128)} custom-call(f32[6,16,128]{2,1,0:T(8,128)} %maximum_bitcast_fusion.target_ref, f32[6,40,128]{2,1,0:T(8,128)} %copy.11.source_ref), custom_call_target="tpu_custom_call" | custom-call | tf_op jit(solution)/shard_map/pallas_call | solution.py:177
  44.6 1.9 %collective-permute-start.4 = (f32[3,1,8,128]{3,2,1,0:T(8,128)S(1)}, f32[3,1,8,128]{3,2,1,0:T(8,128)S(1)}, u32[]{:S(2)}, u32[]{:S(2)}) collective-permute-start(f32[3,1,8,128]{3,2,1,0:T(8,128)S(1)} %get-tuple-element.39), channel_id=1, source_target_pairs={{0,4},{4,8},{8,12},{12,16},{16,20},{20,24},{24,28},{28,32},{32,36}... | collective-permute-start | bytes 36872 | tf_op jit(solution)/shard_map/ppermute | solution.py:30
  46.5 8.8 %collective-permute-start.5 = (f32[3,1,8,128]{3,2,1,0:T(8,128)S(1)}, f32[3,1,8,128]{3,2,1,0:T(8,128)S(1)}, u32[]{:S(2)}, u32[]{:S(2)}) collective-permute-start(f32[3,1,8,128]{3,2,1,0:T(8,128)S(1)} %get-tuple-element.40), channel_id=1, source_target_pairs={{4,0},{8,4},{12,8},{16,12},{20,16},{24,20},{28,24},{32,28},{36,32}... | collective-permute-start | bytes 36872 | tf_op jit(solution)/shard_map/ppermute | solution.py:31
  56.1 2.9 %collective-permute-start.6 = (f32[3,4,1,128]{3,2,1,0:T(1,128)S(1)}, f32[3,4,1,128]{3,2,1,0:T(1,128)S(1)}, u32[]{:S(2)}, u32[]{:S(2)}) collective-permute-start(f32[3,4,1,128]{3,2,1,0:T(1,128)S(1)} %get-tuple-element.31), channel_id=1, source_target_pairs={{0,1},{1,2},{2,3},{4,5},{5,6},{6,7},{8,9},{9,10},{10,11},{12,13},{... | collective-permute-start | bytes 18440 | tf_op jit(solution)/shard_map/ppermute | solution.py:30
  59.0 2.1 %collective-permute-start.7 = (f32[3,4,1,128]{3,2,1,0:T(1,128)S(1)}, f32[3,4,1,128]{3,2,1,0:T(1,128)S(1)}, u32[]{:S(2)}, u32[]{:S(2)}) collective-permute-start(f32[3,4,1,128]{3,2,1,0:T(1,128)S(1)} %get-tuple-element.32), channel_id=1, source_target_pairs={{1,0},{2,1},{3,2},{5,4},{6,5},{7,6},{9,8},{10,9},{11,10},{13,12},{... | collective-permute-start | bytes 18440 | tf_op jit(solution)/shard_map/ppermute | solution.py:31
  61.1 1.4 pad_maximum_fusion.8.target_ref
  62.5 3.2 %collective-permute-done.7 = f32[3,4,1,128]{3,2,1,0:T(1,128)S(1)} collective-permute-done((f32[3,4,1,128]{3,2,1,0:T(1,128)S(1)}, f32[3,4,1,128]{3,2,1,0:T(1,128)S(1)}, u32[]{:S(2)}, u32[]{:S(2)}) %collective-permute-start.7) | collective-permute-done | bytes 6176 | tf_op jit(solution)/shard_map/ppermute | solution.py:31
  66.5 14.4 %shard_map.87 = (f32[4,16,128]{2,1,0:T(8,128)}, f32[144,128,128]{2,1,0:T(8,128)}) custom-call(f32[5,16,128]{2,1,0:T(8,128)} %pad_maximum_fusion.8.target_ref, f32[6,40,128]{2,1,0:T(8,128)} %copy.13.source_ref), custom_call_target="tpu_custom_call" | custom-call | tf_op jit(solution)/shard_map/pallas_call | solution.py:167
  80.9 0.9 fusion.24
  81.8 1.9 %collective-permute-start.8 = (f32[3,1,8,128]{3,2,1,0:T(8,128)S(1)}, f32[3,1,8,128]{3,2,1,0:T(8,128)S(1)}, u32[]{:S(2)}, u32[]{:S(2)}) collective-permute-start(f32[3,1,8,128]{3,2,1,0:T(8,128)S(1)} %get-tuple-element.37), channel_id=1, source_target_pairs={{0,4},{4,8},{8,12},{12,16},{16,20},{20,24},{24,28},{28,32},{32,36}... | collective-permute-start | bytes 36872 | tf_op jit(solution)/shard_map/ppermute | solution.py:30
  83.7 8.7 %collective-permute-start.9 = (f32[3,1,8,128]{3,2,1,0:T(8,128)S(1)}, f32[3,1,8,128]{3,2,1,0:T(8,128)S(1)}, u32[]{:S(2)}, u32[]{:S(2)}) collective-permute-start(f32[3,1,8,128]{3,2,1,0:T(8,128)S(1)} %get-tuple-element.38), channel_id=1, source_target_pairs={{4,0},{8,4},{12,8},{16,12},{20,16},{24,20},{28,24},{32,28},{36,32}... | collective-permute-start | bytes 36872 | tf_op jit(solution)/shard_map/ppermute | solution.py:31
  93.3 2.2 %collective-permute-start.10 = (f32[3,4,1,128]{3,2,1,0:T(1,128)S(1)}, f32[3,4,1,128]{3,2,1,0:T(1,128)S(1)}, u32[]{:S(2)}, u32[]{:S(2)}) collective-permute-start(f32[3,4,1,128]{3,2,1,0:T(1,128)S(1)} %get-tuple-element.29), channel_id=1, source_target_pairs={{0,1},{1,2},{2,3},{4,5},{5,6},{6,7},{8,9},{9,10},{10,11},{12,13},{... | collective-permute-start | bytes 18440 | tf_op jit(solution)/shard_map/ppermute | solution.py:30
  95.5 2.1 %collective-permute-start.11 = (f32[3,4,1,128]{3,2,1,0:T(1,128)S(1)}, f32[3,4,1,128]{3,2,1,0:T(1,128)S(1)}, u32[]{:S(2)}, u32[]{:S(2)}) collective-permute-start(f32[3,4,1,128]{3,2,1,0:T(1,128)S(1)} %get-tuple-element.30), channel_id=1, source_target_pairs={{1,0},{2,1},{3,2},{5,4},{6,5},{7,6},{9,8},{10,9},{11,10},{13,12},{... | collective-permute-start | bytes 18440 | tf_op jit(solution)/shard_map/ppermute | solution.py:31
  98.5 3.5 %collective-permute-done.11 = f32[3,4,1,128]{3,2,1,0:T(1,128)S(1)} collective-permute-done((f32[3,4,1,128]{3,2,1,0:T(1,128)S(1)}, f32[3,4,1,128]{3,2,1,0:T(1,128)S(1)}, u32[]{:S(2)}, u32[]{:S(2)}) %collective-permute-start.11) | collective-permute-done | bytes 6176 | tf_op jit(solution)/shard_map/ppermute | solution.py:31
  102.7 6.5 %shard_map.88 = f32[3,16,128]{2,1,0:T(8,128)} custom-call(f32[1,16,128]{2,1,0:T(8,128)} %copy-done.3, f32[3,40,128]{2,1,0:T(8,128)} %broadcast_multiply_fusion.1.source_ref, f32[144,128,128]{2,1,0:T(8,128)} %get-tuple-element.5.refs_0_), custom_call_target="tpu_custom_call" | custom-call | tf_op jit(solution)/shard_map/pallas_call | solution.py:175
  109.2 0.8 fusion.22
  110.0 1.9 %collective-permute-start.12 = (f32[3,1,8,128]{3,2,1,0:T(8,128)S(1)}, f32[3,1,8,128]{3,2,1,0:T(8,128)S(1)}, u32[]{:S(2)}, u32[]{:S(2)}) collective-permute-start(f32[3,1,8,128]{3,2,1,0:T(8,128)S(1)} %get-tuple-element.35), channel_id=1, source_target_pairs={{0,4},{4,8},{8,12},{12,16},{16,20},{20,24},{24,28},{28,32},{32,36}... | collective-permute-start | bytes 36872 | tf_op jit(solution)/shard_map/ppermute | solution.py:30
  111.9 8.7 %collective-permute-start.13 = (f32[3,1,8,128]{3,2,1,0:T(8,128)S(1)}, f32[3,1,8,128]{3,2,1,0:T(8,128)S(1)}, u32[]{:S(2)}, u32[]{:S(2)}) collective-permute-start(f32[3,1,8,128]{3,2,1,0:T(8,128)S(1)} %get-tuple-element.36), channel_id=1, source_target_pairs={{4,0},{8,4},{12,8},{16,12},{20,16},{24,20},{28,24},{32,28},{36,32}... | collective-permute-start | bytes 36872 | tf_op jit(solution)/shard_map/ppermute | solution.py:31
  121.5 2.2 %collective-permute-start.14 = (f32[3,4,1,128]{3,2,1,0:T(1,128)S(1)}, f32[3,4,1,128]{3,2,1,0:T(1,128)S(1)}, u32[]{:S(2)}, u32[]{:S(2)}) collective-permute-start(f32[3,4,1,128]{3,2,1,0:T(1,128)S(1)} %get-tuple-element.27), channel_id=1, source_target_pairs={{0,1},{1,2},{2,3},{4,5},{5,6},{6,7},{8,9},{9,10},{10,11},{12,13},{... | collective-permute-start | bytes 18440 | tf_op jit(solution)/shard_map/ppermute | solution.py:30
  123.7 2.1 %collective-permute-start.15 = (f32[3,4,1,128]{3,2,1,0:T(1,128)S(1)}, f32[3,4,1,128]{3,2,1,0:T(1,128)S(1)}, u32[]{:S(2)}, u32[]{:S(2)}) collective-permute-start(f32[3,4,1,128]{3,2,1,0:T(1,128)S(1)} %get-tuple-element.28), channel_id=1, source_target_pairs={{1,0},{2,1},{3,2},{5,4},{6,5},{7,6},{9,8},{10,9},{11,10},{13,12},{... | collective-permute-start | bytes 18440 | tf_op jit(solution)/shard_map/ppermute | solution.py:31
  125.8 4.3 %collective-permute-done.15 = f32[3,4,1,128]{3,2,1,0:T(1,128)S(1)} collective-permute-done((f32[3,4,1,128]{3,2,1,0:T(1,128)S(1)}, f32[3,4,1,128]{3,2,1,0:T(1,128)S(1)}, u32[]{:S(2)}, u32[]{:S(2)}) %collective-permute-start.15) | collective-permute-done | bytes 6176 | tf_op jit(solution)/shard_map/ppermute | solution.py:31
  130.8 6.5 %shard_map.89 = f32[3,16,128]{2,1,0:T(8,128)} custom-call(f32[1,16,128]{2,1,0:T(8,128)} %copy-done.3, f32[3,40,128]{2,1,0:T(8,128)} %broadcast_multiply_fusion.source_ref, f32[144,128,128]{2,1,0:T(8,128)} %get-tuple-element.5.refs_0_), custom_call_target="tpu_custom_call" | custom-call | tf_op jit(solution)/shard_map/pallas_call | solution.py:175
  138.2 1.9 %collective-permute-start.16 = (f32[8,8,128]{2,1,0:T(8,128)S(1)}, f32[8,8,128]{2,1,0:T(8,128)S(1)}, u32[]{:S(2)}, u32[]{:S(2)}) collective-permute-start(f32[8,8,128]{2,1,0:T(8,128)S(1)} %pad_maximum_fusion.9), channel_id=1, source_target_pairs={{0,4},{4,8},{8,12},{12,16},{16,20},{20,24},{24,28},{28,32},{32,36}... | collective-permute-start | bytes 98312 | tf_op jit(solution)/shard_map/ppermute | solution.py:39
  140.2 8.1 %collective-permute-done.16 = f32[8,8,128]{2,1,0:T(8,128)S(1)} collective-permute-done((f32[8,8,128]{2,1,0:T(8,128)S(1)}, f32[8,8,128]{2,1,0:T(8,128)S(1)}, u32[]{:S(2)}, u32[]{:S(2)}) %collective-permute-start.16) | collective-permute-done | bytes 32800 | tf_op jit(solution)/shard_map/ppermute | solution.py:39
  (90 shorter events, 14.7 us)
Async XLA Ops:
  0.6 108.5 %copy-start.5 = (f32[3]{0:T(128)S(1)}, f32[3]{0:T(128)}, u32[]{:S(2)}) copy-start(f32[3]{0:T(128)} %constant.56.clone) | copy-start | bytes 40
  0.6 120.0 %copy-start.4 = (s32[2,8]{1,0:T(2,128)S(1)}, s32[2,8]{1,0:T(2,128)}, u32[]{:S(2)}) copy-start(s32[2,8]{1,0:T(2,128)} %param.11) | copy-start | bytes 196
  0.7 108.5 %copy-start = (f32[3,2,8,128]{3,2,1,0:T(8,128)S(1)}, f32[3,2,8,128]{3,2,1,0:T(8,128)}, u32[]{:S(2)}) copy-start(f32[3,2,8,128]{3,2,1,0:T(8,128)} %param.8) | copy-start | bytes 73732
  0.7 120.0 %copy-start.6 = (s32[2,8]{1,0:T(2,128)S(1)}, s32[2,8]{1,0:T(2,128)}, u32[]{:S(2)}) copy-start(s32[2,8]{1,0:T(2,128)} %param.12) | copy-start | bytes 196
  2.2 11.8 %collective-permute-start = (f32[7,1,8,128]{3,2,1,0:T(8,128)S(1)}, f32[7,1,8,128]{3,2,1,0:T(8,128)S(1)}, u32[]{:S(2)}, u32[]{:S(2)}) collective-permute-start(f32[7,1,8,128]{3,2,1,0:T(8,128)S(1)} %get-tuple-element.19), channel_id=1, source_target_pairs={{0,4},{4,8},{8,12},{12,16},{16,20},{20,24},{24,28},{28,32},{32,36}... | collective-permute-start | bytes 86024 | tf_op jit(solution)/shard_map/ppermute | solution.py:30
  5.8 9.3 %collective-permute-start.1 = (f32[7,1,8,128]{3,2,1,0:T(8,128)S(1)}, f32[7,1,8,128]{3,2,1,0:T(8,128)S(1)}, u32[]{:S(2)}, u32[]{:S(2)}) collective-permute-start(f32[7,1,8,128]{3,2,1,0:T(8,128)S(1)} %get-tuple-element.20), channel_id=1, source_target_pairs={{4,0},{8,4},{12,8},{16,12},{20,16},{24,20},{28,24},{32,28},{36,32}... | collective-permute-start | bytes 86024 | tf_op jit(solution)/shard_map/ppermute | solution.py:31
  15.9 9.5 %collective-permute-start.2 = (f32[7,4,1,128]{3,2,1,0:T(1,128)S(1)}, f32[7,4,1,128]{3,2,1,0:T(1,128)S(1)}, u32[]{:S(2)}, u32[]{:S(2)}) collective-permute-start(f32[7,4,1,128]{3,2,1,0:T(1,128)S(1)} %get-tuple-element.14), channel_id=1, source_target_pairs={{0,1},{1,2},{2,3},{4,5},{5,6},{6,7},{8,9},{9,10},{10,11},{12,13},{... | collective-permute-start | bytes 43016 | tf_op jit(solution)/shard_map/ppermute | solution.py:30
  21.4 6.5 %collective-permute-start.3 = (f32[7,4,1,128]{3,2,1,0:T(1,128)S(1)}, f32[7,4,1,128]{3,2,1,0:T(1,128)S(1)}, u32[]{:S(2)}, u32[]{:S(2)}) collective-permute-start(f32[7,4,1,128]{3,2,1,0:T(1,128)S(1)} %get-tuple-element.15), channel_id=1, source_target_pairs={{1,0},{2,1},{3,2},{5,4},{6,5},{7,6},{9,8},{10,9},{11,10},{13,12},{... | collective-permute-start | bytes 43016 | tf_op jit(solution)/shard_map/ppermute | solution.py:31
  44.5 58.1 %copy-start.3 = (f32[1,16,128]{2,1,0:T(8,128)}, f32[1,16,128]{2,1,0:T(8,128)S(1)}, u32[]{:S(2)}) copy-start(f32[1,16,128]{2,1,0:T(8,128)S(1)} %get-tuple-element.34.target_ref) | copy-start | bytes 24580
  44.6 11.5 %collective-permute-start.4 = (f32[3,1,8,128]{3,2,1,0:T(8,128)S(1)}, f32[3,1,8,128]{3,2,1,0:T(8,128)S(1)}, u32[]{:S(2)}, u32[]{:S(2)}) collective-permute-start(f32[3,1,8,128]{3,2,1,0:T(8,128)S(1)} %get-tuple-element.39), channel_id=1, source_target_pairs={{0,4},{4,8},{8,12},{12,16},{16,20},{20,24},{24,28},{28,32},{32,36}... | collective-permute-start | bytes 36872 | tf_op jit(solution)/shard_map/ppermute | solution.py:30
  46.5 9.6 %collective-permute-start.5 = (f32[3,1,8,128]{3,2,1,0:T(8,128)S(1)}, f32[3,1,8,128]{3,2,1,0:T(8,128)S(1)}, u32[]{:S(2)}, u32[]{:S(2)}) collective-permute-start(f32[3,1,8,128]{3,2,1,0:T(8,128)S(1)} %get-tuple-element.40), channel_id=1, source_target_pairs={{4,0},{8,4},{12,8},{16,12},{20,16},{24,20},{28,24},{32,28},{36,32}... | collective-permute-start | bytes 36872 | tf_op jit(solution)/shard_map/ppermute | solution.py:31
  56.1 6.4 %collective-permute-start.6 = (f32[3,4,1,128]{3,2,1,0:T(1,128)S(1)}, f32[3,4,1,128]{3,2,1,0:T(1,128)S(1)}, u32[]{:S(2)}, u32[]{:S(2)}) collective-permute-start(f32[3,4,1,128]{3,2,1,0:T(1,128)S(1)} %get-tuple-element.31), channel_id=1, source_target_pairs={{0,1},{1,2},{2,3},{4,5},{5,6},{6,7},{8,9},{9,10},{10,11},{12,13},{... | collective-permute-start | bytes 18440 | tf_op jit(solution)/shard_map/ppermute | solution.py:30
  59.0 6.6 %collective-permute-start.7 = (f32[3,4,1,128]{3,2,1,0:T(1,128)S(1)}, f32[3,4,1,128]{3,2,1,0:T(1,128)S(1)}, u32[]{:S(2)}, u32[]{:S(2)}) collective-permute-start(f32[3,4,1,128]{3,2,1,0:T(1,128)S(1)} %get-tuple-element.32), channel_id=1, source_target_pairs={{1,0},{2,1},{3,2},{5,4},{6,5},{7,6},{9,8},{10,9},{11,10},{13,12},{... | collective-permute-start | bytes 18440 | tf_op jit(solution)/shard_map/ppermute | solution.py:31
  80.9 28.2 %copy-start.2 = (f32[4,16,128]{2,1,0:T(8,128)S(1)}, f32[4,16,128]{2,1,0:T(8,128)}, u32[]{:S(2)}) copy-start(f32[4,16,128]{2,1,0:T(8,128)} %get-tuple-element.4) | copy-start | bytes 98308
  81.8 10.7 %collective-permute-start.8 = (f32[3,1,8,128]{3,2,1,0:T(8,128)S(1)}, f32[3,1,8,128]{3,2,1,0:T(8,128)S(1)}, u32[]{:S(2)}, u32[]{:S(2)}) collective-permute-start(f32[3,1,8,128]{3,2,1,0:T(8,128)S(1)} %get-tuple-element.37), channel_id=1, source_target_pairs={{0,4},{4,8},{8,12},{12,16},{16,20},{20,24},{24,28},{28,32},{32,36}... | collective-permute-start | bytes 36872 | tf_op jit(solution)/shard_map/ppermute | solution.py:30
  83.7 9.6 %collective-permute-start.9 = (f32[3,1,8,128]{3,2,1,0:T(8,128)S(1)}, f32[3,1,8,128]{3,2,1,0:T(8,128)S(1)}, u32[]{:S(2)}, u32[]{:S(2)}) collective-permute-start(f32[3,1,8,128]{3,2,1,0:T(8,128)S(1)} %get-tuple-element.38), channel_id=1, source_target_pairs={{4,0},{8,4},{12,8},{16,12},{20,16},{24,20},{28,24},{32,28},{36,32}... | collective-permute-start | bytes 36872 | tf_op jit(solution)/shard_map/ppermute | solution.py:31
  93.3 5.2 %collective-permute-start.10 = (f32[3,4,1,128]{3,2,1,0:T(1,128)S(1)}, f32[3,4,1,128]{3,2,1,0:T(1,128)S(1)}, u32[]{:S(2)}, u32[]{:S(2)}) collective-permute-start(f32[3,4,1,128]{3,2,1,0:T(1,128)S(1)} %get-tuple-element.29), channel_id=1, source_target_pairs={{0,1},{1,2},{2,3},{4,5},{5,6},{6,7},{8,9},{9,10},{10,11},{12,13},{... | collective-permute-start | bytes 18440 | tf_op jit(solution)/shard_map/ppermute | solution.py:30
  95.5 6.5 %collective-permute-start.11 = (f32[3,4,1,128]{3,2,1,0:T(1,128)S(1)}, f32[3,4,1,128]{3,2,1,0:T(1,128)S(1)}, u32[]{:S(2)}, u32[]{:S(2)}) collective-permute-start(f32[3,4,1,128]{3,2,1,0:T(1,128)S(1)} %get-tuple-element.30), channel_id=1, source_target_pairs={{1,0},{2,1},{3,2},{5,4},{6,5},{7,6},{9,8},{10,9},{11,10},{13,12},{... | collective-permute-start | bytes 18440 | tf_op jit(solution)/shard_map/ppermute | solution.py:31
  102.7 34.6 %copy-start.1 = (f32[3,2,8,128]{3,2,1,0:T(8,128)S(1)}, f32[3,2,8,128]{3,2,1,0:T(8,128)}, u32[]{:S(2)}) copy-start(f32[3,2,8,128]{3,2,1,0:T(8,128)} %param.7) | copy-start | bytes 73732
  110.0 10.7 %collective-permute-start.12 = (f32[3,1,8,128]{3,2,1,0:T(8,128)S(1)}, f32[3,1,8,128]{3,2,1,0:T(8,128)S(1)}, u32[]{:S(2)}, u32[]{:S(2)}) collective-permute-start(f32[3,1,8,128]{3,2,1,0:T(8,128)S(1)} %get-tuple-element.35), channel_id=1, source_target_pairs={{0,4},{4,8},{8,12},{12,16},{16,20},{20,24},{24,28},{28,32},{32,36}... | collective-permute-start | bytes 36872 | tf_op jit(solution)/shard_map/ppermute | solution.py:30
  111.9 9.6 %collective-permute-start.13 = (f32[3,1,8,128]{3,2,1,0:T(8,128)S(1)}, f32[3,1,8,128]{3,2,1,0:T(8,128)S(1)}, u32[]{:S(2)}, u32[]{:S(2)}) collective-permute-start(f32[3,1,8,128]{3,2,1,0:T(8,128)S(1)} %get-tuple-element.36), channel_id=1, source_target_pairs={{4,0},{8,4},{12,8},{16,12},{20,16},{24,20},{28,24},{32,28},{36,32}... | collective-permute-start | bytes 36872 | tf_op jit(solution)/shard_map/ppermute | solution.py:31
  121.5 4.4 %collective-permute-start.14 = (f32[3,4,1,128]{3,2,1,0:T(1,128)S(1)}, f32[3,4,1,128]{3,2,1,0:T(1,128)S(1)}, u32[]{:S(2)}, u32[]{:S(2)}) collective-permute-start(f32[3,4,1,128]{3,2,1,0:T(1,128)S(1)} %get-tuple-element.27), channel_id=1, source_target_pairs={{0,1},{1,2},{2,3},{4,5},{5,6},{6,7},{8,9},{9,10},{10,11},{12,13},{... | collective-permute-start | bytes 18440 | tf_op jit(solution)/shard_map/ppermute | solution.py:30
  123.7 6.5 %collective-permute-start.15 = (f32[3,4,1,128]{3,2,1,0:T(1,128)S(1)}, f32[3,4,1,128]{3,2,1,0:T(1,128)S(1)}, u32[]{:S(2)}, u32[]{:S(2)}) collective-permute-start(f32[3,4,1,128]{3,2,1,0:T(1,128)S(1)} %get-tuple-element.28), channel_id=1, source_target_pairs={{1,0},{2,1},{3,2},{5,4},{6,5},{7,6},{9,8},{10,9},{11,10},{13,12},{... | collective-permute-start | bytes 18440 | tf_op jit(solution)/shard_map/ppermute | solution.py:31
  138.2 10.0 %collective-permute-start.16 = (f32[8,8,128]{2,1,0:T(8,128)S(1)}, f32[8,8,128]{2,1,0:T(8,128)S(1)}, u32[]{:S(2)}, u32[]{:S(2)}) collective-permute-start(f32[8,8,128]{2,1,0:T(8,128)S(1)} %pad_maximum_fusion.9), channel_id=1, source_target_pairs={{0,4},{4,8},{8,12},{12,16},{16,20},{20,24},{24,28},{28,32},{32,36}... | collective-permute-start | bytes 98312 | tf_op jit(solution)/shard_map/ppermute | solution.py:39
